TPU v7x, 32 devices: a whole 2x2x4 slice. The times are simulated.
32 devices in a mesh: gx: 4 (over y, x), gy: 8 (over z, core).
Axes of the slice: x: 2, y: 2, z: 4, core: 2. Of those that a mesh axis runs over, the one named last changes fastest.
Arguments:
- load_vector: float32 [112, 50176], P('gx', 'gy'), may hold values from -6 to 6
- initial_guess: float32 [112, 50176], P('gx', 'gy'), may hold values from -3 to 3
Outputs:
- smoothed: float32 [112, 50176], P('gx', 'gy')
- level_three: float32 [48, 9216], P('gx', 'gy')
- coarse_err: float32 [16, 1024], P('gx', 'gy')
All inputs are finite; a program needn't handle non-finite values.
Results may differ from a plain program's by a relative error of at most 0.0003.
Values sent between devices are 32-bit elements; how exact they have to be, the bound alone decides.
No kernel may reach another device: no remote copies, remote signals or barrier semaphores. Data moves between devices by JAX's collectives and lax.ppermute only.
A program may use at most 192 MiB of HBM per device.

v0:
```python
import math

import jax
import jax.numpy as jnp
import numpy as np
from jax import lax
from jax.sharding import PartitionSpec as P

EZ = 32
JAC = 4


highest = lax.Precision.HIGHEST
points_seven = (
    -1.0,
    -0.8717401485096066,
    -0.5917001814331423,
    -0.2092992179024789,
    0.2092992179024789,
    0.5917001814331423,
    0.8717401485096066,
    1.0,
)
points_three = (-1.0, -0.4472135954999579, 0.4472135954999579, 1.0)
points_one = (-1.0, 1.0)
damping = 2.0 / 3.0


def extended_2(array, sides, width):
    for axis, dim in sides:
        devices, length = (lax.axis_size(axis), array.shape[dim])
        up = [(i, (i + 1) % devices) for i in range(devices - 1)]
        down = [(j, i) for i, j in up]
        last = lax.slice_in_dim(array, length - width, length, axis=dim)
        first = lax.slice_in_dim(array, 0, width, axis=dim)
        before = lax.ppermute(last, axis, up)
        after = lax.ppermute(first, axis, down)
        array = jnp.concatenate([before, array, after], axis=dim)
    return array


def shifted(array, axis, by):
    devices = lax.axis_size(axis)
    pairs = [(i, i + by) for i in range(devices) if 0 <= i + by < devices]
    return lax.ppermute(array, axis, pairs)


def legendre_at(degree, location):
    previous, current = (1.0, location)
    for level_idx in range(1, degree):
        previous, current = (
            current,
            ((2 * level_idx + 1) * location * current - level_idx * previous) / (level_idx + 1),
        )
    return current


def quadrature_weights():
    return np.array([2.0 / (56.0 * legendre_at(7, x) * legendre_at(7, x)) for x in points_seven])


def derivative_matrix():
    points = np.array(points_seven)
    products = np.array(
        [np.prod([points[i] - points[k] for k in range(8) if k != i]) for i in range(8)]
    )
    result = np.zeros((8, 8))
    for i in range(8):
        for j in range(8):
            if i != j:
                result[i, j] = products[i] / (products[j] * (points[i] - points[j]))
        result[i, i] = np.sum([1.0 / (points[i] - points[k]) for k in range(8) if k != i])
    return result


def element_stiffness():
    derivative = derivative_matrix()
    return derivative.T @ (quadrature_weights()[:, None] * derivative)


def assemble_line(elements):
    stiffness = element_stiffness()
    weights = quadrature_weights()
    extent = 7 * elements + 1
    global_stiff = np.zeros((extent, extent))
    lumped = np.zeros(extent)
    for m in range(elements):
        global_stiff[7 * m : 7 * m + 8, 7 * m : 7 * m + 8] += stiffness
        lumped[7 * m : 7 * m + 8] += weights
    return (global_stiff, lumped)


def jacobi_eigen(matrix):
    rotated_mat = matrix.copy()
    extent = matrix.shape[0]
    vectors = np.eye(extent)
    for sweep_idx in range(12):
        for p in range(extent - 1):
            for q in range(p + 1, extent):
                angle_rot = 0.5 * math.atan2(
                    2.0 * float(rotated_mat[p, q]), float(rotated_mat[q, q] - rotated_mat[p, p])
                )
                rotation = np.eye(extent)
                rotation[p, p] = math.cos(angle_rot)
                rotation[q, q] = math.cos(angle_rot)
                rotation[p, q] = math.sin(angle_rot)
                rotation[q, p] = -math.sin(angle_rot)
                rotated_mat = rotation.T @ rotated_mat @ rotation
                vectors = vectors @ rotation
    return (np.array([rotated_mat[i, i] for i in range(extent)]), vectors)


def patch_basis():
    global_stiff, lumped = assemble_line(2)
    inv_root = 1.0 / np.sqrt(lumped[1:14])
    eigvals, vectors = jacobi_eigen(
        inv_root[:, None] * global_stiff[1:14, 1:14] * inv_root[None, :]
    )
    return (eigvals, inv_root[:, None] * vectors)


def interp_matrix(coarse_pts):
    result = np.ones((8, len(coarse_pts)))
    for a in range(8):
        for c in range(len(coarse_pts)):
            for k in range(len(coarse_pts)):
                if k != c:
                    result[a, c] *= (points_seven[a] - coarse_pts[k]) / (
                        coarse_pts[c] - coarse_pts[k]
                    )
    return result


def restriction_rows(coarse_pts):
    shared = np.ones(8)
    shared[0] = 0.5
    shared[7] = 0.5
    return (interp_matrix(coarse_pts) * shared[:, None]).T


def restriction_line(elements, coarse_pts):
    degree = len(coarse_pts) - 1
    rows_mat = restriction_rows(coarse_pts)
    result = np.zeros((degree * elements + 1, 7 * elements + 1))
    for m in range(elements):
        result[degree * m : degree * m + degree + 1, 7 * m : 7 * m + 8] += rows_mat
    return result


def patch_matrix(eigbasis, vertices, extent):
    result = np.zeros((13 * vertices, extent))
    for b in range(13):
        for v in range(vertices):
            for a in range(13):
                node_idx = 7 * v + a
                result[b * vertices + v, node_idx] = eigbasis[a, b]
    return result


def live_line(device_idx, stride, extent, offset, limit_total):
    position = device_idx * stride + jnp.arange(extent, dtype=jnp.int32) + offset
    return ((position >= 1) & (position < limit_total)).astype(jnp.float32)


def residual_rows(extended, x_elems, y_elems, z_elems, mask_ext):
    x_nodes, y_nodes, z_nodes = (7 * x_elems, 7 * y_elems, 7 * z_elems)
    stiff_x, lumped_x = assemble_line(x_elems + 2)
    stiff_y, lumped_y = assemble_line(y_elems + 2)
    stiff_z, lumped_z = assemble_line(z_elems)
    matrix_x = jnp.asarray(stiff_x[1 : x_nodes + 14], jnp.float32)
    matrix_y = jnp.asarray(stiff_y[1 : y_nodes + 14], jnp.float32)
    matrix_z = jnp.asarray(stiff_z[:z_nodes], jnp.float32)
    mass_x = jnp.asarray(lumped_x[1 : x_nodes + 14], jnp.float32)
    mass_y = jnp.asarray(lumped_y[1 : y_nodes + 14], jnp.float32)
    mass_z = jnp.asarray(lumped_z[:z_nodes], jnp.float32)
    field_win = jnp.pad(
        extended[0, 1 : x_nodes + 16, 1 : y_nodes + 16, :], ((0, 0), (0, 0), (0, 1))
    )
    term_x = (
        jnp.einsum("an,nbz->abz", matrix_x, field_win[:, 1:-1, :z_nodes], precision=highest)
        * (mass_y[:, None] * mass_z[None, :])[None, :, :]
    )
    term_y = (
        jnp.einsum("bn,anz->abz", matrix_y, field_win[1:-1, :, :z_nodes], precision=highest)
        * (mass_x[:, None] * mass_z[None, :])[:, None, :]
    )
    term_z = (
        jnp.einsum("zn,abn->abz", matrix_z, field_win[1:-1, 1:-1, :], precision=highest)
        * (mass_x[:, None] * mass_y[None, :])[:, :, None]
    )
    force_ext = extended[1, 2 : x_nodes + 15, 2 : y_nodes + 15, :]
    return (force_ext - term_x - term_y - term_z) * mask_ext


def local(load_vector, initial_guess):
    z_nodes = 7 * EZ
    x_nodes = load_vector.shape[0]
    y_nodes = load_vector.shape[1] // z_nodes
    load_vector = load_vector.reshape(x_nodes, y_nodes, z_nodes)
    initial_guess = initial_guess.reshape(x_nodes, y_nodes, z_nodes)
    x_elems, y_elems, z_elems = (x_nodes // 7, y_nodes // 7, z_nodes // 7)
    gx_idx = lax.axis_index("gx")
    gy_idx = lax.axis_index("gy")
    gx_count = lax.axis_size("gx")
    gy_count = lax.axis_size("gy")
    z_live = (jnp.arange(z_nodes, dtype=jnp.int32) >= 1).astype(jnp.float32)
    mask_own = (
        live_line(gx_idx, x_nodes, x_nodes, 0, x_nodes * gx_count)[:, None, None]
        * live_line(gy_idx, y_nodes, y_nodes, 0, y_nodes * gy_count)[None, :, None]
        * z_live[None, None, :]
    )
    mask_ext = (
        live_line(gx_idx, x_nodes, x_nodes + 13, -6, x_nodes * gx_count)[:, None, None]
        * live_line(gy_idx, y_nodes, y_nodes + 13, -6, y_nodes * gy_count)[None, :, None]
        * z_live[None, None, :]
    )
    start_field = initial_guess * mask_own
    force_field = load_vector * mask_own
    first_rims = extended_2(jnp.stack([start_field, force_field]), (("gx", 1), ("gy", 2)), 8)
    residual = residual_rows(first_rims, x_elems, y_elems, z_elems, mask_ext)
    eigvals, eigbasis = patch_basis()
    inverse = jnp.asarray(
        1.0 / (eigvals[:, None, None] + eigvals[None, :, None] + eigvals[None, None, :]),
        jnp.float32,
    )
    vert_x, vert_y = (x_elems, y_elems)
    fwd_x = jnp.asarray(patch_matrix(eigbasis, vert_x, x_nodes + 13), jnp.float32)
    fwd_y = jnp.asarray(patch_matrix(eigbasis, vert_y, y_nodes + 13), jnp.float32)
    z_block_len = min(z_elems, 8)
    fwd_z = jnp.asarray(patch_matrix(eigbasis, z_block_len, 7 * z_block_len + 12), jnp.float32)
    active_x = live_line(gx_idx, x_elems, vert_x, 0, x_elems * gx_count)
    active_y = live_line(gy_idx, y_elems, vert_y, 0, y_elems * gy_count)
    factor_xy = (
        inverse[:, None, :, None, :, None]
        * active_x[None, :, None, None, None, None]
        * active_y[None, None, None, :, None, None]
    )
    section_x = jnp.einsum("pn,nyz->pyz", fwd_x, residual, precision=highest)
    section_y = jnp.einsum("qn,pnz->pqz", fwd_y, section_x, precision=highest)
    section_pad = jnp.pad(section_y, ((0, 0), (0, 0), (6, 6)))

    def z_block(accum_z, block_idx):
        offset_z = block_idx * (7 * z_block_len)
        segment = lax.dynamic_slice_in_dim(section_pad, offset_z, 7 * z_block_len + 12, 2)
        spectral = jnp.einsum("sn,pqn->pqs", fwd_z, segment, precision=highest)
        active_z = (block_idx * z_block_len + jnp.arange(z_block_len, dtype=jnp.int32) >= 1).astype(
            jnp.float32
        )
        factor = (factor_xy * active_z).reshape(13 * vert_x, 13 * vert_y, 13 * z_block_len)
        returned = jnp.einsum("sn,pqs->pqn", fwd_z, spectral * factor, precision=highest)
        current = lax.dynamic_slice_in_dim(accum_z, offset_z, 7 * z_block_len + 12, 2)
        return (lax.dynamic_update_slice_in_dim(accum_z, current + returned, offset_z, 2), None)

    accum_z, unused_out = lax.scan(
        z_block,
        jnp.zeros((13 * vert_x, 13 * vert_y, z_nodes + 12), jnp.float32),
        jnp.arange(z_elems // z_block_len, dtype=jnp.int32),
    )
    spectral_back = accum_z[:, :, 6 : 6 + z_nodes]
    correction = jnp.einsum(
        "pn,pqz->nqz", fwd_x[:, : x_nodes + 6], spectral_back, precision=highest
    )
    correction = jnp.einsum("qm,nqz->nmz", fwd_y[:, : y_nodes + 6], correction, precision=highest)
    received = shifted(correction[:, :6, :], "gy", -1)
    correction = jnp.concatenate(
        [correction[:, 6:y_nodes, :], correction[:, y_nodes:, :] + received], 1
    )
    received = shifted(correction[:6], "gx", -1)
    correction = jnp.concatenate([correction[6:x_nodes], correction[x_nodes:] + received], 0)
    weight_x = jnp.asarray(np.where(np.arange(x_nodes) % 7 == 0, 1.0, 0.5), jnp.float32)
    weight_y = jnp.asarray(np.where(np.arange(y_nodes) % 7 == 0, 1.0, 0.5), jnp.float32)
    weight_z = jnp.asarray(np.where(np.arange(z_nodes) % 7 == 0, 1.0, 0.5), jnp.float32)
    node_weight = weight_x[:, None, None] * weight_y[None, :, None] * weight_z[None, None, :]
    smoothed = (start_field + node_weight * correction) * mask_own
    smooth_ext = extended_2(smoothed, (("gx", 0), ("gy", 1)), 8)
    extended = jnp.stack([smooth_ext, first_rims[1]])
    resid_after = residual_rows(extended, x_elems, y_elems, z_elems, mask_ext)[
        6 : x_nodes + 7, 6 : y_nodes + 7, :
    ]
    restrict_x = jnp.asarray(restriction_line(x_elems, points_three), jnp.float32)
    restrict_y = jnp.asarray(restriction_line(y_elems, points_three), jnp.float32)
    restrict_z = jnp.asarray(
        restriction_line(z_elems, points_three)[: 3 * z_elems, :z_nodes], jnp.float32
    )
    level_three = jnp.einsum("in,nyz->iyz", restrict_x, resid_after, precision=highest)
    level_three = jnp.einsum("jy,iyz->ijz", restrict_y, level_three, precision=highest)
    level_three = jnp.einsum("kz,ijz->ijk", restrict_z, level_three, precision=highest)
    linear_x = jnp.asarray(restriction_line(x_elems, points_one), jnp.float32)
    linear_y = jnp.asarray(restriction_line(y_elems, points_one), jnp.float32)
    linear_z = jnp.asarray(restriction_line(z_elems, points_one)[:z_elems, :z_nodes], jnp.float32)
    level_one = jnp.einsum("in,nyz->iyz", linear_x, resid_after, precision=highest)
    level_one = jnp.einsum("jy,iyz->ijz", linear_y, level_one, precision=highest)
    level_one = jnp.einsum("kz,ijz->ijk", linear_z, level_one, precision=highest)
    packed = jnp.concatenate([level_three[:, -1, :].reshape(-1), level_one[:, -1, :].reshape(-1)])
    received = shifted(packed, "gy", 1)
    split_at = level_three.shape[0] * level_three.shape[2]
    recv_three = received[:split_at].reshape(level_three.shape[0], 1, level_three.shape[2])
    recv_one = received[split_at:].reshape(level_one.shape[0], 1, level_one.shape[2])
    level_three = jnp.concatenate([level_three[:, :1, :] + recv_three, level_three[:, 1:-1, :]], 1)
    level_one = jnp.concatenate([level_one[:, :1, :] + recv_one, level_one[:, 1:-1, :]], 1)
    packed = jnp.concatenate([level_three[-1].reshape(-1), level_one[-1].reshape(-1)])
    received = shifted(packed, "gx", 1)
    split_at = level_three.shape[1] * level_three.shape[2]
    recv_three = received[:split_at].reshape(1, level_three.shape[1], level_three.shape[2])
    recv_one = received[split_at:].reshape(1, level_one.shape[1], level_one.shape[2])
    level_three = jnp.concatenate([level_three[:1] + recv_three, level_three[1:-1]], 0)
    level_one = jnp.concatenate([level_one[:1] + recv_one, level_one[1:-1]], 0)
    z_three = (jnp.arange(3 * z_elems, dtype=jnp.int32) >= 1).astype(jnp.float32)
    mask_three = (
        live_line(gx_idx, 3 * x_elems, 3 * x_elems, 0, 3 * x_elems * gx_count)[:, None, None]
        * live_line(gy_idx, 3 * y_elems, 3 * y_elems, 0, 3 * y_elems * gy_count)[None, :, None]
        * z_three[None, None, :]
    )
    level_three = level_three * mask_three
    z_one = (jnp.arange(z_elems, dtype=jnp.int32) >= 1).astype(jnp.float32)
    mask_one = (
        live_line(gx_idx, x_elems, x_elems, 0, x_elems * gx_count)[:, None, None]
        * live_line(gy_idx, y_elems, y_elems, 0, y_elems * gy_count)[None, :, None]
        * z_one[None, None, :]
    )
    level_one = level_one * mask_one
    coarse_err = jnp.zeros_like(level_one)
    for sweep_idx in range(JAC):
        beside_all = extended_2(coarse_err, (("gx", 0), ("gy", 1)), 1)
        above_z = jnp.pad(coarse_err, ((0, 0), (0, 0), (0, 1)))[:, :, 1:]
        below_z = jnp.pad(coarse_err, ((0, 0), (0, 0), (1, 0)))[:, :, :-1]
        neighbours = (
            beside_all[2:, 1:-1]
            + beside_all[:-2, 1:-1]
            + beside_all[1:-1, 2:]
            + beside_all[1:-1, :-2]
            + above_z
            + below_z
        )
        applied = 12.0 * coarse_err - 2.0 * neighbours
        coarse_err = (coarse_err + damping / 12.0 * (level_one - applied)) * mask_one
    return (
        smoothed.reshape(x_nodes, -1),
        level_three.reshape(level_three.shape[0], -1),
        coarse_err.reshape(coarse_err.shape[0], -1),
    )


def solution(mesh):
    in_specs = (P("gx", "gy"), P("gx", "gy"))
    out_specs = (P("gx", "gy"), P("gx", "gy"), P("gx", "gy"))
    return jax.shard_map(local, mesh=mesh, in_specs=in_specs, out_specs=out_specs, check_vma=False)
```

profile of v0, /device:TPU:20, one launch (start us, length us, event | category | flops | bytes accessed | tf_op | source)
XLA Modules:
  0.0 394.1 jit_solution(11549449168154314369)
XLA Ops:
  1.2 3.3 collective-permute-start.12
  4.6 3.1 collective-permute-start.13
  15.4 4.8 %collective-permute-start.1 = (f32[2,8,28,224]{3,2,1,0:T(8,128)S(1)}, f32[2,8,28,224]{3,2,1,0:T(8,128)S(1)}, u32[]{:S(2)}, u32[]{:S(2)}) collective-permute-start(f32[2,8,28,224]{3,2,1,0:T(8,128)S(1)} %get-tuple-element.87), channel_id=1, source_target_pairs={{8,0},{16,8},{24,16},{9,1},{17,9},{25,17},{10,2},{18,10},{26,18},{... | collective-permute-start | bytes 1204232 | tf_op jit(solution)/shard_map/ppermute | solution.py:37
  20.5 10.9 %collective-permute-done = f32[2,8,28,224]{3,2,1,0:T(8,128)S(1)} collective-permute-done((f32[2,8,28,224]{3,2,1,0:T(8,128)}, f32[2,8,28,224]{3,2,1,0:T(8,128)S(1)}, u32[]{:S(2)}, u32[]{:S(2)}) %collective-permute-start) | collective-permute-done | bytes 401440 | tf_op jit(solution)/shard_map/ppermute | solution.py:36
  31.4 6.4 %collective-permute-done.1 = f32[2,8,28,224]{3,2,1,0:T(8,128)S(1)} collective-permute-done((f32[2,8,28,224]{3,2,1,0:T(8,128)S(1)}, f32[2,8,28,224]{3,2,1,0:T(8,128)S(1)}, u32[]{:S(2)}, u32[]{:S(2)}) %collective-permute-start.1) | collective-permute-done | bytes 401440 | tf_op jit(solution)/shard_map/ppermute | solution.py:37
  40.9 3.6 collective-permute-start.3
  47.3 4.6 %collective-permute-done.2 = f32[2,44,8,224]{3,2,1,0:T(8,128)} collective-permute-done((f32[2,44,8,224]{3,2,1,0:T(8,128)}, f32[2,44,8,224]{3,2,1,0:T(8,128)}, u32[]{:S(2)}, u32[]{:S(2)}) %collective-permute-start.2) | collective-permute-done | bytes 630816 | tf_op jit(solution)/shard_map/ppermute | solution.py:36
  59.1 3.1 fusion.25
  66.0 4.5 %fusion.19 = f32[52,41,224]{2,0,1:T(8,128)S(1)} fusion(f32[52,41,1]{1,0,2:T(8,128)S(1)} %copy-done.18, f32[41,224,41]{1,2,0:T(8,128)S(1)} %fusion.16, f32[41,41,224]{2,1,0:T(8,128)S(1)} %bitcast_subtract_fusion.1, f32[41,41,224]{2,0,1:T(8,128)S(1)} %fusion.23, f32[41,41]{0,1:T(8,128)S(1)} %broadcast_multiply_fusion.5, ...), kind=kOutput, calls=%fused_computation.29 | convolution fusion | flops 237222720 | bytes 6488408 | tf_op jit(solution)/shard_map/pn,nyz->pyz/dot_general | solution.py:238
  70.5 3.6 fusion.34
  78.4 174.9 %while.12 = (s32[]{:T(128)}, f32[52,52,236]{2,1,0:T(8,128)}, s32[4]{0:T(128)S(1)}, f32[52,52,236]{2,1,0:T(8,128)}, f32[4]{0:T(128)S(1)}, /*index=5*/f32[13,4,13,...) while((s32[]{:T(128)}, f32[52,52,236]{2,1,0:T(8,128)}, ...), condition=%wide.region_1.2_spmd.clone.clone, body=%wide.region_0.1_spmd.sunk.clone.clone.sunk | while | flops 459725984 | bytes 11556971 | solution.py:254
  79.6 3.2 fusion.133
  83.9 8.0 %mul.953 = f32[13,4,13,4,13,8]{5,4,3,2,1,0:T(8,128)} broadcast(f32[13,4,13,4,13]{4,3,2,1,0:T(4,128)S(1)} %multiply_bitcast_fusion.3), dimensions={0,1,2,3,4} | broadcast | bytes 1265472 | tf_op jit(solution)/shard_map/while/body/eval_jaxpr/mul | solution.py:249
  91.9 14.0 %mul.954 = f32[52,52,104]{2,1,0:T(8,128)S(1)} reshape(f32[13,4,13,4,13,8]{5,4,3,2,1,0:T(8,128)} %mul.953) | data formatting | bytes 2249728 | tf_op jit(solution)/shard_map/while/body/eval_jaxpr/mul | solution.py:249
  105.9 4.3 %dynamic-slice_add_fusion.2 = f32[52,52,68]{2,1,0:T(8,128)} fusion(f32[52,52,236]{2,1,0:T(8,128)} %get-tuple-element.166, s32[]{:T(128)S(6)} %select_n.9, f32[104,68,1]{0,1,2:T(8,128)S(1)} %get-tuple-element.187, f32[52,52,104]{2,1,0:T(8,128)S(1)} %fusion.133, f32[52,52,104]{2,1,0:T(8,128)S(1)} %mul.954, f32[104]{0:T(128)S(1)} %mul.957), kind=kOutput, calls=%fused_computation.6.clone.1 | convolution fusion | flops 230218560 | bytes 3749412 | tf_op jit(solution)/shard_map/while/body/eval_jaxpr/sn,pqs->pqn/dot_general | solution.py:250
  110.2 8.8 %dynamic_update_slice.7 = f32[52,52,236]{2,1,0:T(8,128)} dynamic-update-slice(f32[52,52,236]{2,1,0:T(8,128)} %get-tuple-element.166, f32[52,52,68]{2,1,0:T(8,128)} %dynamic-slice_add_fusion.2, s32[]{:T(128)} %constant.20.clone.1..sunk, s32[]{:T(128)} %constant.20.clone.1..sunk, s32[]{:T(128)S(6)} %select_n.9) | dynamic-update-slice | bytes 1470980 | tf_op jit(solution)/shard_map/while/body/eval_jaxpr/dynamic_update_slice | solution.py:252
  120.3 3.2 fusion.133
  124.6 8.0 %mul.953 = f32[13,4,13,4,13,8]{5,4,3,2,1,0:T(8,128)} broadcast(f32[13,4,13,4,13]{4,3,2,1,0:T(4,128)S(1)} %multiply_bitcast_fusion.3), dimensions={0,1,2,3,4} | broadcast | bytes 1265472 | tf_op jit(solution)/shard_map/while/body/eval_jaxpr/mul | solution.py:249
  132.6 14.0 %mul.954 = f32[52,52,104]{2,1,0:T(8,128)S(1)} reshape(f32[13,4,13,4,13,8]{5,4,3,2,1,0:T(8,128)} %mul.953) | data formatting | bytes 2249728 | tf_op jit(solution)/shard_map/while/body/eval_jaxpr/mul | solution.py:249
  146.6 4.3 %dynamic-slice_add_fusion.2 = f32[52,52,68]{2,1,0:T(8,128)} fusion(f32[52,52,236]{2,1,0:T(8,128)} %get-tuple-element.166, s32[]{:T(128)S(6)} %select_n.9, f32[104,68,1]{0,1,2:T(8,128)S(1)} %get-tuple-element.187, f32[52,52,104]{2,1,0:T(8,128)S(1)} %fusion.133, f32[52,52,104]{2,1,0:T(8,128)S(1)} %mul.954, f32[104]{0:T(128)S(1)} %mul.957), kind=kOutput, calls=%fused_computation.6.clone.1 | convolution fusion | flops 230218560 | bytes 3749412 | tf_op jit(solution)/shard_map/while/body/eval_jaxpr/sn,pqs->pqn/dot_general | solution.py:250
  150.9 13.3 %dynamic_update_slice.7 = f32[52,52,236]{2,1,0:T(8,128)} dynamic-update-slice(f32[52,52,236]{2,1,0:T(8,128)} %get-tuple-element.166, f32[52,52,68]{2,1,0:T(8,128)} %dynamic-slice_add_fusion.2, s32[]{:T(128)} %constant.20.clone.1..sunk, s32[]{:T(128)} %constant.20.clone.1..sunk, s32[]{:T(128)S(6)} %select_n.9) | dynamic-update-slice | bytes 1470980 | tf_op jit(solution)/shard_map/while/body/eval_jaxpr/dynamic_update_slice | solution.py:252
  165.5 3.2 fusion.133
  169.8 8.0 %mul.953 = f32[13,4,13,4,13,8]{5,4,3,2,1,0:T(8,128)} broadcast(f32[13,4,13,4,13]{4,3,2,1,0:T(4,128)S(1)} %multiply_bitcast_fusion.3), dimensions={0,1,2,3,4} | broadcast | bytes 1265472 | tf_op jit(solution)/shard_map/while/body/eval_jaxpr/mul | solution.py:249
  177.8 14.0 %mul.954 = f32[52,52,104]{2,1,0:T(8,128)S(1)} reshape(f32[13,4,13,4,13,8]{5,4,3,2,1,0:T(8,128)} %mul.953) | data formatting | bytes 2249728 | tf_op jit(solution)/shard_map/while/body/eval_jaxpr/mul | solution.py:249
  191.7 4.3 %dynamic-slice_add_fusion.2 = f32[52,52,68]{2,1,0:T(8,128)} fusion(f32[52,52,236]{2,1,0:T(8,128)} %get-tuple-element.166, s32[]{:T(128)S(6)} %select_n.9, f32[104,68,1]{0,1,2:T(8,128)S(1)} %get-tuple-element.187, f32[52,52,104]{2,1,0:T(8,128)S(1)} %fusion.133, f32[52,52,104]{2,1,0:T(8,128)S(1)} %mul.954, f32[104]{0:T(128)S(1)} %mul.957), kind=kOutput, calls=%fused_computation.6.clone.1 | convolution fusion | flops 230218560 | bytes 3749412 | tf_op jit(solution)/shard_map/while/body/eval_jaxpr/sn,pqs->pqn/dot_general | solution.py:250
  196.1 13.3 %dynamic_update_slice.7 = f32[52,52,236]{2,1,0:T(8,128)} dynamic-update-slice(f32[52,52,236]{2,1,0:T(8,128)} %get-tuple-element.166, f32[52,52,68]{2,1,0:T(8,128)} %dynamic-slice_add_fusion.2, s32[]{:T(128)} %constant.20.clone.1..sunk, s32[]{:T(128)} %constant.20.clone.1..sunk, s32[]{:T(128)S(6)} %select_n.9) | dynamic-update-slice | bytes 1470980 | tf_op jit(solution)/shard_map/while/body/eval_jaxpr/dynamic_update_slice | solution.py:252
  210.6 2.8 fusion.133
  214.5 8.0 %mul.953 = f32[13,4,13,4,13,8]{5,4,3,2,1,0:T(8,128)} broadcast(f32[13,4,13,4,13]{4,3,2,1,0:T(4,128)S(1)} %multiply_bitcast_fusion.3), dimensions={0,1,2,3,4} | broadcast | bytes 1265472 | tf_op jit(solution)/shard_map/while/body/eval_jaxpr/mul | solution.py:249
  222.5 14.0 %mul.954 = f32[52,52,104]{2,1,0:T(8,128)S(1)} reshape(f32[13,4,13,4,13,8]{5,4,3,2,1,0:T(8,128)} %mul.953) | data formatting | bytes 2249728 | tf_op jit(solution)/shard_map/while/body/eval_jaxpr/mul | solution.py:249
  236.4 3.9 dynamic-slice_add_fusion.2
  240.3 12.5 %dynamic_update_slice.7 = f32[52,52,236]{2,1,0:T(8,128)} dynamic-update-slice(f32[52,52,236]{2,1,0:T(8,128)} %get-tuple-element.166, f32[52,52,68]{2,1,0:T(8,128)} %dynamic-slice_add_fusion.2, s32[]{:T(128)} %constant.20.clone.1..sunk, s32[]{:T(128)} %constant.20.clone.1..sunk, s32[]{:T(128)S(6)} %select_n.9) | dynamic-update-slice | bytes 1470980 | tf_op jit(solution)/shard_map/while/body/eval_jaxpr/dynamic_update_slice | solution.py:252
  253.3 2.7 slice.300
  256.0 2.8 fusion.11
  260.9 4.0 %collective-permute-start.4 = (f32[34,6,224]{2,1,0:T(8,128)S(1)}, f32[34,6,224]{2,1,0:T(8,128)S(1)}, u32[]{:S(2)}, u32[]{:S(2)}) collective-permute-start(f32[34,6,224]{2,1,0:T(8,128)S(1)} %slice.379), channel_id=1, source_target_pairs={{1,0},{2,1},{3,2},{4,3},{5,4},{6,5},{7,6},{9,8},{10,9},{11,10},{12... | collective-permute-start | bytes 548360 | tf_op jit(solution)/shard_map/ppermute | solution.py:45
  265.0 3.9 collective-permute-done.4
  269.0 5.3 %collective-permute-start.5 = (f32[6,28,224]{2,1,0:T(8,128)S(1)}, f32[6,28,224]{2,1,0:T(8,128)S(1)}, u32[]{:S(2)}, u32[]{:S(2)}) collective-permute-start(f32[6,28,224]{2,1,0:T(8,128)S(1)} %pad_maximum_fusion.10), channel_id=1, source_target_pairs={{8,0},{16,8},{24,16},{9,1},{17,9},{25,17},{10,2},{18,10},{26,18},{... | collective-permute-start | bytes 451592 | tf_op jit(solution)/shard_map/ppermute | solution.py:45
  281.1 5.3 %collective-permute-start.7 = (f32[8,28,224]{2,1,0:T(8,128)S(1)}, f32[8,28,224]{2,1,0:T(8,128)S(1)}, u32[]{:S(2)}, u32[]{:S(2)}) collective-permute-start(f32[8,28,224]{2,1,0:T(8,128)S(1)} %get-tuple-element.91), channel_id=1, source_target_pairs={{8,0},{16,8},{24,16},{9,1},{17,9},{25,17},{10,2},{18,10},{26,18},{... | collective-permute-start | bytes 602120 | tf_op jit(solution)/shard_map/ppermute | solution.py:37
  287.1 4.5 %collective-permute-done.6 = f32[8,28,224]{2,1,0:T(8,128)S(1)} collective-permute-done((f32[8,28,224]{2,1,0:T(8,128)S(1)}, f32[8,28,224]{2,1,0:T(8,128)S(1)}, u32[]{:S(2)}, u32[]{:S(2)}) %collective-permute-start.6) | collective-permute-done | bytes 200736 | tf_op jit(solution)/shard_map/ppermute | solution.py:36
  295.5 3.4 collective-permute-start.9
  306.9 3.1 multiply_bitcast_fusion.1
  310.0 2.6 fusion.21
  321.5 2.6 collective-permute-done.10
  335.0 5.6 %collective-permute-start.16 = (f32[1,4,32]{2,1,0:T(4,128)S(1)}, f32[1,4,32]{2,1,0:T(4,128)S(1)}, u32[]{:S(2)}, u32[]{:S(2)}) collective-permute-start(f32[1,4,32]{2,1,0:T(4,128)S(1)} %get-tuple-element.107), channel_id=1, source_target_pairs={{8,0},{16,8},{24,16},{9,1},{17,9},{25,17},{10,2},{18,10},{26,18},{... | collective-permute-start | bytes 1544 | tf_op jit(solution)/shard_map/ppermute | solution.py:37
  342.5 4.4 %collective-permute-done.17 = f32[1,4,32]{2,1,0:T(4,128)S(1)} collective-permute-done((f32[1,4,32]{2,1,0:T(4,128)S(1)}, f32[1,4,32]{2,1,0:T(4,128)S(1)}, u32[]{:S(2)}, u32[]{:S(2)}) %collective-permute-start.17) | collective-permute-done | bytes 544 | tf_op jit(solution)/shard_map/ppermute | solution.py:36
  360.2 3.0 collective-permute-start.20
  363.2 3.0 collective-permute-start.21
  376.7 3.2 collective-permute-start.24
  382.6 3.7 collective-permute-done.25
  (251 shorter events, 110.1 us)
Async XLA Ops:
  0.6 8.8 %copy-start.9 = (f32[28,6272]{1,0:T(8,128)S(1)}, f32[28,6272]{1,0:T(8,128)}, u32[]{:S(2)}) copy-start(f32[28,6272]{1,0:T(8,128)} %param.29) | copy-start | bytes 2107396
  1.2 325.3 %collective-permute-start.12 = (f32[1,4,32]{2,1,0:T(4,128)}, f32[1,4,32]{2,1,0:T(4,128)}, u32[]{:S(2)}, u32[]{:S(2)}) collective-permute-start(f32[1,4,32]{2,1,0:T(4,128)} %broadcast.522), channel_id=1, source_target_pairs={{8,0},{16,8},{24,16},{9,1},{17,9},{25,17},{10,2},{18,10},{26,18},{... | collective-permute-start | bytes 1544 | tf_op jit(solution)/shard_map/ppermute | solution.py:37
  4.6 322.0 %collective-permute-start.13 = (f32[1,4,32]{2,1,0:T(4,128)}, f32[1,4,32]{2,1,0:T(4,128)}, u32[]{:S(2)}, u32[]{:S(2)}) collective-permute-start(f32[1,4,32]{2,1,0:T(4,128)} %broadcast.522), channel_id=1, source_target_pairs={{0,8},{8,16},{16,24},{1,9},{9,17},{17,25},{2,10},{10,18},{18,26},{... | collective-permute-start | bytes 1544 | tf_op jit(solution)/shard_map/ppermute | solution.py:36
  7.7 271.1 %copy-start.27 = (f32[224]{0:T(256)}, f32[224]{0:T(256)S(1)}, u32[]{:S(2)}) copy-start(f32[224]{0:T(256)S(1)} %compare_convert_fusion.3) | copy-start | bytes 2692
  12.6 7.7 %copy-start.35 = (f32[41]{0:T(128)S(1)}, f32[41]{0:T(128)}, u32[]{:S(2)}) copy-start(f32[41]{0:T(128)} %constant.39.clone) | copy-start | bytes 496
  12.6 7.8 %copy-start.40 = (f32[224]{0:T(256)S(1)}, f32[224]{0:T(256)}, u32[]{:S(2)}) copy-start(f32[224]{0:T(256)} %constant.40.clone) | copy-start | bytes 2692
  13.5 17.9 %collective-permute-start = (f32[2,8,28,224]{3,2,1,0:T(8,128)}, f32[2,8,28,224]{3,2,1,0:T(8,128)S(1)}, u32[]{:S(2)}, u32[]{:S(2)}) collective-permute-start(f32[2,8,28,224]{3,2,1,0:T(8,128)} %get-tuple-element.86), channel_id=1, source_target_pairs={{0,8},{8,16},{16,24},{1,9},{9,17},{17,25},{2,10},{10,18},{18,26},{... | collective-permute-start | bytes 1204232 | tf_op jit(solution)/shard_map/ppermute | solution.py:36
  15.4 22.3 %collective-permute-start.1 = (f32[2,8,28,224]{3,2,1,0:T(8,128)S(1)}, f32[2,8,28,224]{3,2,1,0:T(8,128)S(1)}, u32[]{:S(2)}, u32[]{:S(2)}) collective-permute-start(f32[2,8,28,224]{3,2,1,0:T(8,128)S(1)} %get-tuple-element.87), channel_id=1, source_target_pairs={{8,0},{16,8},{24,16},{9,1},{17,9},{25,17},{10,2},{18,10},{26,18},{... | collective-permute-start | bytes 1204232 | tf_op jit(solution)/shard_map/ppermute | solution.py:37
  20.3 45.6 %copy-start.14 = (f32[41,41]{0,1:T(8,128)}, f32[41,41]{0,1:T(8,128)S(1)}, u32[]{:S(2)}) copy-start(f32[41,41]{0,1:T(8,128)S(1)} %broadcast_multiply_fusion.5) | copy-start | bytes 20176
  39.0 12.9 %collective-permute-start.2 = (f32[2,44,8,224]{3,2,1,0:T(8,128)}, f32[2,44,8,224]{3,2,1,0:T(8,128)}, u32[]{:S(2)}, u32[]{:S(2)}) collective-permute-start(f32[2,44,8,224]{3,2,1,0:T(8,128)} %get-tuple-element.84), channel_id=1, source_target_pairs={{0,1},{1,2},{2,3},{3,4},{4,5},{5,6},{6,7},{8,9},{9,10},{10,11},{11... | collective-permute-start | bytes 1892360 | tf_op jit(solution)/shard_map/ppermute | solution.py:36
  40.9 12.8 %collective-permute-start.3 = (f32[2,44,8,224]{3,2,1,0:T(8,128)}, f32[2,44,8,224]{3,2,1,0:T(8,128)}, u32[]{:S(2)}, u32[]{:S(2)}) collective-permute-start(f32[2,44,8,224]{3,2,1,0:T(8,128)} %get-tuple-element.85), channel_id=1, source_target_pairs={{1,0},{2,1},{3,2},{4,3},{5,4},{6,5},{7,6},{9,8},{10,9},{11,10},{12... | collective-permute-start | bytes 1892360 | tf_op jit(solution)/shard_map/ppermute | solution.py:37
  44.6 11.0 %copy-start.36 = (f32[4]{0:T(128)}, f32[4]{0:T(128)S(1)}, u32[]{:S(2)}) copy-start(f32[4]{0:T(128)S(1)} %get-tuple-element.115) | copy-start | bytes 52
  260.9 14.1 %copy-start.1 = (f32[28,6272]{1,0:T(8,128)S(1)}, f32[28,6272]{1,0:T(8,128)}, u32[]{:S(2)}) copy-start(f32[28,6272]{1,0:T(8,128)} %param.30) | copy-start | bytes 2107396
  260.9 8.0 %collective-permute-start.4 = (f32[34,6,224]{2,1,0:T(8,128)S(1)}, f32[34,6,224]{2,1,0:T(8,128)S(1)}, u32[]{:S(2)}, u32[]{:S(2)}) collective-permute-start(f32[34,6,224]{2,1,0:T(8,128)S(1)} %slice.379), channel_id=1, source_target_pairs={{1,0},{2,1},{3,2},{4,3},{5,4},{6,5},{7,6},{9,8},{10,9},{11,10},{12... | collective-permute-start | bytes 548360 | tf_op jit(solution)/shard_map/ppermute | solution.py:45
  264.9 13.8 %copy-start.16 = (f32[28,28]{1,0:T(8,128)}, f32[28,28]{1,0:T(8,128)S(1)}, u32[]{:S(2)}) copy-start(f32[28,28]{1,0:T(8,128)S(1)} %broadcast_multiply_fusion.6) | copy-start | bytes 9412
  265.0 11.5 %copy-start.15 = (f32[41,41]{0,1:T(8,128)S(1)}, f32[41,41]{0,1:T(8,128)}, u32[]{:S(2)}) copy-start(f32[41,41]{0,1:T(8,128)} %copy-done.14) | copy-start | bytes 20176
  269.0 9.7 %collective-permute-start.5 = (f32[6,28,224]{2,1,0:T(8,128)S(1)}, f32[6,28,224]{2,1,0:T(8,128)S(1)}, u32[]{:S(2)}, u32[]{:S(2)}) collective-permute-start(f32[6,28,224]{2,1,0:T(8,128)S(1)} %pad_maximum_fusion.10), channel_id=1, source_target_pairs={{8,0},{16,8},{24,16},{9,1},{17,9},{25,17},{10,2},{18,10},{26,18},{... | collective-permute-start | bytes 451592 | tf_op jit(solution)/shard_map/ppermute | solution.py:45
  279.2 12.4 %collective-permute-start.6 = (f32[8,28,224]{2,1,0:T(8,128)S(1)}, f32[8,28,224]{2,1,0:T(8,128)S(1)}, u32[]{:S(2)}, u32[]{:S(2)}) collective-permute-start(f32[8,28,224]{2,1,0:T(8,128)S(1)} %get-tuple-element.90), channel_id=1, source_target_pairs={{0,8},{8,16},{16,24},{1,9},{9,17},{17,25},{2,10},{10,18},{18,26},{... | collective-permute-start | bytes 602120 | tf_op jit(solution)/shard_map/ppermute | solution.py:36
  281.1 12.0 %collective-permute-start.7 = (f32[8,28,224]{2,1,0:T(8,128)S(1)}, f32[8,28,224]{2,1,0:T(8,128)S(1)}, u32[]{:S(2)}, u32[]{:S(2)}) collective-permute-start(f32[8,28,224]{2,1,0:T(8,128)S(1)} %get-tuple-element.91), channel_id=1, source_target_pairs={{8,0},{16,8},{24,16},{9,1},{17,9},{25,17},{10,2},{18,10},{26,18},{... | collective-permute-start | bytes 602120 | tf_op jit(solution)/shard_map/ppermute | solution.py:37
  293.2 8.7 %collective-permute-start.8 = (f32[44,8,224]{2,1,0:T(8,128)S(1)}, f32[44,8,224]{2,1,0:T(8,128)S(1)}, u32[]{:S(2)}, u32[]{:S(2)}) collective-permute-start(f32[44,8,224]{2,1,0:T(8,128)S(1)} %get-tuple-element.88), channel_id=1, source_target_pairs={{0,1},{1,2},{2,3},{3,4},{4,5},{5,6},{6,7},{8,9},{9,10},{10,11},{11... | collective-permute-start | bytes 946184 | tf_op jit(solution)/shard_map/ppermute | solution.py:36
  295.5 8.2 %collective-permute-start.9 = (f32[44,8,224]{2,1,0:T(8,128)S(1)}, f32[44,8,224]{2,1,0:T(8,128)S(1)}, u32[]{:S(2)}, u32[]{:S(2)}) collective-permute-start(f32[44,8,224]{2,1,0:T(8,128)S(1)} %get-tuple-element.89), channel_id=1, source_target_pairs={{1,0},{2,1},{3,2},{4,3},{5,4},{6,5},{7,6},{9,8},{10,9},{11,10},{12... | collective-permute-start | bytes 946184 | tf_op jit(solution)/shard_map/ppermute | solution.py:37
  315.9 18.2 %copy-start.21 = (f32[4,4]{1,0:T(4,128)S(1)}, f32[4,4]{1,0:T(4,128)}, u32[]{:S(2)}) copy-start(f32[4,4]{1,0:T(4,128)} %broadcast_multiply_fusion.9) | copy-start | bytes 196
  315.9 36.0 %copy-start.26 = (f32[12,12]{1,0:T(8,128)S(1)}, f32[12,12]{1,0:T(8,128)}, u32[]{:S(2)}) copy-start(f32[12,12]{1,0:T(8,128)} %broadcast_multiply_fusion.8) | copy-start | bytes 1732
  317.1 35.6 %copy-start.13 = (f32[28,28]{1,0:T(8,128)S(1)}, f32[28,28]{1,0:T(8,128)}, u32[]{:S(2)}) copy-start(f32[28,28]{1,0:T(8,128)} %copy-done.11) | copy-start | bytes 9412
  318.4 36.5 %copy-start.17 = (f32[28,28]{1,0:T(8,128)S(1)}, f32[28,28]{1,0:T(8,128)}, u32[]{:S(2)}) copy-start(f32[28,28]{1,0:T(8,128)} %copy-done.16) | copy-start | bytes 9412
  319.0 5.1 %collective-permute-start.10 = (f32[1408]{0:T(1024)S(1)}, f32[1408]{0:T(1024)S(1)}, u32[]{:S(2)}, u32[]{:S(2)}) collective-permute-start(f32[1408]{0:T(1024)S(1)} %pad_maximum_fusion.43), channel_id=1, source_target_pairs={{0,1},{1,2},{2,3},{3,4},{4,5},{5,6},{6,7},{8,9},{9,10},{10,11},{11... | collective-permute-start | bytes 16904 | tf_op jit(solution)/shard_map/ppermute | solution.py:45
  321.5 30.4 %copy-start.29 = (f32[32]{0:T(128)}, f32[32]{0:T(128)S(1)}, u32[]{:S(2)}) copy-start(f32[32]{0:T(128)S(1)} %compare_convert_fusion.1) | copy-start | bytes 388
  321.5 31.3 %copy-start.5 = (f32[13,11,96]{2,1,0:T(8,128)}, f32[13,11,96]{2,1,0:T(8,128)S(1)}, u32[]{:S(2)}) copy-start(f32[13,11,96]{2,1,0:T(8,128)S(1)} %slice.399) | copy-start | bytes 164740
  324.6 7.2 %collective-permute-start.11 = (f32[1280]{0:T(1024)S(1)}, f32[1280]{0:T(1024)S(1)}, u32[]{:S(2)}, u32[]{:S(2)}) collective-permute-start(f32[1280]{0:T(1024)S(1)} %pad_maximum_fusion.44), channel_id=1, source_target_pairs={{0,8},{8,16},{16,24},{1,9},{9,17},{17,25},{2,10},{10,18},{18,26},{... | collective-permute-start | bytes 15368 | tf_op jit(solution)/shard_map/ppermute | solution.py:45
  327.3 4.6 %collective-permute-start.14 = (f32[6,1,32]{2,1,0:T(1,128)S(1)}, f32[6,1,32]{2,1,0:T(1,128)S(1)}, u32[]{:S(2)}, u32[]{:S(2)}) collective-permute-start(f32[6,1,32]{2,1,0:T(1,128)S(1)} %get-tuple-element.100), channel_id=1, source_target_pairs={{1,0},{2,1},{3,2},{4,3},{5,4},{6,5},{7,6},{9,8},{10,9},{11,10},{12... | collective-permute-start | bytes 2312 | tf_op jit(solution)/shard_map/ppermute | solution.py:37
  329.2 4.9 %collective-permute-start.15 = (f32[6,1,32]{2,1,0:T(1,128)S(1)}, f32[6,1,32]{2,1,0:T(1,128)S(1)}, u32[]{:S(2)}, u32[]{:S(2)}) collective-permute-start(f32[6,1,32]{2,1,0:T(1,128)S(1)} %get-tuple-element.101), channel_id=1, source_target_pairs={{0,1},{1,2},{2,3},{3,4},{4,5},{5,6},{6,7},{8,9},{9,10},{10,11},{11... | collective-permute-start | bytes 2312 | tf_op jit(solution)/shard_map/ppermute | solution.py:36
  335.0 7.5 %collective-permute-start.16 = (f32[1,4,32]{2,1,0:T(4,128)S(1)}, f32[1,4,32]{2,1,0:T(4,128)S(1)}, u32[]{:S(2)}, u32[]{:S(2)}) collective-permute-start(f32[1,4,32]{2,1,0:T(4,128)S(1)} %get-tuple-element.107), channel_id=1, source_target_pairs={{8,0},{16,8},{24,16},{9,1},{17,9},{25,17},{10,2},{18,10},{26,18},{... | collective-permute-start | bytes 1544 | tf_op jit(solution)/shard_map/ppermute | solution.py:37
  340.5 6.4 %collective-permute-start.17 = (f32[1,4,32]{2,1,0:T(4,128)S(1)}, f32[1,4,32]{2,1,0:T(4,128)S(1)}, u32[]{:S(2)}, u32[]{:S(2)}) collective-permute-start(f32[1,4,32]{2,1,0:T(4,128)S(1)} %get-tuple-element.106), channel_id=1, source_target_pairs={{0,8},{8,16},{16,24},{1,9},{9,17},{17,25},{2,10},{10,18},{18,26},{... | collective-permute-start | bytes 1544 | tf_op jit(solution)/shard_map/ppermute | solution.py:36
  342.5 9.4 %copy-start.31 = (f32[1,4,32]{2,1,0:T(4,128)}, f32[1,4,32]{2,1,0:T(4,128)S(1)}, u32[]{:S(2)}) copy-start(f32[1,4,32]{2,1,0:T(4,128)S(1)} %collective-permute-done.16) | copy-start | bytes 1540
  347.5 11.8 %collective-permute-start.18 = (f32[6,1,32]{2,1,0:T(1,128)}, f32[6,1,32]{2,1,0:T(1,128)}, u32[]{:S(2)}, u32[]{:S(2)}) collective-permute-start(f32[6,1,32]{2,1,0:T(1,128)} %get-tuple-element.98), channel_id=1, source_target_pairs={{1,0},{2,1},{3,2},{4,3},{5,4},{6,5},{7,6},{9,8},{10,9},{11,10},{12... | collective-permute-start | bytes 2312 | tf_op jit(solution)/shard_map/ppermute | solution.py:37
  349.4 9.9 %collective-permute-start.19 = (f32[6,1,32]{2,1,0:T(1,128)}, f32[6,1,32]{2,1,0:T(1,128)}, u32[]{:S(2)}, u32[]{:S(2)}) collective-permute-start(f32[6,1,32]{2,1,0:T(1,128)} %get-tuple-element.99), channel_id=1, source_target_pairs={{0,1},{1,2},{2,3},{3,4},{4,5},{5,6},{6,7},{8,9},{9,10},{10,11},{11... | collective-permute-start | bytes 2312 | tf_op jit(solution)/shard_map/ppermute | solution.py:36
  356.4 9.7 %copy-start.4 = (f32[28,6272]{1,0:T(8,128)S(1)}, f32[28,6272]{1,0:T(8,128)}, u32[]{:S(2)}) copy-start(f32[28,6272]{1,0:T(8,128)} %mul.568) | copy-start | bytes 2107396
  360.2 8.2 %collective-permute-start.20 = (f32[1,4,32]{2,1,0:T(4,128)S(1)}, f32[1,4,32]{2,1,0:T(4,128)S(1)}, u32[]{:S(2)}, u32[]{:S(2)}) collective-permute-start(f32[1,4,32]{2,1,0:T(4,128)S(1)} %get-tuple-element.105), channel_id=1, source_target_pairs={{8,0},{16,8},{24,16},{9,1},{17,9},{25,17},{10,2},{18,10},{26,18},{... | collective-permute-start | bytes 1544 | tf_op jit(solution)/shard_map/ppermute | solution.py:37
  363.2 10.9 %copy-start.6 = (f32[13,11,96]{2,1,0:T(8,128)S(1)}, f32[13,11,96]{2,1,0:T(8,128)}, u32[]{:S(2)}) copy-start(f32[13,11,96]{2,1,0:T(8,128)} %copy-done.5) | copy-start | bytes 164740
  363.2 11.0 %copy-start.34 = (f32[1280]{0:T(1024)S(1)}, f32[1280]{0:T(1024)}, u32[]{:S(2)}) copy-start(f32[1280]{0:T(1024)} %copy-done.33) | copy-start | bytes 15364
  363.2 27.5 %copy-start.25 = (f32[1152]{0:T(1024)S(1)}, f32[1152]{0:T(1024)}, u32[]{:S(2)}) copy-start(f32[1152]{0:T(1024)} %mul.643) | copy-start | bytes 13828
  363.2 6.5 %collective-permute-start.21 = (f32[1,4,32]{2,1,0:T(4,128)S(1)}, f32[1,4,32]{2,1,0:T(4,128)S(1)}, u32[]{:S(2)}, u32[]{:S(2)}) collective-permute-start(f32[1,4,32]{2,1,0:T(4,128)S(1)} %get-tuple-element.104), channel_id=1, source_target_pairs={{0,8},{8,16},{16,24},{1,9},{9,17},{17,25},{2,10},{10,18},{18,26},{... | collective-permute-start | bytes 1544 | tf_op jit(solution)/shard_map/ppermute | solution.py:36
  369.7 4.6 %collective-permute-start.22 = (f32[6,1,32]{2,1,0:T(1,128)S(1)}, f32[6,1,32]{2,1,0:T(1,128)S(1)}, u32[]{:S(2)}, u32[]{:S(2)}) collective-permute-start(f32[6,1,32]{2,1,0:T(1,128)S(1)} %get-tuple-element.96), channel_id=1, source_target_pairs={{1,0},{2,1},{3,2},{4,3},{5,4},{6,5},{7,6},{9,8},{10,9},{11,10},{12... | collective-permute-start | bytes 2312 | tf_op jit(solution)/shard_map/ppermute | solution.py:37
  371.7 4.9 %collective-permute-start.23 = (f32[6,1,32]{2,1,0:T(1,128)S(1)}, f32[6,1,32]{2,1,0:T(1,128)S(1)}, u32[]{:S(2)}, u32[]{:S(2)}) collective-permute-start(f32[6,1,32]{2,1,0:T(1,128)S(1)} %get-tuple-element.97), channel_id=1, source_target_pairs={{0,1},{1,2},{2,3},{3,4},{4,5},{5,6},{6,7},{8,9},{9,10},{10,11},{11... | collective-permute-start | bytes 2312 | tf_op jit(solution)/shard_map/ppermute | solution.py:36
  376.7 6.0 %collective-permute-start.24 = (f32[1,4,32]{2,1,0:T(4,128)S(1)}, f32[1,4,32]{2,1,0:T(4,128)S(1)}, u32[]{:S(2)}, u32[]{:S(2)}) collective-permute-start(f32[1,4,32]{2,1,0:T(4,128)S(1)} %get-tuple-element.103), channel_id=1, source_target_pairs={{8,0},{16,8},{24,16},{9,1},{17,9},{25,17},{10,2},{18,10},{26,18},{... | collective-permute-start | bytes 1544 | tf_op jit(solution)/shard_map/ppermute | solution.py:37
  379.9 6.4 %collective-permute-start.25 = (f32[1,4,32]{2,1,0:T(4,128)S(1)}, f32[1,4,32]{2,1,0:T(4,128)S(1)}, u32[]{:S(2)}, u32[]{:S(2)}) collective-permute-start(f32[1,4,32]{2,1,0:T(4,128)S(1)} %get-tuple-element.102), channel_id=1, source_target_pairs={{0,8},{8,16},{16,24},{1,9},{9,17},{17,25},{2,10},{10,18},{18,26},{... | collective-permute-start | bytes 1544 | tf_op jit(solution)/shard_map/ppermute | solution.py:36
  386.3 5.0 %collective-permute-start.26 = (f32[6,1,32]{2,1,0:T(1,128)S(1)}, f32[6,1,32]{2,1,0:T(1,128)S(1)}, u32[]{:S(2)}, u32[]{:S(2)}) collective-permute-start(f32[6,1,32]{2,1,0:T(1,128)S(1)} %get-tuple-element.94), channel_id=1, source_target_pairs={{1,0},{2,1},{3,2},{4,3},{5,4},{6,5},{7,6},{9,8},{10,9},{11,10},{12... | collective-permute-start | bytes 2312 | tf_op jit(solution)/shard_map/ppermute | solution.py:37
  388.3 4.9 %collective-permute-start.27 = (f32[6,1,32]{2,1,0:T(1,128)S(1)}, f32[6,1,32]{2,1,0:T(1,128)S(1)}, u32[]{:S(2)}, u32[]{:S(2)}) collective-permute-start(f32[6,1,32]{2,1,0:T(1,128)S(1)} %get-tuple-element.95), channel_id=1, source_target_pairs={{0,1},{1,2},{2,3},{3,4},{4,5},{5,6},{6,7},{8,9},{9,10},{10,11},{11... | collective-permute-start | bytes 2312 | tf_op jit(solution)/shard_map/ppermute | solution.py:36
  (21 other events, 63.5 us)
where the time goes:
time: 401 us; the launch traced here: 394 us
  local copies, waits for them, and re-layouts  165 us (41%)
  starting transfers between devices  81.8 us (20%)
  matrix products  60.6 us (15%)
  waiting for transfers between devices  56.4 us (14%)
  other arithmetic  22.5 us (6%)
  loops' own time  5.86 us (1%)
    mul x16, local copies, waits for them, and re-layouts, z_block(): factor_xy * active_z  88.2 us
    dynamic_update_slice x4, local copies, waits for them, and re-layouts, z_block(): lax.dynamic_update_slice_in_dim(accum_z, current + returned, offset_z, 2)  47.9 us
    ppermute x12, starting transfers between devices, extended_2(): after = lax.ppermute(first, axis, down)  40 us
    ppermute x12, waiting for transfers between devices, extended_2(): before = lax.ppermute(last, axis, up)  36.5 us
    ppermute x12, starting transfers between devices, extended_2(): before = lax.ppermute(last, axis, up)  28.2 us
    dot_general x4, matrix products, z_block(): jnp.einsum('sn,pqs->pqn', fwd_z, spectral * factor, precision=highest)  16.9 us
    ppermute x4, starting transfers between devices, shifted(): return lax.ppermute(array, axis, pairs)  13.6 us
    dot_general x4, matrix products, z_block(): spectral = jnp.einsum('sn,pqn->pqs', fwd_z, segment, precision=highest)  12.4 us
  transfers between devices with their start and end apart: 28, of which 18 were waited for; matrix products, arithmetic and copies ran while one was open for 62% of the time, Pallas kernels for 0%

commit v1 on v0

v1 whole, which is shorter than its diff:
```python
import math

import jax
import jax.numpy as jnp
import numpy as np
from jax import lax
from jax.experimental import pallas as pl
from jax.experimental.pallas import tpu as pltpu
from jax.sharding import PartitionSpec as P

EZ = 32
JAC = 4


points_seven = (
    -1.0,
    -0.8717401485096066,
    -0.5917001814331423,
    -0.2092992179024789,
    0.2092992179024789,
    0.5917001814331423,
    0.8717401485096066,
    1.0,
)
points_three = (-1.0, -0.4472135954999579, 0.4472135954999579, 1.0)
points_one = (-1.0, 1.0)
damping = 2.0 / 3.0


def shifted(array, axis, by):
    devices = lax.axis_size(axis)
    pairs = [(i, i + by) for i in range(devices) if 0 <= i + by < devices]
    return lax.ppermute(array, axis, pairs)


def legendre_at(degree, location):
    previous, current = (1.0, location)
    for level_idx in range(1, degree):
        previous, current = (
            current,
            ((2 * level_idx + 1) * location * current - level_idx * previous) / (level_idx + 1),
        )
    return current


def quadrature_weights():
    return np.array([2.0 / (56.0 * legendre_at(7, x) * legendre_at(7, x)) for x in points_seven])


def derivative_matrix():
    points = np.array(points_seven)
    products = np.array(
        [np.prod([points[i] - points[k] for k in range(8) if k != i]) for i in range(8)]
    )
    result = np.zeros((8, 8))
    for i in range(8):
        for j in range(8):
            if i != j:
                result[i, j] = products[i] / (products[j] * (points[i] - points[j]))
        result[i, i] = np.sum([1.0 / (points[i] - points[k]) for k in range(8) if k != i])
    return result


def element_stiffness():
    derivative = derivative_matrix()
    return derivative.T @ (quadrature_weights()[:, None] * derivative)


def assemble_line(elements):
    stiffness = element_stiffness()
    weights = quadrature_weights()
    extent = 7 * elements + 1
    global_stiff = np.zeros((extent, extent))
    lumped = np.zeros(extent)
    for m in range(elements):
        global_stiff[7 * m : 7 * m + 8, 7 * m : 7 * m + 8] += stiffness
        lumped[7 * m : 7 * m + 8] += weights
    return (global_stiff, lumped)


def jacobi_eigen(matrix):
    rotated_mat = matrix.copy()
    extent = matrix.shape[0]
    vectors = np.eye(extent)
    for sweep_idx in range(12):
        for p in range(extent - 1):
            for q in range(p + 1, extent):
                angle_rot = 0.5 * math.atan2(
                    2.0 * float(rotated_mat[p, q]), float(rotated_mat[q, q] - rotated_mat[p, p])
                )
                rotation = np.eye(extent)
                rotation[p, p] = math.cos(angle_rot)
                rotation[q, q] = math.cos(angle_rot)
                rotation[p, q] = math.sin(angle_rot)
                rotation[q, p] = -math.sin(angle_rot)
                rotated_mat = rotation.T @ rotated_mat @ rotation
                vectors = vectors @ rotation
    return (np.array([rotated_mat[i, i] for i in range(extent)]), vectors)


def patch_basis():
    global_stiff, lumped = assemble_line(2)
    inv_root = 1.0 / np.sqrt(lumped[1:14])
    eigvals, vectors = jacobi_eigen(
        inv_root[:, None] * global_stiff[1:14, 1:14] * inv_root[None, :]
    )
    return (eigvals, inv_root[:, None] * vectors)


def interp_matrix(coarse_pts):
    result = np.ones((8, len(coarse_pts)))
    for a in range(8):
        for c in range(len(coarse_pts)):
            for k in range(len(coarse_pts)):
                if k != c:
                    result[a, c] *= (points_seven[a] - coarse_pts[k]) / (
                        coarse_pts[c] - coarse_pts[k]
                    )
    return result


def restriction_rows(coarse_pts):
    shared = np.ones(8)
    shared[0] = 0.5
    shared[7] = 0.5
    return (interp_matrix(coarse_pts) * shared[:, None]).T


def restriction_line(elements, coarse_pts):
    degree = len(coarse_pts) - 1
    rows_mat = restriction_rows(coarse_pts)
    result = np.zeros((degree * elements + 1, 7 * elements + 1))
    for m in range(elements):
        result[degree * m : degree * m + degree + 1, 7 * m : 7 * m + 8] += rows_mat
    return result


def patch_matrix(eigbasis, vertices, extent):
    result = np.zeros((13 * vertices, extent))
    for b in range(13):
        for v in range(vertices):
            for a in range(13):
                node_idx = 7 * v + a
                result[b * vertices + v, node_idx] = eigbasis[a, b]
    return result


high = lax.Precision.HIGH
LANES = 128
f32 = jnp.float32


def up_to(length, multiple):
    return -(-length // multiple) * multiple


def placed(matrix, shape, row=0, col=0):
    result = np.zeros(shape, np.float32)
    result[row : row + matrix.shape[0], col : col + matrix.shape[1]] = matrix
    return result


def mm(left, right):
    return lax.dot_general(
        left, right, (((1,), (0,)), ((), ())), precision=high, preferred_element_type=f32
    )


class Sizes:
    def __init__(self, x_nodes, y_nodes, z_nodes):
        self.x_nodes, self.y_nodes, self.z_nodes = (x_nodes, y_nodes, z_nodes)
        self.x_elems, self.y_elems, self.z_elems = (x_nodes // 7, y_nodes // 7, z_nodes // 7)
        self.rows = up_to(x_nodes + 9, 8)
        self.lanes = up_to(z_nodes, LANES)
        self.modes_x = up_to(13 * self.x_elems, 8)
        self.modes_z = up_to(13 * self.z_elems, LANES)
        self.coarse_x = 3 * self.x_elems + 4
        self.coarse_y = 3 * self.y_elems + 4
        self.coarse_z = 3 * self.z_elems
        self.coarse_rows = up_to(self.coarse_x, 8)
        self.coarse_lanes = up_to(self.coarse_z, LANES)


def line_tables(elements):
    nodes = 7 * elements
    stiff, lumped = assemble_line(elements + 2)
    restrict = restriction_line(elements + 3, points_three)[3 : 3 * elements + 7, 7 : nodes + 15]
    columns = np.arange(-6, nodes)
    weight = np.where(columns % 7 == 0, 1.0, 0.5)
    mass_part = restrict[:, 1:-1] * (lumped[1 : nodes + 7] * weight)[None, :]
    stiff_part = restrict @ (stiff[: nodes + 8, 1 : nodes + 7] * weight[None, :])
    return dict(
        stiff=stiff[1 : nodes + 7, : nodes + 8],
        mass=lumped[1 : nodes + 7],
        own=restrict[:, 7:-1],
        mass_part=mass_part,
        stiff_part=stiff_part,
    )


def linear_from_cubic(first, last, first_three, last_three):
    result = np.zeros((last - first + 1, last_three - first_three + 1))
    for m in range(first, last + 1):
        for offset, factor in (
            (0, 1.0),
            (1, (1.0 - points_three[1]) / 2.0),
            (2, (1.0 - points_three[2]) / 2.0),
            (-2, (1.0 + points_three[1]) / 2.0),
            (-1, (1.0 + points_three[2]) / 2.0),
        ):
            node = 3 * m + offset - first_three
            if 0 <= node < result.shape[1]:
                result[m - first, node] = factor
    return result


def patch_constants(s):
    line_x = line_tables(s.x_elems)
    stiff_z, lumped_z = assemble_line(s.z_elems)
    stiff_z, lumped_z = (stiff_z[: s.z_nodes, : s.z_nodes], lumped_z[: s.z_nodes])
    weight_z = np.where(np.arange(s.z_nodes) % 7 == 0, 1.0, 0.5)
    restrict_z = restriction_line(s.z_elems, points_three)[: s.coarse_z, : s.z_nodes]
    eigvals, eigbasis = patch_basis()
    square = (s.rows, s.rows)
    mass_z = np.zeros(s.lanes)
    mass_z[: s.z_nodes] = lumped_z
    mass_x = np.zeros(s.rows)
    mass_x[2 : s.x_nodes + 8] = line_x["mass"]
    spread = np.ones((s.rows, s.lanes))
    fwd_x = placed(
        patch_matrix(eigbasis, s.x_elems, s.x_nodes + 6), (s.modes_x, s.rows), col=2
    )
    fwd_z = patch_matrix(eigbasis, s.z_elems, s.z_nodes + 6)[:, 6:]
    vertex_z = np.arange(13 * s.z_elems) % s.z_elems
    fwd_z = np.where((vertex_z >= 1)[:, None], fwd_z, 0.0)
    inverse = 1.0 / (eigvals[:, None, None] + eigvals[None, :, None] + eigvals[None, None, :])
    factor = np.zeros((13, s.modes_x, s.modes_z), np.float32)
    factor[:, : 13 * s.x_elems, : 13 * s.z_elems] = np.repeat(
        np.repeat(inverse, s.x_elems, 1), s.z_elems, 2
    )
    coarse_of_z = np.zeros((s.lanes, 2 * s.coarse_lanes), np.float32)
    coarse_of_z[: s.z_nodes, : s.coarse_z] = (restrict_z * (lumped_z * weight_z)[None, :]).T
    coarse_of_z[: s.z_nodes, s.coarse_lanes : s.coarse_lanes + s.coarse_z] = (
        restrict_z @ (stiff_z * weight_z[None, :])
    ).T
    coarse_of_x = np.zeros((2 * s.coarse_rows, s.rows), np.float32)
    coarse_of_x[: s.coarse_x, 2 : s.x_nodes + 8] = line_x["mass_part"]
    coarse_of_x[s.coarse_rows : s.coarse_rows + s.coarse_x, 2 : s.x_nodes + 8] = line_x[
        "stiff_part"
    ]
    own_x = placed(line_x["own"], (s.coarse_rows, s.rows), col=8)
    own_z = placed(restrict_z.T, (s.lanes, s.coarse_lanes))
    one_z = placed(
        linear_from_cubic(0, s.z_elems - 1, 0, s.coarse_z - 1).T, (s.coarse_lanes, LANES)
    )
    one_x = placed(
        linear_from_cubic(-1, s.x_elems, -3, 3 * s.x_elems), (8, s.coarse_rows)
    )
    return [
        placed(line_x["stiff"], square, row=2, col=1),
        placed(stiff_z, (s.lanes, s.lanes)),
        spread * mass_x[:, None],
        spread * mass_z[None, :],
        mass_x[:, None] * mass_z[None, :],
        fwd_x,
        fwd_x.T,
        placed(fwd_z.T, (s.lanes, s.modes_z)),
        placed(fwd_z, (s.modes_z, s.lanes)),
        factor,
        coarse_of_z,
        coarse_of_x,
        own_z,
        own_x,
        one_z,
        one_x,
    ]


def line_of_planes(coefficients, planes):
    total = None
    for coefficient, plane in zip(coefficients, planes):
        if coefficient != 0.0:
            part = plane() * float(coefficient)
            total = part if total is None else total + part
    return total


def patch_kernel(s):
    rows, lanes, nz = (s.rows, s.lanes, s.z_nodes)
    ey, ny = (s.y_elems, s.y_nodes)
    line_y = line_tables(ey)
    _, eigbasis = patch_basis()
    stiffness = element_stiffness()
    mass_y = line_y["mass"]
    one_y = linear_from_cubic(-1, ey, -3, 3 * ey)

    def kernel(
        guess, load, below, above,
        k_x, k_z, m_x, m_z, m_xz, w_x, w_xt, w_z, w_zt, factor, q_z, q_x, r_z, r_x, o_z, o_x,
        edge_out, own_out, three_out, one_out, down_out, up_out,
        u, r, xf, xb, c, cz, rz, hx, ex, rx,
    ):
        gx = lax.axis_index("gx")
        gy = lax.axis_index("gy")
        lane = lax.broadcasted_iota(jnp.int32, (rows, lanes), 1)
        row = lax.broadcasted_iota(jnp.int32, (rows, lanes), 0)
        live = ((lane >= 1) & (lane < nz) & ((row != 8) | (gx > 0))).astype(f32)
        live_y = (gy > 0).astype(f32)
        for j in range(7):
            u[j] = below[:, nz * j : nz * j + lanes] * live
        for j in range(ny):
            mask = live if j else live * live_y
            u[7 + j] = guess[:, nz * j : nz * j + lanes] * mask
        u[ny + 7] = above[...] * live
        inside = ((lane < nz)).astype(f32)
        for j in range(6):
            r[j] = below[:, nz * (7 + j) : nz * (7 + j) + lanes] * inside
        for j in range(ny):
            r[6 + j] = load[:, nz * j : nz * j + lanes] * inside
        r[ny + 6] = jnp.zeros((rows, lanes), f32)

        def direct(chunk, carry):
            base = chunk * 7
            planes = u[pl.ds(base + 1, 7)]
            z_term = mm(planes.reshape(7 * rows, lanes), k_z[...]).reshape(7, rows, lanes)
            for i in range(7):
                x_term = mm(k_x[...], planes[i])
                both = x_term * m_z[...] + z_term[i] * m_x[...]
                r[base + i] = r[base + i] - float(mass_y[i]) * both
            return carry

        lax.fori_loop(0, ey + 1, direct, 0)

        def along_y(tile, carry):
            at = pl.ds(pl.multiple_of(tile * 8, 8), 8)
            scale = m_xz[at, :]
            corner = None
            for e in range(ey + 1):
                nodes = [u[7 * e + i, at, :] for i in range(8)]
                plus = [nodes[i] + nodes[7 - i] for i in range(4)]
                minus = [nodes[i] - nodes[7 - i] for i in range(4)]
                out = [None] * 8
                for i in range(4):
                    even = sum(
                        plus[k] * float(0.5 * (stiffness[i, k] + stiffness[i, 7 - k]))
                        for k in range(4)
                    )
                    odd = sum(
                        minus[k] * float(0.5 * (stiffness[i, k] - stiffness[i, 7 - k]))
                        for k in range(4)
                    )
                    out[i], out[7 - i] = (even + odd, even - odd)
                if e:
                    out[0] = out[0] + corner
                corner = out[7]
                for i in range(0 if e else 1, 7):
                    plane = 7 * e + i - 1
                    r[plane, at, :] = r[plane, at, :] - out[i] * scale
            active = (gy > 0).astype(f32)
            for v in range(ey):
                first = [r[7 * v + a, at, :] for a in range(13)]
                if v == 0:
                    first = [value * active for value in first]
                even = [first[6]] + [first[6 + a] + first[6 - a] for a in range(1, 7)]
                odd = [first[6 + a] - first[6 - a] for a in range(1, 7)]
                for b in range(13):
                    if symmetric(eigbasis[:, b]):
                        xf[b, v, at, :] = sum(
                            even[a] * float(eigbasis[6 + a, b]) for a in range(7)
                        )
                    else:
                        xf[b, v, at, :] = sum(
                            odd[a] * float(eigbasis[7 + a, b]) for a in range(6)
                        )
            return carry

        lax.fori_loop(0, rows // 8, along_y, 0)
        mode = lax.broadcasted_iota(jnp.int32, (s.modes_x, rows), 0)
        forward_x = w_x[...] * ((mode % s.x_elems != 0) | (gx > 0)).astype(f32)

        def spectral(b, carry):
            parts = [mm(forward_x, xf[b, v]) for v in range(ey)]
            modes = mm(jnp.concatenate(parts, 0), w_z[...])
            scaled = modes.reshape(ey, s.modes_x, s.modes_z) * factor[b][None]
            back = mm(scaled.reshape(ey * s.modes_x, s.modes_z), w_zt[...])
            for v in range(ey):
                xb[b, v] = mm(w_xt[...], back[v * s.modes_x : (v + 1) * s.modes_x])
            return carry

        lax.fori_loop(0, 13, spectral, 0)

        def back_y(tile, carry):
            at = pl.ds(pl.multiple_of(tile * 8, 8), 8)
            tail = None
            for v in range(ey):
                modes = [xb[b, v, at, :] for b in range(13)]
                out = [None] * 13
                for a in range(7):
                    even = sum(
                        modes[b] * float(eigbasis[6 + a, b])
                        for b in range(13)
                        if symmetric(eigbasis[:, b])
                    )
                    if a == 0:
                        out[6] = even
                        continue
                    odd = sum(
                        modes[b] * float(eigbasis[6 + a, b])
                        for b in range(13)
                        if not symmetric(eigbasis[:, b])
                    )
                    out[6 + a], out[6 - a] = (even + odd, even - odd)
                if v:
                    out[:6] = [value + other for value, other in zip(out[:6], tail)]
                tail = out[7:]
                for a in range(13 if v == ey - 1 else 7):
                    c[7 * v + a, at, :] = out[a]
            return carry

        lax.fori_loop(0, rows // 8, back_y, 0)

        for j in range(6):
            down_out[:, lanes * j : lanes * (j + 1)] = c[j]
        edge_out[...] = c[6:, 0:8, :]
        own_out[...] = c[6:, 8:, :]

        half = s.coarse_lanes
        rows_c = s.coarse_rows
        cz[...] = mm(c[...].reshape((ny + 6) * rows, lanes), q_z[...]).reshape(
            ny + 6, rows, 2 * half
        )
        rz[...] = mm(r[6 : ny + 6].reshape(ny * rows, lanes), r_z[...]).reshape(ny, rows, half)
        for y in range(ny + 6):
            plane = mm(q_x[...], cz[y])
            hx[y] = plane[:rows_c, :half]
            ex[y] = plane[rows_c:, :half] + plane[:rows_c, half:]
        for y in range(ny):
            rx[y] = mm(r_x[...], rz[y])
        for j in range(s.coarse_y):
            total = line_of_planes(
                np.concatenate(
                    [line_y["own"][j], -line_y["stiff_part"][j], -line_y["mass_part"][j]]
                ),
                [lambda y=y: rx[y] for y in range(ny)]
                + [lambda y=y: hx[y] for y in range(ny + 6)]
                + [lambda y=y: ex[y] for y in range(ny + 6)],
            )
            three_out[j] = total
        one_all = mm(
            three_out[...].reshape(s.coarse_y * rows_c, half), o_z[...]
        ).reshape(s.coarse_y, rows_c, LANES)
        for m in range(ey + 2):
            mixed = line_of_planes(
                one_y[m], [lambda j=j: one_all[j] for j in range(s.coarse_y)]
            )
            one_out[m] = mm(o_x[...], mixed)
        base = 6 * lanes
        for j in range(4):
            at = base + half * j
            if j < 3:
                down_out[0:rows_c, at : at + half] = three_out[j]
            else:
                down_out[0:rows_c, at : at + half] = jnp.zeros((rows_c, half), f32)
            down_out[rows_c : rows_c + 8, at : at + LANES] = one_out[j]
            down_out[rows_c + 8 :, at : at + half] = jnp.zeros((rows - rows_c - 8, half), f32)
            up_at = half * j
            if j == 0:
                up_out[0:rows_c, up_at : up_at + half] = three_out[s.coarse_y - 1]
            else:
                up_out[0:rows_c, up_at : up_at + half] = jnp.zeros((rows_c, half), f32)
            up_out[rows_c : rows_c + 8, up_at : up_at + LANES] = one_out[ey - 2 + j]

    return kernel


def symmetric(vector):
    return abs(vector[0] - vector[-1]) < abs(vector[0] + vector[-1])


def join_kernel(s):
    lanes, half, rows_c = (s.lanes, s.coarse_lanes, s.coarse_rows)
    ey, ny = (s.y_elems, s.y_nodes)

    def kernel(edge, three, one, down, up, down_out, up_out, three_out, one_out):
        for y in range(ny):
            plane = edge[y]
            if y >= ny - 6:
                j = y - (ny - 6)
                plane = plane + down[0:8, lanes * j : lanes * (j + 1)]
            down_out[:, lanes * y : lanes * (y + 1)] = plane
        base = 6 * lanes
        tiles = ny * lanes
        for j in range(max(3 * ey, ey + 6)):
            at = tiles + half * j
            down_out[:, at : at + half] = jnp.zeros((8, half), f32)
            up_out[:, half * j : half * (j + 1)] = jnp.zeros((8, half), f32)
        for j in range(3 * ey):
            plane = three[3 + j]
            if j >= 3 * ey - 3:
                k = j - (3 * ey - 3)
                plane = plane + down[0:rows_c, base + half * k : base + half * (k + 1)]
            if j == 0:
                plane = plane + up[0:rows_c, 0:half]
            three_out[j] = plane
            at = tiles + half * j
            down_out[0:3, at : at + half] = plane[0:3]
            up_out[0:1, half * j : half * (j + 1)] = plane[s.coarse_x - 1 : s.coarse_x]
        for j in range(ey + 6):
            y = j - 3
            plane = None
            if -1 <= y <= ey:
                plane = one[y + 1]
            if y <= 0:
                k = y + 3
                part = up[rows_c : rows_c + 8, half * k : half * k + LANES]
                plane = part if plane is None else plane + part
            if y >= ey - 1:
                k = y - (ey - 1)
                at = base + half * k
                part = down[rows_c : rows_c + 8, at : at + LANES]
                plane = part if plane is None else plane + part
            one_out[j] = plane
            at = tiles + half * j
            down_out[4:8, at : at + LANES] = plane[0:4]
            up_out[4:8, half * j : half * j + LANES] = plane[s.x_elems - 2 : s.x_elems + 2]

    return kernel


def finish_kernel(s, x_total, y_total):
    lanes, half, rows_c, nz = (s.lanes, s.coarse_lanes, s.coarse_rows, s.z_nodes)
    ex, ey, nx, ny = (s.x_elems, s.y_elems, s.x_nodes, s.y_nodes)
    one_rows = up_to(ex + 6, 8)

    def kernel(
        guess, weight, own, down, right, left, three, one,
        smooth_out, three_out, coarse_out, corr, fine, level,
    ):
        gx = lax.axis_index("gx")
        gy = lax.axis_index("gy")
        lane = lax.broadcasted_iota(jnp.int32, (nx, nz), 1)
        row = lax.broadcasted_iota(jnp.int32, (nx, nz), 0)
        live = ((lane >= 1) & ((row >= 1) | (gx > 0))).astype(f32)
        live_y = (gy > 0).astype(f32)
        for y in range(ny):
            corr[...] = own[y]
            if y >= ny - 6:
                j = y - (ny - 6)
                corr[...] += down[8:, lanes * j : lanes * (j + 1)]
            corr[nx - 6 : nx, :] += right[2:8, lanes * y : lanes * (y + 1)]
            mask = live if y else live * live_y
            factor = weight[...] * (1.0 if y % 7 == 0 else 0.5)
            smooth_out[:, nz * y : nz * (y + 1)] = (
                guess[:, nz * y : nz * (y + 1)] + factor * corr[0:nx, 0:nz]
            ) * mask
        tiles = ny * lanes
        nzc = s.coarse_z
        lane = lax.broadcasted_iota(jnp.int32, (3 * ex, nzc), 1)
        row = lax.broadcasted_iota(jnp.int32, (3 * ex, nzc), 0)
        live = ((lane >= 1) & ((row >= 1) | (gx > 0))).astype(f32)
        for j in range(3 * ey):
            fine[...] = three[j]
            at = tiles + half * j
            fine[3 * ex : 3 * ex + 3, :] += right[0:3, at : at + half]
            fine[3:4, :] += left[0:1, half * j : half * (j + 1)]
            mask = live if j else live * live_y
            three_out[:, nzc * j : nzc * (j + 1)] = fine[3 : 3 * ex + 3, 0:nzc] * mask
        level[...] = jnp.zeros((ey + 6, one_rows, LANES), f32)
        for j in range(ey + 6):
            level[j, 2 : ex + 4, :] = one[j, 0 : ex + 2, :]
            at = tiles + half * j
            level[j, 0:4, :] += left[4:8, half * j : half * j + LANES]
            level[j, ex + 2 : ex + 6, :] += right[4:8, at : at + LANES]
        shape = (one_rows, LANES)
        lane = lax.broadcasted_iota(jnp.int32, shape, 1)
        row = lax.broadcasted_iota(jnp.int32, shape, 0)
        global_x = gx * ex + row - 3
        plane_mask = (
            (lane >= 1) & (lane < s.z_elems) & (row < ex + 6)
            & (global_x >= 1) & (global_x < x_total)
        )
        masks = []
        for j in range(ey + 6):
            global_y = gy * ey + (j - 3)
            inside = (global_y >= 1) & (global_y < y_total)
            masks.append((plane_mask & inside).astype(f32))
        levels = [level[j] for j in range(ey + 6)]
        error = [damping / 12.0 * a * m for a, m in zip(levels, masks)]
        zero = jnp.zeros(shape, f32)
        for sweep in range(1, JAC):
            lower = [zero] + error[:-1]
            upper = error[1:] + [zero]
            fresh = []
            for j in range(ey + 6):
                here = error[j]
                neighbours = (
                    lower[j]
                    + upper[j]
                    + pltpu.roll(here, 1, 0)
                    + pltpu.roll(here, one_rows - 1, 0)
                    + pltpu.roll(here, 1, 1)
                    + pltpu.roll(here, LANES - 1, 1)
                )
                applied = 12.0 * here - 2.0 * neighbours
                fresh.append((here + damping / 12.0 * (levels[j] - applied)) * masks[j])
            error = fresh
        nze = s.z_elems
        for j in range(ey):
            coarse_out[:, nze * j : nze * (j + 1)] = error[3 + j][3 : 3 + ex, 0:nze]

    return kernel


def local(load_vector, initial_guess):
    z_nodes = 7 * EZ
    x_nodes = load_vector.shape[0]
    y_nodes = load_vector.shape[1] // z_nodes
    s = Sizes(x_nodes, y_nodes, z_nodes)
    rows, lanes, half = (s.rows, s.lanes, s.coarse_lanes)
    ny, ey = (s.y_nodes, s.y_elems)
    width = y_nodes * z_nodes
    sent_up = jnp.concatenate([initial_guess[x_nodes - 7 :], load_vector[x_nodes - 6 :]], 0)
    from_below = shifted(sent_up, "gx", 1)
    from_above = shifted(initial_guess[:1], "gx", -1)
    tail = up_to((ny - 1) * z_nodes + lanes, LANES) - width

    def framed(pieces, first):
        used = first + sum(piece.shape[0] for piece in pieces)
        parts = (
            [jnp.zeros((first, width), f32)] + pieces + [jnp.zeros((rows - used, width), f32)]
        )
        return jnp.pad(jnp.concatenate(parts, 0), ((0, 0), (0, tail)))

    guess_ext = framed([from_below[:7], initial_guess, from_above], 1)
    load_ext = framed([from_below[7:], load_vector], 2)
    message = jnp.concatenate(
        [guess_ext[:, (ny - 7) * z_nodes : width], load_ext[:, (ny - 6) * z_nodes : width]], 1
    )
    message = jnp.pad(message, ((0, 0), (0, up_to(12 * z_nodes + lanes, LANES) - 13 * z_nodes)))
    y_below = shifted(message, "gy", 1)
    y_above = shifted(guess_ext[:, :lanes], "gy", -1)
    constants = [jnp.asarray(value, f32) for value in patch_constants(s)]
    shape = lambda *dims: jax.ShapeDtypeStruct(dims, f32)
    params = pltpu.CompilerParams(vmem_limit_bytes=56 * 2**20)
    edge, own, three, one, down, up = pl.pallas_call(
        patch_kernel(s),
        out_shape=(
            shape(ny, 8, lanes),
            shape(ny, rows - 8, lanes),
            shape(s.coarse_y, s.coarse_rows, half),
            shape(ey + 2, 8, LANES),
            shape(rows, 6 * lanes + 4 * half),
            shape(s.coarse_rows + 8, 4 * half),
        ),
        scratch_shapes=[
            pltpu.VMEM((ny + 8, rows, lanes), f32),
            pltpu.VMEM((ny + 7, rows, lanes), f32),
            pltpu.VMEM((13, ey, rows, lanes), f32),
            pltpu.VMEM((13, ey, rows, lanes), f32),
            pltpu.VMEM((ny + 6, rows, lanes), f32),
            pltpu.VMEM((ny + 6, rows, 2 * half), f32),
            pltpu.VMEM((ny, rows, half), f32),
            pltpu.VMEM((ny + 6, s.coarse_rows, half), f32),
            pltpu.VMEM((ny + 6, s.coarse_rows, half), f32),
            pltpu.VMEM((ny, s.coarse_rows, half), f32),
        ],
        compiler_params=params,
        name="patches",
    )(guess_ext, load_ext, y_below, y_above, *constants)
    down = shifted(down, "gy", -1)
    up = shifted(up, "gy", 1)
    tiles = max(3 * ey, ey + 6)
    right, left, three, one = pl.pallas_call(
        join_kernel(s),
        out_shape=(
            shape(8, ny * lanes + tiles * half),
            shape(8, tiles * half),
            shape(3 * ey, s.coarse_rows, half),
            shape(ey + 6, 8, LANES),
        ),
        compiler_params=params,
        name="join",
    )(edge, three, one, down, up)
    right = shifted(right, "gx", -1)
    left = shifted(left, "gx", 1)
    weight = np.where(np.arange(x_nodes) % 7 == 0, 1.0, 0.5)[:, None] * np.where(
        np.arange(z_nodes) % 7 == 0, 1.0, 0.5
    )
    return pl.pallas_call(
        finish_kernel(
            s, s.x_elems * lax.axis_size("gx"), ey * lax.axis_size("gy")
        ),
        out_shape=(
            shape(x_nodes, width),
            shape(3 * s.x_elems, 3 * ey * s.coarse_z),
            shape(s.x_elems, ey * s.z_elems),
        ),
        scratch_shapes=[
            pltpu.VMEM((rows - 8, lanes), f32),
            pltpu.VMEM((s.coarse_rows, half), f32),
            pltpu.VMEM((ey + 6, up_to(s.x_elems + 6, 8), LANES), f32),
        ],
        compiler_params=params,
        name="finish",
    )(initial_guess, jnp.asarray(weight, f32), own, down, right, left, three, one)


def solution(mesh):
    in_specs = (P("gx", "gy"), P("gx", "gy"))
    out_specs = (P("gx", "gy"), P("gx", "gy"), P("gx", "gy"))
    return jax.shard_map(local, mesh=mesh, in_specs=in_specs, out_specs=out_specs, check_vma=False)
```

time: 401 us -> 82.4 us (0.21); the launches traced: 394 us -> 81.7 us
  local copies, waits for them, and re-layouts: 165 us -> 7.81 us
  matrix products: 60.6 us -> 0 us
  starting transfers between devices: 81.8 us -> 22.5 us
  waiting for transfers between devices: 56.4 us -> 19.7 us
  Pallas kernels: 0 us -> 30.5 us
  other arithmetic: 22.5 us -> 0.35 us
  loops' own time: 5.86 us -> 0 us
    mul x28 -> x0, local copies, waits for them, and re-layouts: 94.2 us -> none  [the longest x16 88.2 us: z_block(): factor_xy * active_z]
    ppermute x24 -> x0, starting transfers between devices: 68.2 us -> none  [the longest x12 40 us: extended_2(): after = lax.ppermute(first, axis, down)]
    dot_general x24 -> x0, matrix products: 60.6 us -> none  [the longest x4 16.9 us: z_block(): jnp.einsum('sn,pqs->pqn', fwd_z, spectral * factor, precision=highest)]
    dynamic_update_slice x4 -> x0, local copies, waits for them, and re-layouts: 47.9 us -> none  [z_block(): lax.dynamic_update_slice_in_dim(accum_z, current + returned, offset_z, 2)]
    ppermute x24 -> x0, waiting for transfers between devices: 47.9 us -> none  [the longest x12 36.5 us: extended_2(): before = lax.ppermute(last, axis, up)]
    pallas_call x0 -> x3, Pallas kernels: none -> 30.5 us  [the longest x1 25.5 us: local(): pl.pallas_call(patch_kernel(s), out_shape=(shape(ny, 8, lanes), shape(ny,...]
    mul x23 -> x0, other arithmetic: 15.1 us -> none  [the longest x2 2.52 us: local(): smoothed = (start_field + node_weight * correction) * mask_own]
    ppermute x4 -> x8, waiting for transfers between devices: 8.54 us -> 19.7 us  [shifted(): return lax.ppermute(array, axis, pairs)]
  transfers between devices with their start and end apart: 28 -> 8, of which waited for: 18 -> 4; matrix products, arithmetic and copies ran while one was open for 62% -> 3% of each run, Pallas kernels for 0% -> 0%
where the time goes in v1:
time: 82.4 us; the launch traced here: 81.7 us
  Pallas kernels  30.5 us (37%)
  starting transfers between devices  22.5 us (27%)
  waiting for transfers between devices  19.7 us (24%)
  local copies, waits for them, and re-layouts  7.81 us (9%)
  between operations  0.84 us (1%)
    pallas_call x1, Pallas kernels, local(): pl.pallas_call(patch_kernel(s), out_shape=(shape(ny, 8, lanes), shape(ny,...  25.5 us
    ppermute x8, starting transfers between devices, shifted(): return lax.ppermute(array, axis, pairs)  22.5 us
    ppermute x8, waiting for transfers between devices, shifted(): return lax.ppermute(array, axis, pairs)  19.7 us
    pallas_call x1, Pallas kernels, local(): pl.pallas_call(finish_kernel(s, s.x_elems * lax.axis_size('gx'), ey * lax...  3.09 us
    unnamed x16, local copies, waits for them, and re-layouts  2.82 us
    pad x2, local copies, waits for them, and re-layouts, framed(): return jnp.pad(jnp.concatenate(parts, 0), ((0, 0), (0, tail)))  2.09 us
    pallas_call x1, Pallas kernels, local(): pl.pallas_call(join_kernel(s), out_shape=(shape(8, ny * lanes + tiles * h...  1.87 us
  transfers between devices with their start and end apart: 8, of which 4 were waited for; matrix products, arithmetic and copies ran while one was open for 3% of the time, Pallas kernels for 0%

profile of v1, /device:TPU:20, one launch (start us, length us, event | category | flops | bytes accessed | tf_op | source)
XLA Modules:
  0.0 81.7 jit_solution(17171729310754552860)
XLA Ops:
  0.6 0.0 copy-start
  0.6 1.1 %slice.28 = f32[6,6272]{1,0:T(8,128)S(1)} slice(f32[28,6272]{1,0:T(8,128)} %param.19), slice={[22:28], [0:6272]} | slice | bytes 301056 | tf_op jit(solution)/shard_map/slice | solution.py:622
  1.7 1.0 %slice.27 = f32[7,6272]{1,0:T(8,128)S(1)} slice(f32[28,6272]{1,0:T(8,128)} %guess.1), slice={[21:28], [0:6272]} | slice | bytes 351232 | tf_op jit(solution)/shard_map/slice | solution.py:622
  2.8 0.1 pad_maximum_fusion
  2.8 3.4 %collective-permute-start = (f32[13,6272]{1,0:T(8,128)S(1)}, f32[13,6272]{1,0:T(8,128)S(1)}, u32[]{:S(2)}, u32[]{:S(2)}) collective-permute-start(f32[13,6272]{1,0:T(8,128)S(1)} %pad_maximum_fusion), channel_id=1, source_target_pairs={{0,8},{8,16},{16,24},{1,9},{9,17},{17,25},{2,10},{10,18},{18,26},{... | collective-permute-start | bytes 978440 | tf_op jit(solution)/shard_map/ppermute | solution.py:33
  6.2 0.0 copy-done
  6.3 3.3 %collective-permute-start.1 = (f32[1,6272]{1,0:T(1,128)S(1)}, f32[1,6272]{1,0:T(1,128)S(1)}, u32[]{:S(2)}, u32[]{:S(2)}) collective-permute-start(f32[1,6272]{1,0:T(1,128)S(1)} %slice.30), channel_id=1, source_target_pairs={{8,0},{16,8},{24,16},{9,1},{17,9},{25,17},{10,2},{18,10},{26,18},{... | collective-permute-start | bytes 75272 | tf_op jit(solution)/shard_map/ppermute | solution.py:33
  9.6 0.1 pad.19.clone
  9.7 7.2 %collective-permute-done = f32[13,6272]{1,0:T(8,128)S(1)} collective-permute-done((f32[13,6272]{1,0:T(8,128)S(1)}, f32[13,6272]{1,0:T(8,128)S(1)}, u32[]{:S(2)}, u32[]{:S(2)}) %collective-permute-start) | collective-permute-done | bytes 326176 | tf_op jit(solution)/shard_map/ppermute | solution.py:33
  16.9 0.0 collective-permute-done.1
  17.0 0.0 copy-start.2
  17.0 0.4 concatenate.13
  17.4 0.1 slice.37
  17.6 0.6 copy-done.2
  18.1 0.2 maximum_maximum_fusion
  18.3 0.1 slice.38
  18.4 0.1 select_maximum_fusion
  18.6 1.9 %collective-permute-start.2 = (f32[40,2944]{1,0:T(8,128)S(1)}, f32[40,2944]{1,0:T(8,128)S(1)}, u32[]{:S(2)}, u32[]{:S(2)}) collective-permute-start(f32[40,2944]{1,0:T(8,128)S(1)} %select_maximum_fusion), channel_id=1, source_target_pairs={{0,1},{1,2},{2,3},{3,4},{4,5},{5,6},{6,7},{8,9},{9,10},{10,11},{11... | collective-permute-start | bytes 1413128 | tf_op jit(solution)/shard_map/ppermute | solution.py:33
  20.5 3.6 %collective-permute-start.3 = (f32[40,256]{1,0:T(8,128)S(1)}, f32[40,256]{1,0:T(8,128)S(1)}, u32[]{:S(2)}, u32[]{:S(2)}) collective-permute-start(f32[40,256]{1,0:T(8,128)S(1)} %slice.39), channel_id=1, source_target_pairs={{1,0},{2,1},{3,2},{4,3},{5,4},{6,5},{7,6},{9,8},{10,9},{11,10},{12... | collective-permute-start | bytes 122888 | tf_op jit(solution)/shard_map/ppermute | solution.py:33
  24.2 1.0 %pad.11.guess = f32[40,6400]{1,0:T(8,128)} pad(f32[40,6272]{1,0:T(8,128)S(1)} %concatenate.13, f32[]{:T(128)} %constant.18.clone.1), padding=0_0x0_128 | pad | bytes 2027524 | tf_op jit(solution)/shard_map/jit(_pad)/pad | solution.py:632
  25.2 1.1 %pad.12.load = f32[40,6400]{1,0:T(8,128)} pad(f32[40,6272]{1,0:T(8,128)S(1)} %maximum_maximum_fusion, f32[]{:T(128)} %constant.18.clone.1), padding=0_0x0_128 | pad | bytes 2027524 | tf_op jit(solution)/shard_map/jit(_pad)/pad | solution.py:632
  26.3 0.0 collective-permute-done.3.above
  26.3 0.0 copy-start.7
  26.3 2.2 %collective-permute-done.2.below = f32[40,2944]{1,0:T(8,128)S(1)} collective-permute-done((f32[40,2944]{1,0:T(8,128)S(1)}, f32[40,2944]{1,0:T(8,128)S(1)}, u32[]{:S(2)}, u32[]{:S(2)}) %collective-permute-start.2) | collective-permute-done | bytes 471072 | tf_op jit(solution)/shard_map/ppermute | solution.py:33
  28.5 0.0 copy-done.7
  28.5 0.0 copy-start.3
  28.5 0.8 copy-done.3
  29.3 25.5 %patches.1 = (f32[28,8,256]{2,1,0:T(8,128)}, f32[28,32,256]{2,1,0:T(8,128)}, f32[16,16,128]{2,1,0:T(8,128)}, f32[6,8,128]{2,1,0:T(8,128)}, f32[40,2048]{1,0:T(8,128)}, /*index=5*/f32[24,512]{1,0:T(8,128)}) custom-call(f32[40,6400]{1,0:T(8,128)} %pad.11.guess, f32[40,6400]{1,0:T(8,128)} %pad.12.load, f32[40,2944]{1,0:T(8,128)} %copy-done.3, ...), custom_call_target="tpu_custom_call" | custom-call | tf_op jit(solution)/shard_map/patches/pallas_call | solution.py:645
  54.8 1.9 %collective-permute-start.4 = (f32[40,2048]{1,0:T(8,128)}, f32[40,2048]{1,0:T(8,128)S(1)}, u32[]{:S(2)}, u32[]{:S(2)}) collective-permute-start(f32[40,2048]{1,0:T(8,128)} %get-tuple-element.14), channel_id=1, source_target_pairs={{1,0},{2,1},{3,2},{4,3},{5,4},{6,5},{7,6},{9,8},{10,9},{11,10},{12... | collective-permute-start | bytes 983048 | tf_op jit(solution)/shard_map/ppermute | solution.py:33
  56.7 2.4 %collective-permute-start.5 = (f32[24,512]{1,0:T(8,128)}, f32[24,512]{1,0:T(8,128)S(1)}, u32[]{:S(2)}, u32[]{:S(2)}) collective-permute-start(f32[24,512]{1,0:T(8,128)} %get-tuple-element.18), channel_id=1, source_target_pairs={{0,1},{1,2},{2,3},{3,4},{4,5},{5,6},{6,7},{8,9},{9,10},{10,11},{11... | collective-permute-start | bytes 147464 | tf_op jit(solution)/shard_map/ppermute | solution.py:33
  59.2 3.2 %collective-permute-done.5.up = f32[24,512]{1,0:T(8,128)S(1)} collective-permute-done((f32[24,512]{1,0:T(8,128)}, f32[24,512]{1,0:T(8,128)S(1)}, u32[]{:S(2)}, u32[]{:S(2)}) %collective-permute-start.5) | collective-permute-done | bytes 49184 | tf_op jit(solution)/shard_map/ppermute | solution.py:33
  62.4 0.0 copy-start.5
  62.4 0.0 collective-permute-done.4.down
  62.4 0.0 copy-start.1
  62.4 0.6 copy-done.5
  63.0 0.1 copy-done.1
  63.1 1.9 %join.1 = (f32[8,8704]{1,0:T(8,128)}, f32[8,1536]{1,0:T(8,128)}, f32[12,16,128]{2,1,0:T(8,128)}, f32[10,8,128]{2,1,0:T(8,128)}) custom-call(f32[28,8,256]{2,1,0:T(8,128)} %get-tuple-element.15.edge, f32[16,16,128]{2,1,0:T(8,128)} %get-tuple-element.16.three, f32[6,8,128]{2,1,0:T(8,128)} %get-tuple-element.17.one, f32[40,2048]{1,0:T(8,128)} %copy-done.1, ...), custom_call_target="tpu_custom_call" | custom-call | tf_op jit(solution)/shard_map/join/pallas_call | solution.py:673
  65.0 3.6 %collective-permute-start.6 = (f32[8,8704]{1,0:T(8,128)}, f32[8,8704]{1,0:T(8,128)S(1)}, u32[]{:S(2)}, u32[]{:S(2)}) collective-permute-start(f32[8,8704]{1,0:T(8,128)} %get-tuple-element.19), channel_id=1, source_target_pairs={{8,0},{16,8},{24,16},{9,1},{17,9},{25,17},{10,2},{18,10},{26,18},{... | collective-permute-start | bytes 835592 | tf_op jit(solution)/shard_map/ppermute | solution.py:33
  68.6 2.2 %collective-permute-start.7 = (f32[8,1536]{1,0:T(8,128)}, f32[8,1536]{1,0:T(8,128)S(1)}, u32[]{:S(2)}, u32[]{:S(2)}) collective-permute-start(f32[8,1536]{1,0:T(8,128)} %get-tuple-element.20), channel_id=1, source_target_pairs={{0,8},{8,16},{16,24},{1,9},{9,17},{17,25},{2,10},{10,18},{18,26},{... | collective-permute-start | bytes 147464 | tf_op jit(solution)/shard_map/ppermute | solution.py:33
  70.8 7.1 %collective-permute-done.7.left = f32[8,1536]{1,0:T(8,128)S(1)} collective-permute-done((f32[8,1536]{1,0:T(8,128)}, f32[8,1536]{1,0:T(8,128)S(1)}, u32[]{:S(2)}, u32[]{:S(2)}) %collective-permute-start.7) | collective-permute-done | bytes 49184 | tf_op jit(solution)/shard_map/ppermute | solution.py:33
  77.9 0.0 copy-start.6
  77.9 0.0 collective-permute-done.6.right
  77.9 0.0 copy-start.4
  77.9 0.6 copy-done.6
  78.5 0.1 copy-done.4
  78.6 3.1 %finish.1 = (f32[28,6272]{1,0:T(8,128)}, f32[12,1152]{1,0:T(8,128)}, f32[4,128]{1,0:T(4,128)}) custom-call(f32[28,6272]{1,0:T(8,128)} %guess.1, f32[28,224]{1,0:T(8,128)} %constant.57.clone.weight, f32[28,32,256]{2,1,0:T(8,128)} %get-tuple-element.13.own, f32[40,2048]{1,0:T(8,128)} %copy-done.1, f32[8,8704]{1,0:T(8,128)} %copy-done.4, f32[8,1536]{1,0:T(8,128)} %copy-done.6, ...), custom_call_target="tpu_custom_call" | custom-call | tf_op jit(solution)/shard_map/finish/pallas_call | solution.py:689
  (9 shorter events, 0.1 us)
Async XLA Ops:
  0.6 5.6 %copy-start = (f32[28,6272]{1,0:T(8,128)S(1)}, f32[28,6272]{1,0:T(8,128)}, u32[]{:S(2)}) copy-start(f32[28,6272]{1,0:T(8,128)} %guess.1) | copy-start | bytes 2107396
  2.8 14.1 %collective-permute-start = (f32[13,6272]{1,0:T(8,128)S(1)}, f32[13,6272]{1,0:T(8,128)S(1)}, u32[]{:S(2)}, u32[]{:S(2)}) collective-permute-start(f32[13,6272]{1,0:T(8,128)S(1)} %pad_maximum_fusion), channel_id=1, source_target_pairs={{0,8},{8,16},{16,24},{1,9},{9,17},{17,25},{2,10},{10,18},{18,26},{... | collective-permute-start | bytes 978440 | tf_op jit(solution)/shard_map/ppermute | solution.py:33
  6.3 10.7 %collective-permute-start.1 = (f32[1,6272]{1,0:T(1,128)S(1)}, f32[1,6272]{1,0:T(1,128)S(1)}, u32[]{:S(2)}, u32[]{:S(2)}) collective-permute-start(f32[1,6272]{1,0:T(1,128)S(1)} %slice.30), channel_id=1, source_target_pairs={{8,0},{16,8},{24,16},{9,1},{17,9},{25,17},{10,2},{18,10},{26,18},{... | collective-permute-start | bytes 75272 | tf_op jit(solution)/shard_map/ppermute | solution.py:33
  17.0 1.1 %copy-start.2 = (f32[28,6272]{1,0:T(8,128)S(1)}, f32[28,6272]{1,0:T(8,128)}, u32[]{:S(2)}) copy-start(f32[28,6272]{1,0:T(8,128)} %param.19) | copy-start | bytes 2107396
  18.6 9.9 %collective-permute-start.2 = (f32[40,2944]{1,0:T(8,128)S(1)}, f32[40,2944]{1,0:T(8,128)S(1)}, u32[]{:S(2)}, u32[]{:S(2)}) collective-permute-start(f32[40,2944]{1,0:T(8,128)S(1)} %select_maximum_fusion), channel_id=1, source_target_pairs={{0,1},{1,2},{2,3},{3,4},{4,5},{5,6},{6,7},{8,9},{9,10},{10,11},{11... | collective-permute-start | bytes 1413128 | tf_op jit(solution)/shard_map/ppermute | solution.py:33
  20.5 5.7 %collective-permute-start.3 = (f32[40,256]{1,0:T(8,128)S(1)}, f32[40,256]{1,0:T(8,128)S(1)}, u32[]{:S(2)}, u32[]{:S(2)}) collective-permute-start(f32[40,256]{1,0:T(8,128)S(1)} %slice.39), channel_id=1, source_target_pairs={{1,0},{2,1},{3,2},{4,3},{5,4},{6,5},{7,6},{9,8},{10,9},{11,10},{12... | collective-permute-start | bytes 122888 | tf_op jit(solution)/shard_map/ppermute | solution.py:33
  26.3 2.2 %copy-start.7 = (f32[40,256]{1,0:T(8,128)}, f32[40,256]{1,0:T(8,128)S(1)}, u32[]{:S(2)}) copy-start(f32[40,256]{1,0:T(8,128)S(1)} %collective-permute-done.3.above) | copy-start | bytes 122884
  28.5 0.8 copy-start.3
  54.8 7.6 %collective-permute-start.4 = (f32[40,2048]{1,0:T(8,128)}, f32[40,2048]{1,0:T(8,128)S(1)}, u32[]{:S(2)}, u32[]{:S(2)}) collective-permute-start(f32[40,2048]{1,0:T(8,128)} %get-tuple-element.14), channel_id=1, source_target_pairs={{1,0},{2,1},{3,2},{4,3},{5,4},{6,5},{7,6},{9,8},{10,9},{11,10},{12... | collective-permute-start | bytes 983048 | tf_op jit(solution)/shard_map/ppermute | solution.py:33
  56.7 5.6 %collective-permute-start.5 = (f32[24,512]{1,0:T(8,128)}, f32[24,512]{1,0:T(8,128)S(1)}, u32[]{:S(2)}, u32[]{:S(2)}) collective-permute-start(f32[24,512]{1,0:T(8,128)} %get-tuple-element.18), channel_id=1, source_target_pairs={{0,1},{1,2},{2,3},{3,4},{4,5},{5,6},{6,7},{8,9},{9,10},{10,11},{11... | collective-permute-start | bytes 147464 | tf_op jit(solution)/shard_map/ppermute | solution.py:33
  62.4 0.6 copy-start.5
  62.4 0.7 copy-start.1
  65.0 12.9 %collective-permute-start.6 = (f32[8,8704]{1,0:T(8,128)}, f32[8,8704]{1,0:T(8,128)S(1)}, u32[]{:S(2)}, u32[]{:S(2)}) collective-permute-start(f32[8,8704]{1,0:T(8,128)} %get-tuple-element.19), channel_id=1, source_target_pairs={{8,0},{16,8},{24,16},{9,1},{17,9},{25,17},{10,2},{18,10},{26,18},{... | collective-permute-start | bytes 835592 | tf_op jit(solution)/shard_map/ppermute | solution.py:33
  68.6 9.3 %collective-permute-start.7 = (f32[8,1536]{1,0:T(8,128)}, f32[8,1536]{1,0:T(8,128)S(1)}, u32[]{:S(2)}, u32[]{:S(2)}) collective-permute-start(f32[8,1536]{1,0:T(8,128)} %get-tuple-element.20), channel_id=1, source_target_pairs={{0,8},{8,16},{16,24},{1,9},{9,17},{17,25},{2,10},{10,18},{18,26},{... | collective-permute-start | bytes 147464 | tf_op jit(solution)/shard_map/ppermute | solution.py:33
  77.9 0.6 copy-start.6
  77.9 0.7 copy-start.4

commit v2 on v1

--- a/solution.py
+++ b/solution.py
@@ -641,7 +641,8 @@
     y_above = shifted(guess_ext[:, :lanes], "gy", -1)
     constants = [jnp.asarray(value, f32) for value in patch_constants(s)]
     shape = lambda *dims: jax.ShapeDtypeStruct(dims, f32)
-    params = pltpu.CompilerParams(vmem_limit_bytes=56 * 2**20)
+    params = pltpu.CompilerParams(vmem_limit_bytes=36 * 2**20)
+    vmem = lambda count: [pl.BlockSpec(memory_space=pltpu.VMEM)] * count
     edge, own, three, one, down, up = pl.pallas_call(
         patch_kernel(s),
         out_shape=(
@@ -652,6 +653,8 @@
             shape(rows, 6 * lanes + 4 * half),
             shape(s.coarse_rows + 8, 4 * half),
         ),
+        in_specs=vmem(4 + len(constants)),
+        out_specs=tuple(vmem(6)),
         scratch_shapes=[
             pltpu.VMEM((ny + 8, rows, lanes), f32),
             pltpu.VMEM((ny + 7, rows, lanes), f32),
@@ -678,6 +681,8 @@
             shape(3 * ey, s.coarse_rows, half),
             shape(ey + 6, 8, LANES),
         ),
+        in_specs=vmem(5),
+        out_specs=tuple(vmem(4)),
         compiler_params=params,
         name="join",
     )(edge, three, one, down, up)
@@ -695,6 +700,8 @@
             shape(3 * s.x_elems, 3 * ey * s.coarse_z),
             shape(s.x_elems, ey * s.z_elems),
         ),
+        in_specs=vmem(8),
+        out_specs=tuple(vmem(3)),
         scratch_shapes=[
             pltpu.VMEM((rows - 8, lanes), f32),
             pltpu.VMEM((s.coarse_rows, half), f32),

time: 82.4 us -> 72.7 us (0.88)
  Pallas kernels: 30.5 us -> 23.4 us
  local copies, waits for them, and re-layouts: 7.81 us -> 3.76 us
  waiting for transfers between devices: 19.7 us -> 21 us
    pallas_call x1, Pallas kernels: 25.5 us -> 21.8 us  [local(): pl.pallas_call(patch_kernel(s), out_shape=(shape(ny, 8, lanes), shape(ny,...]
    unnamed x16 -> x38, local copies, waits for them, and re-layouts: 2.82 us -> 0.71 us
    pad x2, local copies, waits for them, and re-layouts: 2.09 us -> 0.14 us  [framed(): return jnp.pad(jnp.concatenate(parts, 0), ((0, 0), (0, tail)))]
    pallas_call x1, Pallas kernels: 1.87 us -> 0.04 us  [local(): pl.pallas_call(join_kernel(s), out_shape=(shape(8, ny * lanes + tiles * h...]
    pallas_call x1, Pallas kernels: 3.09 us -> 1.49 us  [local(): pl.pallas_call(finish_kernel(s, s.x_elems * lax.axis_size('gx'), ey * lax...]
    ppermute x8, waiting for transfers between devices: 19.7 us -> 21 us  [shifted(): return lax.ppermute(array, axis, pairs)]
  transfers between devices with their start and end apart: 8 -> 8, of which waited for: 4 -> 5; matrix products, arithmetic and copies ran while one was open for 3% -> 0% of each run, Pallas kernels for 0% -> 0%
where the time goes in v2:
time: 72.7 us; the launch traced here: 72.1 us
  Pallas kernels  23.4 us (32%)
  starting transfers between devices  22.5 us (31%)
  waiting for transfers between devices  21 us (29%)
  local copies, waits for them, and re-layouts  3.76 us (5%)
  between operations  1.09 us (1%)
    ppermute x8, starting transfers between devices, shifted(): return lax.ppermute(array, axis, pairs)  22.5 us
    pallas_call x1, Pallas kernels, local(): pl.pallas_call(patch_kernel(s), out_shape=(shape(ny, 8, lanes), shape(ny,...  21.8 us
    ppermute x8, waiting for transfers between devices, shifted(): return lax.ppermute(array, axis, pairs)  21 us
    pallas_call x1, Pallas kernels, local(): pl.pallas_call(finish_kernel(s, s.x_elems * lax.axis_size('gx'), ey * lax...  1.49 us
  transfers between devices with their start and end apart: 8, of which 5 were waited for; matrix products, arithmetic and copies ran while one was open for 0% of the time, Pallas kernels for 0%

profile of v2, /device:TPU:20, one launch (start us, length us, event | category | flops | bytes accessed | tf_op | source)
XLA Modules:
  0.0 72.1 jit_solution(9375802803907402050)
XLA Ops:
  0.6 0.0 copy-start
  0.6 1.1 %slice.28 = f32[6,6272]{1,0:T(8,128)S(1)} slice(f32[28,6272]{1,0:T(8,128)} %param.19), slice={[22:28], [0:6272]} | slice | bytes 301056 | tf_op jit(solution)/shard_map/slice | solution.py:622
  1.7 1.0 %slice.27 = f32[7,6272]{1,0:T(8,128)S(1)} slice(f32[28,6272]{1,0:T(8,128)} %guess.1), slice={[21:28], [0:6272]} | slice | bytes 351232 | tf_op jit(solution)/shard_map/slice | solution.py:622
  2.8 0.1 pad_maximum_fusion
  2.8 3.4 %collective-permute-start = (f32[13,6272]{1,0:T(8,128)S(1)}, f32[13,6272]{1,0:T(8,128)S(1)}, u32[]{:S(2)}, u32[]{:S(2)}) collective-permute-start(f32[13,6272]{1,0:T(8,128)S(1)} %pad_maximum_fusion), channel_id=1, source_target_pairs={{0,8},{8,16},{16,24},{1,9},{9,17},{17,25},{2,10},{10,18},{18,26},{... | collective-permute-start | bytes 978440 | tf_op jit(solution)/shard_map/ppermute | solution.py:33
  6.3 3.3 %collective-permute-start.1 = (f32[1,6272]{1,0:T(1,128)S(1)}, f32[1,6272]{1,0:T(1,128)S(1)}, u32[]{:S(2)}, u32[]{:S(2)}) collective-permute-start(f32[1,6272]{1,0:T(1,128)S(1)} %slice.30), channel_id=1, source_target_pairs={{8,0},{16,8},{24,16},{9,1},{17,9},{25,17},{10,2},{18,10},{26,18},{... | collective-permute-start | bytes 75272 | tf_op jit(solution)/shard_map/ppermute | solution.py:33
  9.6 0.1 pad.19.clone
  9.7 7.2 %collective-permute-done = f32[13,6272]{1,0:T(8,128)S(1)} collective-permute-done((f32[13,6272]{1,0:T(8,128)S(1)}, f32[13,6272]{1,0:T(8,128)S(1)}, u32[]{:S(2)}, u32[]{:S(2)}) %collective-permute-start) | collective-permute-done | bytes 326176 | tf_op jit(solution)/shard_map/ppermute | solution.py:33
  16.9 0.0 collective-permute-done.1
  17.0 0.0 copy-start.18
  17.0 0.4 concatenate.13
  17.4 0.1 slice.37
  17.6 0.6 copy-done.18
  18.1 0.2 maximum_maximum_fusion
  18.3 0.1 slice.38
  18.4 0.1 select_maximum_fusion
  18.6 1.9 %collective-permute-start.2 = (f32[40,2944]{1,0:T(8,128)S(1)}, f32[40,2944]{1,0:T(8,128)S(1)}, u32[]{:S(2)}, u32[]{:S(2)}) collective-permute-start(f32[40,2944]{1,0:T(8,128)S(1)} %select_maximum_fusion), channel_id=1, source_target_pairs={{0,1},{1,2},{2,3},{3,4},{4,5},{5,6},{6,7},{8,9},{9,10},{10,11},{11... | collective-permute-start | bytes 1413128 | tf_op jit(solution)/shard_map/ppermute | solution.py:33
  20.5 3.6 %collective-permute-start.3 = (f32[40,256]{1,0:T(8,128)S(1)}, f32[40,256]{1,0:T(8,128)S(1)}, u32[]{:S(2)}, u32[]{:S(2)}) collective-permute-start(f32[40,256]{1,0:T(8,128)S(1)} %slice.39), channel_id=1, source_target_pairs={{1,0},{2,1},{3,2},{4,3},{5,4},{6,5},{7,6},{9,8},{10,9},{11,10},{12... | collective-permute-start | bytes 122888 | tf_op jit(solution)/shard_map/ppermute | solution.py:33
  24.2 0.0 copy-start.3
  24.2 0.0 copy-start.4
  24.2 0.0 copy-start.5
  24.2 0.0 copy-start.6
  24.2 0.0 copy-start.7
  24.2 0.0 copy-start.8
  24.2 0.0 copy-start.9
  24.2 0.0 copy-start.10
  24.3 0.0 copy-start.12
  24.3 0.0 copy-start.13
  24.3 0.0 copy-start.14
  24.3 0.0 copy-start.15
  24.3 0.1 pad.11.guess
  24.4 0.0 copy-start.1
  24.4 0.0 copy-start.2
  24.4 0.0 copy-start.16
  24.4 0.0 copy-start.17
  24.4 0.1 pad.12.load
  24.5 0.0 copy-start.11
  24.5 1.3 %collective-permute-done.3.above = f32[40,256]{1,0:T(8,128)S(1)} collective-permute-done((f32[40,256]{1,0:T(8,128)S(1)}, f32[40,256]{1,0:T(8,128)S(1)}, u32[]{:S(2)}, u32[]{:S(2)}) %collective-permute-start.3) | collective-permute-done | bytes 40992 | tf_op jit(solution)/shard_map/ppermute | solution.py:33
  25.8 2.7 %collective-permute-done.2.below = f32[40,2944]{1,0:T(8,128)S(1)} collective-permute-done((f32[40,2944]{1,0:T(8,128)S(1)}, f32[40,2944]{1,0:T(8,128)S(1)}, u32[]{:S(2)}, u32[]{:S(2)}) %collective-permute-start.2) | collective-permute-done | bytes 471072 | tf_op jit(solution)/shard_map/ppermute | solution.py:33
  28.6 21.8 %patches.1 = (f32[28,8,256]{2,1,0:T(8,128)S(1)}, f32[28,32,256]{2,1,0:T(8,128)S(1)}, f32[16,16,128]{2,1,0:T(8,128)S(1)}, f32[6,8,128]{2,1,0:T(8,128)S(1)}, f32[4...) custom-call(f32[40,6400]{1,0:T(8,128)S(1)} %pad.11.guess, f32[40,6400]{1,0:T(8,128)S(1)} %pad.12.load, ...), custom_call_target="tpu_custom_call" | custom-call | tf_op jit(solution)/shard_map/patches/pallas_call | solution.py:646
  50.5 1.9 %collective-permute-start.4 = (f32[40,2048]{1,0:T(8,128)S(1)}, f32[40,2048]{1,0:T(8,128)S(1)}, u32[]{:S(2)}, u32[]{:S(2)}) collective-permute-start(f32[40,2048]{1,0:T(8,128)S(1)} %get-tuple-element.14), channel_id=1, source_target_pairs={{1,0},{2,1},{3,2},{4,3},{5,4},{6,5},{7,6},{9,8},{10,9},{11,10},{12... | collective-permute-start | bytes 983048 | tf_op jit(solution)/shard_map/ppermute | solution.py:33
  52.4 2.4 %collective-permute-start.5 = (f32[24,512]{1,0:T(8,128)S(1)}, f32[24,512]{1,0:T(8,128)S(1)}, u32[]{:S(2)}, u32[]{:S(2)}) collective-permute-start(f32[24,512]{1,0:T(8,128)S(1)} %get-tuple-element.18), channel_id=1, source_target_pairs={{0,1},{1,2},{2,3},{3,4},{4,5},{5,6},{6,7},{8,9},{9,10},{10,11},{11... | collective-permute-start | bytes 147464 | tf_op jit(solution)/shard_map/ppermute | solution.py:33
  54.8 3.0 %collective-permute-done.5.up = f32[24,512]{1,0:T(8,128)S(1)} collective-permute-done((f32[24,512]{1,0:T(8,128)S(1)}, f32[24,512]{1,0:T(8,128)S(1)}, u32[]{:S(2)}, u32[]{:S(2)}) %collective-permute-start.5) | collective-permute-done | bytes 49184 | tf_op jit(solution)/shard_map/ppermute | solution.py:33
  57.8 0.0 collective-permute-done.4.down
  57.9 3.6 %collective-permute-start.6 = (f32[8,8704]{1,0:T(8,128)S(1)}, f32[8,8704]{1,0:T(8,128)S(1)}, u32[]{:S(2)}, u32[]{:S(2)}) collective-permute-start(f32[8,8704]{1,0:T(8,128)S(1)} %get-tuple-element.19), channel_id=1, source_target_pairs={{8,0},{16,8},{24,16},{9,1},{17,9},{25,17},{10,2},{18,10},{26,18},{... | collective-permute-start | bytes 835592 | tf_op jit(solution)/shard_map/ppermute | solution.py:33
  61.5 2.2 %collective-permute-start.7 = (f32[8,1536]{1,0:T(8,128)S(1)}, f32[8,1536]{1,0:T(8,128)S(1)}, u32[]{:S(2)}, u32[]{:S(2)}) collective-permute-start(f32[8,1536]{1,0:T(8,128)S(1)} %get-tuple-element.20), channel_id=1, source_target_pairs={{0,8},{8,16},{16,24},{1,9},{9,17},{17,25},{2,10},{10,18},{18,26},{... | collective-permute-start | bytes 147464 | tf_op jit(solution)/shard_map/ppermute | solution.py:33
  63.8 6.8 %collective-permute-done.7.left = f32[8,1536]{1,0:T(8,128)S(1)} collective-permute-done((f32[8,1536]{1,0:T(8,128)S(1)}, f32[8,1536]{1,0:T(8,128)S(1)}, u32[]{:S(2)}, u32[]{:S(2)}) %collective-permute-start.7) | collective-permute-done | bytes 49184 | tf_op jit(solution)/shard_map/ppermute | solution.py:33
  70.6 1.5 %finish.1 = (f32[28,6272]{1,0:T(8,128)}, f32[12,1152]{1,0:T(8,128)}, f32[4,128]{1,0:T(4,128)}) custom-call(f32[28,6272]{1,0:T(8,128)S(1)} %copy-done, f32[28,224]{1,0:T(8,128)S(1)} %copy-done.11, f32[28,32,256]{2,1,0:T(8,128)S(1)} %get-tuple-element.13.own, f32[40,2048]{1,0:T(8,128)S(1)} %collective-permute-done.4.down, ...), custom_call_target="tpu_custom_call" | custom-call | tf_op jit(solution)/shard_map/finish/pallas_call | solution.py:694
  (29 shorter events, 0.2 us)
Async XLA Ops:
  0.6 5.6 %copy-start = (f32[28,6272]{1,0:T(8,128)S(1)}, f32[28,6272]{1,0:T(8,128)}, u32[]{:S(2)}) copy-start(f32[28,6272]{1,0:T(8,128)} %guess.1) | copy-start | bytes 2107396
  2.8 14.1 %collective-permute-start = (f32[13,6272]{1,0:T(8,128)S(1)}, f32[13,6272]{1,0:T(8,128)S(1)}, u32[]{:S(2)}, u32[]{:S(2)}) collective-permute-start(f32[13,6272]{1,0:T(8,128)S(1)} %pad_maximum_fusion), channel_id=1, source_target_pairs={{0,8},{8,16},{16,24},{1,9},{9,17},{17,25},{2,10},{10,18},{18,26},{... | collective-permute-start | bytes 978440 | tf_op jit(solution)/shard_map/ppermute | solution.py:33
  6.3 10.7 %collective-permute-start.1 = (f32[1,6272]{1,0:T(1,128)S(1)}, f32[1,6272]{1,0:T(1,128)S(1)}, u32[]{:S(2)}, u32[]{:S(2)}) collective-permute-start(f32[1,6272]{1,0:T(1,128)S(1)} %slice.30), channel_id=1, source_target_pairs={{8,0},{16,8},{24,16},{9,1},{17,9},{25,17},{10,2},{18,10},{26,18},{... | collective-permute-start | bytes 75272 | tf_op jit(solution)/shard_map/ppermute | solution.py:33
  17.0 1.1 %copy-start.18 = (f32[28,6272]{1,0:T(8,128)S(1)}, f32[28,6272]{1,0:T(8,128)}, u32[]{:S(2)}) copy-start(f32[28,6272]{1,0:T(8,128)} %param.19) | copy-start | bytes 2107396
  18.6 9.9 %collective-permute-start.2 = (f32[40,2944]{1,0:T(8,128)S(1)}, f32[40,2944]{1,0:T(8,128)S(1)}, u32[]{:S(2)}, u32[]{:S(2)}) collective-permute-start(f32[40,2944]{1,0:T(8,128)S(1)} %select_maximum_fusion), channel_id=1, source_target_pairs={{0,1},{1,2},{2,3},{3,4},{4,5},{5,6},{6,7},{8,9},{9,10},{10,11},{11... | collective-permute-start | bytes 1413128 | tf_op jit(solution)/shard_map/ppermute | solution.py:33
  20.5 5.3 %collective-permute-start.3 = (f32[40,256]{1,0:T(8,128)S(1)}, f32[40,256]{1,0:T(8,128)S(1)}, u32[]{:S(2)}, u32[]{:S(2)}) collective-permute-start(f32[40,256]{1,0:T(8,128)S(1)} %slice.39), channel_id=1, source_target_pairs={{1,0},{2,1},{3,2},{4,3},{5,4},{6,5},{7,6},{9,8},{10,9},{11,10},{12... | collective-permute-start | bytes 122888 | tf_op jit(solution)/shard_map/ppermute | solution.py:33
  24.2 4.3 %copy-start.3 = (f32[256,512]{1,0:T(8,128)S(1)}, f32[256,512]{1,0:T(8,128)}, u32[]{:S(2)}) copy-start(f32[256,512]{1,0:T(8,128)} %constant.48.clone.w_z) | copy-start | bytes 1572868
  24.2 4.3 %copy-start.4 = (f32[256,256]{1,0:T(8,128)S(1)}, f32[256,256]{1,0:T(8,128)}, u32[]{:S(2)}) copy-start(f32[256,256]{1,0:T(8,128)} %constant.51.clone.q_z) | copy-start | bytes 786436
  24.2 4.3 %copy-start.5 = (f32[256,256]{1,0:T(8,128)S(1)}, f32[256,256]{1,0:T(8,128)}, u32[]{:S(2)}) copy-start(f32[256,256]{1,0:T(8,128)} %constant.20.clone.k_z) | copy-start | bytes 786436
  24.2 4.3 %copy-start.6 = (f32[256,128]{1,0:T(8,128)S(1)}, f32[256,128]{1,0:T(8,128)}, u32[]{:S(2)}) copy-start(f32[256,128]{1,0:T(8,128)} %constant.53.clone.r_z) | copy-start | bytes 393220
  24.2 4.3 %copy-start.7 = (f32[128,128]{1,0:T(8,128)S(1)}, f32[128,128]{1,0:T(8,128)}, u32[]{:S(2)}) copy-start(f32[128,128]{1,0:T(8,128)} %constant.55.clone.o_z) | copy-start | bytes 196612
  24.2 4.3 %copy-start.8 = (f32[40,256]{1,0:T(8,128)S(1)}, f32[40,256]{1,0:T(8,128)}, u32[]{:S(2)}) copy-start(f32[40,256]{1,0:T(8,128)} %constant.45.clone.m_xz) | copy-start | bytes 122884
  24.2 4.3 %copy-start.9 = (f32[40,256]{1,0:T(8,128)S(1)}, f32[40,256]{1,0:T(8,128)}, u32[]{:S(2)}) copy-start(f32[40,256]{1,0:T(8,128)} %constant.44.clone.m_z) | copy-start | bytes 122884
  24.2 4.3 %copy-start.10 = (f32[40,256]{1,0:T(8,128)S(1)}, f32[40,256]{1,0:T(8,128)}, u32[]{:S(2)}) copy-start(f32[40,256]{1,0:T(8,128)} %constant.21.clone.m_x) | copy-start | bytes 122884
  24.3 4.3 %copy-start.12 = (f32[56,40]{1,0:T(8,128)S(1)}, f32[56,40]{1,0:T(8,128)}, u32[]{:S(2)}) copy-start(f32[56,40]{1,0:T(8,128)} %constant.46.clone.w_x) | copy-start | bytes 26884
  24.3 4.3 %copy-start.13 = (f32[40,56]{1,0:T(8,128)S(1)}, f32[40,56]{1,0:T(8,128)}, u32[]{:S(2)}) copy-start(f32[40,56]{1,0:T(8,128)} %constant.47.clone.w_xt) | copy-start | bytes 26884
  24.3 4.3 %copy-start.14 = (f32[40,40]{1,0:T(8,128)S(1)}, f32[40,40]{1,0:T(8,128)}, u32[]{:S(2)}) copy-start(f32[40,40]{1,0:T(8,128)} %constant.19.clone.k_x) | copy-start | bytes 19204
  24.3 4.3 %copy-start.15 = (f32[32,40]{1,0:T(8,128)S(1)}, f32[32,40]{1,0:T(8,128)}, u32[]{:S(2)}) copy-start(f32[32,40]{1,0:T(8,128)} %constant.52.clone.q_x) | copy-start | bytes 15364
  24.4 4.2 %copy-start.1 = (f32[13,56,512]{2,1,0:T(8,128)S(1)}, f32[13,56,512]{2,1,0:T(8,128)}, u32[]{:S(2)}) copy-start(f32[13,56,512]{2,1,0:T(8,128)} %constant.50.clone.factor) | copy-start | bytes 4472836
  24.4 4.2 %copy-start.2 = (f32[512,256]{1,0:T(8,128)S(1)}, f32[512,256]{1,0:T(8,128)}, u32[]{:S(2)}) copy-start(f32[512,256]{1,0:T(8,128)} %constant.49.clone.w_zt) | copy-start | bytes 1572868
  24.4 4.2 %copy-start.16 = (f32[16,40]{1,0:T(8,128)S(1)}, f32[16,40]{1,0:T(8,128)}, u32[]{:S(2)}) copy-start(f32[16,40]{1,0:T(8,128)} %constant.54.clone.r_x) | copy-start | bytes 7684
  24.4 4.2 %copy-start.17 = (f32[8,16]{1,0:T(8,128)S(1)}, f32[8,16]{1,0:T(8,128)}, u32[]{:S(2)}) copy-start(f32[8,16]{1,0:T(8,128)} %constant.56.clone.o_x) | copy-start | bytes 1540
  24.5 46.0 %copy-start.11 = (f32[28,224]{1,0:T(8,128)S(1)}, f32[28,224]{1,0:T(8,128)}, u32[]{:S(2)}) copy-start(f32[28,224]{1,0:T(8,128)} %constant.57.clone.weight) | copy-start | bytes 75268
  50.5 7.4 %collective-permute-start.4 = (f32[40,2048]{1,0:T(8,128)S(1)}, f32[40,2048]{1,0:T(8,128)S(1)}, u32[]{:S(2)}, u32[]{:S(2)}) collective-permute-start(f32[40,2048]{1,0:T(8,128)S(1)} %get-tuple-element.14), channel_id=1, source_target_pairs={{1,0},{2,1},{3,2},{4,3},{5,4},{6,5},{7,6},{9,8},{10,9},{11,10},{12... | collective-permute-start | bytes 983048 | tf_op jit(solution)/shard_map/ppermute | solution.py:33
  52.4 5.4 %collective-permute-start.5 = (f32[24,512]{1,0:T(8,128)S(1)}, f32[24,512]{1,0:T(8,128)S(1)}, u32[]{:S(2)}, u32[]{:S(2)}) collective-permute-start(f32[24,512]{1,0:T(8,128)S(1)} %get-tuple-element.18), channel_id=1, source_target_pairs={{0,1},{1,2},{2,3},{3,4},{4,5},{5,6},{6,7},{8,9},{9,10},{10,11},{11... | collective-permute-start | bytes 147464 | tf_op jit(solution)/shard_map/ppermute | solution.py:33
  57.9 12.7 %collective-permute-start.6 = (f32[8,8704]{1,0:T(8,128)S(1)}, f32[8,8704]{1,0:T(8,128)S(1)}, u32[]{:S(2)}, u32[]{:S(2)}) collective-permute-start(f32[8,8704]{1,0:T(8,128)S(1)} %get-tuple-element.19), channel_id=1, source_target_pairs={{8,0},{16,8},{24,16},{9,1},{17,9},{25,17},{10,2},{18,10},{26,18},{... | collective-permute-start | bytes 835592 | tf_op jit(solution)/shard_map/ppermute | solution.py:33
  61.5 9.0 %collective-permute-start.7 = (f32[8,1536]{1,0:T(8,128)S(1)}, f32[8,1536]{1,0:T(8,128)S(1)}, u32[]{:S(2)}, u32[]{:S(2)}) collective-permute-start(f32[8,1536]{1,0:T(8,128)S(1)} %get-tuple-element.20), channel_id=1, source_target_pairs={{0,8},{8,16},{16,24},{1,9},{9,17},{17,25},{2,10},{10,18},{18,26},{... | collective-permute-start | bytes 147464 | tf_op jit(solution)/shard_map/ppermute | solution.py:33

commit v3 on v1

v3 whole, which is shorter than its diff:
```python
import math

import jax
import jax.numpy as jnp
import numpy as np
from jax import lax
from jax.experimental import pallas as pl
from jax.experimental.pallas import tpu as pltpu
from jax.sharding import PartitionSpec as P

EZ = 32
JAC = 4


points_seven = (
    -1.0,
    -0.8717401485096066,
    -0.5917001814331423,
    -0.2092992179024789,
    0.2092992179024789,
    0.5917001814331423,
    0.8717401485096066,
    1.0,
)
points_three = (-1.0, -0.4472135954999579, 0.4472135954999579, 1.0)
points_one = (-1.0, 1.0)
damping = 2.0 / 3.0


def shifted(array, axis, by):
    devices = lax.axis_size(axis)
    pairs = [(i, i + by) for i in range(devices) if 0 <= i + by < devices]
    return lax.ppermute(array, axis, pairs)


def legendre_at(degree, location):
    previous, current = (1.0, location)
    for level_idx in range(1, degree):
        previous, current = (
            current,
            ((2 * level_idx + 1) * location * current - level_idx * previous) / (level_idx + 1),
        )
    return current


def quadrature_weights():
    return np.array([2.0 / (56.0 * legendre_at(7, x) * legendre_at(7, x)) for x in points_seven])


def derivative_matrix():
    points = np.array(points_seven)
    products = np.array(
        [np.prod([points[i] - points[k] for k in range(8) if k != i]) for i in range(8)]
    )
    result = np.zeros((8, 8))
    for i in range(8):
        for j in range(8):
            if i != j:
                result[i, j] = products[i] / (products[j] * (points[i] - points[j]))
        result[i, i] = np.sum([1.0 / (points[i] - points[k]) for k in range(8) if k != i])
    return result


def element_stiffness():
    derivative = derivative_matrix()
    return derivative.T @ (quadrature_weights()[:, None] * derivative)


def assemble_line(elements):
    stiffness = element_stiffness()
    weights = quadrature_weights()
    extent = 7 * elements + 1
    global_stiff = np.zeros((extent, extent))
    lumped = np.zeros(extent)
    for m in range(elements):
        global_stiff[7 * m : 7 * m + 8, 7 * m : 7 * m + 8] += stiffness
        lumped[7 * m : 7 * m + 8] += weights
    return (global_stiff, lumped)


def jacobi_eigen(matrix):
    rotated_mat = matrix.copy()
    extent = matrix.shape[0]
    vectors = np.eye(extent)
    for sweep_idx in range(12):
        for p in range(extent - 1):
            for q in range(p + 1, extent):
                angle_rot = 0.5 * math.atan2(
                    2.0 * float(rotated_mat[p, q]), float(rotated_mat[q, q] - rotated_mat[p, p])
                )
                rotation = np.eye(extent)
                rotation[p, p] = math.cos(angle_rot)
                rotation[q, q] = math.cos(angle_rot)
                rotation[p, q] = math.sin(angle_rot)
                rotation[q, p] = -math.sin(angle_rot)
                rotated_mat = rotation.T @ rotated_mat @ rotation
                vectors = vectors @ rotation
    return (np.array([rotated_mat[i, i] for i in range(extent)]), vectors)


def patch_basis():
    global_stiff, lumped = assemble_line(2)
    inv_root = 1.0 / np.sqrt(lumped[1:14])
    eigvals, vectors = jacobi_eigen(
        inv_root[:, None] * global_stiff[1:14, 1:14] * inv_root[None, :]
    )
    return (eigvals, inv_root[:, None] * vectors)


def interp_matrix(coarse_pts):
    result = np.ones((8, len(coarse_pts)))
    for a in range(8):
        for c in range(len(coarse_pts)):
            for k in range(len(coarse_pts)):
                if k != c:
                    result[a, c] *= (points_seven[a] - coarse_pts[k]) / (
                        coarse_pts[c] - coarse_pts[k]
                    )
    return result


def restriction_rows(coarse_pts):
    shared = np.ones(8)
    shared[0] = 0.5
    shared[7] = 0.5
    return (interp_matrix(coarse_pts) * shared[:, None]).T


def restriction_line(elements, coarse_pts):
    degree = len(coarse_pts) - 1
    rows_mat = restriction_rows(coarse_pts)
    result = np.zeros((degree * elements + 1, 7 * elements + 1))
    for m in range(elements):
        result[degree * m : degree * m + degree + 1, 7 * m : 7 * m + 8] += rows_mat
    return result


def patch_matrix(eigbasis, vertices, extent):
    result = np.zeros((13 * vertices, extent))
    for b in range(13):
        for v in range(vertices):
            for a in range(13):
                node_idx = 7 * v + a
                result[b * vertices + v, node_idx] = eigbasis[a, b]
    return result


high = lax.Precision.HIGH
LANES = 128
f32 = jnp.float32


def up_to(length, multiple):
    return -(-length // multiple) * multiple


def placed(matrix, shape, row=0, col=0):
    result = np.zeros(shape, np.float32)
    result[row : row + matrix.shape[0], col : col + matrix.shape[1]] = matrix
    return result


def mm(left, right):
    return lax.dot_general(
        left, right, (((1,), (0,)), ((), ())), precision=high, preferred_element_type=f32
    )


class Sizes:
    def __init__(self, x_nodes, y_nodes, z_nodes):
        self.x_nodes, self.y_nodes, self.z_nodes = (x_nodes, y_nodes, z_nodes)
        self.x_elems, self.y_elems, self.z_elems = (x_nodes // 7, y_nodes // 7, z_nodes // 7)
        self.own_rows = up_to(x_nodes + 1, 8)
        self.rows = up_to(x_nodes + 8, 8)
        self.half_z = self.z_elems // 2
        self.lanes = 2 * LANES
        self.modes_x = up_to(13 * self.x_elems, 8)
        self.modes_z = up_to(13 * self.half_z, LANES)
        self.coarse_x = 3 * self.x_elems + 4
        self.coarse_y = 3 * self.y_elems + 4
        self.coarse_z = 3 * self.z_elems
        self.coarse_rows = up_to(self.coarse_x, 8)
        self.coarse_lanes = up_to(self.coarse_z, LANES)
        split = 7 * self.half_z
        self.split = split
        self.node_of_lane = np.full(self.lanes, -1)
        self.node_of_lane[6 : 6 + split] = np.arange(split)
        self.node_of_lane[LANES : LANES + split + 6] = np.arange(split - 6, 2 * split)
        self.first_copy = self.node_of_lane >= 0
        self.first_copy[LANES : LANES + 6] = False


def line_tables(elements):
    nodes = 7 * elements
    stiff, lumped = assemble_line(elements + 2)
    restrict = restriction_line(elements + 3, points_three)[3 : 3 * elements + 7, 7 : nodes + 15]
    columns = np.arange(-6, nodes)
    weight = np.where(columns % 7 == 0, 1.0, 0.5)
    mass_part = restrict[:, 1:-1] * (lumped[1 : nodes + 7] * weight)[None, :]
    stiff_part = restrict @ (stiff[: nodes + 8, 1 : nodes + 7] * weight[None, :])
    return dict(
        own_stiff=stiff[7 : nodes + 8, 7 : nodes + 7],
        mass=lumped[1 : nodes + 7],
        own=restrict[:, 7:-1],
        mass_part=mass_part,
        stiff_part=stiff_part,
    )


def rows_by_node(s, matrix, every_copy):
    used = s.node_of_lane >= 0 if every_copy else s.first_copy
    return np.where(used[:, None], matrix[np.maximum(s.node_of_lane, 0)], 0.0)


def two_parts(matrix):
    high_part = matrix.astype(np.float32).astype(jnp.bfloat16)
    low_part = (matrix - high_part.astype(np.float64)).astype(jnp.bfloat16)
    return high_part, low_part


def residual_constants(s):
    line_x = line_tables(s.x_elems)
    stiff_z, lumped_z = assemble_line(s.z_elems)
    stiff_z, lumped_z = (stiff_z[: s.z_nodes, : s.z_nodes], lumped_z[: s.z_nodes])
    mass_x = np.zeros(s.own_rows)
    mass_x[: s.x_nodes] = line_x["mass"][6:]
    mass_z = rows_by_node(s, lumped_z[:, None], True)[:, 0]
    spread = np.ones((s.own_rows, s.lanes))
    stiff = rows_by_node(s, stiff_z, False)
    stiff = rows_by_node(s, stiff.T, True).T
    wide = placed(line_x["own_stiff"], (s.own_rows, s.lanes))
    return np.concatenate(
        [
            stiff,
            spread * mass_x[:, None],
            spread * mass_z[None, :],
            mass_x[:, None] * mass_z[None, :],
            wide,
        ]
    )


def coupling_constants(s):
    stiffness = element_stiffness()
    lumped_z = assemble_line(s.z_elems)[1][: s.z_nodes]
    mass_z = rows_by_node(s, lumped_z[:, None], True)[:, 0]
    below, above = (np.zeros(s.rows), np.zeros(s.rows))
    below[2:8] = stiffness[1:7, 7]
    above[8 + s.x_nodes - 7 : 8 + s.x_nodes] = stiffness[:7, 7]
    return [below[:, None] * mass_z[None, :], above[:, None] * mass_z[None, :]]


def patch_constants(s):
    line_x = line_tables(s.x_elems)
    stiff_z, lumped_z = assemble_line(s.z_elems)
    stiff_z, lumped_z = (stiff_z[: s.z_nodes, : s.z_nodes], lumped_z[: s.z_nodes])
    weight_z = np.where(np.arange(s.z_nodes) % 7 == 0, 1.0, 0.5)
    restrict_z = restriction_line(s.z_elems, points_three)[: s.coarse_z, : s.z_nodes]
    eigvals, eigbasis = patch_basis()
    mass_z = rows_by_node(s, lumped_z[:, None], True)[:, 0]
    mass_x = np.zeros(s.rows)
    mass_x[2 : s.x_nodes + 8] = line_x["mass"]
    fwd_x = placed(
        patch_matrix(eigbasis, s.x_elems, s.x_nodes + 6), (s.modes_x, s.rows), col=2
    )
    high_x, low_x = two_parts(fwd_x.astype(np.float64))
    fwd_z = np.zeros((LANES, s.modes_z))
    fwd_z[:, : 13 * s.half_z] = patch_matrix(eigbasis, s.half_z, LANES).T
    high_z, low_z = two_parts(fwd_z)
    sums = np.ones((s.modes_x, s.modes_z))
    sums[: 13 * s.x_elems, : 13 * s.half_z] = (
        np.repeat(eigvals, s.x_elems)[:, None] + np.repeat(eigvals, s.half_z)[None, :]
    )
    coarse_of_z = np.zeros((s.z_nodes, 2 * s.coarse_lanes))
    coarse_of_z[:, : s.coarse_z] = (restrict_z * (lumped_z * weight_z)[None, :]).T
    coarse_of_z[:, s.coarse_lanes : s.coarse_lanes + s.coarse_z] = (
        restrict_z @ (stiff_z * weight_z[None, :])
    ).T
    coarse_of_x = np.zeros((2 * s.coarse_rows, s.rows))
    coarse_of_x[: s.coarse_x, 2 : s.x_nodes + 8] = line_x["mass_part"]
    coarse_of_x[s.coarse_rows : s.coarse_rows + s.coarse_x, 2 : s.x_nodes + 8] = line_x[
        "stiff_part"
    ]
    own_z = np.zeros((s.z_nodes, s.coarse_lanes))
    own_z[:, : s.coarse_z] = restrict_z.T
    one_z = placed(
        linear_from_cubic(0, s.z_elems - 1, 0, s.coarse_z - 1).T, (s.coarse_lanes, LANES)
    )
    one_x = placed(linear_from_cubic(-1, s.x_elems, -3, 3 * s.x_elems), (8, s.coarse_rows))
    singles = [
        mass_x[:, None] * mass_z[None, :],
        sums,
        rows_by_node(s, coarse_of_z, True),
        coarse_of_x,
        rows_by_node(s, own_z, False),
        placed(line_x["own"], (s.coarse_rows, s.rows), col=8),
        one_z,
        one_x,
    ]
    halves = [
        np.concatenate([high_x, high_x, low_x], 1),
        np.concatenate([high_x.T, high_x.T, low_x.T], 1),
        np.concatenate([high_z, high_z], 0),
        low_z,
        np.concatenate([high_z.T, low_z.T], 1),
        high_z.T,
    ]
    return (
        [jnp.asarray(eigvals, f32)]
        + [jnp.asarray(value, f32) for value in singles]
        + [jnp.asarray(value, jnp.bfloat16) for value in halves]
    )


def halves_of(value):
    high_part = value.astype(jnp.bfloat16)
    return high_part, (value - high_part.astype(f32)).astype(jnp.bfloat16)


def stacked_rows(value):
    high_part = value.astype(jnp.bfloat16).astype(f32)
    return jnp.concatenate([high_part, value - high_part, high_part], 0).astype(jnp.bfloat16)


def dot(left, right):
    return lax.dot_general(left, right, (((1,), (0,)), ((), ())), preferred_element_type=f32)


def linear_from_cubic(first, last, first_three, last_three):
    result = np.zeros((last - first + 1, last_three - first_three + 1))
    for m in range(first, last + 1):
        for offset, factor in (
            (0, 1.0),
            (1, (1.0 - points_three[1]) / 2.0),
            (2, (1.0 - points_three[2]) / 2.0),
            (-2, (1.0 + points_three[1]) / 2.0),
            (-1, (1.0 + points_three[2]) / 2.0),
        ):
            node = 3 * m + offset - first_three
            if 0 <= node < result.shape[1]:
                result[m - first, node] = factor
    return result


def line_of_planes(coefficients, planes):
    total = None
    for coefficient, plane in zip(coefficients, planes):
        if coefficient != 0.0:
            part = plane() * float(coefficient)
            total = part if total is None else total + part
    return total


def symmetric(vector):
    return abs(vector[0] - vector[-1]) < abs(vector[0] + vector[-1])


def lane_window(ref, start, width):
    if start < 0:
        return pltpu.roll(ref[:, 0:LANES], -start, 1)
    if start + LANES > width:
        return pltpu.roll(ref[:, width - LANES : width], width - start, 1)
    return ref[:, start : start + LANES]


def lane_mask(s, shape, first):
    lane = lax.broadcasted_iota(jnp.int32, shape, 1)
    return ((lane >= 6 + first) & (lane < 6 + s.split)) | (
        (lane >= LANES) & (lane < LANES + s.split + 6)
    )


def put_line(s, ref, index, plane):
    at = s.z_nodes * index
    rows = plane.shape[0]
    ref[0:rows, at : at + s.split] = plane[:, 6 : 6 + s.split]
    ref[0:rows, at + s.split : at + 2 * s.split] = plane[:, LANES + 6 : LANES + 6 + s.split]


def get_line(s, ref, index, width):
    at = s.z_nodes * index
    return jnp.concatenate(
        [lane_window(ref, at - 6, width), lane_window(ref, at + s.split - 6, width)], 1
    )


def residual_kernel(s):
    rows, lanes = (s.own_rows, s.lanes)
    ex, ey, nx, ny = (s.x_elems, s.y_elems, s.x_nodes, s.y_nodes)
    width = ny * s.z_nodes
    mass_y = line_tables(ey)["mass"][6:]
    stiffness = element_stiffness()

    def kernel(guess_hbm, load_hbm, table_hbm, r, edge, up_out, down_out, u, guess, load, table, sems):
        copies = [
            pltpu.make_async_copy(source, target, sems.at[index])
            for index, (source, target) in enumerate(
                [(guess_hbm, guess), (load_hbm, load), (table_hbm, table)]
            )
        ]
        for copy in copies:
            copy.start()
        k_z = table.at[0:lanes]
        m_x, m_z, m_xz, k_x_wide = [
            table.at[lanes + rows * i : lanes + rows * (i + 1)] for i in range(4)
        ]
        k_x = k_x_wide.at[:, 0:rows]
        gx = lax.axis_index("gx")
        gy = lax.axis_index("gy")
        shape = (nx, lanes)
        row = lax.broadcasted_iota(jnp.int32, shape, 0)
        live = (lane_mask(s, shape, 1) & ((row != 0) | (gx > 0))).astype(f32)
        live_y = (gy > 0).astype(f32)
        inside = lane_mask(s, shape, 0).astype(f32)
        pad = jnp.zeros((rows - nx, lanes), f32)
        copies[0].wait()
        for y in range(ny):
            mask = live if y else live * live_y
            u[y, 0:nx] = get_line(s, guess, y, width) * mask
            u[y, nx:] = pad
        copies[1].wait()
        for y in range(ny):
            r[y, 0:nx] = get_line(s, load, y, width) * inside
            r[y, nx:] = pad
        u[ny] = jnp.zeros((rows, lanes), f32)
        r[ny] = jnp.zeros((rows, lanes), f32)

        copies[2].wait()

        def direct(chunk, carry):
            base = chunk * 7
            planes = u[pl.ds(base, 7)]
            z_term = mm(planes.reshape(7 * rows, lanes), k_z[...]).reshape(7, rows, lanes)
            for i in range(7):
                x_term = mm(k_x[...], planes[i])
                both = x_term * m_z[...] + z_term[i] * m_x[...]
                r[base + i] = r[base + i] - float(mass_y[i]) * both
            return carry

        lax.fori_loop(0, ey, direct, 0)

        def along_y(tile, carry):
            at = pl.ds(pl.multiple_of(tile * 8, 8), 8)
            scale = m_xz[at, :]
            corner = None
            for e in range(ey):
                nodes = [u[7 * e + i, at, :] for i in range(8)]
                plus = [nodes[i] + nodes[7 - i] for i in range(4)]
                minus = [nodes[i] - nodes[7 - i] for i in range(4)]
                out = [None] * 8
                for i in range(4):
                    even = sum(
                        plus[k] * float(0.5 * (stiffness[i, k] + stiffness[i, 7 - k]))
                        for k in range(4)
                    )
                    odd = sum(
                        minus[k] * float(0.5 * (stiffness[i, k] - stiffness[i, 7 - k]))
                        for k in range(4)
                    )
                    out[i], out[7 - i] = (even + odd, even - odd)
                if e:
                    out[0] = out[0] + corner
                else:
                    out[0] = out[0] + nodes[0] * float(stiffness[7, 7])
                corner = out[7]
                for i in range(8 if e == ey - 1 else 7):
                    plane = 7 * e + i
                    r[plane, at, :] = r[plane, at, :] - out[i] * scale
            return carry

        lax.fori_loop(0, rows // 8, along_y, 0)
        for y in range(ny + 1):
            put_line(s, up_out, y, r[y, nx - 6 : nx + 1, :])
        up_out[7:8, :] = jnp.zeros((1, up_out.shape[1]), f32)
        put_line(s, up_out, ny + 1, u[0, nx - 6 : nx, :])
        up_out[6:7, (ny + 1) * s.z_nodes :] = jnp.zeros(
            (1, up_out.shape[1] - (ny + 1) * s.z_nodes), f32
        )
        for y in range(ny):
            down_out[y : y + 1, :] = u[y, 0:1, :]
        down_out[ny:, :] = jnp.zeros((down_out.shape[0] - ny, lanes), f32)
        edge[...] = u[0]

    return kernel


def joined_x_kernel(s):
    rows, lanes = (s.rows, s.lanes)
    nx, ny = (s.x_nodes, s.y_nodes)
    mass_y = line_tables(s.y_elems)["mass"][6:]

    def kernel(r_own, edge, u_first, below, above, c_below, c_above, r, line, up_out):
        width = below.shape[1]
        shape = (8, lanes)
        row = lax.broadcasted_iota(jnp.int32, shape, 0)
        inside = lane_mask(s, shape, 0)
        keep = (inside & (row < 6)).astype(f32)
        only = (inside & (row == 6)).astype(f32)
        zero = jnp.zeros((rows - 8 - nx, lanes), f32) if rows - 8 - nx else None
        for y in range(ny + 2):
            got = get_line(s, below, y, width)
            place = line if y == ny + 1 else r.at[y]
            own = edge[0:nx] if y == ny + 1 else r_own[y, 0:nx, :]
            place[0:2, :] = jnp.zeros((2, lanes), f32)
            place[2:8, :] = (got * keep)[0:6]
            place[8 : 8 + nx, :] = own
            if zero is not None:
                place[8 + nx :, :] = zero
            if y < ny:
                place[8:9, :] += (got * only)[6:7]
                both = (
                    c_below[...] * u_first[y : y + 1, :] + c_above[...] * above[y : y + 1, :]
                ) * float(mass_y[y])
                place[...] = place[...] - both
        for j in range(7):
            put_line(s, up_out, j, r[ny - 6 + j])
        up_out[:, 7 * s.z_nodes :] = jnp.zeros((rows, up_out.shape[1] - 7 * s.z_nodes), f32)

    return kernel


def patch_kernel(s):
    rows, lanes = (s.rows, s.lanes)
    ey, ny = (s.y_elems, s.y_nodes)
    line_y = line_tables(ey)
    _, eigbasis = patch_basis()
    stiffness = element_stiffness()
    one_y = linear_from_cubic(-1, ey, -3, 3 * ey)
    evens = [b for b in range(13) if symmetric(eigbasis[:, b])]
    odds = [b for b in range(13) if b not in evens]

    def kernel(
        r_own, line, below, above,
        lam, m_xz, sums, q_z, q_x, r_z, r_x, o_z, o_x, f_x, b_x, f_z, f_z_low, b_z, b_z_high,
        edge_out, own_out, three_out, one_out, down_out, up_out,
        r, xf, xb, c, cz, rz, hx, ex, rx, live,
    ):
        gx = lax.axis_index("gx")
        gy = lax.axis_index("gy")
        inside = lane_mask(s, (rows, lanes), 0).astype(f32)
        width = below.shape[1]
        lower = line[...] * m_xz[...]
        upper = above[...] * m_xz[...]
        for j in range(7):
            got = get_line(s, below, j, width) * inside
            if j < 6:
                r[j] = got - lower * float(stiffness[1 + j, 7])
            else:
                r[6] = r_own[0] + got
        for y in range(1, ny):
            plane = r_own[y]
            if y >= ny - 7:
                plane = plane - upper * float(stiffness[y - (ny - 7), 7])
            r[6 + y] = plane
        shape = (s.modes_x, s.modes_z)
        mode = lax.broadcasted_iota(jnp.int32, shape, 0)
        vertex = lax.broadcasted_iota(jnp.int32, shape, 1) % s.half_z
        live_x = (mode % s.x_elems != 0) | (gx > 0)
        live[0] = (live_x & (vertex != 0)).astype(f32)
        live[1] = live_x.astype(f32)
        active = (gy > 0).astype(f32)

        def along_y(tile, carry):
            at = pl.ds(pl.multiple_of(tile * 8, 8), 8)
            for v in range(ey):
                first = [r[7 * v + a, at, :] for a in range(13)]
                if v == 0:
                    first = [value * active for value in first]
                even = [first[6]] + [first[6 + a] + first[6 - a] for a in range(1, 7)]
                odd = [first[6 + a] - first[6 - a] for a in range(1, 7)]
                for b in range(13):
                    if b in evens:
                        xf[b, v, at, :] = sum(
                            even[a] * float(eigbasis[6 + a, b]) for a in range(7)
                        )
                    else:
                        xf[b, v, at, :] = sum(
                            odd[a] * float(eigbasis[7 + a, b]) for a in range(6)
                        )
            return carry

        lax.fori_loop(0, rows // 8, along_y, 0)

        def spectral(b, carry):
            planes = [dot(f_x[...], stacked_rows(xf[b, v])) for v in range(ey)]
            modes = jnp.concatenate(
                [plane[:, :LANES] for plane in planes] + [plane[:, LANES:] for plane in planes], 0
            )
            high_part, low_part = halves_of(modes)
            modes = dot(jnp.concatenate([high_part, low_part], 1), f_z[...]) + dot(
                high_part, f_z_low[...]
            )
            factor = 1.0 / (sums[...] + lam[b])
            modes = modes.reshape(2, ey, s.modes_x, s.modes_z)
            modes = jnp.concatenate(
                [
                    (modes[t] * (factor * live[t])[None]).reshape(ey * s.modes_x, s.modes_z)
                    for t in range(2)
                ],
                0,
            )
            high_part, low_part = halves_of(modes)
            both = dot(high_part, b_z[...])
            back = both[:, :LANES] + both[:, LANES:] + dot(low_part, b_z_high[...])
            for v in range(ey):
                first = v * s.modes_x
                second = (ey + v) * s.modes_x
                plane = jnp.concatenate(
                    [back[first : first + s.modes_x], back[second : second + s.modes_x]], 1
                )
                xb[b, v] = dot(b_x[...], stacked_rows(plane))
            return carry

        lax.fori_loop(0, 13, spectral, 0)

        def back_y(tile, carry):
            at = pl.ds(pl.multiple_of(tile * 8, 8), 8)
            tail = None
            for v in range(ey):
                modes = [xb[b, v, at, :] for b in range(13)]
                out = [None] * 13
                for a in range(7):
                    even = sum(modes[b] * float(eigbasis[6 + a, b]) for b in evens)
                    if a == 0:
                        out[6] = even
                        continue
                    odd = sum(modes[b] * float(eigbasis[6 + a, b]) for b in odds)
                    out[6 + a], out[6 - a] = (even + odd, even - odd)
                if v:
                    out[:6] = [value + other for value, other in zip(out[:6], tail)]
                tail = out[7:]
                for a in range(13 if v == ey - 1 else 7):
                    c[7 * v + a, at, :] = out[a]
            return carry

        lax.fori_loop(0, rows // 8, back_y, 0)

        for j in range(6):
            down_out[:, lanes * j : lanes * (j + 1)] = c[j]
        edge_out[...] = c[6:, 0:8, :]
        own_out[...] = c[6:, 8:, :]

        half = s.coarse_lanes
        rows_c = s.coarse_rows
        cz[...] = mm(c[...].reshape((ny + 6) * rows, lanes), q_z[...]).reshape(
            ny + 6, rows, 2 * half
        )
        rz[...] = mm(r[6 : ny + 6].reshape(ny * rows, lanes), r_z[...]).reshape(ny, rows, half)
        for y in range(ny + 6):
            plane = mm(q_x[...], cz[y])
            hx[y] = plane[:rows_c, :half]
            ex[y] = plane[rows_c:, :half] + plane[:rows_c, half:]
        for y in range(ny):
            rx[y] = mm(r_x[...], rz[y])
        for j in range(s.coarse_y):
            three_out[j] = line_of_planes(
                np.concatenate(
                    [line_y["own"][j], -line_y["stiff_part"][j], -line_y["mass_part"][j]]
                ),
                [lambda y=y: rx[y] for y in range(ny)]
                + [lambda y=y: hx[y] for y in range(ny + 6)]
                + [lambda y=y: ex[y] for y in range(ny + 6)],
            )
        one_all = mm(
            three_out[...].reshape(s.coarse_y * rows_c, half), o_z[...]
        ).reshape(s.coarse_y, rows_c, LANES)
        for m in range(ey + 2):
            mixed = line_of_planes(
                one_y[m], [lambda j=j: one_all[j] for j in range(s.coarse_y)]
            )
            one_out[m] = mm(o_x[...], mixed)
        base = 6 * lanes
        for j in range(4):
            at = base + half * j
            if j < 3:
                down_out[0:rows_c, at : at + half] = three_out[j]
            else:
                down_out[0:rows_c, at : at + half] = jnp.zeros((rows_c, half), f32)
            down_out[rows_c : rows_c + 8, at : at + LANES] = one_out[j]
            down_out[rows_c + 8 :, at : at + half] = jnp.zeros((rows - rows_c - 8, half), f32)
            up_at = half * j
            if j == 0:
                up_out[0:rows_c, up_at : up_at + half] = three_out[s.coarse_y - 1]
            else:
                up_out[0:rows_c, up_at : up_at + half] = jnp.zeros((rows_c, half), f32)
            up_out[rows_c : rows_c + 8, up_at : up_at + LANES] = one_out[ey - 2 + j]

    return kernel


def join_kernel(s):
    lanes, half, rows_c = (s.lanes, s.coarse_lanes, s.coarse_rows)
    ey, ny = (s.y_elems, s.y_nodes)

    def kernel(edge, three, one, down, up, down_out, up_out, three_out, one_out):
        for y in range(ny):
            plane = edge[y]
            if y >= ny - 6:
                j = y - (ny - 6)
                plane = plane + down[0:8, lanes * j : lanes * (j + 1)]
            down_out[6 * y : 6 * y + 6, :] = plane[2:8]
        base = 6 * lanes
        first = 6 * ny
        down_out[first:, :] = jnp.zeros((down_out.shape[0] - first, lanes), f32)
        up_out[...] = jnp.zeros(up_out.shape, f32)
        for j in range(3 * ey):
            plane = three[3 + j]
            if j >= 3 * ey - 3:
                k = j - (3 * ey - 3)
                plane = plane + down[0:rows_c, base + half * k : base + half * (k + 1)]
            if j == 0:
                plane = plane + up[0:rows_c, 0:half]
            three_out[j] = plane
            down_out[first + 3 * j : first + 3 * j + 3, 0:half] = plane[0:3]
            up_out[j : j + 1, 0:half] = plane[s.coarse_x - 1 : s.coarse_x]
        for j in range(ey + 6):
            y = j - 3
            plane = None
            if -1 <= y <= ey:
                plane = one[y + 1]
            if y <= 0:
                k = y + 3
                part = up[rows_c : rows_c + 8, half * k : half * k + LANES]
                plane = part if plane is None else plane + part
            if y >= ey - 1:
                k = y - (ey - 1)
                at = base + half * k
                part = down[rows_c : rows_c + 8, at : at + LANES]
                plane = part if plane is None else plane + part
            one_out[j] = plane
            down_out[first + 4 * j : first + 4 * j + 4, half : half + LANES] = plane[0:4]
            up_out[4 * j : 4 * j + 4, half : half + LANES] = plane[s.x_elems - 2 : s.x_elems + 2]

    return kernel


def shared_lanes(s, shape):
    lane = lax.broadcasted_iota(jnp.int32, shape, 1)
    return ((lane >= s.split) & (lane < s.split + 6)).astype(f32)


def base_kernel(s):
    lanes, nx, ny = (s.lanes, s.x_nodes, s.y_nodes)
    width = ny * s.z_nodes

    def kernel(guess, weight, own, down, out):
        gx = lax.axis_index("gx")
        gy = lax.axis_index("gy")
        shape = (nx, lanes)
        row = lax.broadcasted_iota(jnp.int32, shape, 0)
        live = (lane_mask(s, shape, 1) & ((row != 0) | (gx > 0))).astype(f32)
        live_y = (gy > 0).astype(f32)
        shared = shared_lanes(s, shape)
        for y in range(ny):
            plane = own[y, 0:nx, :]
            if y >= ny - 6:
                j = y - (ny - 6)
                plane = plane + down[8 : 8 + nx, lanes * j : lanes * (j + 1)]
            plane = plane + pltpu.roll(plane, lanes - (LANES - s.split), 1) * shared
            mask = live if y else live * live_y
            factor = weight[...] * (1.0 if y % 7 == 0 else 0.5)
            put_line(s, out, y, (get_line(s, guess, y, width) + factor * plane) * mask)

    return kernel


def finish_kernel(s, x_total, y_total):
    lanes, half, rows_c, nz = (s.lanes, s.coarse_lanes, s.coarse_rows, s.z_nodes)
    ex, ey, nx, ny = (s.x_elems, s.y_elems, s.x_nodes, s.y_nodes)
    one_rows = up_to(ex + 6, 8)
    split = s.split

    def kernel(
        base, weight, right, left, three, one,
        smooth_out, three_out, coarse_out, fine, level,
    ):
        gx = lax.axis_index("gx")
        gy = lax.axis_index("gy")
        live_y = (gy > 0).astype(f32)
        shared = shared_lanes(s, (6, lanes))
        smooth_out[...] = base[...]
        for y in range(ny):
            plane = right[6 * y : 6 * y + 6, :]
            plane = plane + pltpu.roll(plane, lanes - (LANES - split), 1) * shared
            plane = plane * weight[nx - 6 : nx, :] * (1.0 if y % 7 == 0 else 0.5)
            for t in range(2):
                at = nz * y + split * t
                lanes_at = LANES * t + 6
                smooth_out[nx - 6 : nx, at : at + split] += plane[:, lanes_at : lanes_at + split]
        first = 6 * ny
        nzc = s.coarse_z
        lane = lax.broadcasted_iota(jnp.int32, (3 * ex, nzc), 1)
        row = lax.broadcasted_iota(jnp.int32, (3 * ex, nzc), 0)
        live = ((lane >= 1) & ((row >= 1) | (gx > 0))).astype(f32)
        for j in range(3 * ey):
            fine[j] = three[j]
            fine[j, 3 * ex : 3 * ex + 3, :] += right[first + 3 * j : first + 3 * j + 3, 0:half]
            fine[j, 3:4, :] += left[j : j + 1, 0:half]
            mask = live if j else live * live_y
            three_out[:, nzc * j : nzc * (j + 1)] = fine[j, 3 : 3 * ex + 3, 0:nzc] * mask
        level[...] = jnp.zeros((ey + 6, one_rows, LANES), f32)
        for j in range(ey + 6):
            level[j, 2 : ex + 4, :] = one[j, 0 : ex + 2, :]
            level[j, 0:4, :] += left[4 * j : 4 * j + 4, half : half + LANES]
            level[j, ex + 2 : ex + 6, :] += right[
                first + 4 * j : first + 4 * j + 4, half : half + LANES
            ]
        shape = (one_rows, LANES)
        lane = lax.broadcasted_iota(jnp.int32, shape, 1)
        row = lax.broadcasted_iota(jnp.int32, shape, 0)
        global_x = gx * ex + row - 3
        plane_mask = (
            (lane >= 1) & (lane < s.z_elems) & (row < ex + 6)
            & (global_x >= 1) & (global_x < x_total)
        )
        masks = []
        for j in range(ey + 6):
            global_y = gy * ey + (j - 3)
            inside = (global_y >= 1) & (global_y < y_total)
            masks.append((plane_mask & inside).astype(f32))
        levels = [level[j] for j in range(ey + 6)]
        error = [damping / 12.0 * a * m for a, m in zip(levels, masks)]
        zero = jnp.zeros(shape, f32)
        for sweep in range(1, JAC):
            lower = [zero] + error[:-1]
            upper = error[1:] + [zero]
            fresh = []
            for j in range(ey + 6):
                here = error[j]
                neighbours = (
                    lower[j]
                    + upper[j]
                    + pltpu.roll(here, 1, 0)
                    + pltpu.roll(here, one_rows - 1, 0)
                    + pltpu.roll(here, 1, 1)
                    + pltpu.roll(here, LANES - 1, 1)
                )
                applied = 12.0 * here - 2.0 * neighbours
                fresh.append((here + damping / 12.0 * (levels[j] - applied)) * masks[j])
            error = fresh
        nze = s.z_elems
        for j in range(ey):
            coarse_out[:, nze * j : nze * (j + 1)] = error[3 + j][3 : 3 + ex, 0:nze]

    return kernel


def local(load_vector, initial_guess):
    z_nodes = 7 * EZ
    x_nodes = load_vector.shape[0]
    y_nodes = load_vector.shape[1] // z_nodes
    s = Sizes(x_nodes, y_nodes, z_nodes)
    rows, lanes, half = (s.rows, s.lanes, s.coarse_lanes)
    ny, ey = (s.y_nodes, s.y_elems)
    width = y_nodes * z_nodes
    shape = lambda *dims: jax.ShapeDtypeStruct(dims, f32)
    params = pltpu.CompilerParams(vmem_limit_bytes=36 * 2**20)
    vmem = lambda count: [pl.BlockSpec(memory_space=pltpu.VMEM)] * count

    def call(kernel, name, outputs, operands, scratch=(), spaces=None, semaphores=0):
        specs = vmem(len(operands))
        for index, space in (spaces or {}).items():
            specs[index] = pl.BlockSpec(memory_space=space)
        return pl.pallas_call(
            kernel,
            out_shape=tuple(shape(*dims) for dims in outputs),
            in_specs=specs,
            out_specs=tuple(vmem(len(outputs))),
            scratch_shapes=[pltpu.VMEM(dims, f32) for dims in scratch]
            + ([pltpu.SemaphoreType.DMA((semaphores,))] if semaphores else []),
            compiler_params=params,
            name=name,
        )(*operands)

    table = residual_constants(s)
    r_own, edge, up, u_first = call(
        residual_kernel(s),
        "residual",
        (
            (ny + 1, s.own_rows, lanes),
            (s.own_rows, lanes),
            (8, up_to((ny + 2) * z_nodes, LANES)),
            (up_to(ny, 8), lanes),
        ),
        [
            pltpu.with_memory_space_constraint(value, pltpu.HBM)
            for value in (initial_guess, load_vector, jnp.asarray(table, f32))
        ],
        [
            (ny + 1, s.own_rows, lanes),
            initial_guess.shape,
            load_vector.shape,
            table.shape,
        ],
        spaces={0: pltpu.HBM, 1: pltpu.HBM, 2: pltpu.HBM},
        semaphores=3,
    )
    below = shifted(up, "gx", 1)
    above = shifted(u_first, "gx", -1)
    r_x, line, up = call(
        joined_x_kernel(s),
        "joined_x",
        (
            (ny + 1, rows, lanes),
            (rows, lanes),
            (rows, up_to(7 * z_nodes, LANES)),
        ),
        [r_own, edge, u_first, below, above]
        + [jnp.asarray(v, f32) for v in coupling_constants(s)],
    )
    below = shifted(up, "gy", 1)
    above = shifted(line, "gy", -1)
    edge, own, three, one, down, up = call(
        patch_kernel(s),
        "patches",
        (
            (ny, 8, lanes),
            (ny, rows - 8, lanes),
            (s.coarse_y, s.coarse_rows, half),
            (ey + 2, 8, LANES),
            (rows, 6 * lanes + 4 * half),
            (s.coarse_rows + 8, 4 * half),
        ),
        [r_x, line, below, above] + patch_constants(s),
        [
            (ny + 6, rows, lanes),
            (13, ey, rows, lanes),
            (13, ey, rows, lanes),
            (ny + 6, rows, lanes),
            (ny + 6, rows, 2 * half),
            (ny, rows, half),
            (ny + 6, s.coarse_rows, half),
            (ny + 6, s.coarse_rows, half),
            (ny, s.coarse_rows, half),
            (2, s.modes_x, s.modes_z),
        ],
        spaces={4: pltpu.SMEM},
    )
    down = shifted(down, "gy", -1)
    up = shifted(up, "gy", 1)
    coarse_part = up_to(max(9 * ey, 4 * ey + 24), 8)
    right, left, three, one = call(
        join_kernel(s),
        "join",
        (
            (6 * ny + coarse_part, lanes),
            (up_to(max(3 * ey, 4 * ey + 24), 8), lanes),
            (3 * ey, s.coarse_rows, half),
            (ey + 6, 8, LANES),
        ),
        [edge, three, one, down, up],
    )
    right = shifted(right, "gx", -1)
    left = shifted(left, "gx", 1)
    weight_z = np.where(np.arange(z_nodes) % 7 == 0, 1.0, 0.5)
    weight = jnp.asarray(
        np.where(np.arange(x_nodes) % 7 == 0, 1.0, 0.5)[:, None]
        * rows_by_node(s, weight_z[:, None], True)[:, 0],
        f32,
    )
    (base,) = call(
        base_kernel(s), "base", ((x_nodes, width),), [initial_guess, weight, own, down]
    )
    return call(
        finish_kernel(s, s.x_elems * lax.axis_size("gx"), ey * lax.axis_size("gy")),
        "finish",
        (
            (x_nodes, width),
            (3 * s.x_elems, 3 * ey * s.coarse_z),
            (s.x_elems, ey * s.z_elems),
        ),
        [base, weight, right, left, three, one],
        [
            (3 * ey, s.coarse_rows, half),
            (ey + 6, up_to(s.x_elems + 6, 8), LANES),
        ],
    )


def solution(mesh):
    in_specs = (P("gx", "gy"), P("gx", "gy"))
    out_specs = (P("gx", "gy"), P("gx", "gy"), P("gx", "gy"))
    return jax.shard_map(local, mesh=mesh, in_specs=in_specs, out_specs=out_specs, check_vma=False)
```

time: 82.4 us -> 62.5 us (0.76)
  waiting for transfers between devices: 19.7 us -> 11.9 us
  local copies, waits for them, and re-layouts: 7.81 us -> 0.13 us
  Pallas kernels: 30.5 us -> 25.5 us
    ppermute x8, waiting for transfers between devices: 19.7 us -> 11.9 us  [shifted(): return lax.ppermute(array, axis, pairs)]
    pallas_call x3 -> x6, Pallas kernels: 30.5 us -> 25.5 us  [call(): pl.pallas_call(kernel, out_shape=tuple((shape(*dims) for dims in outputs)...]
    unnamed x16 -> x38, local copies, waits for them, and re-layouts: 2.82 us -> 0.13 us
    slice x8 -> x0, local copies, waits for them, and re-layouts: 2.42 us -> none  [the longest x1 1.1 us: local(): load_vector[x_nodes - 6:]]
    pad x2 -> x0, local copies, waits for them, and re-layouts: 2.09 us -> none  [framed(): return jnp.pad(jnp.concatenate(parts, 0), ((0, 0), (0, tail)))]
  transfers between devices with their start and end apart: 8 -> 8, of which waited for: 4 -> 6; matrix products, arithmetic and copies ran while one was open for 3% -> 0% of each run, Pallas kernels for 0% -> 4%
where the time goes in v3:
time: 62.5 us; the launch traced here: 61.8 us
  Pallas kernels  25.5 us (41%)
  starting transfers between devices  23.3 us (37%)
  waiting for transfers between devices  11.9 us (19%)
  between operations  0.99 us (2%)
    pallas_call x6, Pallas kernels, call(): pl.pallas_call(kernel, out_shape=tuple((shape(*dims) for dims in outputs)...  25.5 us
    ppermute x8, starting transfers between devices, shifted(): return lax.ppermute(array, axis, pairs)  23.3 us
    ppermute x8, waiting for transfers between devices, shifted(): return lax.ppermute(array, axis, pairs)  11.9 us
  transfers between devices with their start and end apart: 8, of which 6 were waited for; matrix products, arithmetic and copies ran while one was open for 0% of the time, Pallas kernels for 4%

profile of v3, /device:TPU:20, one launch (start us, length us, event | category | flops | bytes accessed | tf_op | source)
XLA Modules:
  0.0 61.8 jit_solution(18117378238622882069)
XLA Ops:
  0.6 0.0 copy-start.11
  0.6 0.0 copy-start.12
  0.7 0.0 copy-start.1
  0.7 0.0 copy-start.3
  0.7 0.0 copy-start.4
  0.7 0.0 copy-start.5
  0.7 0.0 copy-start.6
  0.7 0.0 copy-start.7
  0.7 0.0 copy-start.8
  0.7 0.0 copy-start.9
  0.8 0.0 copy-start.10
  0.8 0.0 copy-start.13
  0.8 0.0 copy-start.14
  0.8 0.0 copy-start.15
  0.8 0.0 copy-start.16
  0.8 0.0 copy-start.17
  0.8 0.0 copy-start.18
  0.8 4.3 %residual.1 = (f32[29,32,256]{2,1,0:T(8,128)S(1)}, f32[32,256]{1,0:T(8,128)S(1)}, f32[8,6784]{1,0:T(8,128)S(1)}, f32[32,256]{1,0:T(8,128)S(1)}) custom-call(f32[28,6272]{1,0:T(8,128)} %guess.1, f32[28,6272]{1,0:T(8,128)} %load_hbm.1, f32[384,256]{1,0:T(8,128)} %constant.38.clone.table_hbm), custom_call_target="tpu_custom_call" | custom-call | tf_op jit(solution)/shard_map/residual/pallas_call | solution.py:864
  5.1 3.4 %collective-permute-start = (f32[8,6784]{1,0:T(8,128)S(1)}, f32[8,6784]{1,0:T(8,128)S(1)}, u32[]{:S(2)}, u32[]{:S(2)}) collective-permute-start(f32[8,6784]{1,0:T(8,128)S(1)} %get-tuple-element.23), channel_id=1, source_target_pairs={{0,8},{8,16},{16,24},{1,9},{9,17},{17,25},{2,10},{10,18},{18,26},{... | collective-permute-start | bytes 651272 | tf_op jit(solution)/shard_map/ppermute | solution.py:33
  8.5 3.3 %collective-permute-start.1 = (f32[32,256]{1,0:T(8,128)S(1)}, f32[32,256]{1,0:T(8,128)S(1)}, u32[]{:S(2)}, u32[]{:S(2)}) collective-permute-start(f32[32,256]{1,0:T(8,128)S(1)} %get-tuple-element.22.u_first), channel_id=1, source_target_pairs={{8,0},{16,8},{24,16},{9,1},{17,9},{25,17},{10,2},{18,10},{26,18},{... | collective-permute-start | bytes 98312 | tf_op jit(solution)/shard_map/ppermute | solution.py:33
  11.9 2.5 %collective-permute-done.1.above = f32[32,256]{1,0:T(8,128)S(1)} collective-permute-done((f32[32,256]{1,0:T(8,128)S(1)}, f32[32,256]{1,0:T(8,128)S(1)}, u32[]{:S(2)}, u32[]{:S(2)}) %collective-permute-start.1) | collective-permute-done | bytes 32800 | tf_op jit(solution)/shard_map/ppermute | solution.py:33
  14.3 1.0 %collective-permute-done.below = f32[8,6784]{1,0:T(8,128)S(1)} collective-permute-done((f32[8,6784]{1,0:T(8,128)S(1)}, f32[8,6784]{1,0:T(8,128)S(1)}, u32[]{:S(2)}, u32[]{:S(2)}) %collective-permute-start) | collective-permute-done | bytes 217120 | tf_op jit(solution)/shard_map/ppermute | solution.py:33
  15.3 0.0 copy-done.11
  15.3 0.5 joined_x.1
  15.8 1.9 %collective-permute-start.2 = (f32[40,1664]{1,0:T(8,128)S(1)}, f32[40,1664]{1,0:T(8,128)S(1)}, u32[]{:S(2)}, u32[]{:S(2)}) collective-permute-start(f32[40,1664]{1,0:T(8,128)S(1)} %get-tuple-element.26), channel_id=1, source_target_pairs={{0,1},{1,2},{2,3},{3,4},{4,5},{5,6},{6,7},{8,9},{9,10},{10,11},{11... | collective-permute-start | bytes 798728 | tf_op jit(solution)/shard_map/ppermute | solution.py:33
  17.8 3.6 %collective-permute-start.3 = (f32[40,256]{1,0:T(8,128)S(1)}, f32[40,256]{1,0:T(8,128)S(1)}, u32[]{:S(2)}, u32[]{:S(2)}) collective-permute-start(f32[40,256]{1,0:T(8,128)S(1)} %get-tuple-element.25.line), channel_id=1, source_target_pairs={{1,0},{2,1},{3,2},{4,3},{5,4},{6,5},{7,6},{9,8},{10,9},{11,10},{12... | collective-permute-start | bytes 122888 | tf_op jit(solution)/shard_map/ppermute | solution.py:33
  21.4 1.7 %collective-permute-done.3.above = f32[40,256]{1,0:T(8,128)S(1)} collective-permute-done((f32[40,256]{1,0:T(8,128)S(1)}, f32[40,256]{1,0:T(8,128)S(1)}, u32[]{:S(2)}, u32[]{:S(2)}) %collective-permute-start.3) | collective-permute-done | bytes 40992 | tf_op jit(solution)/shard_map/ppermute | solution.py:33
  23.1 0.5 collective-permute-done.2.below
  23.6 0.0 copy-done.5
  23.6 0.0 copy-done.6
  23.6 0.0 copy-done.7
  23.6 0.0 copy-done.8
  23.6 0.0 copy-done.9
  23.6 0.0 copy-done.10
  23.6 0.0 copy-done.13
  23.7 0.0 copy-start
  23.7 0.0 copy-start.2
  23.7 16.5 %patches.1 = (f32[28,8,256]{2,1,0:T(8,128)S(1)}, f32[28,32,256]{2,1,0:T(8,128)S(1)}, f32[16,16,128]{2,1,0:T(8,128)S(1)}, f32[6,8,128]{2,1,0:T(8,128)S(1)}, f32[4...) custom-call(f32[29,40,256]{2,1,0:T(8,128)S(1)} %get-tuple-element.24.r_own, f32[40,256]{1,0:T(8,128)S(1)} %get-tuple-element.25.line, ...), custom_call_target="tpu_custom_call" | custom-call | tf_op jit(solution)/shard_map/patches/pallas_call | solution.py:864
  40.2 3.2 %collective-permute-start.4 = (f32[40,2048]{1,0:T(8,128)S(1)}, f32[40,2048]{1,0:T(8,128)S(1)}, u32[]{:S(2)}, u32[]{:S(2)}) collective-permute-start(f32[40,2048]{1,0:T(8,128)S(1)} %get-tuple-element.28), channel_id=1, source_target_pairs={{1,0},{2,1},{3,2},{4,3},{5,4},{6,5},{7,6},{9,8},{10,9},{11,10},{12... | collective-permute-start | bytes 983048 | tf_op jit(solution)/shard_map/ppermute | solution.py:33
  43.4 1.9 %collective-permute-start.5 = (f32[24,512]{1,0:T(8,128)S(1)}, f32[24,512]{1,0:T(8,128)S(1)}, u32[]{:S(2)}, u32[]{:S(2)}) collective-permute-start(f32[24,512]{1,0:T(8,128)S(1)} %get-tuple-element.32), channel_id=1, source_target_pairs={{0,1},{1,2},{2,3},{3,4},{4,5},{5,6},{6,7},{8,9},{9,10},{10,11},{11... | collective-permute-start | bytes 147464 | tf_op jit(solution)/shard_map/ppermute | solution.py:33
  45.3 3.5 %collective-permute-done.5.up = f32[24,512]{1,0:T(8,128)S(1)} collective-permute-done((f32[24,512]{1,0:T(8,128)S(1)}, f32[24,512]{1,0:T(8,128)S(1)}, u32[]{:S(2)}, u32[]{:S(2)}) %collective-permute-start.5) | collective-permute-done | bytes 49184 | tf_op jit(solution)/shard_map/ppermute | solution.py:33
  48.8 0.0 collective-permute-done.4.down
  48.9 3.8 %collective-permute-start.6 = (f32[208,256]{1,0:T(8,128)S(1)}, f32[208,256]{1,0:T(8,128)S(1)}, u32[]{:S(2)}, u32[]{:S(2)}) collective-permute-start(f32[208,256]{1,0:T(8,128)S(1)} %get-tuple-element.33), channel_id=1, source_target_pairs={{8,0},{16,8},{24,16},{9,1},{17,9},{25,17},{10,2},{18,10},{26,18},{... | collective-permute-start | bytes 638984 | tf_op jit(solution)/shard_map/ppermute | solution.py:33
  52.6 2.1 %collective-permute-start.7 = (f32[40,256]{1,0:T(8,128)S(1)}, f32[40,256]{1,0:T(8,128)S(1)}, u32[]{:S(2)}, u32[]{:S(2)}) collective-permute-start(f32[40,256]{1,0:T(8,128)S(1)} %get-tuple-element.34), channel_id=1, source_target_pairs={{0,8},{8,16},{16,24},{1,9},{9,17},{17,25},{2,10},{10,18},{18,26},{... | collective-permute-start | bytes 122888 | tf_op jit(solution)/shard_map/ppermute | solution.py:33
  54.7 2.5 %base.1 = f32[28,6272]{1,0:T(8,128)S(1)} custom-call(f32[28,6272]{1,0:T(8,128)S(1)} %copy-done, f32[28,256]{1,0:T(8,128)S(1)} %copy-done.2, f32[28,32,256]{2,1,0:T(8,128)S(1)} %get-tuple-element.27.own, f32[40,2048]{1,0:T(8,128)S(1)} %collective-permute-done.4.down), custom_call_target="tpu_custom_call" | custom-call | tf_op jit(solution)/shard_map/base/pallas_call | solution.py:864
  57.2 2.8 %collective-permute-done.7.left = f32[40,256]{1,0:T(8,128)S(1)} collective-permute-done((f32[40,256]{1,0:T(8,128)S(1)}, f32[40,256]{1,0:T(8,128)S(1)}, u32[]{:S(2)}, u32[]{:S(2)}) %collective-permute-start.7) | collective-permute-done | bytes 40992 | tf_op jit(solution)/shard_map/ppermute | solution.py:33
  60.1 0.0 collective-permute-done.6.right
  60.1 1.8 %finish.1 = (f32[28,6272]{1,0:T(8,128)}, f32[12,1152]{1,0:T(8,128)}, f32[4,128]{1,0:T(4,128)}) custom-call(f32[28,6272]{1,0:T(8,128)S(1)} %base.1, f32[28,256]{1,0:T(8,128)S(1)} %copy-done.2, f32[208,256]{1,0:T(8,128)S(1)} %collective-permute-done.6.right, f32[40,256]{1,0:T(8,128)S(1)} %collective-permute-done.7.left, ...), custom_call_target="tpu_custom_call" | custom-call | tf_op jit(solution)/shard_map/finish/pallas_call | solution.py:864
  (12 shorter events, 0.1 us)
Async XLA Ops:
  0.6 14.7 %copy-start.11 = (f32[40,256]{1,0:T(8,128)S(1)}, f32[40,256]{1,0:T(8,128)}, u32[]{:S(2)}) copy-start(f32[40,256]{1,0:T(8,128)} %constant.40.clone.c_above) | copy-start | bytes 122884
  0.6 14.7 %copy-start.12 = (f32[40,256]{1,0:T(8,128)S(1)}, f32[40,256]{1,0:T(8,128)}, u32[]{:S(2)}) copy-start(f32[40,256]{1,0:T(8,128)} %constant.39.clone.c_below) | copy-start | bytes 122884
  0.7 22.9 %copy-start.1 = (f32[256,256]{1,0:T(8,128)S(1)}, f32[256,256]{1,0:T(8,128)}, u32[]{:S(2)}) copy-start(f32[256,256]{1,0:T(8,128)} %constant.44.clone.q_z) | copy-start | bytes 786436
  0.7 22.9 %copy-start.3 = (bf16[256,256]{1,0:T(8,128)(2,1)S(1)}, bf16[256,256]{1,0:T(8,128)(2,1)}, u32[]{:S(2)}) copy-start(bf16[256,256]{1,0:T(8,128)(2,1)} %constant.54.clone.b_z) | copy-start | bytes 393220
  0.7 22.9 %copy-start.4 = (bf16[256,256]{1,0:T(8,128)(2,1)S(1)}, bf16[256,256]{1,0:T(8,128)(2,1)}, u32[]{:S(2)}) copy-start(bf16[256,256]{1,0:T(8,128)(2,1)} %constant.52.clone.f_z) | copy-start | bytes 393220
  0.7 22.9 %copy-start.5 = (f32[256,128]{1,0:T(8,128)S(1)}, f32[256,128]{1,0:T(8,128)}, u32[]{:S(2)}) copy-start(f32[256,128]{1,0:T(8,128)} %constant.46.clone.r_z) | copy-start | bytes 393220
  0.7 22.9 %copy-start.6 = (bf16[256,128]{1,0:T(8,128)(2,1)S(1)}, bf16[256,128]{1,0:T(8,128)(2,1)}, u32[]{:S(2)}) copy-start(bf16[256,128]{1,0:T(8,128)(2,1)} %constant.55.clone.b_z_high) | copy-start | bytes 196612
  0.7 22.9 %copy-start.7 = (bf16[128,256]{1,0:T(8,128)(2,1)S(1)}, bf16[128,256]{1,0:T(8,128)(2,1)}, u32[]{:S(2)}) copy-start(bf16[128,256]{1,0:T(8,128)(2,1)} %constant.53.clone.f_z_low) | copy-start | bytes 196612
  0.7 22.9 %copy-start.8 = (f32[128,128]{1,0:T(8,128)S(1)}, f32[128,128]{1,0:T(8,128)}, u32[]{:S(2)}) copy-start(f32[128,128]{1,0:T(8,128)} %constant.48.clone.o_z) | copy-start | bytes 196612
  0.7 22.9 %copy-start.9 = (f32[56,256]{1,0:T(8,128)S(1)}, f32[56,256]{1,0:T(8,128)}, u32[]{:S(2)}) copy-start(f32[56,256]{1,0:T(8,128)} %constant.43.clone.sums) | copy-start | bytes 172036
  0.8 22.9 %copy-start.10 = (f32[40,256]{1,0:T(8,128)S(1)}, f32[40,256]{1,0:T(8,128)}, u32[]{:S(2)}) copy-start(f32[40,256]{1,0:T(8,128)} %constant.42.clone.m_xz) | copy-start | bytes 122884
  0.8 22.9 %copy-start.13 = (bf16[40,168]{1,0:T(8,128)(2,1)S(1)}, bf16[40,168]{1,0:T(8,128)(2,1)}, u32[]{:S(2)}) copy-start(bf16[40,168]{1,0:T(8,128)(2,1)} %constant.51.clone.b_x) | copy-start | bytes 40324
  0.8 22.9 %copy-start.14 = (f32[32,40]{1,0:T(8,128)S(1)}, f32[32,40]{1,0:T(8,128)}, u32[]{:S(2)}) copy-start(f32[32,40]{1,0:T(8,128)} %constant.45.clone.q_x) | copy-start | bytes 15364
  0.8 22.9 %copy-start.15 = (bf16[56,120]{1,0:T(8,128)(2,1)S(1)}, bf16[56,120]{1,0:T(8,128)(2,1)}, u32[]{:S(2)}) copy-start(bf16[56,120]{1,0:T(8,128)(2,1)} %constant.50.clone.f_x) | copy-start | bytes 40324
  0.8 22.9 %copy-start.16 = (f32[16,40]{1,0:T(8,128)S(1)}, f32[16,40]{1,0:T(8,128)}, u32[]{:S(2)}) copy-start(f32[16,40]{1,0:T(8,128)} %constant.47.clone.r_x) | copy-start | bytes 7684
  0.8 22.9 %copy-start.17 = (f32[8,16]{1,0:T(8,128)S(1)}, f32[8,16]{1,0:T(8,128)}, u32[]{:S(2)}) copy-start(f32[8,16]{1,0:T(8,128)} %constant.49.clone.o_x) | copy-start | bytes 1540
  0.8 22.9 %copy-start.18 = (f32[13]{0:T(128)S(1)}, f32[13]{0:T(128)}, u32[]{:S(2)}) copy-start(f32[13]{0:T(128)} %constant.41.clone.lam) | copy-start | bytes 160
  5.1 10.2 %collective-permute-start = (f32[8,6784]{1,0:T(8,128)S(1)}, f32[8,6784]{1,0:T(8,128)S(1)}, u32[]{:S(2)}, u32[]{:S(2)}) collective-permute-start(f32[8,6784]{1,0:T(8,128)S(1)} %get-tuple-element.23), channel_id=1, source_target_pairs={{0,8},{8,16},{16,24},{1,9},{9,17},{17,25},{2,10},{10,18},{18,26},{... | collective-permute-start | bytes 651272 | tf_op jit(solution)/shard_map/ppermute | solution.py:33
  8.5 5.8 %collective-permute-start.1 = (f32[32,256]{1,0:T(8,128)S(1)}, f32[32,256]{1,0:T(8,128)S(1)}, u32[]{:S(2)}, u32[]{:S(2)}) collective-permute-start(f32[32,256]{1,0:T(8,128)S(1)} %get-tuple-element.22.u_first), channel_id=1, source_target_pairs={{8,0},{16,8},{24,16},{9,1},{17,9},{25,17},{10,2},{18,10},{26,18},{... | collective-permute-start | bytes 98312 | tf_op jit(solution)/shard_map/ppermute | solution.py:33
  15.8 7.7 %collective-permute-start.2 = (f32[40,1664]{1,0:T(8,128)S(1)}, f32[40,1664]{1,0:T(8,128)S(1)}, u32[]{:S(2)}, u32[]{:S(2)}) collective-permute-start(f32[40,1664]{1,0:T(8,128)S(1)} %get-tuple-element.26), channel_id=1, source_target_pairs={{0,1},{1,2},{2,3},{3,4},{4,5},{5,6},{6,7},{8,9},{9,10},{10,11},{11... | collective-permute-start | bytes 798728 | tf_op jit(solution)/shard_map/ppermute | solution.py:33
  17.8 5.3 %collective-permute-start.3 = (f32[40,256]{1,0:T(8,128)S(1)}, f32[40,256]{1,0:T(8,128)S(1)}, u32[]{:S(2)}, u32[]{:S(2)}) collective-permute-start(f32[40,256]{1,0:T(8,128)S(1)} %get-tuple-element.25.line), channel_id=1, source_target_pairs={{1,0},{2,1},{3,2},{4,3},{5,4},{6,5},{7,6},{9,8},{10,9},{11,10},{12... | collective-permute-start | bytes 122888 | tf_op jit(solution)/shard_map/ppermute | solution.py:33
  23.7 31.0 %copy-start = (f32[28,6272]{1,0:T(8,128)S(1)}, f32[28,6272]{1,0:T(8,128)}, u32[]{:S(2)}) copy-start(f32[28,6272]{1,0:T(8,128)} %guess.1) | copy-start | bytes 2107396
  23.7 31.0 %copy-start.2 = (f32[28,256]{1,0:T(8,128)S(1)}, f32[28,256]{1,0:T(8,128)}, u32[]{:S(2)}) copy-start(f32[28,256]{1,0:T(8,128)} %constant.56.clone.weight) | copy-start | bytes 86020
  40.2 8.6 %collective-permute-start.4 = (f32[40,2048]{1,0:T(8,128)S(1)}, f32[40,2048]{1,0:T(8,128)S(1)}, u32[]{:S(2)}, u32[]{:S(2)}) collective-permute-start(f32[40,2048]{1,0:T(8,128)S(1)} %get-tuple-element.28), channel_id=1, source_target_pairs={{1,0},{2,1},{3,2},{4,3},{5,4},{6,5},{7,6},{9,8},{10,9},{11,10},{12... | collective-permute-start | bytes 983048 | tf_op jit(solution)/shard_map/ppermute | solution.py:33
  43.4 5.4 %collective-permute-start.5 = (f32[24,512]{1,0:T(8,128)S(1)}, f32[24,512]{1,0:T(8,128)S(1)}, u32[]{:S(2)}, u32[]{:S(2)}) collective-permute-start(f32[24,512]{1,0:T(8,128)S(1)} %get-tuple-element.32), channel_id=1, source_target_pairs={{0,1},{1,2},{2,3},{3,4},{4,5},{5,6},{6,7},{8,9},{9,10},{10,11},{11... | collective-permute-start | bytes 147464 | tf_op jit(solution)/shard_map/ppermute | solution.py:33
  48.9 11.2 %collective-permute-start.6 = (f32[208,256]{1,0:T(8,128)S(1)}, f32[208,256]{1,0:T(8,128)S(1)}, u32[]{:S(2)}, u32[]{:S(2)}) collective-permute-start(f32[208,256]{1,0:T(8,128)S(1)} %get-tuple-element.33), channel_id=1, source_target_pairs={{8,0},{16,8},{24,16},{9,1},{17,9},{25,17},{10,2},{18,10},{26,18},{... | collective-permute-start | bytes 638984 | tf_op jit(solution)/shard_map/ppermute | solution.py:33
  52.6 7.5 %collective-permute-start.7 = (f32[40,256]{1,0:T(8,128)S(1)}, f32[40,256]{1,0:T(8,128)S(1)}, u32[]{:S(2)}, u32[]{:S(2)}) collective-permute-start(f32[40,256]{1,0:T(8,128)S(1)} %get-tuple-element.34), channel_id=1, source_target_pairs={{0,8},{8,16},{16,24},{1,9},{9,17},{17,25},{2,10},{10,18},{18,26},{... | collective-permute-start | bytes 122888 | tf_op jit(solution)/shard_map/ppermute | solution.py:33

commit v4 on v3

--- a/solution.py
+++ b/solution.py
@@ -147,6 +147,7 @@
 
 high = lax.Precision.HIGH
 LANES = 128
+GROUP = 7
 f32 = jnp.float32
 
 
@@ -581,37 +582,34 @@
 
         lax.fori_loop(0, rows // 8, along_y, 0)
 
-        def spectral(b, carry):
-            planes = [dot(f_x[...], stacked_rows(xf[b, v])) for v in range(ey)]
-            modes = jnp.concatenate(
-                [plane[:, :LANES] for plane in planes] + [plane[:, LANES:] for plane in planes], 0
-            )
-            high_part, low_part = halves_of(modes)
+        def spectral(modes_of):
+            pieces = []
+            for b in modes_of:
+                planes = [dot(f_x[...], stacked_rows(xf[b, v])) for v in range(ey)]
+                pieces += [plane[:, :LANES] for plane in planes]
+                pieces += [plane[:, LANES:] for plane in planes]
+            high_part, low_part = halves_of(jnp.concatenate(pieces, 0))
             modes = dot(jnp.concatenate([high_part, low_part], 1), f_z[...]) + dot(
                 high_part, f_z_low[...]
             )
-            factor = 1.0 / (sums[...] + lam[b])
-            modes = modes.reshape(2, ey, s.modes_x, s.modes_z)
-            modes = jnp.concatenate(
-                [
-                    (modes[t] * (factor * live[t])[None]).reshape(ey * s.modes_x, s.modes_z)
-                    for t in range(2)
-                ],
-                0,
-            )
-            high_part, low_part = halves_of(modes)
+            modes = modes.reshape(len(modes_of), 2, ey, s.modes_x, s.modes_z)
+            pieces = []
+            for i, b in enumerate(modes_of):
+                factor = 1.0 / (sums[...] + lam[b])
+                for t in range(2):
+                    scaled = modes[i, t] * (factor * live[t])[None]
+                    pieces.append(scaled.reshape(ey * s.modes_x, s.modes_z))
+            high_part, low_part = halves_of(jnp.concatenate(pieces, 0))
             both = dot(high_part, b_z[...])
             back = both[:, :LANES] + both[:, LANES:] + dot(low_part, b_z_high[...])
-            for v in range(ey):
-                first = v * s.modes_x
-                second = (ey + v) * s.modes_x
-                plane = jnp.concatenate(
-                    [back[first : first + s.modes_x], back[second : second + s.modes_x]], 1
-                )
-                xb[b, v] = dot(b_x[...], stacked_rows(plane))
-            return carry
-
-        lax.fori_loop(0, 13, spectral, 0)
+            back = back.reshape(len(modes_of), 2, ey, s.modes_x, LANES)
+            for i, b in enumerate(modes_of):
+                for v in range(ey):
+                    plane = jnp.concatenate([back[i, 0, v], back[i, 1, v]], 1)
+                    xb[b, v] = dot(b_x[...], stacked_rows(plane))
+
+        for first in range(0, 13, GROUP):
+            spectral(range(first, min(13, first + GROUP)))
 
         def back_y(tile, carry):
             at = pl.ds(pl.multiple_of(tile * 8, 8), 8)

time: 62.5 us -> 57.2 us (0.915)
  Pallas kernels: 25.5 us -> 20.2 us
    pallas_call x6, Pallas kernels: 25.5 us -> 20.2 us  [call(): pl.pallas_call(kernel, out_shape=tuple((shape(*dims) for dims in outputs)...]
where the time goes in v4:
time: 57.2 us; the launch traced here: 56.5 us
  starting transfers between devices  23.2 us (41%)
  Pallas kernels  20.2 us (35%)
  waiting for transfers between devices  11.9 us (21%)
  between operations  0.99 us (2%)
    ppermute x8, starting transfers between devices, shifted(): return lax.ppermute(array, axis, pairs)  23.2 us
    pallas_call x6, Pallas kernels, call(): pl.pallas_call(kernel, out_shape=tuple((shape(*dims) for dims in outputs)...  20.2 us
    ppermute x8, waiting for transfers between devices, shifted(): return lax.ppermute(array, axis, pairs)  11.9 us
  transfers between devices with their start and end apart: 8, of which 6 were waited for; matrix products, arithmetic and copies ran while one was open for 0% of the time, Pallas kernels for 4%

profile of v4, /device:TPU:20, one launch (start us, length us, event | category | flops | bytes accessed | tf_op | source)
XLA Modules:
  0.0 56.5 jit_solution(16054116641654947307)
XLA Ops:
  0.6 0.0 copy-start.11
  0.6 0.0 copy-start.12
  0.7 0.0 copy-start.1
  0.7 0.0 copy-start.3
  0.7 0.0 copy-start.4
  0.7 0.0 copy-start.5
  0.7 0.0 copy-start.6
  0.7 0.0 copy-start.7
  0.7 0.0 copy-start.8
  0.7 0.0 copy-start.9
  0.8 0.0 copy-start.10
  0.8 0.0 copy-start.13
  0.8 0.0 copy-start.14
  0.8 0.0 copy-start.15
  0.8 0.0 copy-start.16
  0.8 0.0 copy-start.17
  0.8 0.0 copy-start.18
  0.8 4.3 %residual.1 = (f32[29,32,256]{2,1,0:T(8,128)S(1)}, f32[32,256]{1,0:T(8,128)S(1)}, f32[8,6784]{1,0:T(8,128)S(1)}, f32[32,256]{1,0:T(8,128)S(1)}) custom-call(f32[28,6272]{1,0:T(8,128)} %guess.1, f32[28,6272]{1,0:T(8,128)} %load_hbm.1, f32[384,256]{1,0:T(8,128)} %constant.38.clone.table_hbm), custom_call_target="tpu_custom_call" | custom-call | tf_op jit(solution)/shard_map/residual/pallas_call | solution.py:862
  5.1 3.4 %collective-permute-start = (f32[8,6784]{1,0:T(8,128)S(1)}, f32[8,6784]{1,0:T(8,128)S(1)}, u32[]{:S(2)}, u32[]{:S(2)}) collective-permute-start(f32[8,6784]{1,0:T(8,128)S(1)} %get-tuple-element.23), channel_id=1, source_target_pairs={{0,8},{8,16},{16,24},{1,9},{9,17},{17,25},{2,10},{10,18},{18,26},{... | collective-permute-start | bytes 651272 | tf_op jit(solution)/shard_map/ppermute | solution.py:33
  8.5 3.3 %collective-permute-start.1 = (f32[32,256]{1,0:T(8,128)S(1)}, f32[32,256]{1,0:T(8,128)S(1)}, u32[]{:S(2)}, u32[]{:S(2)}) collective-permute-start(f32[32,256]{1,0:T(8,128)S(1)} %get-tuple-element.22.u_first), channel_id=1, source_target_pairs={{8,0},{16,8},{24,16},{9,1},{17,9},{25,17},{10,2},{18,10},{26,18},{... | collective-permute-start | bytes 98312 | tf_op jit(solution)/shard_map/ppermute | solution.py:33
  11.9 2.5 %collective-permute-done.1.above = f32[32,256]{1,0:T(8,128)S(1)} collective-permute-done((f32[32,256]{1,0:T(8,128)S(1)}, f32[32,256]{1,0:T(8,128)S(1)}, u32[]{:S(2)}, u32[]{:S(2)}) %collective-permute-start.1) | collective-permute-done | bytes 32800 | tf_op jit(solution)/shard_map/ppermute | solution.py:33
  14.3 1.0 %collective-permute-done.below = f32[8,6784]{1,0:T(8,128)S(1)} collective-permute-done((f32[8,6784]{1,0:T(8,128)S(1)}, f32[8,6784]{1,0:T(8,128)S(1)}, u32[]{:S(2)}, u32[]{:S(2)}) %collective-permute-start) | collective-permute-done | bytes 217120 | tf_op jit(solution)/shard_map/ppermute | solution.py:33
  15.3 0.0 copy-done.11
  15.3 0.0 copy-done.12
  15.3 0.5 joined_x.1
  15.8 1.9 %collective-permute-start.2 = (f32[40,1664]{1,0:T(8,128)S(1)}, f32[40,1664]{1,0:T(8,128)S(1)}, u32[]{:S(2)}, u32[]{:S(2)}) collective-permute-start(f32[40,1664]{1,0:T(8,128)S(1)} %get-tuple-element.26), channel_id=1, source_target_pairs={{0,1},{1,2},{2,3},{3,4},{4,5},{5,6},{6,7},{8,9},{9,10},{10,11},{11... | collective-permute-start | bytes 798728 | tf_op jit(solution)/shard_map/ppermute | solution.py:33
  17.8 3.6 %collective-permute-start.3 = (f32[40,256]{1,0:T(8,128)S(1)}, f32[40,256]{1,0:T(8,128)S(1)}, u32[]{:S(2)}, u32[]{:S(2)}) collective-permute-start(f32[40,256]{1,0:T(8,128)S(1)} %get-tuple-element.25.line), channel_id=1, source_target_pairs={{1,0},{2,1},{3,2},{4,3},{5,4},{6,5},{7,6},{9,8},{10,9},{11,10},{12... | collective-permute-start | bytes 122888 | tf_op jit(solution)/shard_map/ppermute | solution.py:33
  21.4 1.7 %collective-permute-done.3.above = f32[40,256]{1,0:T(8,128)S(1)} collective-permute-done((f32[40,256]{1,0:T(8,128)S(1)}, f32[40,256]{1,0:T(8,128)S(1)}, u32[]{:S(2)}, u32[]{:S(2)}) %collective-permute-start.3) | collective-permute-done | bytes 40992 | tf_op jit(solution)/shard_map/ppermute | solution.py:33
  23.1 0.5 collective-permute-done.2.below
  23.6 0.0 copy-done.1
  23.6 0.0 copy-done.3
  23.6 0.0 copy-done.4
  23.6 0.0 copy-done.5
  23.6 0.0 copy-done.6
  23.6 0.0 copy-done.7
  23.7 0.0 copy-start
  23.7 0.0 copy-start.2
  23.7 11.2 %patches.1 = (f32[28,8,256]{2,1,0:T(8,128)S(1)}, f32[28,32,256]{2,1,0:T(8,128)S(1)}, f32[16,16,128]{2,1,0:T(8,128)S(1)}, f32[6,8,128]{2,1,0:T(8,128)S(1)}, f32[4...) custom-call(f32[29,40,256]{2,1,0:T(8,128)S(1)} %get-tuple-element.24.r_own, f32[40,256]{1,0:T(8,128)S(1)} %get-tuple-element.25.line, ...), custom_call_target="tpu_custom_call" | custom-call | tf_op jit(solution)/shard_map/patches/pallas_call | solution.py:862
  34.9 3.2 %collective-permute-start.4 = (f32[40,2048]{1,0:T(8,128)S(1)}, f32[40,2048]{1,0:T(8,128)S(1)}, u32[]{:S(2)}, u32[]{:S(2)}) collective-permute-start(f32[40,2048]{1,0:T(8,128)S(1)} %get-tuple-element.28), channel_id=1, source_target_pairs={{1,0},{2,1},{3,2},{4,3},{5,4},{6,5},{7,6},{9,8},{10,9},{11,10},{12... | collective-permute-start | bytes 983048 | tf_op jit(solution)/shard_map/ppermute | solution.py:33
  38.1 1.9 %collective-permute-start.5 = (f32[24,512]{1,0:T(8,128)S(1)}, f32[24,512]{1,0:T(8,128)S(1)}, u32[]{:S(2)}, u32[]{:S(2)}) collective-permute-start(f32[24,512]{1,0:T(8,128)S(1)} %get-tuple-element.32), channel_id=1, source_target_pairs={{0,1},{1,2},{2,3},{3,4},{4,5},{5,6},{6,7},{8,9},{9,10},{10,11},{11... | collective-permute-start | bytes 147464 | tf_op jit(solution)/shard_map/ppermute | solution.py:33
  40.0 3.5 %collective-permute-done.5.up = f32[24,512]{1,0:T(8,128)S(1)} collective-permute-done((f32[24,512]{1,0:T(8,128)S(1)}, f32[24,512]{1,0:T(8,128)S(1)}, u32[]{:S(2)}, u32[]{:S(2)}) %collective-permute-start.5) | collective-permute-done | bytes 49184 | tf_op jit(solution)/shard_map/ppermute | solution.py:33
  43.5 0.0 collective-permute-done.4.down
  43.5 3.8 %collective-permute-start.6 = (f32[208,256]{1,0:T(8,128)S(1)}, f32[208,256]{1,0:T(8,128)S(1)}, u32[]{:S(2)}, u32[]{:S(2)}) collective-permute-start(f32[208,256]{1,0:T(8,128)S(1)} %get-tuple-element.33), channel_id=1, source_target_pairs={{8,0},{16,8},{24,16},{9,1},{17,9},{25,17},{10,2},{18,10},{26,18},{... | collective-permute-start | bytes 638984 | tf_op jit(solution)/shard_map/ppermute | solution.py:33
  47.3 2.1 %collective-permute-start.7 = (f32[40,256]{1,0:T(8,128)S(1)}, f32[40,256]{1,0:T(8,128)S(1)}, u32[]{:S(2)}, u32[]{:S(2)}) collective-permute-start(f32[40,256]{1,0:T(8,128)S(1)} %get-tuple-element.34), channel_id=1, source_target_pairs={{0,8},{8,16},{16,24},{1,9},{9,17},{17,25},{2,10},{10,18},{18,26},{... | collective-permute-start | bytes 122888 | tf_op jit(solution)/shard_map/ppermute | solution.py:33
  49.4 2.5 %base.1 = f32[28,6272]{1,0:T(8,128)S(1)} custom-call(f32[28,6272]{1,0:T(8,128)S(1)} %copy-done, f32[28,256]{1,0:T(8,128)S(1)} %copy-done.2, f32[28,32,256]{2,1,0:T(8,128)S(1)} %get-tuple-element.27.own, f32[40,2048]{1,0:T(8,128)S(1)} %collective-permute-done.4.down), custom_call_target="tpu_custom_call" | custom-call | tf_op jit(solution)/shard_map/base/pallas_call | solution.py:862
  51.9 2.8 %collective-permute-done.7.left = f32[40,256]{1,0:T(8,128)S(1)} collective-permute-done((f32[40,256]{1,0:T(8,128)S(1)}, f32[40,256]{1,0:T(8,128)S(1)}, u32[]{:S(2)}, u32[]{:S(2)}) %collective-permute-start.7) | collective-permute-done | bytes 40992 | tf_op jit(solution)/shard_map/ppermute | solution.py:33
  54.7 0.0 collective-permute-done.6.right
  54.7 1.8 %finish.1 = (f32[28,6272]{1,0:T(8,128)}, f32[12,1152]{1,0:T(8,128)}, f32[4,128]{1,0:T(4,128)}) custom-call(f32[28,6272]{1,0:T(8,128)S(1)} %base.1, f32[28,256]{1,0:T(8,128)S(1)} %copy-done.2, f32[208,256]{1,0:T(8,128)S(1)} %collective-permute-done.6.right, f32[40,256]{1,0:T(8,128)S(1)} %collective-permute-done.7.left, ...), custom_call_target="tpu_custom_call" | custom-call | tf_op jit(solution)/shard_map/finish/pallas_call | solution.py:862
  (12 shorter events, 0.1 us)
Async XLA Ops:
  0.6 14.7 %copy-start.11 = (f32[40,256]{1,0:T(8,128)S(1)}, f32[40,256]{1,0:T(8,128)}, u32[]{:S(2)}) copy-start(f32[40,256]{1,0:T(8,128)} %constant.40.clone.c_above) | copy-start | bytes 122884
  0.6 14.7 %copy-start.12 = (f32[40,256]{1,0:T(8,128)S(1)}, f32[40,256]{1,0:T(8,128)}, u32[]{:S(2)}) copy-start(f32[40,256]{1,0:T(8,128)} %constant.39.clone.c_below) | copy-start | bytes 122884
  0.7 22.9 %copy-start.1 = (f32[256,256]{1,0:T(8,128)S(1)}, f32[256,256]{1,0:T(8,128)}, u32[]{:S(2)}) copy-start(f32[256,256]{1,0:T(8,128)} %constant.44.clone.q_z) | copy-start | bytes 786436
  0.7 22.9 %copy-start.3 = (bf16[256,256]{1,0:T(8,128)(2,1)S(1)}, bf16[256,256]{1,0:T(8,128)(2,1)}, u32[]{:S(2)}) copy-start(bf16[256,256]{1,0:T(8,128)(2,1)} %constant.54.clone.b_z) | copy-start | bytes 393220
  0.7 22.9 %copy-start.4 = (bf16[256,256]{1,0:T(8,128)(2,1)S(1)}, bf16[256,256]{1,0:T(8,128)(2,1)}, u32[]{:S(2)}) copy-start(bf16[256,256]{1,0:T(8,128)(2,1)} %constant.52.clone.f_z) | copy-start | bytes 393220
  0.7 22.9 %copy-start.5 = (f32[256,128]{1,0:T(8,128)S(1)}, f32[256,128]{1,0:T(8,128)}, u32[]{:S(2)}) copy-start(f32[256,128]{1,0:T(8,128)} %constant.46.clone.r_z) | copy-start | bytes 393220
  0.7 22.9 %copy-start.6 = (bf16[256,128]{1,0:T(8,128)(2,1)S(1)}, bf16[256,128]{1,0:T(8,128)(2,1)}, u32[]{:S(2)}) copy-start(bf16[256,128]{1,0:T(8,128)(2,1)} %constant.55.clone.b_z_high) | copy-start | bytes 196612
  0.7 22.9 %copy-start.7 = (bf16[128,256]{1,0:T(8,128)(2,1)S(1)}, bf16[128,256]{1,0:T(8,128)(2,1)}, u32[]{:S(2)}) copy-start(bf16[128,256]{1,0:T(8,128)(2,1)} %constant.53.clone.f_z_low) | copy-start | bytes 196612
  0.7 22.9 %copy-start.8 = (f32[128,128]{1,0:T(8,128)S(1)}, f32[128,128]{1,0:T(8,128)}, u32[]{:S(2)}) copy-start(f32[128,128]{1,0:T(8,128)} %constant.48.clone.o_z) | copy-start | bytes 196612
  0.7 22.9 %copy-start.9 = (f32[56,256]{1,0:T(8,128)S(1)}, f32[56,256]{1,0:T(8,128)}, u32[]{:S(2)}) copy-start(f32[56,256]{1,0:T(8,128)} %constant.43.clone.sums) | copy-start | bytes 172036
  0.8 22.9 %copy-start.10 = (f32[40,256]{1,0:T(8,128)S(1)}, f32[40,256]{1,0:T(8,128)}, u32[]{:S(2)}) copy-start(f32[40,256]{1,0:T(8,128)} %constant.42.clone.m_xz) | copy-start | bytes 122884
  0.8 22.9 %copy-start.13 = (bf16[40,168]{1,0:T(8,128)(2,1)S(1)}, bf16[40,168]{1,0:T(8,128)(2,1)}, u32[]{:S(2)}) copy-start(bf16[40,168]{1,0:T(8,128)(2,1)} %constant.51.clone.b_x) | copy-start | bytes 40324
  0.8 22.9 %copy-start.14 = (f32[32,40]{1,0:T(8,128)S(1)}, f32[32,40]{1,0:T(8,128)}, u32[]{:S(2)}) copy-start(f32[32,40]{1,0:T(8,128)} %constant.45.clone.q_x) | copy-start | bytes 15364
  0.8 22.9 %copy-start.15 = (bf16[56,120]{1,0:T(8,128)(2,1)S(1)}, bf16[56,120]{1,0:T(8,128)(2,1)}, u32[]{:S(2)}) copy-start(bf16[56,120]{1,0:T(8,128)(2,1)} %constant.50.clone.f_x) | copy-start | bytes 40324
  0.8 22.9 %copy-start.16 = (f32[16,40]{1,0:T(8,128)S(1)}, f32[16,40]{1,0:T(8,128)}, u32[]{:S(2)}) copy-start(f32[16,40]{1,0:T(8,128)} %constant.47.clone.r_x) | copy-start | bytes 7684
  0.8 22.9 %copy-start.17 = (f32[8,16]{1,0:T(8,128)S(1)}, f32[8,16]{1,0:T(8,128)}, u32[]{:S(2)}) copy-start(f32[8,16]{1,0:T(8,128)} %constant.49.clone.o_x) | copy-start | bytes 1540
  0.8 22.9 %copy-start.18 = (f32[13]{0:T(128)S(1)}, f32[13]{0:T(128)}, u32[]{:S(2)}) copy-start(f32[13]{0:T(128)} %constant.41.clone.lam) | copy-start | bytes 160
  5.1 10.2 %collective-permute-start = (f32[8,6784]{1,0:T(8,128)S(1)}, f32[8,6784]{1,0:T(8,128)S(1)}, u32[]{:S(2)}, u32[]{:S(2)}) collective-permute-start(f32[8,6784]{1,0:T(8,128)S(1)} %get-tuple-element.23), channel_id=1, source_target_pairs={{0,8},{8,16},{16,24},{1,9},{9,17},{17,25},{2,10},{10,18},{18,26},{... | collective-permute-start | bytes 651272 | tf_op jit(solution)/shard_map/ppermute | solution.py:33
  8.5 5.8 %collective-permute-start.1 = (f32[32,256]{1,0:T(8,128)S(1)}, f32[32,256]{1,0:T(8,128)S(1)}, u32[]{:S(2)}, u32[]{:S(2)}) collective-permute-start(f32[32,256]{1,0:T(8,128)S(1)} %get-tuple-element.22.u_first), channel_id=1, source_target_pairs={{8,0},{16,8},{24,16},{9,1},{17,9},{25,17},{10,2},{18,10},{26,18},{... | collective-permute-start | bytes 98312 | tf_op jit(solution)/shard_map/ppermute | solution.py:33
  15.8 7.7 %collective-permute-start.2 = (f32[40,1664]{1,0:T(8,128)S(1)}, f32[40,1664]{1,0:T(8,128)S(1)}, u32[]{:S(2)}, u32[]{:S(2)}) collective-permute-start(f32[40,1664]{1,0:T(8,128)S(1)} %get-tuple-element.26), channel_id=1, source_target_pairs={{0,1},{1,2},{2,3},{3,4},{4,5},{5,6},{6,7},{8,9},{9,10},{10,11},{11... | collective-permute-start | bytes 798728 | tf_op jit(solution)/shard_map/ppermute | solution.py:33
  17.8 5.3 %collective-permute-start.3 = (f32[40,256]{1,0:T(8,128)S(1)}, f32[40,256]{1,0:T(8,128)S(1)}, u32[]{:S(2)}, u32[]{:S(2)}) collective-permute-start(f32[40,256]{1,0:T(8,128)S(1)} %get-tuple-element.25.line), channel_id=1, source_target_pairs={{1,0},{2,1},{3,2},{4,3},{5,4},{6,5},{7,6},{9,8},{10,9},{11,10},{12... | collective-permute-start | bytes 122888 | tf_op jit(solution)/shard_map/ppermute | solution.py:33
  23.7 25.7 %copy-start = (f32[28,6272]{1,0:T(8,128)S(1)}, f32[28,6272]{1,0:T(8,128)}, u32[]{:S(2)}) copy-start(f32[28,6272]{1,0:T(8,128)} %guess.1) | copy-start | bytes 2107396
  23.7 25.7 %copy-start.2 = (f32[28,256]{1,0:T(8,128)S(1)}, f32[28,256]{1,0:T(8,128)}, u32[]{:S(2)}) copy-start(f32[28,256]{1,0:T(8,128)} %constant.56.clone.weight) | copy-start | bytes 86020
  34.9 8.6 %collective-permute-start.4 = (f32[40,2048]{1,0:T(8,128)S(1)}, f32[40,2048]{1,0:T(8,128)S(1)}, u32[]{:S(2)}, u32[]{:S(2)}) collective-permute-start(f32[40,2048]{1,0:T(8,128)S(1)} %get-tuple-element.28), channel_id=1, source_target_pairs={{1,0},{2,1},{3,2},{4,3},{5,4},{6,5},{7,6},{9,8},{10,9},{11,10},{12... | collective-permute-start | bytes 983048 | tf_op jit(solution)/shard_map/ppermute | solution.py:33
  38.1 5.4 %collective-permute-start.5 = (f32[24,512]{1,0:T(8,128)S(1)}, f32[24,512]{1,0:T(8,128)S(1)}, u32[]{:S(2)}, u32[]{:S(2)}) collective-permute-start(f32[24,512]{1,0:T(8,128)S(1)} %get-tuple-element.32), channel_id=1, source_target_pairs={{0,1},{1,2},{2,3},{3,4},{4,5},{5,6},{6,7},{8,9},{9,10},{10,11},{11... | collective-permute-start | bytes 147464 | tf_op jit(solution)/shard_map/ppermute | solution.py:33
  43.5 11.2 %collective-permute-start.6 = (f32[208,256]{1,0:T(8,128)S(1)}, f32[208,256]{1,0:T(8,128)S(1)}, u32[]{:S(2)}, u32[]{:S(2)}) collective-permute-start(f32[208,256]{1,0:T(8,128)S(1)} %get-tuple-element.33), channel_id=1, source_target_pairs={{8,0},{16,8},{24,16},{9,1},{17,9},{25,17},{10,2},{18,10},{26,18},{... | collective-permute-start | bytes 638984 | tf_op jit(solution)/shard_map/ppermute | solution.py:33
  47.3 7.4 %collective-permute-start.7 = (f32[40,256]{1,0:T(8,128)S(1)}, f32[40,256]{1,0:T(8,128)S(1)}, u32[]{:S(2)}, u32[]{:S(2)}) collective-permute-start(f32[40,256]{1,0:T(8,128)S(1)} %get-tuple-element.34), channel_id=1, source_target_pairs={{0,8},{8,16},{16,24},{1,9},{9,17},{17,25},{2,10},{10,18},{18,26},{... | collective-permute-start | bytes 122888 | tf_op jit(solution)/shard_map/ppermute | solution.py:33

commit v5 on v4

--- a/solution.py
+++ b/solution.py
@@ -219,26 +219,32 @@
     return high_part, low_part
 
 
-def residual_constants(s):
+def residual_constants(s, low):
     line_x = line_tables(s.x_elems)
     stiff_z, lumped_z = assemble_line(s.z_elems)
     stiff_z, lumped_z = (stiff_z[: s.z_nodes, : s.z_nodes], lumped_z[: s.z_nodes])
+    rows = s.own_rows - low
     mass_x = np.zeros(s.own_rows)
     mass_x[: s.x_nodes] = line_x["mass"][6:]
+    mass_x = mass_x[low:]
     mass_z = rows_by_node(s, lumped_z[:, None], True)[:, 0]
-    spread = np.ones((s.own_rows, s.lanes))
+    spread = np.ones((rows, s.lanes))
     stiff = rows_by_node(s, stiff_z, False)
     stiff = rows_by_node(s, stiff.T, True).T
-    wide = placed(line_x["own_stiff"], (s.own_rows, s.lanes))
-    return np.concatenate(
+    own_x = placed(line_x["own_stiff"], (s.own_rows, s.own_rows)).astype(np.float64)
+    high_x, low_x = two_parts(own_x[low:, low:])
+    table = np.concatenate(
         [
             stiff,
             spread * mass_x[:, None],
             spread * mass_z[None, :],
             mass_x[:, None] * mass_z[None, :],
-            wide,
         ]
     )
+    return [
+        jnp.asarray(table, f32),
+        jnp.asarray(np.concatenate([high_x, high_x, low_x], 1), jnp.bfloat16),
+    ]
 
 
 def coupling_constants(s):
@@ -285,20 +291,25 @@
     own_z = np.zeros((s.z_nodes, s.coarse_lanes))
     own_z[:, : s.coarse_z] = restrict_z.T
     one_z = placed(
-        linear_from_cubic(0, s.z_elems - 1, 0, s.coarse_z - 1).T, (s.coarse_lanes, LANES)
+        linear_from_cubic(0, s.z_elems - 1, 0, s.coarse_z - 1).T,
+        (s.coarse_lanes, LANES),
+        col=s.coarse_z,
     )
     one_x = placed(linear_from_cubic(-1, s.x_elems, -3, 3 * s.x_elems), (8, s.coarse_rows))
     singles = [
         mass_x[:, None] * mass_z[None, :],
         sums,
         rows_by_node(s, coarse_of_z, True),
-        coarse_of_x,
         rows_by_node(s, own_z, False),
-        placed(line_x["own"], (s.coarse_rows, s.rows), col=8),
         one_z,
         one_x,
     ]
+    own_x = placed(line_x["own"], (s.coarse_rows, s.rows), col=8).astype(np.float64)
+    high_q, low_q = two_parts(coarse_of_x)
+    high_r, low_r = two_parts(own_x)
     halves = [
+        np.concatenate([high_q, high_q, low_q], 1),
+        np.concatenate([high_r, high_r, low_r], 1),
         np.concatenate([high_x, high_x, low_x], 1),
         np.concatenate([high_x.T, high_x.T, low_x.T], 1),
         np.concatenate([high_z, high_z], 0),
@@ -385,101 +396,126 @@
     )
 
 
-def residual_kernel(s):
-    rows, lanes = (s.own_rows, s.lanes)
-    ex, ey, nx, ny = (s.x_elems, s.y_elems, s.x_nodes, s.y_nodes)
+def own_residual(s, low, first_copies, u, r, guess, load, table, k_x):
+    lanes = s.lanes
+    rows = s.own_rows - low
+    ey, ny = (s.y_elems, s.y_nodes)
+    nx = s.x_nodes - low
     width = ny * s.z_nodes
     mass_y = line_tables(ey)["mass"][6:]
     stiffness = element_stiffness()
-
-    def kernel(guess_hbm, load_hbm, table_hbm, r, edge, up_out, down_out, u, guess, load, table, sems):
-        copies = [
-            pltpu.make_async_copy(source, target, sems.at[index])
-            for index, (source, target) in enumerate(
-                [(guess_hbm, guess), (load_hbm, load), (table_hbm, table)]
-            )
-        ]
-        for copy in copies:
-            copy.start()
-        k_z = table.at[0:lanes]
-        m_x, m_z, m_xz, k_x_wide = [
-            table.at[lanes + rows * i : lanes + rows * (i + 1)] for i in range(4)
-        ]
-        k_x = k_x_wide.at[:, 0:rows]
+    gx = lax.axis_index("gx")
+    gy = lax.axis_index("gy")
+    shape = (nx, lanes)
+    row = lax.broadcasted_iota(jnp.int32, shape, 0) + low
+    live = (lane_mask(s, shape, 1) & ((row != 0) | (gx > 0))).astype(f32)
+    live_y = (gy > 0).astype(f32)
+    inside = lane_mask(s, shape, 0).astype(f32)
+    pad = jnp.zeros((rows - nx, lanes), f32)
+    first_copies[0].wait()
+    for y in range(ny):
+        mask = live if y else live * live_y
+        u[y, 0:nx] = get_line(s, guess, y, width) * mask
+        u[y, nx:] = pad
+    first_copies[1].wait()
+    for y in range(ny):
+        r[y, 0:nx] = get_line(s, load, y, width) * inside
+        r[y, nx:] = pad
+    u[ny] = jnp.zeros((rows, lanes), f32)
+    r[ny] = jnp.zeros((rows, lanes), f32)
+    for copy in first_copies[2:]:
+        copy.wait()
+    m_x, m_z, m_xz = [
+        table.at[lanes + rows * i : lanes + rows * (i + 1)] for i in range(3)
+    ]
+    z_term = mm(u[0:ny].reshape(ny * rows, lanes), table[0:lanes]).reshape(ny, rows, lanes)
+    for y in range(ny):
+        x_term = dot(k_x[...], stacked_rows(u[y]))
+        both = x_term * m_z[...] + z_term[y] * m_x[...]
+        r[y] = r[y] - float(mass_y[y]) * both
+
+    def along_y(tile, carry):
+        at = pl.ds(pl.multiple_of(tile * 8, 8), 8)
+        scale = m_xz[at, :]
+        corner = None
+        for e in range(ey):
+            nodes = [u[7 * e + i, at, :] for i in range(8)]
+            plus = [nodes[i] + nodes[7 - i] for i in range(4)]
+            minus = [nodes[i] - nodes[7 - i] for i in range(4)]
+            out = [None] * 8
+            for i in range(4):
+                even = sum(
+                    plus[k] * float(0.5 * (stiffness[i, k] + stiffness[i, 7 - k]))
+                    for k in range(4)
+                )
+                odd = sum(
+                    minus[k] * float(0.5 * (stiffness[i, k] - stiffness[i, 7 - k]))
+                    for k in range(4)
+                )
+                out[i], out[7 - i] = (even + odd, even - odd)
+            if e:
+                out[0] = out[0] + corner
+            else:
+                out[0] = out[0] + nodes[0] * float(stiffness[7, 7])
+            corner = out[7]
+            for i in range(8 if e == ey - 1 else 7):
+                plane = 7 * e + i
+                r[plane, at, :] = r[plane, at, :] - out[i] * scale
+        return carry
+
+    lax.fori_loop(0, rows // 8, along_y, 0)
+
+
+def started(sources, targets, sems):
+    copies = [
+        pltpu.make_async_copy(source, target, sems.at[index])
+        for index, (source, target) in enumerate(zip(sources, targets))
+    ]
+    for copy in copies:
+        copy.start()
+    return copies
+
+
+def send_kernel(s):
+    low = (s.x_nodes - 7) // 8 * 8
+    lanes, nx, ny = (s.lanes, s.x_nodes, s.y_nodes)
+    width = ny * s.z_nodes
+
+    def kernel(
+        guess_hbm, load_hbm, table_hbm, k_x_hbm,
+        up_out, down_out,
+        u, r, guess, load, table, k_x, top, sems,
+    ):
+        sources = [guess_hbm.at[low:nx], load_hbm.at[low:nx], table_hbm, k_x_hbm]
+        sources += [guess_hbm.at[0:8]]
+        copies = started(sources, [guess, load, table, k_x, top], sems)
+        own_residual(s, low, copies[:4], u, r, guess, load, table, k_x)
+        up_out[6:8, :] = jnp.zeros((2, up_out.shape[1]), f32)
+        for y in range(ny + 1):
+            put_line(s, up_out, y, r[y, nx - 6 - low : nx + 1 - low, :])
+        put_line(s, up_out, ny + 1, u[0, nx - 6 - low : nx - low, :])
+        copies[4].wait()
         gx = lax.axis_index("gx")
         gy = lax.axis_index("gy")
-        shape = (nx, lanes)
-        row = lax.broadcasted_iota(jnp.int32, shape, 0)
-        live = (lane_mask(s, shape, 1) & ((row != 0) | (gx > 0))).astype(f32)
+        live = lane_mask(s, (1, lanes), 1).astype(f32) * (gx > 0).astype(f32)
         live_y = (gy > 0).astype(f32)
-        inside = lane_mask(s, shape, 0).astype(f32)
-        pad = jnp.zeros((rows - nx, lanes), f32)
-        copies[0].wait()
         for y in range(ny):
             mask = live if y else live * live_y
-            u[y, 0:nx] = get_line(s, guess, y, width) * mask
-            u[y, nx:] = pad
-        copies[1].wait()
-        for y in range(ny):
-            r[y, 0:nx] = get_line(s, load, y, width) * inside
-            r[y, nx:] = pad
-        u[ny] = jnp.zeros((rows, lanes), f32)
-        r[ny] = jnp.zeros((rows, lanes), f32)
-
-        copies[2].wait()
-
-        def direct(chunk, carry):
-            base = chunk * 7
-            planes = u[pl.ds(base, 7)]
-            z_term = mm(planes.reshape(7 * rows, lanes), k_z[...]).reshape(7, rows, lanes)
-            for i in range(7):
-                x_term = mm(k_x[...], planes[i])
-                both = x_term * m_z[...] + z_term[i] * m_x[...]
-                r[base + i] = r[base + i] - float(mass_y[i]) * both
-            return carry
-
-        lax.fori_loop(0, ey, direct, 0)
-
-        def along_y(tile, carry):
-            at = pl.ds(pl.multiple_of(tile * 8, 8), 8)
-            scale = m_xz[at, :]
-            corner = None
-            for e in range(ey):
-                nodes = [u[7 * e + i, at, :] for i in range(8)]
-                plus = [nodes[i] + nodes[7 - i] for i in range(4)]
-                minus = [nodes[i] - nodes[7 - i] for i in range(4)]
-                out = [None] * 8
-                for i in range(4):
-                    even = sum(
-                        plus[k] * float(0.5 * (stiffness[i, k] + stiffness[i, 7 - k]))
-                        for k in range(4)
-                    )
-                    odd = sum(
-                        minus[k] * float(0.5 * (stiffness[i, k] - stiffness[i, 7 - k]))
-                        for k in range(4)
-                    )
-                    out[i], out[7 - i] = (even + odd, even - odd)
-                if e:
-                    out[0] = out[0] + corner
-                else:
-                    out[0] = out[0] + nodes[0] * float(stiffness[7, 7])
-                corner = out[7]
-                for i in range(8 if e == ey - 1 else 7):
-                    plane = 7 * e + i
-                    r[plane, at, :] = r[plane, at, :] - out[i] * scale
-            return carry
-
-        lax.fori_loop(0, rows // 8, along_y, 0)
-        for y in range(ny + 1):
-            put_line(s, up_out, y, r[y, nx - 6 : nx + 1, :])
-        up_out[7:8, :] = jnp.zeros((1, up_out.shape[1]), f32)
-        put_line(s, up_out, ny + 1, u[0, nx - 6 : nx, :])
-        up_out[6:7, (ny + 1) * s.z_nodes :] = jnp.zeros(
-            (1, up_out.shape[1] - (ny + 1) * s.z_nodes), f32
-        )
-        for y in range(ny):
-            down_out[y : y + 1, :] = u[y, 0:1, :]
+            down_out[y : y + 1, :] = get_line(s, top, y, width)[0:1] * mask
         down_out[ny:, :] = jnp.zeros((down_out.shape[0] - ny, lanes), f32)
+
+    return kernel
+
+
+def residual_kernel(s):
+    def kernel(
+        guess_hbm, load_hbm, table_hbm, k_x_hbm,
+        r, edge,
+        u, guess, load, table, k_x, sems,
+    ):
+        sources = [guess_hbm, load_hbm, table_hbm, k_x_hbm]
+        copies = started(sources, [guess, load, table, k_x], sems)
+        own_residual(s, 0, copies, u, r, guess, load, table, k_x)
         edge[...] = u[0]
 
     return kernel
@@ -532,7 +568,7 @@
 
     def kernel(
         r_own, line, below, above,
-        lam, m_xz, sums, q_z, q_x, r_z, r_x, o_z, o_x, f_x, b_x, f_z, f_z_low, b_z, b_z_high,
+        lam, m_xz, sums, q_z, r_z, o_z, o_x, q_x, r_x, f_x, b_x, f_z, f_z_low, b_z, b_z_high,
         edge_out, own_out, three_out, one_out, down_out, up_out,
         r, xf, xb, c, cz, rz, hx, ex, rx, live,
     ):
@@ -645,11 +681,11 @@
         )
         rz[...] = mm(r[6 : ny + 6].reshape(ny * rows, lanes), r_z[...]).reshape(ny, rows, half)
         for y in range(ny + 6):
-            plane = mm(q_x[...], cz[y])
+            plane = dot(q_x[...], stacked_rows(cz[y]))
             hx[y] = plane[:rows_c, :half]
             ex[y] = plane[rows_c:, :half] + plane[:rows_c, half:]
         for y in range(ny):
-            rx[y] = mm(r_x[...], rz[y])
+            rx[y] = dot(r_x[...], stacked_rows(rz[y]))
         for j in range(s.coarse_y):
             three_out[j] = line_of_planes(
                 np.concatenate(
@@ -668,22 +704,26 @@
             )
             one_out[m] = mm(o_x[...], mixed)
         base = 6 * lanes
+        down_out[:, base:] = jnp.zeros((rows, 2 * half), f32)
+        up_out[...] = jnp.zeros(up_out.shape, f32)
+        up_out[:, 0:half] = three_out[s.coarse_y - 1]
         for j in range(4):
-            at = base + half * j
+            first, at = (rows_c * (j % 2), base + half * (j // 2))
             if j < 3:
-                down_out[0:rows_c, at : at + half] = three_out[j]
-            else:
-                down_out[0:rows_c, at : at + half] = jnp.zeros((rows_c, half), f32)
-            down_out[rows_c : rows_c + 8, at : at + LANES] = one_out[j]
-            down_out[rows_c + 8 :, at : at + half] = jnp.zeros((rows - rows_c - 8, half), f32)
-            up_at = half * j
-            if j == 0:
-                up_out[0:rows_c, up_at : up_at + half] = three_out[s.coarse_y - 1]
-            else:
-                up_out[0:rows_c, up_at : up_at + half] = jnp.zeros((rows_c, half), f32)
-            up_out[rows_c : rows_c + 8, up_at : up_at + LANES] = one_out[ey - 2 + j]
+                down_out[first : first + rows_c, at : at + half] = three_out[j]
+            down_out[first : first + 8, at : at + half] += one_out[j]
+            up_out[0:8, half * j : half * (j + 1)] += one_out[ey - 2 + j]
 
     return kernel
+
+
+def coarse_place(s, index):
+    high_rows = coarse_height(s)
+    return index % high_rows, LANES * (index // high_rows)
+
+
+def coarse_height(s):
+    return up_to(-(-max(9 * s.y_elems, 4 * s.y_elems + 24) // 2), 24)
 
 
 def join_kernel(s):
@@ -691,6 +731,9 @@
     ey, ny = (s.y_elems, s.y_nodes)
 
     def kernel(edge, three, one, down, up, down_out, up_out, three_out, one_out):
+        lane = lax.broadcasted_iota(jnp.int32, (rows_c, half), 1)
+        is_three = (lane < s.coarse_z).astype(f32)
+        is_one = (lane >= s.coarse_z).astype(f32)[0:8]
         for y in range(ny):
             plane = edge[y]
             if y >= ny - 6:
@@ -701,16 +744,23 @@
         first = 6 * ny
         down_out[first:, :] = jnp.zeros((down_out.shape[0] - first, lanes), f32)
         up_out[...] = jnp.zeros(up_out.shape, f32)
+
+        def from_above(k, count):
+            row, at = (rows_c * (k % 2), base + half * (k // 2))
+            return down[row : row + count, at : at + half]
+
         for j in range(3 * ey):
             plane = three[3 + j]
             if j >= 3 * ey - 3:
-                k = j - (3 * ey - 3)
-                plane = plane + down[0:rows_c, base + half * k : base + half * (k + 1)]
+                plane = plane + from_above(j - (3 * ey - 3), rows_c)
             if j == 0:
                 plane = plane + up[0:rows_c, 0:half]
+            plane = plane * is_three
             three_out[j] = plane
-            down_out[first + 3 * j : first + 3 * j + 3, 0:half] = plane[0:3]
-            up_out[j : j + 1, 0:half] = plane[s.coarse_x - 1 : s.coarse_x]
+            row, at = coarse_place(s, 3 * j)
+            down_out[first + row : first + row + 3, at : at + half] = plane[0:3]
+            row, at = coarse_place(s, j)
+            up_out[row : row + 1, at : at + half] = plane[s.coarse_x - 1 : s.coarse_x]
         for j in range(ey + 6):
             y = j - 3
             plane = None
@@ -718,16 +768,16 @@
                 plane = one[y + 1]
             if y <= 0:
                 k = y + 3
-                part = up[rows_c : rows_c + 8, half * k : half * k + LANES]
+                part = up[0:8, half * k : half * (k + 1)]
                 plane = part if plane is None else plane + part
             if y >= ey - 1:
-                k = y - (ey - 1)
-                at = base + half * k
-                part = down[rows_c : rows_c + 8, at : at + LANES]
+                part = from_above(y - (ey - 1), 8)
                 plane = part if plane is None else plane + part
+            plane = plane * is_one
             one_out[j] = plane
-            down_out[first + 4 * j : first + 4 * j + 4, half : half + LANES] = plane[0:4]
-            up_out[4 * j : 4 * j + 4, half : half + LANES] = plane[s.x_elems - 2 : s.x_elems + 2]
+            row, at = coarse_place(s, 4 * j)
+            down_out[first + row : first + row + 4, at : at + half] += plane[0:4]
+            up_out[row : row + 4, at : at + half] += plane[s.x_elems - 2 : s.x_elems + 2]
 
     return kernel
 
@@ -792,23 +842,26 @@
         live = ((lane >= 1) & ((row >= 1) | (gx > 0))).astype(f32)
         for j in range(3 * ey):
             fine[j] = three[j]
-            fine[j, 3 * ex : 3 * ex + 3, :] += right[first + 3 * j : first + 3 * j + 3, 0:half]
-            fine[j, 3:4, :] += left[j : j + 1, 0:half]
+            at_row, at = coarse_place(s, 3 * j)
+            at_row += first
+            fine[j, 3 * ex : 3 * ex + 3, :] += right[at_row : at_row + 3, at : at + half]
+            at_row, at = coarse_place(s, j)
+            fine[j, 3:4, :] += left[at_row : at_row + 1, at : at + half]
             mask = live if j else live * live_y
             three_out[:, nzc * j : nzc * (j + 1)] = fine[j, 3 : 3 * ex + 3, 0:nzc] * mask
         level[...] = jnp.zeros((ey + 6, one_rows, LANES), f32)
         for j in range(ey + 6):
             level[j, 2 : ex + 4, :] = one[j, 0 : ex + 2, :]
-            level[j, 0:4, :] += left[4 * j : 4 * j + 4, half : half + LANES]
-            level[j, ex + 2 : ex + 6, :] += right[
-                first + 4 * j : first + 4 * j + 4, half : half + LANES
-            ]
+            at_row, at = coarse_place(s, 4 * j)
+            level[j, 0:4, :] += left[at_row : at_row + 4, at : at + half]
+            at_row += first
+            level[j, ex + 2 : ex + 6, :] += right[at_row : at_row + 4, at : at + half]
         shape = (one_rows, LANES)
         lane = lax.broadcasted_iota(jnp.int32, shape, 1)
         row = lax.broadcasted_iota(jnp.int32, shape, 0)
         global_x = gx * ex + row - 3
         plane_mask = (
-            (lane >= 1) & (lane < s.z_elems) & (row < ex + 6)
+            (lane > s.coarse_z) & (lane < s.coarse_z + s.z_elems) & (row < ex + 6)
             & (global_x >= 1) & (global_x < x_total)
         )
         masks = []
@@ -838,7 +891,9 @@
             error = fresh
         nze = s.z_elems
         for j in range(ey):
-            coarse_out[:, nze * j : nze * (j + 1)] = error[3 + j][3 : 3 + ex, 0:nze]
+            coarse_out[:, nze * j : nze * (j + 1)] = error[3 + j][
+                3 : 3 + ex, s.coarse_z : s.coarse_z + nze
+            ]
 
     return kernel
 
@@ -864,37 +919,51 @@
             out_shape=tuple(shape(*dims) for dims in outputs),
             in_specs=specs,
             out_specs=tuple(vmem(len(outputs))),
-            scratch_shapes=[pltpu.VMEM(dims, f32) for dims in scratch]
+            scratch_shapes=[pltpu.VMEM(d, f32) if isinstance(d, tuple) else d for d in scratch]
             + ([pltpu.SemaphoreType.DMA((semaphores,))] if semaphores else []),
             compiler_params=params,
             name=name,
         )(*operands)
 
-    table = residual_constants(s)
-    r_own, edge, up, u_first = call(
+    in_hbm = lambda values: [pltpu.with_memory_space_constraint(v, pltpu.HBM) for v in values]
+    hbm = {index: pltpu.HBM for index in range(4)}
+    low = (x_nodes - 7) // 8 * 8
+    constants = residual_constants(s, low)
+    up, u_first = call(
+        send_kernel(s),
+        "send",
+        ((8, up_to((ny + 2) * z_nodes, LANES)), (up_to(ny, 8), lanes)),
+        in_hbm([initial_guess, load_vector] + constants),
+        [
+            (ny + 1, s.own_rows - low, lanes),
+            (ny + 1, s.own_rows - low, lanes),
+            (x_nodes - low, width),
+            (x_nodes - low, width),
+            constants[0].shape,
+            pltpu.VMEM(constants[1].shape, jnp.bfloat16),
+            (8, width),
+        ],
+        spaces=hbm,
+        semaphores=5,
+    )
+    below = shifted(up, "gx", 1)
+    above = shifted(u_first, "gx", -1)
+    constants = residual_constants(s, 0)
+    r_own, edge = call(
         residual_kernel(s),
         "residual",
-        (
-            (ny + 1, s.own_rows, lanes),
-            (s.own_rows, lanes),
-            (8, up_to((ny + 2) * z_nodes, LANES)),
-            (up_to(ny, 8), lanes),
-        ),
-        [
-            pltpu.with_memory_space_constraint(value, pltpu.HBM)
-            for value in (initial_guess, load_vector, jnp.asarray(table, f32))
-        ],
+        ((ny + 1, s.own_rows, lanes), (s.own_rows, lanes)),
+        in_hbm([initial_guess, load_vector] + constants),
         [
             (ny + 1, s.own_rows, lanes),
             initial_guess.shape,
             load_vector.shape,
-            table.shape,
+            constants[0].shape,
+            pltpu.VMEM(constants[1].shape, jnp.bfloat16),
         ],
-        spaces={0: pltpu.HBM, 1: pltpu.HBM, 2: pltpu.HBM},
-        semaphores=3,
-    )
-    below = shifted(up, "gx", 1)
-    above = shifted(u_first, "gx", -1)
+        spaces=hbm,
+        semaphores=4,
+    )
     r_x, line, up = call(
         joined_x_kernel(s),
         "joined_x",
@@ -916,8 +985,8 @@
             (ny, rows - 8, lanes),
             (s.coarse_y, s.coarse_rows, half),
             (ey + 2, 8, LANES),
-            (rows, 6 * lanes + 4 * half),
-            (s.coarse_rows + 8, 4 * half),
+            (rows, 6 * lanes + 2 * half),
+            (s.coarse_rows, 4 * half),
         ),
         [r_x, line, below, above] + patch_constants(s),
         [
@@ -936,13 +1005,12 @@
     )
     down = shifted(down, "gy", -1)
     up = shifted(up, "gy", 1)
-    coarse_part = up_to(max(9 * ey, 4 * ey + 24), 8)
     right, left, three, one = call(
         join_kernel(s),
         "join",
         (
-            (6 * ny + coarse_part, lanes),
-            (up_to(max(3 * ey, 4 * ey + 24), 8), lanes),
+            (6 * ny + coarse_height(s), lanes),
+            (coarse_height(s), lanes),
             (3 * ey, s.coarse_rows, half),
             (ey + 6, 8, LANES),
         ),

time: 57.2 us -> 54.6 us (0.955)
  waiting for transfers between devices: 11.9 us -> 7 us
  Pallas kernels: 20.2 us -> 21.8 us
    ppermute x8, waiting for transfers between devices: 11.9 us -> 7 us  [shifted(): return lax.ppermute(array, axis, pairs)]
    pallas_call x6 -> x7, Pallas kernels: 20.2 us -> 21.8 us  [call(): pl.pallas_call(kernel, out_shape=tuple((shape(*dims) for dims in outputs)...]
  transfers between devices with their start and end apart: 8 -> 8, of which waited for: 6 -> 4; matrix products, arithmetic and copies ran while one was open for 0% -> 0% of each run, Pallas kernels for 4% -> 11%
where the time goes in v5:
time: 54.6 us; the launch traced here: 53.6 us
  starting transfers between devices  23.7 us (43%)
  Pallas kernels  21.8 us (40%)
  waiting for transfers between devices  7 us (13%)
  between operations  1.02 us (2%)
    ppermute x8, starting transfers between devices, shifted(): return lax.ppermute(array, axis, pairs)  23.7 us
    pallas_call x7, Pallas kernels, call(): pl.pallas_call(kernel, out_shape=tuple((shape(*dims) for dims in outputs)...  21.8 us
    ppermute x8, waiting for transfers between devices, shifted(): return lax.ppermute(array, axis, pairs)  7 us
  transfers between devices with their start and end apart: 8, of which 4 were waited for; matrix products, arithmetic and copies ran while one was open for 0% of the time, Pallas kernels for 11%

profile of v5, /device:TPU:20, one launch (start us, length us, event | category | flops | bytes accessed | tf_op | source)
XLA Modules:
  0.0 53.6 jit_solution(13247732383515356655)
XLA Ops:
  0.6 2.6 %send.1 = (f32[8,6784]{1,0:T(8,128)S(1)}, f32[32,256]{1,0:T(8,128)S(1)}) custom-call(f32[28,6272]{1,0:T(8,128)} %guess.1, f32[28,6272]{1,0:T(8,128)} %load_hbm.3, f32[304,256]{1,0:T(8,128)} %constant.44.clone.table_hbm, bf16[16,48]{1,0:T(8,128)(2,1)} %constant.45.clone.k_x_hbm), custom_call_target="tpu_custom_call" | custom-call | tf_op jit(solution)/shard_map/send/pallas_call | solution.py:917
  3.3 0.0 copy-start.11
  3.3 0.0 copy-start.12
  3.3 3.5 %collective-permute-start = (f32[8,6784]{1,0:T(8,128)S(1)}, f32[8,6784]{1,0:T(8,128)S(1)}, u32[]{:S(2)}, u32[]{:S(2)}) collective-permute-start(f32[8,6784]{1,0:T(8,128)S(1)} %get-tuple-element.23), channel_id=1, source_target_pairs={{0,8},{8,16},{16,24},{1,9},{9,17},{17,25},{2,10},{10,18},{18,26},{... | collective-permute-start | bytes 651272 | tf_op jit(solution)/shard_map/ppermute | solution.py:33
  6.8 0.0 copy-start.1
  6.8 0.0 copy-start.3
  6.9 0.0 copy-start.4
  6.9 0.0 copy-start.5
  6.9 0.0 copy-start.6
  6.9 0.0 copy-start.7
  6.9 0.0 copy-start.8
  6.9 0.0 copy-start.9
  6.9 0.0 copy-start.10
  6.9 0.0 copy-start.13
  7.0 0.0 copy-start.14
  7.0 0.0 copy-start.15
  7.0 0.0 copy-start.16
  7.0 0.0 copy-start.17
  7.0 0.0 copy-start.18
  7.0 3.5 %collective-permute-start.1 = (f32[32,256]{1,0:T(8,128)S(1)}, f32[32,256]{1,0:T(8,128)S(1)}, u32[]{:S(2)}, u32[]{:S(2)}) collective-permute-start(f32[32,256]{1,0:T(8,128)S(1)} %get-tuple-element.22.u_first), channel_id=1, source_target_pairs={{8,0},{16,8},{24,16},{9,1},{17,9},{25,17},{10,2},{18,10},{26,18},{... | collective-permute-start | bytes 98312 | tf_op jit(solution)/shard_map/ppermute | solution.py:33
  10.5 3.4 %residual.1 = (f32[29,32,256]{2,1,0:T(8,128)S(1)}, f32[32,256]{1,0:T(8,128)S(1)}) custom-call(f32[28,6272]{1,0:T(8,128)} %guess.1, f32[28,6272]{1,0:T(8,128)} %load_hbm.3, f32[352,256]{1,0:T(8,128)} %constant.46.clone.table_hbm, bf16[32,96]{1,0:T(8,128)(2,1)} %constant.47.clone.k_x_hbm), custom_call_target="tpu_custom_call" | custom-call | tf_op jit(solution)/shard_map/residual/pallas_call | solution.py:917
  13.9 0.0 collective-permute-done.1.above
  13.9 0.0 collective-permute-done.below
  13.9 0.0 copy-done.11
  13.9 0.0 copy-done.12
  13.9 0.5 joined_x.1
  14.4 1.9 %collective-permute-start.2 = (f32[40,1664]{1,0:T(8,128)S(1)}, f32[40,1664]{1,0:T(8,128)S(1)}, u32[]{:S(2)}, u32[]{:S(2)}) collective-permute-start(f32[40,1664]{1,0:T(8,128)S(1)} %get-tuple-element.26), channel_id=1, source_target_pairs={{0,1},{1,2},{2,3},{3,4},{4,5},{5,6},{6,7},{8,9},{9,10},{10,11},{11... | collective-permute-start | bytes 798728 | tf_op jit(solution)/shard_map/ppermute | solution.py:33
  16.3 3.8 %collective-permute-start.3 = (f32[40,256]{1,0:T(8,128)S(1)}, f32[40,256]{1,0:T(8,128)S(1)}, u32[]{:S(2)}, u32[]{:S(2)}) collective-permute-start(f32[40,256]{1,0:T(8,128)S(1)} %get-tuple-element.25.line), channel_id=1, source_target_pairs={{1,0},{2,1},{3,2},{4,3},{5,4},{6,5},{7,6},{9,8},{10,9},{11,10},{12... | collective-permute-start | bytes 122888 | tf_op jit(solution)/shard_map/ppermute | solution.py:33
  20.2 1.5 %collective-permute-done.3.above = f32[40,256]{1,0:T(8,128)S(1)} collective-permute-done((f32[40,256]{1,0:T(8,128)S(1)}, f32[40,256]{1,0:T(8,128)S(1)}, u32[]{:S(2)}, u32[]{:S(2)}) %collective-permute-start.3) | collective-permute-done | bytes 40992 | tf_op jit(solution)/shard_map/ppermute | solution.py:33
  21.6 0.5 collective-permute-done.2.below
  22.2 0.0 copy-done.5
  22.2 0.0 copy-done.6
  22.2 0.0 copy-done.7
  22.2 0.0 copy-done.8
  22.3 0.0 copy-start
  22.3 0.0 copy-start.2
  22.3 11.0 %patches.1 = (f32[28,8,256]{2,1,0:T(8,128)S(1)}, f32[28,32,256]{2,1,0:T(8,128)S(1)}, f32[16,16,128]{2,1,0:T(8,128)S(1)}, f32[6,8,128]{2,1,0:T(8,128)S(1)}, f32[4...) custom-call(f32[29,40,256]{2,1,0:T(8,128)S(1)} %get-tuple-element.24.r_own, f32[40,256]{1,0:T(8,128)S(1)} %get-tuple-element.25.line, ...), custom_call_target="tpu_custom_call" | custom-call | tf_op jit(solution)/shard_map/patches/pallas_call | solution.py:917
  33.3 3.2 %collective-permute-start.4 = (f32[40,1792]{1,0:T(8,128)S(1)}, f32[40,1792]{1,0:T(8,128)S(1)}, u32[]{:S(2)}, u32[]{:S(2)}) collective-permute-start(f32[40,1792]{1,0:T(8,128)S(1)} %get-tuple-element.28), channel_id=1, source_target_pairs={{1,0},{2,1},{3,2},{4,3},{5,4},{6,5},{7,6},{9,8},{10,9},{11,10},{12... | collective-permute-start | bytes 860168 | tf_op jit(solution)/shard_map/ppermute | solution.py:33
  36.4 1.9 %collective-permute-start.5 = (f32[16,512]{1,0:T(8,128)S(1)}, f32[16,512]{1,0:T(8,128)S(1)}, u32[]{:S(2)}, u32[]{:S(2)}) collective-permute-start(f32[16,512]{1,0:T(8,128)S(1)} %get-tuple-element.32), channel_id=1, source_target_pairs={{0,1},{1,2},{2,3},{3,4},{4,5},{5,6},{6,7},{8,9},{9,10},{10,11},{11... | collective-permute-start | bytes 98312 | tf_op jit(solution)/shard_map/ppermute | solution.py:33
  38.4 3.3 %collective-permute-done.5.up = f32[16,512]{1,0:T(8,128)S(1)} collective-permute-done((f32[16,512]{1,0:T(8,128)S(1)}, f32[16,512]{1,0:T(8,128)S(1)}, u32[]{:S(2)}, u32[]{:S(2)}) %collective-permute-start.5) | collective-permute-done | bytes 32800 | tf_op jit(solution)/shard_map/ppermute | solution.py:33
  41.7 0.0 collective-permute-done.4.down
  41.7 0.1 join.1
  41.7 3.5 %collective-permute-start.6 = (f32[192,256]{1,0:T(8,128)S(1)}, f32[192,256]{1,0:T(8,128)S(1)}, u32[]{:S(2)}, u32[]{:S(2)}) collective-permute-start(f32[192,256]{1,0:T(8,128)S(1)} %get-tuple-element.33), channel_id=1, source_target_pairs={{8,0},{16,8},{24,16},{9,1},{17,9},{25,17},{10,2},{18,10},{26,18},{... | collective-permute-start | bytes 589832 | tf_op jit(solution)/shard_map/ppermute | solution.py:33
  45.2 2.4 %collective-permute-start.7 = (f32[24,256]{1,0:T(8,128)S(1)}, f32[24,256]{1,0:T(8,128)S(1)}, u32[]{:S(2)}, u32[]{:S(2)}) collective-permute-start(f32[24,256]{1,0:T(8,128)S(1)} %get-tuple-element.34), channel_id=1, source_target_pairs={{0,8},{8,16},{16,24},{1,9},{9,17},{17,25},{2,10},{10,18},{18,26},{... | collective-permute-start | bytes 73736 | tf_op jit(solution)/shard_map/ppermute | solution.py:33
  47.6 2.5 %base.1 = f32[28,6272]{1,0:T(8,128)S(1)} custom-call(f32[28,6272]{1,0:T(8,128)S(1)} %copy-done, f32[28,256]{1,0:T(8,128)S(1)} %copy-done.2, f32[28,32,256]{2,1,0:T(8,128)S(1)} %get-tuple-element.27.own, f32[40,1792]{1,0:T(8,128)S(1)} %collective-permute-done.4.down), custom_call_target="tpu_custom_call" | custom-call | tf_op jit(solution)/shard_map/base/pallas_call | solution.py:917
  50.1 1.7 %collective-permute-done.7.left = f32[24,256]{1,0:T(8,128)S(1)} collective-permute-done((f32[24,256]{1,0:T(8,128)S(1)}, f32[24,256]{1,0:T(8,128)S(1)}, u32[]{:S(2)}, u32[]{:S(2)}) %collective-permute-start.7) | collective-permute-done | bytes 24608 | tf_op jit(solution)/shard_map/ppermute | solution.py:33
  51.9 0.0 collective-permute-done.6.right
  51.9 1.8 %finish.1 = (f32[28,6272]{1,0:T(8,128)}, f32[12,1152]{1,0:T(8,128)}, f32[4,128]{1,0:T(4,128)}) custom-call(f32[28,6272]{1,0:T(8,128)S(1)} %base.1, f32[28,256]{1,0:T(8,128)S(1)} %copy-done.2, f32[192,256]{1,0:T(8,128)S(1)} %collective-permute-done.6.right, f32[24,256]{1,0:T(8,128)S(1)} %collective-permute-done.7.left, ...), custom_call_target="tpu_custom_call" | custom-call | tf_op jit(solution)/shard_map/finish/pallas_call | solution.py:917
  (13 shorter events, 0.0 us)
Async XLA Ops:
  3.3 10.6 %copy-start.11 = (f32[40,256]{1,0:T(8,128)S(1)}, f32[40,256]{1,0:T(8,128)}, u32[]{:S(2)}) copy-start(f32[40,256]{1,0:T(8,128)} %constant.49.clone.c_above) | copy-start | bytes 122884
  3.3 10.6 %copy-start.12 = (f32[40,256]{1,0:T(8,128)S(1)}, f32[40,256]{1,0:T(8,128)}, u32[]{:S(2)}) copy-start(f32[40,256]{1,0:T(8,128)} %constant.48.clone.c_below) | copy-start | bytes 122884
  3.3 10.6 %collective-permute-start = (f32[8,6784]{1,0:T(8,128)S(1)}, f32[8,6784]{1,0:T(8,128)S(1)}, u32[]{:S(2)}, u32[]{:S(2)}) collective-permute-start(f32[8,6784]{1,0:T(8,128)S(1)} %get-tuple-element.23), channel_id=1, source_target_pairs={{0,8},{8,16},{16,24},{1,9},{9,17},{17,25},{2,10},{10,18},{18,26},{... | collective-permute-start | bytes 651272 | tf_op jit(solution)/shard_map/ppermute | solution.py:33
  6.8 15.3 %copy-start.1 = (f32[256,256]{1,0:T(8,128)S(1)}, f32[256,256]{1,0:T(8,128)}, u32[]{:S(2)}) copy-start(f32[256,256]{1,0:T(8,128)} %constant.53.clone.q_z) | copy-start | bytes 786436
  6.8 15.3 %copy-start.3 = (bf16[256,256]{1,0:T(8,128)(2,1)S(1)}, bf16[256,256]{1,0:T(8,128)(2,1)}, u32[]{:S(2)}) copy-start(bf16[256,256]{1,0:T(8,128)(2,1)} %constant.63.clone.b_z) | copy-start | bytes 393220
  6.9 15.3 %copy-start.4 = (bf16[256,256]{1,0:T(8,128)(2,1)S(1)}, bf16[256,256]{1,0:T(8,128)(2,1)}, u32[]{:S(2)}) copy-start(bf16[256,256]{1,0:T(8,128)(2,1)} %constant.61.clone.f_z) | copy-start | bytes 393220
  6.9 15.3 %copy-start.5 = (f32[256,128]{1,0:T(8,128)S(1)}, f32[256,128]{1,0:T(8,128)}, u32[]{:S(2)}) copy-start(f32[256,128]{1,0:T(8,128)} %constant.54.clone.r_z) | copy-start | bytes 393220
  6.9 15.3 %copy-start.6 = (bf16[256,128]{1,0:T(8,128)(2,1)S(1)}, bf16[256,128]{1,0:T(8,128)(2,1)}, u32[]{:S(2)}) copy-start(bf16[256,128]{1,0:T(8,128)(2,1)} %constant.64.clone.b_z_high) | copy-start | bytes 196612
  6.9 15.3 %copy-start.7 = (bf16[128,256]{1,0:T(8,128)(2,1)S(1)}, bf16[128,256]{1,0:T(8,128)(2,1)}, u32[]{:S(2)}) copy-start(bf16[128,256]{1,0:T(8,128)(2,1)} %constant.62.clone.f_z_low) | copy-start | bytes 196612
  6.9 15.3 %copy-start.8 = (f32[128,128]{1,0:T(8,128)S(1)}, f32[128,128]{1,0:T(8,128)}, u32[]{:S(2)}) copy-start(f32[128,128]{1,0:T(8,128)} %constant.55.clone.o_z) | copy-start | bytes 196612
  6.9 15.3 %copy-start.9 = (f32[56,256]{1,0:T(8,128)S(1)}, f32[56,256]{1,0:T(8,128)}, u32[]{:S(2)}) copy-start(f32[56,256]{1,0:T(8,128)} %constant.52.clone.sums) | copy-start | bytes 172036
  6.9 15.3 %copy-start.10 = (f32[40,256]{1,0:T(8,128)S(1)}, f32[40,256]{1,0:T(8,128)}, u32[]{:S(2)}) copy-start(f32[40,256]{1,0:T(8,128)} %constant.51.clone.m_xz) | copy-start | bytes 122884
  6.9 15.3 %copy-start.13 = (bf16[40,168]{1,0:T(8,128)(2,1)S(1)}, bf16[40,168]{1,0:T(8,128)(2,1)}, u32[]{:S(2)}) copy-start(bf16[40,168]{1,0:T(8,128)(2,1)} %constant.60.clone.b_x) | copy-start | bytes 40324
  7.0 15.3 %copy-start.14 = (bf16[56,120]{1,0:T(8,128)(2,1)S(1)}, bf16[56,120]{1,0:T(8,128)(2,1)}, u32[]{:S(2)}) copy-start(bf16[56,120]{1,0:T(8,128)(2,1)} %constant.59.clone.f_x) | copy-start | bytes 40324
  7.0 15.3 %copy-start.15 = (bf16[32,120]{1,0:T(8,128)(2,1)S(1)}, bf16[32,120]{1,0:T(8,128)(2,1)}, u32[]{:S(2)}) copy-start(bf16[32,120]{1,0:T(8,128)(2,1)} %constant.57.clone.q_x) | copy-start | bytes 23044
  7.0 15.3 %copy-start.16 = (bf16[16,120]{1,0:T(8,128)(2,1)S(1)}, bf16[16,120]{1,0:T(8,128)(2,1)}, u32[]{:S(2)}) copy-start(bf16[16,120]{1,0:T(8,128)(2,1)} %constant.58.clone.r_x) | copy-start | bytes 11524
  7.0 15.3 %copy-start.17 = (f32[8,16]{1,0:T(8,128)S(1)}, f32[8,16]{1,0:T(8,128)}, u32[]{:S(2)}) copy-start(f32[8,16]{1,0:T(8,128)} %constant.56.clone.o_x) | copy-start | bytes 1540
  7.0 15.3 %copy-start.18 = (f32[13]{0:T(128)S(1)}, f32[13]{0:T(128)}, u32[]{:S(2)}) copy-start(f32[13]{0:T(128)} %constant.50.clone.lam) | copy-start | bytes 160
  7.0 6.9 %collective-permute-start.1 = (f32[32,256]{1,0:T(8,128)S(1)}, f32[32,256]{1,0:T(8,128)S(1)}, u32[]{:S(2)}, u32[]{:S(2)}) collective-permute-start(f32[32,256]{1,0:T(8,128)S(1)} %get-tuple-element.22.u_first), channel_id=1, source_target_pairs={{8,0},{16,8},{24,16},{9,1},{17,9},{25,17},{10,2},{18,10},{26,18},{... | collective-permute-start | bytes 98312 | tf_op jit(solution)/shard_map/ppermute | solution.py:33
  14.4 7.7 %collective-permute-start.2 = (f32[40,1664]{1,0:T(8,128)S(1)}, f32[40,1664]{1,0:T(8,128)S(1)}, u32[]{:S(2)}, u32[]{:S(2)}) collective-permute-start(f32[40,1664]{1,0:T(8,128)S(1)} %get-tuple-element.26), channel_id=1, source_target_pairs={{0,1},{1,2},{2,3},{3,4},{4,5},{5,6},{6,7},{8,9},{9,10},{10,11},{11... | collective-permute-start | bytes 798728 | tf_op jit(solution)/shard_map/ppermute | solution.py:33
  16.3 5.3 %collective-permute-start.3 = (f32[40,256]{1,0:T(8,128)S(1)}, f32[40,256]{1,0:T(8,128)S(1)}, u32[]{:S(2)}, u32[]{:S(2)}) collective-permute-start(f32[40,256]{1,0:T(8,128)S(1)} %get-tuple-element.25.line), channel_id=1, source_target_pairs={{1,0},{2,1},{3,2},{4,3},{5,4},{6,5},{7,6},{9,8},{10,9},{11,10},{12... | collective-permute-start | bytes 122888 | tf_op jit(solution)/shard_map/ppermute | solution.py:33
  22.3 25.3 %copy-start = (f32[28,6272]{1,0:T(8,128)S(1)}, f32[28,6272]{1,0:T(8,128)}, u32[]{:S(2)}) copy-start(f32[28,6272]{1,0:T(8,128)} %guess.1) | copy-start | bytes 2107396
  22.3 25.3 %copy-start.2 = (f32[28,256]{1,0:T(8,128)S(1)}, f32[28,256]{1,0:T(8,128)}, u32[]{:S(2)}) copy-start(f32[28,256]{1,0:T(8,128)} %constant.65.clone.weight) | copy-start | bytes 86020
  33.3 8.4 %collective-permute-start.4 = (f32[40,1792]{1,0:T(8,128)S(1)}, f32[40,1792]{1,0:T(8,128)S(1)}, u32[]{:S(2)}, u32[]{:S(2)}) collective-permute-start(f32[40,1792]{1,0:T(8,128)S(1)} %get-tuple-element.28), channel_id=1, source_target_pairs={{1,0},{2,1},{3,2},{4,3},{5,4},{6,5},{7,6},{9,8},{10,9},{11,10},{12... | collective-permute-start | bytes 860168 | tf_op jit(solution)/shard_map/ppermute | solution.py:33
  36.4 5.2 %collective-permute-start.5 = (f32[16,512]{1,0:T(8,128)S(1)}, f32[16,512]{1,0:T(8,128)S(1)}, u32[]{:S(2)}, u32[]{:S(2)}) collective-permute-start(f32[16,512]{1,0:T(8,128)S(1)} %get-tuple-element.32), channel_id=1, source_target_pairs={{0,1},{1,2},{2,3},{3,4},{4,5},{5,6},{6,7},{8,9},{9,10},{10,11},{11... | collective-permute-start | bytes 98312 | tf_op jit(solution)/shard_map/ppermute | solution.py:33
  41.7 10.1 %collective-permute-start.6 = (f32[192,256]{1,0:T(8,128)S(1)}, f32[192,256]{1,0:T(8,128)S(1)}, u32[]{:S(2)}, u32[]{:S(2)}) collective-permute-start(f32[192,256]{1,0:T(8,128)S(1)} %get-tuple-element.33), channel_id=1, source_target_pairs={{8,0},{16,8},{24,16},{9,1},{17,9},{25,17},{10,2},{18,10},{26,18},{... | collective-permute-start | bytes 589832 | tf_op jit(solution)/shard_map/ppermute | solution.py:33
  45.2 6.6 %collective-permute-start.7 = (f32[24,256]{1,0:T(8,128)S(1)}, f32[24,256]{1,0:T(8,128)S(1)}, u32[]{:S(2)}, u32[]{:S(2)}) collective-permute-start(f32[24,256]{1,0:T(8,128)S(1)} %get-tuple-element.34), channel_id=1, source_target_pairs={{0,8},{8,16},{16,24},{1,9},{9,17},{17,25},{2,10},{10,18},{18,26},{... | collective-permute-start | bytes 73736 | tf_op jit(solution)/shard_map/ppermute | solution.py:33

commit v6 on v5

--- a/solution.py
+++ b/solution.py
@@ -147,7 +147,7 @@
 
 high = lax.Precision.HIGH
 LANES = 128
-GROUP = 7
+GROUP = 13
 f32 = jnp.float32
 
 
@@ -298,7 +298,6 @@
     one_x = placed(linear_from_cubic(-1, s.x_elems, -3, 3 * s.x_elems), (8, s.coarse_rows))
     singles = [
         mass_x[:, None] * mass_z[None, :],
-        sums,
         rows_by_node(s, coarse_of_z, True),
         rows_by_node(s, own_z, False),
         one_z,
@@ -307,9 +306,7 @@
     own_x = placed(line_x["own"], (s.coarse_rows, s.rows), col=8).astype(np.float64)
     high_q, low_q = two_parts(coarse_of_x)
     high_r, low_r = two_parts(own_x)
-    halves = [
-        np.concatenate([high_q, high_q, low_q], 1),
-        np.concatenate([high_r, high_r, low_r], 1),
+    solve = [
         np.concatenate([high_x, high_x, low_x], 1),
         np.concatenate([high_x.T, high_x.T, low_x.T], 1),
         np.concatenate([high_z, high_z], 0),
@@ -317,10 +314,15 @@
         np.concatenate([high_z.T, low_z.T], 1),
         high_z.T,
     ]
+    coarse = [
+        np.concatenate([high_q, high_q, low_q], 1),
+        np.concatenate([high_r, high_r, low_r], 1),
+    ]
     return (
-        [jnp.asarray(eigvals, f32)]
-        + [jnp.asarray(value, f32) for value in singles]
-        + [jnp.asarray(value, jnp.bfloat16) for value in halves]
+        [jnp.asarray(eigvals, f32), jnp.asarray(sums, f32)]
+        + [jnp.asarray(value, jnp.bfloat16) for value in solve],
+        [jnp.asarray(value, f32) for value in singles]
+        + [jnp.asarray(value, jnp.bfloat16) for value in coarse],
     )
 
 
@@ -556,6 +558,84 @@
     return kernel
 
 
+def patch_modes(s, vertices, plane_of, matrices, xf, xb, live):
+    lam, sums, f_x, b_x, f_z, f_z_low, b_z, b_z_high = matrices
+    rows = s.rows
+    count = len(vertices)
+    _, eigbasis = patch_basis()
+    evens = [b for b in range(13) if symmetric(eigbasis[:, b])]
+    gx = lax.axis_index("gx")
+    gy = lax.axis_index("gy")
+    shape = (s.modes_x, s.modes_z)
+    mode = lax.broadcasted_iota(jnp.int32, shape, 0)
+    vertex = lax.broadcasted_iota(jnp.int32, shape, 1) % s.half_z
+    live_x = (mode % s.x_elems != 0) | (gx > 0)
+    live[0] = (live_x & (vertex != 0)).astype(f32)
+    live[1] = live_x.astype(f32)
+    active = (gy > 0).astype(f32)
+
+    def along_y(tile, carry):
+        at = pl.ds(pl.multiple_of(tile * 8, 8), 8)
+        for i, v in enumerate(vertices):
+            first = [plane_of(7 * v + a - 6, at) for a in range(13)]
+            if v == 0:
+                first = [value * active for value in first]
+            even = [first[6]] + [first[6 + a] + first[6 - a] for a in range(1, 7)]
+            odd = [first[6 + a] - first[6 - a] for a in range(1, 7)]
+            for b in range(13):
+                if b in evens:
+                    xf[b, i, at, :] = sum(even[a] * float(eigbasis[6 + a, b]) for a in range(7))
+                else:
+                    xf[b, i, at, :] = sum(odd[a] * float(eigbasis[7 + a, b]) for a in range(6))
+        return carry
+
+    lax.fori_loop(0, rows // 8, along_y, 0)
+
+    def spectral(modes_of):
+        pieces = []
+        for b in modes_of:
+            planes = [dot(f_x[...], stacked_rows(xf[b, v])) for v in range(count)]
+            pieces += [plane[:, :LANES] for plane in planes]
+            pieces += [plane[:, LANES:] for plane in planes]
+        high_part, low_part = halves_of(jnp.concatenate(pieces, 0))
+        modes = dot(jnp.concatenate([high_part, low_part], 1), f_z[...]) + dot(
+            high_part, f_z_low[...]
+        )
+        modes = modes.reshape(len(modes_of), 2, count, s.modes_x, s.modes_z)
+        pieces = []
+        for i, b in enumerate(modes_of):
+            factor = 1.0 / (sums[...] + lam[b])
+            for t in range(2):
+                scaled = modes[i, t] * (factor * live[t])[None]
+                pieces.append(scaled.reshape(count * s.modes_x, s.modes_z))
+        high_part, low_part = halves_of(jnp.concatenate(pieces, 0))
+        both = dot(high_part, b_z[...])
+        back = both[:, :LANES] + both[:, LANES:] + dot(low_part, b_z_high[...])
+        back = back.reshape(len(modes_of), 2, count, s.modes_x, LANES)
+        for i, b in enumerate(modes_of):
+            for v in range(count):
+                plane = jnp.concatenate([back[i, 0, v], back[i, 1, v]], 1)
+                xb[b, v] = dot(b_x[...], stacked_rows(plane))
+
+    for first in range(0, 13, GROUP):
+        spectral(range(first, min(13, first + GROUP)))
+
+
+def inner_kernel(s):
+    def kernel(r_own, lam, sums, f_x, b_x, f_z, f_z_low, b_z, b_z_high, xb, xf, live):
+        patch_modes(
+            s,
+            list(range(1, s.y_elems - 1)),
+            lambda y, at: r_own[y, at, :],
+            (lam, sums, f_x, b_x, f_z, f_z_low, b_z, b_z_high),
+            xf,
+            xb,
+            live,
+        )
+
+    return kernel
+
+
 def patch_kernel(s):
     rows, lanes = (s.rows, s.lanes)
     ey, ny = (s.y_elems, s.y_nodes)
@@ -567,13 +647,12 @@
     odds = [b for b in range(13) if b not in evens]
 
     def kernel(
-        r_own, line, below, above,
-        lam, m_xz, sums, q_z, r_z, o_z, o_x, q_x, r_x, f_x, b_x, f_z, f_z_low, b_z, b_z_high,
+        r_own, line, below, above, inner,
+        lam, sums, f_x, b_x, f_z, f_z_low, b_z, b_z_high,
+        m_xz, q_z, r_z, o_z, o_x, q_x, r_x,
         edge_out, own_out, three_out, one_out, down_out, up_out,
         r, xf, xb, c, cz, rz, hx, ex, rx, live,
     ):
-        gx = lax.axis_index("gx")
-        gy = lax.axis_index("gy")
         inside = lane_mask(s, (rows, lanes), 0).astype(f32)
         width = below.shape[1]
         lower = line[...] * m_xz[...]
@@ -589,69 +668,24 @@
             if y >= ny - 7:
                 plane = plane - upper * float(stiffness[y - (ny - 7), 7])
             r[6 + y] = plane
-        shape = (s.modes_x, s.modes_z)
-        mode = lax.broadcasted_iota(jnp.int32, shape, 0)
-        vertex = lax.broadcasted_iota(jnp.int32, shape, 1) % s.half_z
-        live_x = (mode % s.x_elems != 0) | (gx > 0)
-        live[0] = (live_x & (vertex != 0)).astype(f32)
-        live[1] = live_x.astype(f32)
-        active = (gy > 0).astype(f32)
-
-        def along_y(tile, carry):
-            at = pl.ds(pl.multiple_of(tile * 8, 8), 8)
-            for v in range(ey):
-                first = [r[7 * v + a, at, :] for a in range(13)]
-                if v == 0:
-                    first = [value * active for value in first]
-                even = [first[6]] + [first[6 + a] + first[6 - a] for a in range(1, 7)]
-                odd = [first[6 + a] - first[6 - a] for a in range(1, 7)]
-                for b in range(13):
-                    if b in evens:
-                        xf[b, v, at, :] = sum(
-                            even[a] * float(eigbasis[6 + a, b]) for a in range(7)
-                        )
-                    else:
-                        xf[b, v, at, :] = sum(
-                            odd[a] * float(eigbasis[7 + a, b]) for a in range(6)
-                        )
-            return carry
-
-        lax.fori_loop(0, rows // 8, along_y, 0)
-
-        def spectral(modes_of):
-            pieces = []
-            for b in modes_of:
-                planes = [dot(f_x[...], stacked_rows(xf[b, v])) for v in range(ey)]
-                pieces += [plane[:, :LANES] for plane in planes]
-                pieces += [plane[:, LANES:] for plane in planes]
-            high_part, low_part = halves_of(jnp.concatenate(pieces, 0))
-            modes = dot(jnp.concatenate([high_part, low_part], 1), f_z[...]) + dot(
-                high_part, f_z_low[...]
-            )
-            modes = modes.reshape(len(modes_of), 2, ey, s.modes_x, s.modes_z)
-            pieces = []
-            for i, b in enumerate(modes_of):
-                factor = 1.0 / (sums[...] + lam[b])
-                for t in range(2):
-                    scaled = modes[i, t] * (factor * live[t])[None]
-                    pieces.append(scaled.reshape(ey * s.modes_x, s.modes_z))
-            high_part, low_part = halves_of(jnp.concatenate(pieces, 0))
-            both = dot(high_part, b_z[...])
-            back = both[:, :LANES] + both[:, LANES:] + dot(low_part, b_z_high[...])
-            back = back.reshape(len(modes_of), 2, ey, s.modes_x, LANES)
-            for i, b in enumerate(modes_of):
-                for v in range(ey):
-                    plane = jnp.concatenate([back[i, 0, v], back[i, 1, v]], 1)
-                    xb[b, v] = dot(b_x[...], stacked_rows(plane))
-
-        for first in range(0, 13, GROUP):
-            spectral(range(first, min(13, first + GROUP)))
+        patch_modes(
+            s,
+            [0, ey - 1],
+            lambda y, at: r[y + 6, at, :],
+            (lam, sums, f_x, b_x, f_z, f_z_low, b_z, b_z_high),
+            xf,
+            xb,
+            live,
+        )
 
         def back_y(tile, carry):
             at = pl.ds(pl.multiple_of(tile * 8, 8), 8)
             tail = None
             for v in range(ey):
-                modes = [xb[b, v, at, :] for b in range(13)]
+                if 0 < v < ey - 1:
+                    modes = [inner[b, v - 1, at, :] for b in range(13)]
+                else:
+                    modes = [xb[b, min(v, 1), at, :] for b in range(13)]
                 out = [None] * 13
                 for a in range(7):
                     even = sum(modes[b] * float(eigbasis[6 + a, b]) for b in evens)
@@ -977,6 +1011,15 @@
     )
     below = shifted(up, "gy", 1)
     above = shifted(line, "gy", -1)
+    solve, coarse = patch_constants(s)
+    (inner,) = call(
+        inner_kernel(s),
+        "inner",
+        ((13, ey - 2, rows, lanes),),
+        [r_x] + solve,
+        [(13, ey - 2, rows, lanes), (2, s.modes_x, s.modes_z)],
+        spaces={1: pltpu.SMEM},
+    )
     edge, own, three, one, down, up = call(
         patch_kernel(s),
         "patches",
@@ -988,11 +1031,11 @@
             (rows, 6 * lanes + 2 * half),
             (s.coarse_rows, 4 * half),
         ),
-        [r_x, line, below, above] + patch_constants(s),
+        [r_x, line, below, above, inner] + solve + coarse,
         [
             (ny + 6, rows, lanes),
-            (13, ey, rows, lanes),
-            (13, ey, rows, lanes),
+            (13, 2, rows, lanes),
+            (13, 2, rows, lanes),
             (ny + 6, rows, lanes),
             (ny + 6, rows, 2 * half),
             (ny, rows, half),
@@ -1001,7 +1044,7 @@
             (ny, s.coarse_rows, half),
             (2, s.modes_x, s.modes_z),
         ],
-        spaces={4: pltpu.SMEM},
+        spaces={5: pltpu.SMEM},
     )
     down = shifted(down, "gy", -1)
     up = shifted(up, "gy", 1)

time: 54.6 us -> 52.4 us (0.960)
  waiting for transfers between devices: 7 us -> 4.64 us
  Pallas kernels: 21.8 us -> 22.6 us
  starting transfers between devices: 23.7 us -> 22.9 us
    ppermute x8, waiting for transfers between devices: 7 us -> 4.64 us  [shifted(): return lax.ppermute(array, axis, pairs)]
    pallas_call x7 -> x8, Pallas kernels: 21.8 us -> 22.6 us  [call(): pl.pallas_call(kernel, out_shape=tuple((shape(*dims) for dims in outputs)...]
    ppermute x8, starting transfers between devices: 23.7 us -> 22.9 us  [shifted(): return lax.ppermute(array, axis, pairs)]
  transfers between devices with their start and end apart: 8 -> 8, of which waited for: 4 -> 2; matrix products, arithmetic and copies ran while one was open for 0% -> 0% of each run, Pallas kernels for 11% -> 20%
where the time goes in v6:
time: 52.4 us; the launch traced here: 51.4 us
  starting transfers between devices  22.9 us (44%)
  Pallas kernels  22.6 us (43%)
  waiting for transfers between devices  4.64 us (9%)
  between operations  1.06 us (2%)
    ppermute x8, starting transfers between devices, shifted(): return lax.ppermute(array, axis, pairs)  22.9 us
    pallas_call x8, Pallas kernels, call(): pl.pallas_call(kernel, out_shape=tuple((shape(*dims) for dims in outputs)...  22.6 us
    ppermute x8, waiting for transfers between devices, shifted(): return lax.ppermute(array, axis, pairs)  4.64 us
  transfers between devices with their start and end apart: 8, of which 2 were waited for; matrix products, arithmetic and copies ran while one was open for 0% of the time, Pallas kernels for 20%

profile of v6, /device:TPU:20, one launch (start us, length us, event | category | flops | bytes accessed | tf_op | source)
XLA Modules:
  0.0 51.4 jit_solution(11289567531605620390)
XLA Ops:
  0.6 2.6 %send.1 = (f32[8,6784]{1,0:T(8,128)S(1)}, f32[32,256]{1,0:T(8,128)S(1)}) custom-call(f32[28,6272]{1,0:T(8,128)} %guess.1, f32[28,6272]{1,0:T(8,128)} %load_hbm.3, f32[304,256]{1,0:T(8,128)} %constant.44.clone.table_hbm, bf16[16,48]{1,0:T(8,128)(2,1)} %constant.45.clone.k_x_hbm), custom_call_target="tpu_custom_call" | custom-call | tf_op jit(solution)/shard_map/send/pallas_call | solution.py:951
  3.3 0.0 copy-start.13
  3.3 0.0 copy-start.14
  3.3 3.5 %collective-permute-start = (f32[8,6784]{1,0:T(8,128)S(1)}, f32[8,6784]{1,0:T(8,128)S(1)}, u32[]{:S(2)}, u32[]{:S(2)}) collective-permute-start(f32[8,6784]{1,0:T(8,128)S(1)} %get-tuple-element.23), channel_id=1, source_target_pairs={{0,8},{8,16},{16,24},{1,9},{9,17},{17,25},{2,10},{10,18},{18,26},{... | collective-permute-start | bytes 651272 | tf_op jit(solution)/shard_map/ppermute | solution.py:33
  6.8 0.0 copy-start.1
  6.8 0.0 copy-start.2
  6.9 0.0 copy-start.3
  6.9 0.0 copy-start.4
  6.9 0.0 copy-start.6
  6.9 0.0 copy-start.9
  6.9 0.0 copy-start.11
  6.9 0.0 copy-start.18
  6.9 3.5 %collective-permute-start.1 = (f32[32,256]{1,0:T(8,128)S(1)}, f32[32,256]{1,0:T(8,128)S(1)}, u32[]{:S(2)}, u32[]{:S(2)}) collective-permute-start(f32[32,256]{1,0:T(8,128)S(1)} %get-tuple-element.22.u_first), channel_id=1, source_target_pairs={{8,0},{16,8},{24,16},{9,1},{17,9},{25,17},{10,2},{18,10},{26,18},{... | collective-permute-start | bytes 98312 | tf_op jit(solution)/shard_map/ppermute | solution.py:33
  10.4 3.4 %residual.1 = (f32[29,32,256]{2,1,0:T(8,128)S(1)}, f32[32,256]{1,0:T(8,128)S(1)}) custom-call(f32[28,6272]{1,0:T(8,128)} %guess.1, f32[28,6272]{1,0:T(8,128)} %load_hbm.3, f32[352,256]{1,0:T(8,128)} %constant.46.clone.table_hbm, bf16[32,96]{1,0:T(8,128)(2,1)} %constant.47.clone.k_x_hbm), custom_call_target="tpu_custom_call" | custom-call | tf_op jit(solution)/shard_map/residual/pallas_call | solution.py:951
  13.8 0.0 collective-permute-done.1.above
  13.8 0.0 collective-permute-done.below
  13.8 0.0 copy-done.13
  13.8 0.0 copy-done.14
  13.8 0.5 joined_x.1
  14.3 1.9 %collective-permute-start.2 = (f32[40,1664]{1,0:T(8,128)S(1)}, f32[40,1664]{1,0:T(8,128)S(1)}, u32[]{:S(2)}, u32[]{:S(2)}) collective-permute-start(f32[40,1664]{1,0:T(8,128)S(1)} %get-tuple-element.26), channel_id=1, source_target_pairs={{0,1},{1,2},{2,3},{3,4},{4,5},{5,6},{6,7},{8,9},{9,10},{10,11},{11... | collective-permute-start | bytes 798728 | tf_op jit(solution)/shard_map/ppermute | solution.py:33
  16.3 3.8 %collective-permute-start.3 = (f32[40,256]{1,0:T(8,128)S(1)}, f32[40,256]{1,0:T(8,128)S(1)}, u32[]{:S(2)}, u32[]{:S(2)}) collective-permute-start(f32[40,256]{1,0:T(8,128)S(1)} %get-tuple-element.25.line), channel_id=1, source_target_pairs={{1,0},{2,1},{3,2},{4,3},{5,4},{6,5},{7,6},{9,8},{10,9},{11,10},{12... | collective-permute-start | bytes 122888 | tf_op jit(solution)/shard_map/ppermute | solution.py:33
  20.1 0.0 copy-done.1
  20.1 0.0 copy-done.2
  20.1 0.0 copy-done.3
  20.2 0.0 copy-start.5
  20.2 0.0 copy-start.8
  20.2 0.0 copy-start.10
  20.2 0.0 copy-start.12
  20.2 0.0 copy-start.15
  20.2 0.0 copy-start.16
  20.2 0.0 copy-start.17
  20.2 4.2 %inner.1 = f32[13,2,40,256]{3,2,1,0:T(8,128)S(1)} custom-call(f32[29,40,256]{2,1,0:T(8,128)S(1)} %get-tuple-element.24.r_own, f32[13]{0:T(128)S(1)} %copy-done.18, f32[56,256]{1,0:T(8,128)S(1)} %copy-done.6, bf16[56,120]{1,0:T(8,128)(2,1)S(1)} %copy-done.11, bf16[40,168]{1,0:T(8,128)(2,1)S(1)} %copy-done.9, bf16[256,256]{1,0:T(8,128)(2,1)S(1)} %copy-done.2, ...), custom_call_target="tpu_custom_call" | custom-call | tf_op jit(solution)/shard_map/inner/pallas_call | solution.py:951
  24.5 0.0 copy-start.7
  24.5 0.0 collective-permute-done.3.above
  24.5 0.0 collective-permute-done.2.below
  24.6 0.0 copy-start
  24.6 7.6 %patches.1 = (f32[28,8,256]{2,1,0:T(8,128)S(1)}, f32[28,32,256]{2,1,0:T(8,128)S(1)}, f32[16,16,128]{2,1,0:T(8,128)S(1)}, f32[6,8,128]{2,1,0:T(8,128)S(1)}, f32[4...) custom-call(f32[29,40,256]{2,1,0:T(8,128)S(1)} %get-tuple-element.24.r_own, f32[40,256]{1,0:T(8,128)S(1)} %get-tuple-element.25.line, ...), custom_call_target="tpu_custom_call" | custom-call | tf_op jit(solution)/shard_map/patches/pallas_call | solution.py:951
  32.2 1.9 %collective-permute-start.4 = (f32[40,1792]{1,0:T(8,128)S(1)}, f32[40,1792]{1,0:T(8,128)S(1)}, u32[]{:S(2)}, u32[]{:S(2)}) collective-permute-start(f32[40,1792]{1,0:T(8,128)S(1)} %get-tuple-element.28), channel_id=1, source_target_pairs={{1,0},{2,1},{3,2},{4,3},{5,4},{6,5},{7,6},{9,8},{10,9},{11,10},{12... | collective-permute-start | bytes 860168 | tf_op jit(solution)/shard_map/ppermute | solution.py:33
  34.1 2.4 %collective-permute-start.5 = (f32[16,512]{1,0:T(8,128)S(1)}, f32[16,512]{1,0:T(8,128)S(1)}, u32[]{:S(2)}, u32[]{:S(2)}) collective-permute-start(f32[16,512]{1,0:T(8,128)S(1)} %get-tuple-element.32), channel_id=1, source_target_pairs={{0,1},{1,2},{2,3},{3,4},{4,5},{5,6},{6,7},{8,9},{9,10},{10,11},{11... | collective-permute-start | bytes 98312 | tf_op jit(solution)/shard_map/ppermute | solution.py:33
  36.5 2.8 %collective-permute-done.5.up = f32[16,512]{1,0:T(8,128)S(1)} collective-permute-done((f32[16,512]{1,0:T(8,128)S(1)}, f32[16,512]{1,0:T(8,128)S(1)}, u32[]{:S(2)}, u32[]{:S(2)}) %collective-permute-start.5) | collective-permute-done | bytes 32800 | tf_op jit(solution)/shard_map/ppermute | solution.py:33
  39.4 0.0 collective-permute-done.4.down
  39.4 0.1 join.1
  39.4 3.6 %collective-permute-start.6 = (f32[192,256]{1,0:T(8,128)S(1)}, f32[192,256]{1,0:T(8,128)S(1)}, u32[]{:S(2)}, u32[]{:S(2)}) collective-permute-start(f32[192,256]{1,0:T(8,128)S(1)} %get-tuple-element.33), channel_id=1, source_target_pairs={{8,0},{16,8},{24,16},{9,1},{17,9},{25,17},{10,2},{18,10},{26,18},{... | collective-permute-start | bytes 589832 | tf_op jit(solution)/shard_map/ppermute | solution.py:33
  43.0 2.3 %collective-permute-start.7 = (f32[24,256]{1,0:T(8,128)S(1)}, f32[24,256]{1,0:T(8,128)S(1)}, u32[]{:S(2)}, u32[]{:S(2)}) collective-permute-start(f32[24,256]{1,0:T(8,128)S(1)} %get-tuple-element.34), channel_id=1, source_target_pairs={{0,8},{8,16},{16,24},{1,9},{9,17},{17,25},{2,10},{10,18},{18,26},{... | collective-permute-start | bytes 73736 | tf_op jit(solution)/shard_map/ppermute | solution.py:33
  45.3 2.5 %base.1 = f32[28,6272]{1,0:T(8,128)S(1)} custom-call(f32[28,6272]{1,0:T(8,128)S(1)} %copy-done, f32[28,256]{1,0:T(8,128)S(1)} %copy-done.7, f32[28,32,256]{2,1,0:T(8,128)S(1)} %get-tuple-element.27.own, f32[40,1792]{1,0:T(8,128)S(1)} %collective-permute-done.4.down), custom_call_target="tpu_custom_call" | custom-call | tf_op jit(solution)/shard_map/base/pallas_call | solution.py:951
  47.8 1.8 %collective-permute-done.7.left = f32[24,256]{1,0:T(8,128)S(1)} collective-permute-done((f32[24,256]{1,0:T(8,128)S(1)}, f32[24,256]{1,0:T(8,128)S(1)}, u32[]{:S(2)}, u32[]{:S(2)}) %collective-permute-start.7) | collective-permute-done | bytes 24608 | tf_op jit(solution)/shard_map/ppermute | solution.py:33
  49.6 0.0 collective-permute-done.6.right
  49.6 1.8 %finish.1 = (f32[28,6272]{1,0:T(8,128)}, f32[12,1152]{1,0:T(8,128)}, f32[4,128]{1,0:T(4,128)}) custom-call(f32[28,6272]{1,0:T(8,128)S(1)} %base.1, f32[28,256]{1,0:T(8,128)S(1)} %copy-done.7, f32[192,256]{1,0:T(8,128)S(1)} %collective-permute-done.6.right, f32[24,256]{1,0:T(8,128)S(1)} %collective-permute-done.7.left, ...), custom_call_target="tpu_custom_call" | custom-call | tf_op jit(solution)/shard_map/finish/pallas_call | solution.py:951
  (14 shorter events, 0.0 us)
Async XLA Ops:
  3.3 10.6 %copy-start.13 = (f32[40,256]{1,0:T(8,128)S(1)}, f32[40,256]{1,0:T(8,128)}, u32[]{:S(2)}) copy-start(f32[40,256]{1,0:T(8,128)} %constant.49.clone.c_above) | copy-start | bytes 122884
  3.3 10.6 %copy-start.14 = (f32[40,256]{1,0:T(8,128)S(1)}, f32[40,256]{1,0:T(8,128)}, u32[]{:S(2)}) copy-start(f32[40,256]{1,0:T(8,128)} %constant.48.clone.c_below) | copy-start | bytes 122884
  3.3 10.5 %collective-permute-start = (f32[8,6784]{1,0:T(8,128)S(1)}, f32[8,6784]{1,0:T(8,128)S(1)}, u32[]{:S(2)}, u32[]{:S(2)}) collective-permute-start(f32[8,6784]{1,0:T(8,128)S(1)} %get-tuple-element.23), channel_id=1, source_target_pairs={{0,8},{8,16},{16,24},{1,9},{9,17},{17,25},{2,10},{10,18},{18,26},{... | collective-permute-start | bytes 651272 | tf_op jit(solution)/shard_map/ppermute | solution.py:33
  6.8 13.3 %copy-start.1 = (bf16[256,256]{1,0:T(8,128)(2,1)S(1)}, bf16[256,256]{1,0:T(8,128)(2,1)}, u32[]{:S(2)}) copy-start(bf16[256,256]{1,0:T(8,128)(2,1)} %constant.56.clone.b_z) | copy-start | bytes 393220
  6.8 13.2 %copy-start.2 = (bf16[256,256]{1,0:T(8,128)(2,1)S(1)}, bf16[256,256]{1,0:T(8,128)(2,1)}, u32[]{:S(2)}) copy-start(bf16[256,256]{1,0:T(8,128)(2,1)} %constant.54.clone.f_z) | copy-start | bytes 393220
  6.9 13.2 %copy-start.3 = (bf16[256,128]{1,0:T(8,128)(2,1)S(1)}, bf16[256,128]{1,0:T(8,128)(2,1)}, u32[]{:S(2)}) copy-start(bf16[256,128]{1,0:T(8,128)(2,1)} %constant.57.clone.b_z_high) | copy-start | bytes 196612
  6.9 13.2 %copy-start.4 = (bf16[128,256]{1,0:T(8,128)(2,1)S(1)}, bf16[128,256]{1,0:T(8,128)(2,1)}, u32[]{:S(2)}) copy-start(bf16[128,256]{1,0:T(8,128)(2,1)} %constant.55.clone.f_z_low) | copy-start | bytes 196612
  6.9 13.2 %copy-start.6 = (f32[56,256]{1,0:T(8,128)S(1)}, f32[56,256]{1,0:T(8,128)}, u32[]{:S(2)}) copy-start(f32[56,256]{1,0:T(8,128)} %constant.51.clone.sums) | copy-start | bytes 172036
  6.9 13.2 %copy-start.9 = (bf16[40,168]{1,0:T(8,128)(2,1)S(1)}, bf16[40,168]{1,0:T(8,128)(2,1)}, u32[]{:S(2)}) copy-start(bf16[40,168]{1,0:T(8,128)(2,1)} %constant.53.clone.b_x) | copy-start | bytes 40324
  6.9 13.2 %copy-start.11 = (bf16[56,120]{1,0:T(8,128)(2,1)S(1)}, bf16[56,120]{1,0:T(8,128)(2,1)}, u32[]{:S(2)}) copy-start(bf16[56,120]{1,0:T(8,128)(2,1)} %constant.52.clone.f_x) | copy-start | bytes 40324
  6.9 13.2 %copy-start.18 = (f32[13]{0:T(128)S(1)}, f32[13]{0:T(128)}, u32[]{:S(2)}) copy-start(f32[13]{0:T(128)} %constant.50.clone.lam) | copy-start | bytes 160
  6.9 6.9 %collective-permute-start.1 = (f32[32,256]{1,0:T(8,128)S(1)}, f32[32,256]{1,0:T(8,128)S(1)}, u32[]{:S(2)}, u32[]{:S(2)}) collective-permute-start(f32[32,256]{1,0:T(8,128)S(1)} %get-tuple-element.22.u_first), channel_id=1, source_target_pairs={{8,0},{16,8},{24,16},{9,1},{17,9},{25,17},{10,2},{18,10},{26,18},{... | collective-permute-start | bytes 98312 | tf_op jit(solution)/shard_map/ppermute | solution.py:33
  14.3 10.2 %collective-permute-start.2 = (f32[40,1664]{1,0:T(8,128)S(1)}, f32[40,1664]{1,0:T(8,128)S(1)}, u32[]{:S(2)}, u32[]{:S(2)}) collective-permute-start(f32[40,1664]{1,0:T(8,128)S(1)} %get-tuple-element.26), channel_id=1, source_target_pairs={{0,1},{1,2},{2,3},{3,4},{4,5},{5,6},{6,7},{8,9},{9,10},{10,11},{11... | collective-permute-start | bytes 798728 | tf_op jit(solution)/shard_map/ppermute | solution.py:33
  16.3 8.2 %collective-permute-start.3 = (f32[40,256]{1,0:T(8,128)S(1)}, f32[40,256]{1,0:T(8,128)S(1)}, u32[]{:S(2)}, u32[]{:S(2)}) collective-permute-start(f32[40,256]{1,0:T(8,128)S(1)} %get-tuple-element.25.line), channel_id=1, source_target_pairs={{1,0},{2,1},{3,2},{4,3},{5,4},{6,5},{7,6},{9,8},{10,9},{11,10},{12... | collective-permute-start | bytes 122888 | tf_op jit(solution)/shard_map/ppermute | solution.py:33
  20.2 4.3 %copy-start.5 = (f32[256,256]{1,0:T(8,128)S(1)}, f32[256,256]{1,0:T(8,128)}, u32[]{:S(2)}) copy-start(f32[256,256]{1,0:T(8,128)} %constant.59.clone.q_z) | copy-start | bytes 786436
  20.2 4.3 %copy-start.8 = (f32[256,128]{1,0:T(8,128)S(1)}, f32[256,128]{1,0:T(8,128)}, u32[]{:S(2)}) copy-start(f32[256,128]{1,0:T(8,128)} %constant.60.clone.r_z) | copy-start | bytes 393220
  20.2 4.3 %copy-start.10 = (f32[128,128]{1,0:T(8,128)S(1)}, f32[128,128]{1,0:T(8,128)}, u32[]{:S(2)}) copy-start(f32[128,128]{1,0:T(8,128)} %constant.61.clone.o_z) | copy-start | bytes 196612
  20.2 4.3 %copy-start.12 = (f32[40,256]{1,0:T(8,128)S(1)}, f32[40,256]{1,0:T(8,128)}, u32[]{:S(2)}) copy-start(f32[40,256]{1,0:T(8,128)} %constant.58.clone.m_xz) | copy-start | bytes 122884
  20.2 4.3 %copy-start.15 = (bf16[32,120]{1,0:T(8,128)(2,1)S(1)}, bf16[32,120]{1,0:T(8,128)(2,1)}, u32[]{:S(2)}) copy-start(bf16[32,120]{1,0:T(8,128)(2,1)} %constant.63.clone.q_x) | copy-start | bytes 23044
  20.2 4.3 %copy-start.16 = (bf16[16,120]{1,0:T(8,128)(2,1)S(1)}, bf16[16,120]{1,0:T(8,128)(2,1)}, u32[]{:S(2)}) copy-start(bf16[16,120]{1,0:T(8,128)(2,1)} %constant.64.clone.r_x) | copy-start | bytes 11524
  20.2 4.3 %copy-start.17 = (f32[8,16]{1,0:T(8,128)S(1)}, f32[8,16]{1,0:T(8,128)}, u32[]{:S(2)}) copy-start(f32[8,16]{1,0:T(8,128)} %constant.62.clone.o_x) | copy-start | bytes 1540
  24.5 20.8 %copy-start.7 = (f32[28,256]{1,0:T(8,128)S(1)}, f32[28,256]{1,0:T(8,128)}, u32[]{:S(2)}) copy-start(f32[28,256]{1,0:T(8,128)} %constant.65.clone.weight) | copy-start | bytes 86020
  24.6 20.7 %copy-start = (f32[28,6272]{1,0:T(8,128)S(1)}, f32[28,6272]{1,0:T(8,128)}, u32[]{:S(2)}) copy-start(f32[28,6272]{1,0:T(8,128)} %guess.1) | copy-start | bytes 2107396
  32.2 7.2 %collective-permute-start.4 = (f32[40,1792]{1,0:T(8,128)S(1)}, f32[40,1792]{1,0:T(8,128)S(1)}, u32[]{:S(2)}, u32[]{:S(2)}) collective-permute-start(f32[40,1792]{1,0:T(8,128)S(1)} %get-tuple-element.28), channel_id=1, source_target_pairs={{1,0},{2,1},{3,2},{4,3},{5,4},{6,5},{7,6},{9,8},{10,9},{11,10},{12... | collective-permute-start | bytes 860168 | tf_op jit(solution)/shard_map/ppermute | solution.py:33
  34.1 5.2 %collective-permute-start.5 = (f32[16,512]{1,0:T(8,128)S(1)}, f32[16,512]{1,0:T(8,128)S(1)}, u32[]{:S(2)}, u32[]{:S(2)}) collective-permute-start(f32[16,512]{1,0:T(8,128)S(1)} %get-tuple-element.32), channel_id=1, source_target_pairs={{0,1},{1,2},{2,3},{3,4},{4,5},{5,6},{6,7},{8,9},{9,10},{10,11},{11... | collective-permute-start | bytes 98312 | tf_op jit(solution)/shard_map/ppermute | solution.py:33
  39.4 10.2 %collective-permute-start.6 = (f32[192,256]{1,0:T(8,128)S(1)}, f32[192,256]{1,0:T(8,128)S(1)}, u32[]{:S(2)}, u32[]{:S(2)}) collective-permute-start(f32[192,256]{1,0:T(8,128)S(1)} %get-tuple-element.33), channel_id=1, source_target_pairs={{8,0},{16,8},{24,16},{9,1},{17,9},{25,17},{10,2},{18,10},{26,18},{... | collective-permute-start | bytes 589832 | tf_op jit(solution)/shard_map/ppermute | solution.py:33
  43.0 6.6 %collective-permute-start.7 = (f32[24,256]{1,0:T(8,128)S(1)}, f32[24,256]{1,0:T(8,128)S(1)}, u32[]{:S(2)}, u32[]{:S(2)}) collective-permute-start(f32[24,256]{1,0:T(8,128)S(1)} %get-tuple-element.34), channel_id=1, source_target_pairs={{0,8},{8,16},{16,24},{1,9},{9,17},{17,25},{2,10},{10,18},{18,26},{... | collective-permute-start | bytes 73736 | tf_op jit(solution)/shard_map/ppermute | solution.py:33

commit v7 on v6

--- a/solution.py
+++ b/solution.py
@@ -146,6 +146,7 @@
 
 
 high = lax.Precision.HIGH
+highest = lax.Precision.HIGHEST
 LANES = 128
 GROUP = 13
 f32 = jnp.float32
@@ -161,9 +162,9 @@
     return result
 
 
-def mm(left, right):
+def mm(left, right, precision=high):
     return lax.dot_general(
-        left, right, (((1,), (0,)), ((), ())), precision=high, preferred_element_type=f32
+        left, right, (((1,), (0,)), ((), ())), precision=precision, preferred_element_type=f32
     )
 
 
@@ -213,9 +214,9 @@
     return np.where(used[:, None], matrix[np.maximum(s.node_of_lane, 0)], 0.0)
 
 
-def two_parts(matrix):
+def two_parts(matrix, low_type=jnp.bfloat16):
     high_part = matrix.astype(np.float32).astype(jnp.bfloat16)
-    low_part = (matrix - high_part.astype(np.float64)).astype(jnp.bfloat16)
+    low_part = (matrix - high_part.astype(np.float64)).astype(low_type)
     return high_part, low_part
 
 
@@ -232,7 +233,8 @@
     stiff = rows_by_node(s, stiff_z, False)
     stiff = rows_by_node(s, stiff.T, True).T
     own_x = placed(line_x["own_stiff"], (s.own_rows, s.own_rows)).astype(np.float64)
-    high_x, low_x = two_parts(own_x[low:, low:])
+    high_x, rest = two_parts(own_x[low:, low:], np.float64)
+    mid_x, low_x = two_parts(rest)
     table = np.concatenate(
         [
             stiff,
@@ -243,7 +245,9 @@
     )
     return [
         jnp.asarray(table, f32),
-        jnp.asarray(np.concatenate([high_x, high_x, low_x], 1), jnp.bfloat16),
+        jnp.asarray(
+            np.concatenate([high_x, high_x, high_x, mid_x, mid_x, low_x], 1), jnp.bfloat16
+        ),
     ]
 
 
@@ -329,6 +333,15 @@
 def halves_of(value):
     high_part = value.astype(jnp.bfloat16)
     return high_part, (value - high_part.astype(f32)).astype(jnp.bfloat16)
+
+
+def stacked_whole(value):
+    high_part = value.astype(jnp.bfloat16).astype(f32)
+    rest = value - high_part
+    mid_part = rest.astype(jnp.bfloat16).astype(f32)
+    return jnp.concatenate(
+        [high_part, mid_part, rest - mid_part, high_part, mid_part, high_part], 0
+    ).astype(jnp.bfloat16)
 
 
 def stacked_rows(value):
@@ -430,9 +443,10 @@
     m_x, m_z, m_xz = [
         table.at[lanes + rows * i : lanes + rows * (i + 1)] for i in range(3)
     ]
-    z_term = mm(u[0:ny].reshape(ny * rows, lanes), table[0:lanes]).reshape(ny, rows, lanes)
+    planes = u[0:ny].reshape(ny * rows, lanes)
+    z_term = mm(planes, table[0:lanes], highest).reshape(ny, rows, lanes)
     for y in range(ny):
-        x_term = dot(k_x[...], stacked_rows(u[y]))
+        x_term = dot(k_x[...], stacked_whole(u[y]))
         both = x_term * m_z[...] + z_term[y] * m_x[...]
         r[y] = r[y] - float(mass_y[y]) * both
 
@@ -718,8 +732,12 @@
             plane = dot(q_x[...], stacked_rows(cz[y]))
             hx[y] = plane[:rows_c, :half]
             ex[y] = plane[rows_c:, :half] + plane[:rows_c, half:]
-        for y in range(ny):
-            rx[y] = dot(r_x[...], stacked_rows(rz[y]))
+        for y in range(0, ny - 1, 2):
+            pair = jnp.concatenate([rz[y], rz[y + 1]], 1)
+            pair = dot(r_x[...], stacked_rows(pair))
+            rx[y], rx[y + 1] = (pair[:, :half], pair[:, half:])
+        if ny % 2:
+            rx[ny - 1] = dot(r_x[...], stacked_rows(rz[ny - 1]))
         for j in range(s.coarse_y):
             three_out[j] = line_of_planes(
                 np.concatenate(

time: 52.4 us -> 52.6 us (level)
  Pallas kernels: 22.6 us -> 23.4 us
  waiting for transfers between devices: 4.64 us -> 4.09 us
    pallas_call x8, Pallas kernels: 22.6 us -> 23.4 us  [call(): pl.pallas_call(kernel, out_shape=tuple((shape(*dims) for dims in outputs)...]
    ppermute x8, waiting for transfers between devices: 4.64 us -> 4.09 us  [shifted(): return lax.ppermute(array, axis, pairs)]
  transfers between devices with their start and end apart: 8 -> 8, of which waited for: 2 -> 2; matrix products, arithmetic and copies ran while one was open for 0% -> 0% of each run, Pallas kernels for 20% -> 21%
where the time goes in v7:
time: 52.6 us; the launch traced here: 51.6 us
  Pallas kernels  23.4 us (44%)
  starting transfers between devices  22.9 us (44%)
  waiting for transfers between devices  4.09 us (8%)
  between operations  1.06 us (2%)
    pallas_call x8, Pallas kernels, call(): pl.pallas_call(kernel, out_shape=tuple((shape(*dims) for dims in outputs)...  23.4 us
    ppermute x8, starting transfers between devices, shifted(): return lax.ppermute(array, axis, pairs)  22.9 us
    ppermute x8, waiting for transfers between devices, shifted(): return lax.ppermute(array, axis, pairs)  4.09 us
  transfers between devices with their start and end apart: 8, of which 2 were waited for; matrix products, arithmetic and copies ran while one was open for 0% of the time, Pallas kernels for 21%

profile of v7, /device:TPU:20, one launch (start us, length us, event | category | flops | bytes accessed | tf_op | source)
XLA Modules:
  0.0 51.6 jit_solution(18055133049678803302)
XLA Ops:
  0.6 2.9 %send.1 = (f32[8,6784]{1,0:T(8,128)S(1)}, f32[32,256]{1,0:T(8,128)S(1)}) custom-call(f32[28,6272]{1,0:T(8,128)} %guess.1, f32[28,6272]{1,0:T(8,128)} %load_hbm.3, f32[304,256]{1,0:T(8,128)} %constant.44.clone.table_hbm, bf16[16,96]{1,0:T(8,128)(2,1)} %constant.45.clone.k_x_hbm), custom_call_target="tpu_custom_call" | custom-call | tf_op jit(solution)/shard_map/send/pallas_call | solution.py:969
  3.5 0.0 copy-start.13
  3.6 0.0 copy-start.14
  3.6 3.5 %collective-permute-start = (f32[8,6784]{1,0:T(8,128)S(1)}, f32[8,6784]{1,0:T(8,128)S(1)}, u32[]{:S(2)}, u32[]{:S(2)}) collective-permute-start(f32[8,6784]{1,0:T(8,128)S(1)} %get-tuple-element.23), channel_id=1, source_target_pairs={{0,8},{8,16},{16,24},{1,9},{9,17},{17,25},{2,10},{10,18},{18,26},{... | collective-permute-start | bytes 651272 | tf_op jit(solution)/shard_map/ppermute | solution.py:33
  7.1 0.0 copy-start.1
  7.1 0.0 copy-start.2
  7.1 0.0 copy-start.3
  7.1 0.0 copy-start.4
  7.2 0.0 copy-start.6
  7.2 0.0 copy-start.9
  7.2 0.0 copy-start.11
  7.2 0.0 copy-start.18
  7.2 3.5 %collective-permute-start.1 = (f32[32,256]{1,0:T(8,128)S(1)}, f32[32,256]{1,0:T(8,128)S(1)}, u32[]{:S(2)}, u32[]{:S(2)}) collective-permute-start(f32[32,256]{1,0:T(8,128)S(1)} %get-tuple-element.22.u_first), channel_id=1, source_target_pairs={{8,0},{16,8},{24,16},{9,1},{17,9},{25,17},{10,2},{18,10},{26,18},{... | collective-permute-start | bytes 98312 | tf_op jit(solution)/shard_map/ppermute | solution.py:33
  10.7 3.9 %residual.1 = (f32[29,32,256]{2,1,0:T(8,128)S(1)}, f32[32,256]{1,0:T(8,128)S(1)}) custom-call(f32[28,6272]{1,0:T(8,128)} %guess.1, f32[28,6272]{1,0:T(8,128)} %load_hbm.3, f32[352,256]{1,0:T(8,128)} %constant.46.clone.table_hbm, bf16[32,192]{1,0:T(8,128)(2,1)} %constant.47.clone.k_x_hbm), custom_call_target="tpu_custom_call" | custom-call | tf_op jit(solution)/shard_map/residual/pallas_call | solution.py:969
  14.6 0.0 collective-permute-done.1.above
  14.6 0.0 collective-permute-done.below
  14.6 0.0 copy-done.13
  14.6 0.0 copy-done.14
  14.7 0.5 joined_x.1
  15.1 1.9 %collective-permute-start.2 = (f32[40,1664]{1,0:T(8,128)S(1)}, f32[40,1664]{1,0:T(8,128)S(1)}, u32[]{:S(2)}, u32[]{:S(2)}) collective-permute-start(f32[40,1664]{1,0:T(8,128)S(1)} %get-tuple-element.26), channel_id=1, source_target_pairs={{0,1},{1,2},{2,3},{3,4},{4,5},{5,6},{6,7},{8,9},{9,10},{10,11},{11... | collective-permute-start | bytes 798728 | tf_op jit(solution)/shard_map/ppermute | solution.py:33
  17.1 3.8 %collective-permute-start.3 = (f32[40,256]{1,0:T(8,128)S(1)}, f32[40,256]{1,0:T(8,128)S(1)}, u32[]{:S(2)}, u32[]{:S(2)}) collective-permute-start(f32[40,256]{1,0:T(8,128)S(1)} %get-tuple-element.25.line), channel_id=1, source_target_pairs={{1,0},{2,1},{3,2},{4,3},{5,4},{6,5},{7,6},{9,8},{10,9},{11,10},{12... | collective-permute-start | bytes 122888 | tf_op jit(solution)/shard_map/ppermute | solution.py:33
  20.9 0.0 copy-done.1
  20.9 0.0 copy-done.2
  20.9 0.0 copy-done.3
  21.0 0.0 copy-start.5
  21.0 0.0 copy-start.8
  21.0 0.0 copy-start.10
  21.0 0.0 copy-start.12
  21.0 0.0 copy-start.15
  21.0 0.0 copy-start.16
  21.1 0.0 copy-start.17
  21.1 4.2 %inner.1 = f32[13,2,40,256]{3,2,1,0:T(8,128)S(1)} custom-call(f32[29,40,256]{2,1,0:T(8,128)S(1)} %get-tuple-element.24.r_own, f32[13]{0:T(128)S(1)} %copy-done.18, f32[56,256]{1,0:T(8,128)S(1)} %copy-done.6, bf16[56,120]{1,0:T(8,128)(2,1)S(1)} %copy-done.11, bf16[40,168]{1,0:T(8,128)(2,1)S(1)} %copy-done.9, bf16[256,256]{1,0:T(8,128)(2,1)S(1)} %copy-done.2, ...), custom_call_target="tpu_custom_call" | custom-call | tf_op jit(solution)/shard_map/inner/pallas_call | solution.py:969
  25.3 0.0 copy-start.7
  25.3 0.0 collective-permute-done.3.above
  25.3 0.0 collective-permute-done.2.below
  25.4 0.0 copy-start
  25.4 7.5 %patches.1 = (f32[28,8,256]{2,1,0:T(8,128)S(1)}, f32[28,32,256]{2,1,0:T(8,128)S(1)}, f32[16,16,128]{2,1,0:T(8,128)S(1)}, f32[6,8,128]{2,1,0:T(8,128)S(1)}, f32[4...) custom-call(f32[29,40,256]{2,1,0:T(8,128)S(1)} %get-tuple-element.24.r_own, f32[40,256]{1,0:T(8,128)S(1)} %get-tuple-element.25.line, ...), custom_call_target="tpu_custom_call" | custom-call | tf_op jit(solution)/shard_map/patches/pallas_call | solution.py:969
  32.9 1.9 %collective-permute-start.4 = (f32[40,1792]{1,0:T(8,128)S(1)}, f32[40,1792]{1,0:T(8,128)S(1)}, u32[]{:S(2)}, u32[]{:S(2)}) collective-permute-start(f32[40,1792]{1,0:T(8,128)S(1)} %get-tuple-element.28), channel_id=1, source_target_pairs={{1,0},{2,1},{3,2},{4,3},{5,4},{6,5},{7,6},{9,8},{10,9},{11,10},{12... | collective-permute-start | bytes 860168 | tf_op jit(solution)/shard_map/ppermute | solution.py:33
  34.9 2.4 %collective-permute-start.5 = (f32[16,512]{1,0:T(8,128)S(1)}, f32[16,512]{1,0:T(8,128)S(1)}, u32[]{:S(2)}, u32[]{:S(2)}) collective-permute-start(f32[16,512]{1,0:T(8,128)S(1)} %get-tuple-element.32), channel_id=1, source_target_pairs={{0,1},{1,2},{2,3},{3,4},{4,5},{5,6},{6,7},{8,9},{9,10},{10,11},{11... | collective-permute-start | bytes 98312 | tf_op jit(solution)/shard_map/ppermute | solution.py:33
  37.3 2.8 %collective-permute-done.5.up = f32[16,512]{1,0:T(8,128)S(1)} collective-permute-done((f32[16,512]{1,0:T(8,128)S(1)}, f32[16,512]{1,0:T(8,128)S(1)}, u32[]{:S(2)}, u32[]{:S(2)}) %collective-permute-start.5) | collective-permute-done | bytes 32800 | tf_op jit(solution)/shard_map/ppermute | solution.py:33
  40.1 0.0 collective-permute-done.4.down
  40.1 0.1 join.1
  40.2 3.0 %collective-permute-start.6 = (f32[192,256]{1,0:T(8,128)S(1)}, f32[192,256]{1,0:T(8,128)S(1)}, u32[]{:S(2)}, u32[]{:S(2)}) collective-permute-start(f32[192,256]{1,0:T(8,128)S(1)} %get-tuple-element.33), channel_id=1, source_target_pairs={{8,0},{16,8},{24,16},{9,1},{17,9},{25,17},{10,2},{18,10},{26,18},{... | collective-permute-start | bytes 589832 | tf_op jit(solution)/shard_map/ppermute | solution.py:33
  43.2 2.8 %collective-permute-start.7 = (f32[24,256]{1,0:T(8,128)S(1)}, f32[24,256]{1,0:T(8,128)S(1)}, u32[]{:S(2)}, u32[]{:S(2)}) collective-permute-start(f32[24,256]{1,0:T(8,128)S(1)} %get-tuple-element.34), channel_id=1, source_target_pairs={{0,8},{8,16},{16,24},{1,9},{9,17},{17,25},{2,10},{10,18},{18,26},{... | collective-permute-start | bytes 73736 | tf_op jit(solution)/shard_map/ppermute | solution.py:33
  46.1 2.5 %base.1 = f32[28,6272]{1,0:T(8,128)S(1)} custom-call(f32[28,6272]{1,0:T(8,128)S(1)} %copy-done, f32[28,256]{1,0:T(8,128)S(1)} %copy-done.7, f32[28,32,256]{2,1,0:T(8,128)S(1)} %get-tuple-element.27.own, f32[40,1792]{1,0:T(8,128)S(1)} %collective-permute-done.4.down), custom_call_target="tpu_custom_call" | custom-call | tf_op jit(solution)/shard_map/base/pallas_call | solution.py:969
  48.6 1.3 %collective-permute-done.7.left = f32[24,256]{1,0:T(8,128)S(1)} collective-permute-done((f32[24,256]{1,0:T(8,128)S(1)}, f32[24,256]{1,0:T(8,128)S(1)}, u32[]{:S(2)}, u32[]{:S(2)}) %collective-permute-start.7) | collective-permute-done | bytes 24608 | tf_op jit(solution)/shard_map/ppermute | solution.py:33
  49.8 0.0 collective-permute-done.6.right
  49.8 1.8 %finish.1 = (f32[28,6272]{1,0:T(8,128)}, f32[12,1152]{1,0:T(8,128)}, f32[4,128]{1,0:T(4,128)}) custom-call(f32[28,6272]{1,0:T(8,128)S(1)} %base.1, f32[28,256]{1,0:T(8,128)S(1)} %copy-done.7, f32[192,256]{1,0:T(8,128)S(1)} %collective-permute-done.6.right, f32[24,256]{1,0:T(8,128)S(1)} %collective-permute-done.7.left, ...), custom_call_target="tpu_custom_call" | custom-call | tf_op jit(solution)/shard_map/finish/pallas_call | solution.py:969
  (14 shorter events, 0.0 us)
Async XLA Ops:
  3.5 11.1 %copy-start.13 = (f32[40,256]{1,0:T(8,128)S(1)}, f32[40,256]{1,0:T(8,128)}, u32[]{:S(2)}) copy-start(f32[40,256]{1,0:T(8,128)} %constant.49.clone.c_above) | copy-start | bytes 122884
  3.6 11.1 %copy-start.14 = (f32[40,256]{1,0:T(8,128)S(1)}, f32[40,256]{1,0:T(8,128)}, u32[]{:S(2)}) copy-start(f32[40,256]{1,0:T(8,128)} %constant.48.clone.c_below) | copy-start | bytes 122884
  3.6 11.1 %collective-permute-start = (f32[8,6784]{1,0:T(8,128)S(1)}, f32[8,6784]{1,0:T(8,128)S(1)}, u32[]{:S(2)}, u32[]{:S(2)}) collective-permute-start(f32[8,6784]{1,0:T(8,128)S(1)} %get-tuple-element.23), channel_id=1, source_target_pairs={{0,8},{8,16},{16,24},{1,9},{9,17},{17,25},{2,10},{10,18},{18,26},{... | collective-permute-start | bytes 651272 | tf_op jit(solution)/shard_map/ppermute | solution.py:33
  7.1 13.8 %copy-start.1 = (bf16[256,256]{1,0:T(8,128)(2,1)S(1)}, bf16[256,256]{1,0:T(8,128)(2,1)}, u32[]{:S(2)}) copy-start(bf16[256,256]{1,0:T(8,128)(2,1)} %constant.56.clone.b_z) | copy-start | bytes 393220
  7.1 13.8 %copy-start.2 = (bf16[256,256]{1,0:T(8,128)(2,1)S(1)}, bf16[256,256]{1,0:T(8,128)(2,1)}, u32[]{:S(2)}) copy-start(bf16[256,256]{1,0:T(8,128)(2,1)} %constant.54.clone.f_z) | copy-start | bytes 393220
  7.1 13.8 %copy-start.3 = (bf16[256,128]{1,0:T(8,128)(2,1)S(1)}, bf16[256,128]{1,0:T(8,128)(2,1)}, u32[]{:S(2)}) copy-start(bf16[256,128]{1,0:T(8,128)(2,1)} %constant.57.clone.b_z_high) | copy-start | bytes 196612
  7.1 13.8 %copy-start.4 = (bf16[128,256]{1,0:T(8,128)(2,1)S(1)}, bf16[128,256]{1,0:T(8,128)(2,1)}, u32[]{:S(2)}) copy-start(bf16[128,256]{1,0:T(8,128)(2,1)} %constant.55.clone.f_z_low) | copy-start | bytes 196612
  7.2 13.8 %copy-start.6 = (f32[56,256]{1,0:T(8,128)S(1)}, f32[56,256]{1,0:T(8,128)}, u32[]{:S(2)}) copy-start(f32[56,256]{1,0:T(8,128)} %constant.51.clone.sums) | copy-start | bytes 172036
  7.2 13.8 %copy-start.9 = (bf16[40,168]{1,0:T(8,128)(2,1)S(1)}, bf16[40,168]{1,0:T(8,128)(2,1)}, u32[]{:S(2)}) copy-start(bf16[40,168]{1,0:T(8,128)(2,1)} %constant.53.clone.b_x) | copy-start | bytes 40324
  7.2 13.8 %copy-start.11 = (bf16[56,120]{1,0:T(8,128)(2,1)S(1)}, bf16[56,120]{1,0:T(8,128)(2,1)}, u32[]{:S(2)}) copy-start(bf16[56,120]{1,0:T(8,128)(2,1)} %constant.52.clone.f_x) | copy-start | bytes 40324
  7.2 13.8 %copy-start.18 = (f32[13]{0:T(128)S(1)}, f32[13]{0:T(128)}, u32[]{:S(2)}) copy-start(f32[13]{0:T(128)} %constant.50.clone.lam) | copy-start | bytes 160
  7.2 7.4 %collective-permute-start.1 = (f32[32,256]{1,0:T(8,128)S(1)}, f32[32,256]{1,0:T(8,128)S(1)}, u32[]{:S(2)}, u32[]{:S(2)}) collective-permute-start(f32[32,256]{1,0:T(8,128)S(1)} %get-tuple-element.22.u_first), channel_id=1, source_target_pairs={{8,0},{16,8},{24,16},{9,1},{17,9},{25,17},{10,2},{18,10},{26,18},{... | collective-permute-start | bytes 98312 | tf_op jit(solution)/shard_map/ppermute | solution.py:33
  15.1 10.2 %collective-permute-start.2 = (f32[40,1664]{1,0:T(8,128)S(1)}, f32[40,1664]{1,0:T(8,128)S(1)}, u32[]{:S(2)}, u32[]{:S(2)}) collective-permute-start(f32[40,1664]{1,0:T(8,128)S(1)} %get-tuple-element.26), channel_id=1, source_target_pairs={{0,1},{1,2},{2,3},{3,4},{4,5},{5,6},{6,7},{8,9},{9,10},{10,11},{11... | collective-permute-start | bytes 798728 | tf_op jit(solution)/shard_map/ppermute | solution.py:33
  17.1 8.2 %collective-permute-start.3 = (f32[40,256]{1,0:T(8,128)S(1)}, f32[40,256]{1,0:T(8,128)S(1)}, u32[]{:S(2)}, u32[]{:S(2)}) collective-permute-start(f32[40,256]{1,0:T(8,128)S(1)} %get-tuple-element.25.line), channel_id=1, source_target_pairs={{1,0},{2,1},{3,2},{4,3},{5,4},{6,5},{7,6},{9,8},{10,9},{11,10},{12... | collective-permute-start | bytes 122888 | tf_op jit(solution)/shard_map/ppermute | solution.py:33
  21.0 4.3 %copy-start.5 = (f32[256,256]{1,0:T(8,128)S(1)}, f32[256,256]{1,0:T(8,128)}, u32[]{:S(2)}) copy-start(f32[256,256]{1,0:T(8,128)} %constant.59.clone.q_z) | copy-start | bytes 786436
  21.0 4.3 %copy-start.8 = (f32[256,128]{1,0:T(8,128)S(1)}, f32[256,128]{1,0:T(8,128)}, u32[]{:S(2)}) copy-start(f32[256,128]{1,0:T(8,128)} %constant.60.clone.r_z) | copy-start | bytes 393220
  21.0 4.3 %copy-start.10 = (f32[128,128]{1,0:T(8,128)S(1)}, f32[128,128]{1,0:T(8,128)}, u32[]{:S(2)}) copy-start(f32[128,128]{1,0:T(8,128)} %constant.61.clone.o_z) | copy-start | bytes 196612
  21.0 4.3 %copy-start.12 = (f32[40,256]{1,0:T(8,128)S(1)}, f32[40,256]{1,0:T(8,128)}, u32[]{:S(2)}) copy-start(f32[40,256]{1,0:T(8,128)} %constant.58.clone.m_xz) | copy-start | bytes 122884
  21.0 4.3 %copy-start.15 = (bf16[32,120]{1,0:T(8,128)(2,1)S(1)}, bf16[32,120]{1,0:T(8,128)(2,1)}, u32[]{:S(2)}) copy-start(bf16[32,120]{1,0:T(8,128)(2,1)} %constant.63.clone.q_x) | copy-start | bytes 23044
  21.0 4.3 %copy-start.16 = (bf16[16,120]{1,0:T(8,128)(2,1)S(1)}, bf16[16,120]{1,0:T(8,128)(2,1)}, u32[]{:S(2)}) copy-start(bf16[16,120]{1,0:T(8,128)(2,1)} %constant.64.clone.r_x) | copy-start | bytes 11524
  21.1 4.3 %copy-start.17 = (f32[8,16]{1,0:T(8,128)S(1)}, f32[8,16]{1,0:T(8,128)}, u32[]{:S(2)}) copy-start(f32[8,16]{1,0:T(8,128)} %constant.62.clone.o_x) | copy-start | bytes 1540
  25.3 20.8 %copy-start.7 = (f32[28,256]{1,0:T(8,128)S(1)}, f32[28,256]{1,0:T(8,128)}, u32[]{:S(2)}) copy-start(f32[28,256]{1,0:T(8,128)} %constant.65.clone.weight) | copy-start | bytes 86020
  25.4 20.7 %copy-start = (f32[28,6272]{1,0:T(8,128)S(1)}, f32[28,6272]{1,0:T(8,128)}, u32[]{:S(2)}) copy-start(f32[28,6272]{1,0:T(8,128)} %guess.1) | copy-start | bytes 2107396
  32.9 7.2 %collective-permute-start.4 = (f32[40,1792]{1,0:T(8,128)S(1)}, f32[40,1792]{1,0:T(8,128)S(1)}, u32[]{:S(2)}, u32[]{:S(2)}) collective-permute-start(f32[40,1792]{1,0:T(8,128)S(1)} %get-tuple-element.28), channel_id=1, source_target_pairs={{1,0},{2,1},{3,2},{4,3},{5,4},{6,5},{7,6},{9,8},{10,9},{11,10},{12... | collective-permute-start | bytes 860168 | tf_op jit(solution)/shard_map/ppermute | solution.py:33
  34.9 5.2 %collective-permute-start.5 = (f32[16,512]{1,0:T(8,128)S(1)}, f32[16,512]{1,0:T(8,128)S(1)}, u32[]{:S(2)}, u32[]{:S(2)}) collective-permute-start(f32[16,512]{1,0:T(8,128)S(1)} %get-tuple-element.32), channel_id=1, source_target_pairs={{0,1},{1,2},{2,3},{3,4},{4,5},{5,6},{6,7},{8,9},{9,10},{10,11},{11... | collective-permute-start | bytes 98312 | tf_op jit(solution)/shard_map/ppermute | solution.py:33
  40.2 9.7 %collective-permute-start.6 = (f32[192,256]{1,0:T(8,128)S(1)}, f32[192,256]{1,0:T(8,128)S(1)}, u32[]{:S(2)}, u32[]{:S(2)}) collective-permute-start(f32[192,256]{1,0:T(8,128)S(1)} %get-tuple-element.33), channel_id=1, source_target_pairs={{8,0},{16,8},{24,16},{9,1},{17,9},{25,17},{10,2},{18,10},{26,18},{... | collective-permute-start | bytes 589832 | tf_op jit(solution)/shard_map/ppermute | solution.py:33
  43.2 6.6 %collective-permute-start.7 = (f32[24,256]{1,0:T(8,128)S(1)}, f32[24,256]{1,0:T(8,128)S(1)}, u32[]{:S(2)}, u32[]{:S(2)}) collective-permute-start(f32[24,256]{1,0:T(8,128)S(1)} %get-tuple-element.34), channel_id=1, source_target_pairs={{0,8},{8,16},{16,24},{1,9},{9,17},{17,25},{2,10},{10,18},{18,26},{... | collective-permute-start | bytes 73736 | tf_op jit(solution)/shard_map/ppermute | solution.py:33

commit v8 on v7

--- a/solution.py
+++ b/solution.py
@@ -224,15 +224,15 @@
     line_x = line_tables(s.x_elems)
     stiff_z, lumped_z = assemble_line(s.z_elems)
     stiff_z, lumped_z = (stiff_z[: s.z_nodes, : s.z_nodes], lumped_z[: s.z_nodes])
-    rows = s.own_rows - low
-    mass_x = np.zeros(s.own_rows)
+    rows = up_to(s.x_nodes + 1 - low, 8)
+    mass_x = np.zeros(low + rows)
     mass_x[: s.x_nodes] = line_x["mass"][6:]
     mass_x = mass_x[low:]
     mass_z = rows_by_node(s, lumped_z[:, None], True)[:, 0]
     spread = np.ones((rows, s.lanes))
     stiff = rows_by_node(s, stiff_z, False)
     stiff = rows_by_node(s, stiff.T, True).T
-    own_x = placed(line_x["own_stiff"], (s.own_rows, s.own_rows)).astype(np.float64)
+    own_x = placed(line_x["own_stiff"], (low + rows, low + rows)).astype(np.float64)
     high_x, rest = two_parts(own_x[low:, low:], np.float64)
     mid_x, low_x = two_parts(rest)
     table = np.concatenate(
@@ -411,9 +411,9 @@
     )
 
 
-def own_residual(s, low, first_copies, u, r, guess, load, table, k_x):
+def own_residual(s, low, first_copies, u, r, guess, load, table, k_x, skip=0):
     lanes = s.lanes
-    rows = s.own_rows - low
+    rows = up_to(s.x_nodes + 1 - low, 8)
     ey, ny = (s.y_elems, s.y_nodes)
     nx = s.x_nodes - low
     width = ny * s.z_nodes
@@ -430,11 +430,11 @@
     first_copies[0].wait()
     for y in range(ny):
         mask = live if y else live * live_y
-        u[y, 0:nx] = get_line(s, guess, y, width) * mask
+        u[y, 0:nx] = get_line(s, guess, y, width)[skip:] * mask
         u[y, nx:] = pad
     first_copies[1].wait()
     for y in range(ny):
-        r[y, 0:nx] = get_line(s, load, y, width) * inside
+        r[y, 0:nx] = get_line(s, load, y, width)[skip:] * inside
         r[y, nx:] = pad
     u[ny] = jnp.zeros((rows, lanes), f32)
     r[ny] = jnp.zeros((rows, lanes), f32)
@@ -493,7 +493,8 @@
 
 
 def send_kernel(s):
-    low = (s.x_nodes - 7) // 8 * 8
+    low = s.x_nodes - 7
+    tile_low = low // 8 * 8
     lanes, nx, ny = (s.lanes, s.x_nodes, s.y_nodes)
     width = ny * s.z_nodes
 
@@ -502,10 +503,11 @@
         up_out, down_out,
         u, r, guess, load, table, k_x, top, sems,
     ):
-        sources = [guess_hbm.at[low:nx], load_hbm.at[low:nx], table_hbm, k_x_hbm]
+        sources = [guess_hbm.at[tile_low:nx], load_hbm.at[tile_low:nx], table_hbm, k_x_hbm]
         sources += [guess_hbm.at[0:8]]
         copies = started(sources, [guess, load, table, k_x, top], sems)
-        own_residual(s, low, copies[:4], u, r, guess, load, table, k_x)
+        skip = low - tile_low
+        own_residual(s, low, copies[:4], u, r, guess, load, table, k_x, skip)
         up_out[6:8, :] = jnp.zeros((2, up_out.shape[1]), f32)
         for y in range(ny + 1):
             put_line(s, up_out, y, r[y, nx - 6 - low : nx + 1 - low, :])
@@ -979,7 +981,8 @@
 
     in_hbm = lambda values: [pltpu.with_memory_space_constraint(v, pltpu.HBM) for v in values]
     hbm = {index: pltpu.HBM for index in range(4)}
-    low = (x_nodes - 7) // 8 * 8
+    low = x_nodes - 7
+    taken = x_nodes - low // 8 * 8
     constants = residual_constants(s, low)
     up, u_first = call(
         send_kernel(s),
@@ -987,10 +990,10 @@
         ((8, up_to((ny + 2) * z_nodes, LANES)), (up_to(ny, 8), lanes)),
         in_hbm([initial_guess, load_vector] + constants),
         [
-            (ny + 1, s.own_rows - low, lanes),
-            (ny + 1, s.own_rows - low, lanes),
-            (x_nodes - low, width),
-            (x_nodes - low, width),
+            (ny + 1, 8, lanes),
+            (ny + 1, 8, lanes),
+            (taken, width),
+            (taken, width),
             constants[0].shape,
             pltpu.VMEM(constants[1].shape, jnp.bfloat16),
             (8, width),

time: 52.6 us -> 52.1 us (level)
  no operation moved by 1% of the time
where the time goes in v8:
time: 52.1 us; the launch traced here: 51.1 us
  Pallas kernels  22.9 us (44%)
  starting transfers between devices  22.9 us (44%)
  waiting for transfers between devices  4.09 us (8%)
  between operations  1.06 us (2%)
    pallas_call x8, Pallas kernels, call(): pl.pallas_call(kernel, out_shape=tuple((shape(*dims) for dims in outputs)...  22.9 us
    ppermute x8, starting transfers between devices, shifted(): return lax.ppermute(array, axis, pairs)  22.9 us
    ppermute x8, waiting for transfers between devices, shifted(): return lax.ppermute(array, axis, pairs)  4.09 us
  transfers between devices with their start and end apart: 8, of which 2 were waited for; matrix products, arithmetic and copies ran while one was open for 0% of the time, Pallas kernels for 21%

profile of v8, /device:TPU:20, one launch (start us, length us, event | category | flops | bytes accessed | tf_op | source)
XLA Modules:
  0.0 51.1 jit_solution(15449292324192863966)
XLA Ops:
  0.6 2.4 %send.1 = (f32[8,6784]{1,0:T(8,128)S(1)}, f32[32,256]{1,0:T(8,128)S(1)}) custom-call(f32[28,6272]{1,0:T(8,128)} %guess.1, f32[28,6272]{1,0:T(8,128)} %load_hbm.3, f32[280,256]{1,0:T(8,128)} %constant.44.clone.table_hbm, bf16[8,48]{1,0:T(8,128)(2,1)} %constant.45.clone.k_x_hbm), custom_call_target="tpu_custom_call" | custom-call | tf_op jit(solution)/shard_map/send/pallas_call | solution.py:971
  3.1 0.0 copy-start.13
  3.1 0.0 copy-start.14
  3.1 3.5 %collective-permute-start = (f32[8,6784]{1,0:T(8,128)S(1)}, f32[8,6784]{1,0:T(8,128)S(1)}, u32[]{:S(2)}, u32[]{:S(2)}) collective-permute-start(f32[8,6784]{1,0:T(8,128)S(1)} %get-tuple-element.23), channel_id=1, source_target_pairs={{0,8},{8,16},{16,24},{1,9},{9,17},{17,25},{2,10},{10,18},{18,26},{... | collective-permute-start | bytes 651272 | tf_op jit(solution)/shard_map/ppermute | solution.py:33
  6.6 0.0 copy-start.1
  6.7 0.0 copy-start.2
  6.7 0.0 copy-start.3
  6.7 0.0 copy-start.4
  6.7 0.0 copy-start.6
  6.7 0.0 copy-start.9
  6.7 0.0 copy-start.11
  6.7 0.0 copy-start.18
  6.8 3.5 %collective-permute-start.1 = (f32[32,256]{1,0:T(8,128)S(1)}, f32[32,256]{1,0:T(8,128)S(1)}, u32[]{:S(2)}, u32[]{:S(2)}) collective-permute-start(f32[32,256]{1,0:T(8,128)S(1)} %get-tuple-element.22.u_first), channel_id=1, source_target_pairs={{8,0},{16,8},{24,16},{9,1},{17,9},{25,17},{10,2},{18,10},{26,18},{... | collective-permute-start | bytes 98312 | tf_op jit(solution)/shard_map/ppermute | solution.py:33
  10.2 3.9 %residual.1 = (f32[29,32,256]{2,1,0:T(8,128)S(1)}, f32[32,256]{1,0:T(8,128)S(1)}) custom-call(f32[28,6272]{1,0:T(8,128)} %guess.1, f32[28,6272]{1,0:T(8,128)} %load_hbm.3, f32[352,256]{1,0:T(8,128)} %constant.46.clone.table_hbm, bf16[32,192]{1,0:T(8,128)(2,1)} %constant.47.clone.k_x_hbm), custom_call_target="tpu_custom_call" | custom-call | tf_op jit(solution)/shard_map/residual/pallas_call | solution.py:971
  14.2 0.0 collective-permute-done.1.above
  14.2 0.0 collective-permute-done.below
  14.2 0.0 copy-done.13
  14.2 0.0 copy-done.14
  14.2 0.5 joined_x.1
  14.7 1.9 %collective-permute-start.2 = (f32[40,1664]{1,0:T(8,128)S(1)}, f32[40,1664]{1,0:T(8,128)S(1)}, u32[]{:S(2)}, u32[]{:S(2)}) collective-permute-start(f32[40,1664]{1,0:T(8,128)S(1)} %get-tuple-element.26), channel_id=1, source_target_pairs={{0,1},{1,2},{2,3},{3,4},{4,5},{5,6},{6,7},{8,9},{9,10},{10,11},{11... | collective-permute-start | bytes 798728 | tf_op jit(solution)/shard_map/ppermute | solution.py:33
  16.6 3.8 %collective-permute-start.3 = (f32[40,256]{1,0:T(8,128)S(1)}, f32[40,256]{1,0:T(8,128)S(1)}, u32[]{:S(2)}, u32[]{:S(2)}) collective-permute-start(f32[40,256]{1,0:T(8,128)S(1)} %get-tuple-element.25.line), channel_id=1, source_target_pairs={{1,0},{2,1},{3,2},{4,3},{5,4},{6,5},{7,6},{9,8},{10,9},{11,10},{12... | collective-permute-start | bytes 122888 | tf_op jit(solution)/shard_map/ppermute | solution.py:33
  20.4 0.0 copy-done.1
  20.5 0.0 copy-done.2
  20.5 0.0 copy-done.3
  20.5 0.0 copy-start.5
  20.5 0.0 copy-start.8
  20.6 0.0 copy-start.10
  20.6 0.0 copy-start.12
  20.6 0.0 copy-start.15
  20.6 0.0 copy-start.16
  20.6 0.0 copy-start.17
  20.6 4.2 %inner.1 = f32[13,2,40,256]{3,2,1,0:T(8,128)S(1)} custom-call(f32[29,40,256]{2,1,0:T(8,128)S(1)} %get-tuple-element.24.r_own, f32[13]{0:T(128)S(1)} %copy-done.18, f32[56,256]{1,0:T(8,128)S(1)} %copy-done.6, bf16[56,120]{1,0:T(8,128)(2,1)S(1)} %copy-done.11, bf16[40,168]{1,0:T(8,128)(2,1)S(1)} %copy-done.9, bf16[256,256]{1,0:T(8,128)(2,1)S(1)} %copy-done.2, ...), custom_call_target="tpu_custom_call" | custom-call | tf_op jit(solution)/shard_map/inner/pallas_call | solution.py:971
  24.8 0.0 copy-start.7
  24.8 0.0 collective-permute-done.3.above
  24.8 0.0 collective-permute-done.2.below
  24.9 0.0 copy-start
  24.9 7.5 %patches.1 = (f32[28,8,256]{2,1,0:T(8,128)S(1)}, f32[28,32,256]{2,1,0:T(8,128)S(1)}, f32[16,16,128]{2,1,0:T(8,128)S(1)}, f32[6,8,128]{2,1,0:T(8,128)S(1)}, f32[4...) custom-call(f32[29,40,256]{2,1,0:T(8,128)S(1)} %get-tuple-element.24.r_own, f32[40,256]{1,0:T(8,128)S(1)} %get-tuple-element.25.line, ...), custom_call_target="tpu_custom_call" | custom-call | tf_op jit(solution)/shard_map/patches/pallas_call | solution.py:971
  32.5 1.9 %collective-permute-start.4 = (f32[40,1792]{1,0:T(8,128)S(1)}, f32[40,1792]{1,0:T(8,128)S(1)}, u32[]{:S(2)}, u32[]{:S(2)}) collective-permute-start(f32[40,1792]{1,0:T(8,128)S(1)} %get-tuple-element.28), channel_id=1, source_target_pairs={{1,0},{2,1},{3,2},{4,3},{5,4},{6,5},{7,6},{9,8},{10,9},{11,10},{12... | collective-permute-start | bytes 860168 | tf_op jit(solution)/shard_map/ppermute | solution.py:33
  34.4 2.4 %collective-permute-start.5 = (f32[16,512]{1,0:T(8,128)S(1)}, f32[16,512]{1,0:T(8,128)S(1)}, u32[]{:S(2)}, u32[]{:S(2)}) collective-permute-start(f32[16,512]{1,0:T(8,128)S(1)} %get-tuple-element.32), channel_id=1, source_target_pairs={{0,1},{1,2},{2,3},{3,4},{4,5},{5,6},{6,7},{8,9},{9,10},{10,11},{11... | collective-permute-start | bytes 98312 | tf_op jit(solution)/shard_map/ppermute | solution.py:33
  36.8 2.8 %collective-permute-done.5.up = f32[16,512]{1,0:T(8,128)S(1)} collective-permute-done((f32[16,512]{1,0:T(8,128)S(1)}, f32[16,512]{1,0:T(8,128)S(1)}, u32[]{:S(2)}, u32[]{:S(2)}) %collective-permute-start.5) | collective-permute-done | bytes 32800 | tf_op jit(solution)/shard_map/ppermute | solution.py:33
  39.7 0.0 collective-permute-done.4.down
  39.7 0.1 join.1
  39.7 3.0 %collective-permute-start.6 = (f32[192,256]{1,0:T(8,128)S(1)}, f32[192,256]{1,0:T(8,128)S(1)}, u32[]{:S(2)}, u32[]{:S(2)}) collective-permute-start(f32[192,256]{1,0:T(8,128)S(1)} %get-tuple-element.33), channel_id=1, source_target_pairs={{8,0},{16,8},{24,16},{9,1},{17,9},{25,17},{10,2},{18,10},{26,18},{... | collective-permute-start | bytes 589832 | tf_op jit(solution)/shard_map/ppermute | solution.py:33
  42.8 2.8 %collective-permute-start.7 = (f32[24,256]{1,0:T(8,128)S(1)}, f32[24,256]{1,0:T(8,128)S(1)}, u32[]{:S(2)}, u32[]{:S(2)}) collective-permute-start(f32[24,256]{1,0:T(8,128)S(1)} %get-tuple-element.34), channel_id=1, source_target_pairs={{0,8},{8,16},{16,24},{1,9},{9,17},{17,25},{2,10},{10,18},{18,26},{... | collective-permute-start | bytes 73736 | tf_op jit(solution)/shard_map/ppermute | solution.py:33
  45.6 2.5 %base.1 = f32[28,6272]{1,0:T(8,128)S(1)} custom-call(f32[28,6272]{1,0:T(8,128)S(1)} %copy-done, f32[28,256]{1,0:T(8,128)S(1)} %copy-done.7, f32[28,32,256]{2,1,0:T(8,128)S(1)} %get-tuple-element.27.own, f32[40,1792]{1,0:T(8,128)S(1)} %collective-permute-done.4.down), custom_call_target="tpu_custom_call" | custom-call | tf_op jit(solution)/shard_map/base/pallas_call | solution.py:971
  48.1 1.3 %collective-permute-done.7.left = f32[24,256]{1,0:T(8,128)S(1)} collective-permute-done((f32[24,256]{1,0:T(8,128)S(1)}, f32[24,256]{1,0:T(8,128)S(1)}, u32[]{:S(2)}, u32[]{:S(2)}) %collective-permute-start.7) | collective-permute-done | bytes 24608 | tf_op jit(solution)/shard_map/ppermute | solution.py:33
  49.4 0.0 collective-permute-done.6.right
  49.4 1.8 %finish.1 = (f32[28,6272]{1,0:T(8,128)}, f32[12,1152]{1,0:T(8,128)}, f32[4,128]{1,0:T(4,128)}) custom-call(f32[28,6272]{1,0:T(8,128)S(1)} %base.1, f32[28,256]{1,0:T(8,128)S(1)} %copy-done.7, f32[192,256]{1,0:T(8,128)S(1)} %collective-permute-done.6.right, f32[24,256]{1,0:T(8,128)S(1)} %collective-permute-done.7.left, ...), custom_call_target="tpu_custom_call" | custom-call | tf_op jit(solution)/shard_map/finish/pallas_call | solution.py:971
  (14 shorter events, 0.0 us)
Async XLA Ops:
  3.1 11.1 %copy-start.13 = (f32[40,256]{1,0:T(8,128)S(1)}, f32[40,256]{1,0:T(8,128)}, u32[]{:S(2)}) copy-start(f32[40,256]{1,0:T(8,128)} %constant.49.clone.c_above) | copy-start | bytes 122884
  3.1 11.1 %copy-start.14 = (f32[40,256]{1,0:T(8,128)S(1)}, f32[40,256]{1,0:T(8,128)}, u32[]{:S(2)}) copy-start(f32[40,256]{1,0:T(8,128)} %constant.48.clone.c_below) | copy-start | bytes 122884
  3.1 11.1 %collective-permute-start = (f32[8,6784]{1,0:T(8,128)S(1)}, f32[8,6784]{1,0:T(8,128)S(1)}, u32[]{:S(2)}, u32[]{:S(2)}) collective-permute-start(f32[8,6784]{1,0:T(8,128)S(1)} %get-tuple-element.23), channel_id=1, source_target_pairs={{0,8},{8,16},{16,24},{1,9},{9,17},{17,25},{2,10},{10,18},{18,26},{... | collective-permute-start | bytes 651272 | tf_op jit(solution)/shard_map/ppermute | solution.py:33
  6.6 13.8 %copy-start.1 = (bf16[256,256]{1,0:T(8,128)(2,1)S(1)}, bf16[256,256]{1,0:T(8,128)(2,1)}, u32[]{:S(2)}) copy-start(bf16[256,256]{1,0:T(8,128)(2,1)} %constant.56.clone.b_z) | copy-start | bytes 393220
  6.7 13.8 %copy-start.2 = (bf16[256,256]{1,0:T(8,128)(2,1)S(1)}, bf16[256,256]{1,0:T(8,128)(2,1)}, u32[]{:S(2)}) copy-start(bf16[256,256]{1,0:T(8,128)(2,1)} %constant.54.clone.f_z) | copy-start | bytes 393220
  6.7 13.8 %copy-start.3 = (bf16[256,128]{1,0:T(8,128)(2,1)S(1)}, bf16[256,128]{1,0:T(8,128)(2,1)}, u32[]{:S(2)}) copy-start(bf16[256,128]{1,0:T(8,128)(2,1)} %constant.57.clone.b_z_high) | copy-start | bytes 196612
  6.7 13.8 %copy-start.4 = (bf16[128,256]{1,0:T(8,128)(2,1)S(1)}, bf16[128,256]{1,0:T(8,128)(2,1)}, u32[]{:S(2)}) copy-start(bf16[128,256]{1,0:T(8,128)(2,1)} %constant.55.clone.f_z_low) | copy-start | bytes 196612
  6.7 13.8 %copy-start.6 = (f32[56,256]{1,0:T(8,128)S(1)}, f32[56,256]{1,0:T(8,128)}, u32[]{:S(2)}) copy-start(f32[56,256]{1,0:T(8,128)} %constant.51.clone.sums) | copy-start | bytes 172036
  6.7 13.8 %copy-start.9 = (bf16[40,168]{1,0:T(8,128)(2,1)S(1)}, bf16[40,168]{1,0:T(8,128)(2,1)}, u32[]{:S(2)}) copy-start(bf16[40,168]{1,0:T(8,128)(2,1)} %constant.53.clone.b_x) | copy-start | bytes 40324
  6.7 13.8 %copy-start.11 = (bf16[56,120]{1,0:T(8,128)(2,1)S(1)}, bf16[56,120]{1,0:T(8,128)(2,1)}, u32[]{:S(2)}) copy-start(bf16[56,120]{1,0:T(8,128)(2,1)} %constant.52.clone.f_x) | copy-start | bytes 40324
  6.7 13.8 %copy-start.18 = (f32[13]{0:T(128)S(1)}, f32[13]{0:T(128)}, u32[]{:S(2)}) copy-start(f32[13]{0:T(128)} %constant.50.clone.lam) | copy-start | bytes 160
  6.8 7.4 %collective-permute-start.1 = (f32[32,256]{1,0:T(8,128)S(1)}, f32[32,256]{1,0:T(8,128)S(1)}, u32[]{:S(2)}, u32[]{:S(2)}) collective-permute-start(f32[32,256]{1,0:T(8,128)S(1)} %get-tuple-element.22.u_first), channel_id=1, source_target_pairs={{8,0},{16,8},{24,16},{9,1},{17,9},{25,17},{10,2},{18,10},{26,18},{... | collective-permute-start | bytes 98312 | tf_op jit(solution)/shard_map/ppermute | solution.py:33
  14.7 10.2 %collective-permute-start.2 = (f32[40,1664]{1,0:T(8,128)S(1)}, f32[40,1664]{1,0:T(8,128)S(1)}, u32[]{:S(2)}, u32[]{:S(2)}) collective-permute-start(f32[40,1664]{1,0:T(8,128)S(1)} %get-tuple-element.26), channel_id=1, source_target_pairs={{0,1},{1,2},{2,3},{3,4},{4,5},{5,6},{6,7},{8,9},{9,10},{10,11},{11... | collective-permute-start | bytes 798728 | tf_op jit(solution)/shard_map/ppermute | solution.py:33
  16.6 8.2 %collective-permute-start.3 = (f32[40,256]{1,0:T(8,128)S(1)}, f32[40,256]{1,0:T(8,128)S(1)}, u32[]{:S(2)}, u32[]{:S(2)}) collective-permute-start(f32[40,256]{1,0:T(8,128)S(1)} %get-tuple-element.25.line), channel_id=1, source_target_pairs={{1,0},{2,1},{3,2},{4,3},{5,4},{6,5},{7,6},{9,8},{10,9},{11,10},{12... | collective-permute-start | bytes 122888 | tf_op jit(solution)/shard_map/ppermute | solution.py:33
  20.5 4.3 %copy-start.5 = (f32[256,256]{1,0:T(8,128)S(1)}, f32[256,256]{1,0:T(8,128)}, u32[]{:S(2)}) copy-start(f32[256,256]{1,0:T(8,128)} %constant.59.clone.q_z) | copy-start | bytes 786436
  20.5 4.3 %copy-start.8 = (f32[256,128]{1,0:T(8,128)S(1)}, f32[256,128]{1,0:T(8,128)}, u32[]{:S(2)}) copy-start(f32[256,128]{1,0:T(8,128)} %constant.60.clone.r_z) | copy-start | bytes 393220
  20.6 4.3 %copy-start.10 = (f32[128,128]{1,0:T(8,128)S(1)}, f32[128,128]{1,0:T(8,128)}, u32[]{:S(2)}) copy-start(f32[128,128]{1,0:T(8,128)} %constant.61.clone.o_z) | copy-start | bytes 196612
  20.6 4.3 %copy-start.12 = (f32[40,256]{1,0:T(8,128)S(1)}, f32[40,256]{1,0:T(8,128)}, u32[]{:S(2)}) copy-start(f32[40,256]{1,0:T(8,128)} %constant.58.clone.m_xz) | copy-start | bytes 122884
  20.6 4.3 %copy-start.15 = (bf16[32,120]{1,0:T(8,128)(2,1)S(1)}, bf16[32,120]{1,0:T(8,128)(2,1)}, u32[]{:S(2)}) copy-start(bf16[32,120]{1,0:T(8,128)(2,1)} %constant.63.clone.q_x) | copy-start | bytes 23044
  20.6 4.3 %copy-start.16 = (bf16[16,120]{1,0:T(8,128)(2,1)S(1)}, bf16[16,120]{1,0:T(8,128)(2,1)}, u32[]{:S(2)}) copy-start(bf16[16,120]{1,0:T(8,128)(2,1)} %constant.64.clone.r_x) | copy-start | bytes 11524
  20.6 4.3 %copy-start.17 = (f32[8,16]{1,0:T(8,128)S(1)}, f32[8,16]{1,0:T(8,128)}, u32[]{:S(2)}) copy-start(f32[8,16]{1,0:T(8,128)} %constant.62.clone.o_x) | copy-start | bytes 1540
  24.8 20.8 %copy-start.7 = (f32[28,256]{1,0:T(8,128)S(1)}, f32[28,256]{1,0:T(8,128)}, u32[]{:S(2)}) copy-start(f32[28,256]{1,0:T(8,128)} %constant.65.clone.weight) | copy-start | bytes 86020
  24.9 20.7 %copy-start = (f32[28,6272]{1,0:T(8,128)S(1)}, f32[28,6272]{1,0:T(8,128)}, u32[]{:S(2)}) copy-start(f32[28,6272]{1,0:T(8,128)} %guess.1) | copy-start | bytes 2107396
  32.5 7.2 %collective-permute-start.4 = (f32[40,1792]{1,0:T(8,128)S(1)}, f32[40,1792]{1,0:T(8,128)S(1)}, u32[]{:S(2)}, u32[]{:S(2)}) collective-permute-start(f32[40,1792]{1,0:T(8,128)S(1)} %get-tuple-element.28), channel_id=1, source_target_pairs={{1,0},{2,1},{3,2},{4,3},{5,4},{6,5},{7,6},{9,8},{10,9},{11,10},{12... | collective-permute-start | bytes 860168 | tf_op jit(solution)/shard_map/ppermute | solution.py:33
  34.4 5.2 %collective-permute-start.5 = (f32[16,512]{1,0:T(8,128)S(1)}, f32[16,512]{1,0:T(8,128)S(1)}, u32[]{:S(2)}, u32[]{:S(2)}) collective-permute-start(f32[16,512]{1,0:T(8,128)S(1)} %get-tuple-element.32), channel_id=1, source_target_pairs={{0,1},{1,2},{2,3},{3,4},{4,5},{5,6},{6,7},{8,9},{9,10},{10,11},{11... | collective-permute-start | bytes 98312 | tf_op jit(solution)/shard_map/ppermute | solution.py:33
  39.7 9.7 %collective-permute-start.6 = (f32[192,256]{1,0:T(8,128)S(1)}, f32[192,256]{1,0:T(8,128)S(1)}, u32[]{:S(2)}, u32[]{:S(2)}) collective-permute-start(f32[192,256]{1,0:T(8,128)S(1)} %get-tuple-element.33), channel_id=1, source_target_pairs={{8,0},{16,8},{24,16},{9,1},{17,9},{25,17},{10,2},{18,10},{26,18},{... | collective-permute-start | bytes 589832 | tf_op jit(solution)/shard_map/ppermute | solution.py:33
  42.8 6.6 %collective-permute-start.7 = (f32[24,256]{1,0:T(8,128)S(1)}, f32[24,256]{1,0:T(8,128)S(1)}, u32[]{:S(2)}, u32[]{:S(2)}) collective-permute-start(f32[24,256]{1,0:T(8,128)S(1)} %get-tuple-element.34), channel_id=1, source_target_pairs={{0,8},{8,16},{16,24},{1,9},{9,17},{17,25},{2,10},{10,18},{18,26},{... | collective-permute-start | bytes 73736 | tf_op jit(solution)/shard_map/ppermute | solution.py:33

commit v9 on v8

--- a/solution.py
+++ b/solution.py
@@ -776,6 +776,10 @@
     return index % high_rows, LANES * (index // high_rows)
 
 
+def line_lanes(s):
+    return up_to(-(-s.y_nodes // 4) * s.z_nodes, LANES)
+
+
 def coarse_height(s):
     return up_to(-(-max(9 * s.y_elems, 4 * s.y_elems + 24) // 2), 24)
 
@@ -788,15 +792,23 @@
         lane = lax.broadcasted_iota(jnp.int32, (rows_c, half), 1)
         is_three = (lane < s.coarse_z).astype(f32)
         is_one = (lane >= s.coarse_z).astype(f32)[0:8]
+        down_out[...] = jnp.zeros(down_out.shape, f32)
+        shared = shared_lanes(s, (8, lanes))
         for y in range(ny):
             plane = edge[y]
             if y >= ny - 6:
                 j = y - (ny - 6)
                 plane = plane + down[0:8, lanes * j : lanes * (j + 1)]
-            down_out[6 * y : 6 * y + 6, :] = plane[2:8]
+            plane = plane + pltpu.roll(plane, lanes - (LANES - s.split), 1) * shared
+            here = pl.ds(6 * (y % 4), 6)
+            at = s.z_nodes * (y // 4)
+            for t in range(2):
+                first = LANES * t + 6
+                down_out[here, at + s.split * t : at + s.split * (t + 1)] = plane[
+                    2:8, first : first + s.split
+                ]
         base = 6 * lanes
-        first = 6 * ny
-        down_out[first:, :] = jnp.zeros((down_out.shape[0] - first, lanes), f32)
+        tiles = line_lanes(s)
         up_out[...] = jnp.zeros(up_out.shape, f32)
 
         def from_above(k, count):
@@ -812,7 +824,7 @@
             plane = plane * is_three
             three_out[j] = plane
             row, at = coarse_place(s, 3 * j)
-            down_out[first + row : first + row + 3, at : at + half] = plane[0:3]
+            down_out[row : row + 3, tiles + at : tiles + at + half] = plane[0:3]
             row, at = coarse_place(s, j)
             up_out[row : row + 1, at : at + half] = plane[s.coarse_x - 1 : s.coarse_x]
         for j in range(ey + 6):
@@ -830,7 +842,7 @@
             plane = plane * is_one
             one_out[j] = plane
             row, at = coarse_place(s, 4 * j)
-            down_out[first + row : first + row + 4, at : at + half] += plane[0:4]
+            down_out[row : row + 4, tiles + at : tiles + at + half] += plane[0:4]
             up_out[row : row + 4, at : at + half] += plane[s.x_elems - 2 : s.x_elems + 2]
 
     return kernel
@@ -879,17 +891,12 @@
         gx = lax.axis_index("gx")
         gy = lax.axis_index("gy")
         live_y = (gy > 0).astype(f32)
-        shared = shared_lanes(s, (6, lanes))
         smooth_out[...] = base[...]
         for y in range(ny):
-            plane = right[6 * y : 6 * y + 6, :]
-            plane = plane + pltpu.roll(plane, lanes - (LANES - split), 1) * shared
-            plane = plane * weight[nx - 6 : nx, :] * (1.0 if y % 7 == 0 else 0.5)
-            for t in range(2):
-                at = nz * y + split * t
-                lanes_at = LANES * t + 6
-                smooth_out[nx - 6 : nx, at : at + split] += plane[:, lanes_at : lanes_at + split]
-        first = 6 * ny
+            at = nz * (y // 4)
+            piece = right[6 * (y % 4) : 6 * (y % 4) + 6, at : at + nz] * weight[...]
+            smooth_out[nx - 6 : nx, nz * y : nz * (y + 1)] += piece * (1.0 if y % 7 == 0 else 0.5)
+        tiles = line_lanes(s)
         nzc = s.coarse_z
         lane = lax.broadcasted_iota(jnp.int32, (3 * ex, nzc), 1)
         row = lax.broadcasted_iota(jnp.int32, (3 * ex, nzc), 0)
@@ -897,7 +904,7 @@
         for j in range(3 * ey):
             fine[j] = three[j]
             at_row, at = coarse_place(s, 3 * j)
-            at_row += first
+            at += tiles
             fine[j, 3 * ex : 3 * ex + 3, :] += right[at_row : at_row + 3, at : at + half]
             at_row, at = coarse_place(s, j)
             fine[j, 3:4, :] += left[at_row : at_row + 1, at : at + half]
@@ -908,7 +915,7 @@
             level[j, 2 : ex + 4, :] = one[j, 0 : ex + 2, :]
             at_row, at = coarse_place(s, 4 * j)
             level[j, 0:4, :] += left[at_row : at_row + 4, at : at + half]
-            at_row += first
+            at += tiles
             level[j, ex + 2 : ex + 6, :] += right[at_row : at_row + 4, at : at + half]
         shape = (one_rows, LANES)
         lane = lax.broadcasted_iota(jnp.int32, shape, 1)
@@ -1073,7 +1080,7 @@
         join_kernel(s),
         "join",
         (
-            (6 * ny + coarse_height(s), lanes),
+            (coarse_height(s), line_lanes(s) + 2 * half),
             (coarse_height(s), lanes),
             (3 * ey, s.coarse_rows, half),
             (ey + 6, 8, LANES),
@@ -1088,6 +1095,8 @@
         * rows_by_node(s, weight_z[:, None], True)[:, 0],
         f32,
     )
+    weight_x = np.where(np.arange(x_nodes) % 7 == 0, 1.0, 0.5)[-6:]
+    edge_weight = jnp.asarray(weight_x[:, None] * weight_z[None, :], f32)
     (base,) = call(
         base_kernel(s), "base", ((x_nodes, width),), [initial_guess, weight, own, down]
     )
@@ -1099,7 +1108,7 @@
             (3 * s.x_elems, 3 * ey * s.coarse_z),
             (s.x_elems, ey * s.z_elems),
         ),
-        [base, weight, right, left, three, one],
+        [base, edge_weight, right, left, three, one],
         [
             (3 * ey, s.coarse_rows, half),
             (ey + 6, up_to(s.x_elems + 6, 8), LANES),

time: 52.1 us -> 51.7 us (level)
  no operation moved by 1% of the time
where the time goes in v9:
time: 51.7 us; the launch traced here: 51 us
  starting transfers between devices  22.9 us (44%)
  Pallas kernels  22.7 us (44%)
  waiting for transfers between devices  4.08 us (8%)
  between operations  1.07 us (2%)
    ppermute x8, starting transfers between devices, shifted(): return lax.ppermute(array, axis, pairs)  22.9 us
    pallas_call x8, Pallas kernels, call(): pl.pallas_call(kernel, out_shape=tuple((shape(*dims) for dims in outputs)...  22.7 us
    ppermute x8, waiting for transfers between devices, shifted(): return lax.ppermute(array, axis, pairs)  4.08 us
  transfers between devices with their start and end apart: 8, of which 2 were waited for; matrix products, arithmetic and copies ran while one was open for 0% of the time, Pallas kernels for 21%

profile of v9, /device:TPU:20, one launch (start us, length us, event | category | flops | bytes accessed | tf_op | source)
XLA Modules:
  0.0 51.0 jit_solution(1238920052252669184)
XLA Ops:
  0.6 2.4 %send.1 = (f32[8,6784]{1,0:T(8,128)S(1)}, f32[32,256]{1,0:T(8,128)S(1)}) custom-call(f32[28,6272]{1,0:T(8,128)} %guess.1, f32[28,6272]{1,0:T(8,128)} %load_hbm.3, f32[280,256]{1,0:T(8,128)} %constant.46.clone.table_hbm, bf16[8,48]{1,0:T(8,128)(2,1)} %constant.47.clone.k_x_hbm), custom_call_target="tpu_custom_call" | custom-call | tf_op jit(solution)/shard_map/send/pallas_call | solution.py:978
  3.1 0.0 copy-start.12
  3.1 0.0 copy-start.13
  3.1 3.5 %collective-permute-start = (f32[8,6784]{1,0:T(8,128)S(1)}, f32[8,6784]{1,0:T(8,128)S(1)}, u32[]{:S(2)}, u32[]{:S(2)}) collective-permute-start(f32[8,6784]{1,0:T(8,128)S(1)} %get-tuple-element.23), channel_id=1, source_target_pairs={{0,8},{8,16},{16,24},{1,9},{9,17},{17,25},{2,10},{10,18},{18,26},{... | collective-permute-start | bytes 651272 | tf_op jit(solution)/shard_map/ppermute | solution.py:33
  6.6 0.0 copy-start.1
  6.7 0.0 copy-start.2
  6.7 0.0 copy-start.3
  6.7 0.0 copy-start.4
  6.7 0.0 copy-start.6
  6.7 0.0 copy-start.8
  6.7 0.0 copy-start.10
  6.7 0.0 copy-start.19
  6.8 3.5 %collective-permute-start.1 = (f32[32,256]{1,0:T(8,128)S(1)}, f32[32,256]{1,0:T(8,128)S(1)}, u32[]{:S(2)}, u32[]{:S(2)}) collective-permute-start(f32[32,256]{1,0:T(8,128)S(1)} %get-tuple-element.22.u_first), channel_id=1, source_target_pairs={{8,0},{16,8},{24,16},{9,1},{17,9},{25,17},{10,2},{18,10},{26,18},{... | collective-permute-start | bytes 98312 | tf_op jit(solution)/shard_map/ppermute | solution.py:33
  10.2 3.9 %residual.1 = (f32[29,32,256]{2,1,0:T(8,128)S(1)}, f32[32,256]{1,0:T(8,128)S(1)}) custom-call(f32[28,6272]{1,0:T(8,128)} %guess.1, f32[28,6272]{1,0:T(8,128)} %load_hbm.3, f32[352,256]{1,0:T(8,128)} %constant.48.clone.table_hbm, bf16[32,192]{1,0:T(8,128)(2,1)} %constant.49.clone.k_x_hbm), custom_call_target="tpu_custom_call" | custom-call | tf_op jit(solution)/shard_map/residual/pallas_call | solution.py:978
  14.2 0.0 collective-permute-done.1.above
  14.2 0.0 collective-permute-done.below
  14.2 0.0 copy-done.12
  14.2 0.0 copy-done.13
  14.2 0.5 joined_x.1
  14.7 1.9 %collective-permute-start.2 = (f32[40,1664]{1,0:T(8,128)S(1)}, f32[40,1664]{1,0:T(8,128)S(1)}, u32[]{:S(2)}, u32[]{:S(2)}) collective-permute-start(f32[40,1664]{1,0:T(8,128)S(1)} %get-tuple-element.26), channel_id=1, source_target_pairs={{0,1},{1,2},{2,3},{3,4},{4,5},{5,6},{6,7},{8,9},{9,10},{10,11},{11... | collective-permute-start | bytes 798728 | tf_op jit(solution)/shard_map/ppermute | solution.py:33
  16.6 3.8 %collective-permute-start.3 = (f32[40,256]{1,0:T(8,128)S(1)}, f32[40,256]{1,0:T(8,128)S(1)}, u32[]{:S(2)}, u32[]{:S(2)}) collective-permute-start(f32[40,256]{1,0:T(8,128)S(1)} %get-tuple-element.25.line), channel_id=1, source_target_pairs={{1,0},{2,1},{3,2},{4,3},{5,4},{6,5},{7,6},{9,8},{10,9},{11,10},{12... | collective-permute-start | bytes 122888 | tf_op jit(solution)/shard_map/ppermute | solution.py:33
  20.4 0.0 copy-done.1
  20.5 0.0 copy-done.2
  20.5 0.0 copy-start.5
  20.5 0.0 copy-start.7
  20.6 0.0 copy-start.9
  20.6 0.0 copy-start.11
  20.6 0.0 copy-start.16
  20.6 0.0 copy-start.17
  20.6 0.0 copy-start.18
  20.6 4.2 %inner.1 = f32[13,2,40,256]{3,2,1,0:T(8,128)S(1)} custom-call(f32[29,40,256]{2,1,0:T(8,128)S(1)} %get-tuple-element.24.r_own, f32[13]{0:T(128)S(1)} %copy-done.19, f32[56,256]{1,0:T(8,128)S(1)} %copy-done.6, bf16[56,120]{1,0:T(8,128)(2,1)S(1)} %copy-done.10, bf16[40,168]{1,0:T(8,128)(2,1)S(1)} %copy-done.8, bf16[256,256]{1,0:T(8,128)(2,1)S(1)} %copy-done.2, ...), custom_call_target="tpu_custom_call" | custom-call | tf_op jit(solution)/shard_map/inner/pallas_call | solution.py:978
  24.8 0.0 copy-start.14
  24.8 0.0 collective-permute-done.3.above
  24.8 0.0 collective-permute-done.2.below
  24.9 0.0 copy-start
  24.9 7.5 %patches.1 = (f32[28,8,256]{2,1,0:T(8,128)S(1)}, f32[28,32,256]{2,1,0:T(8,128)S(1)}, f32[16,16,128]{2,1,0:T(8,128)S(1)}, f32[6,8,128]{2,1,0:T(8,128)S(1)}, f32[4...) custom-call(f32[29,40,256]{2,1,0:T(8,128)S(1)} %get-tuple-element.24.r_own, f32[40,256]{1,0:T(8,128)S(1)} %get-tuple-element.25.line, ...), custom_call_target="tpu_custom_call" | custom-call | tf_op jit(solution)/shard_map/patches/pallas_call | solution.py:978
  32.5 1.9 %collective-permute-start.4 = (f32[40,1792]{1,0:T(8,128)S(1)}, f32[40,1792]{1,0:T(8,128)S(1)}, u32[]{:S(2)}, u32[]{:S(2)}) collective-permute-start(f32[40,1792]{1,0:T(8,128)S(1)} %get-tuple-element.28), channel_id=1, source_target_pairs={{1,0},{2,1},{3,2},{4,3},{5,4},{6,5},{7,6},{9,8},{10,9},{11,10},{12... | collective-permute-start | bytes 860168 | tf_op jit(solution)/shard_map/ppermute | solution.py:33
  34.4 2.4 %collective-permute-start.5 = (f32[16,512]{1,0:T(8,128)S(1)}, f32[16,512]{1,0:T(8,128)S(1)}, u32[]{:S(2)}, u32[]{:S(2)}) collective-permute-start(f32[16,512]{1,0:T(8,128)S(1)} %get-tuple-element.32), channel_id=1, source_target_pairs={{0,1},{1,2},{2,3},{3,4},{4,5},{5,6},{6,7},{8,9},{9,10},{10,11},{11... | collective-permute-start | bytes 98312 | tf_op jit(solution)/shard_map/ppermute | solution.py:33
  36.8 2.8 %collective-permute-done.5.up = f32[16,512]{1,0:T(8,128)S(1)} collective-permute-done((f32[16,512]{1,0:T(8,128)S(1)}, f32[16,512]{1,0:T(8,128)S(1)}, u32[]{:S(2)}, u32[]{:S(2)}) %collective-permute-start.5) | collective-permute-done | bytes 32800 | tf_op jit(solution)/shard_map/ppermute | solution.py:33
  39.7 0.0 collective-permute-done.4.down
  39.7 0.3 join.1
  40.0 3.0 %collective-permute-start.6 = (f32[24,1920]{1,0:T(8,128)S(1)}, f32[24,1920]{1,0:T(8,128)S(1)}, u32[]{:S(2)}, u32[]{:S(2)}) collective-permute-start(f32[24,1920]{1,0:T(8,128)S(1)} %get-tuple-element.33), channel_id=1, source_target_pairs={{8,0},{16,8},{24,16},{9,1},{17,9},{25,17},{10,2},{18,10},{26,18},{... | collective-permute-start | bytes 552968 | tf_op jit(solution)/shard_map/ppermute | solution.py:33
  43.0 2.8 %collective-permute-start.7 = (f32[24,256]{1,0:T(8,128)S(1)}, f32[24,256]{1,0:T(8,128)S(1)}, u32[]{:S(2)}, u32[]{:S(2)}) collective-permute-start(f32[24,256]{1,0:T(8,128)S(1)} %get-tuple-element.34), channel_id=1, source_target_pairs={{0,8},{8,16},{16,24},{1,9},{9,17},{17,25},{2,10},{10,18},{18,26},{... | collective-permute-start | bytes 73736 | tf_op jit(solution)/shard_map/ppermute | solution.py:33
  45.8 0.0 copy-start.15
  45.9 2.5 %base.1 = f32[28,6272]{1,0:T(8,128)S(1)} custom-call(f32[28,6272]{1,0:T(8,128)S(1)} %copy-done, f32[28,256]{1,0:T(8,128)S(1)} %copy-done.14, f32[28,32,256]{2,1,0:T(8,128)S(1)} %get-tuple-element.27.own, f32[40,1792]{1,0:T(8,128)S(1)} %collective-permute-done.4.down), custom_call_target="tpu_custom_call" | custom-call | tf_op jit(solution)/shard_map/base/pallas_call | solution.py:978
  48.4 1.2 %collective-permute-done.7.left = f32[24,256]{1,0:T(8,128)S(1)} collective-permute-done((f32[24,256]{1,0:T(8,128)S(1)}, f32[24,256]{1,0:T(8,128)S(1)}, u32[]{:S(2)}, u32[]{:S(2)}) %collective-permute-start.7) | collective-permute-done | bytes 24608 | tf_op jit(solution)/shard_map/ppermute | solution.py:33
  49.6 0.0 collective-permute-done.6.right
  49.6 1.4 %finish.1 = (f32[28,6272]{1,0:T(8,128)}, f32[12,1152]{1,0:T(8,128)}, f32[4,128]{1,0:T(4,128)}) custom-call(f32[28,6272]{1,0:T(8,128)S(1)} %base.1, f32[6,224]{1,0:T(8,128)S(1)} %copy-done.15, f32[24,1920]{1,0:T(8,128)S(1)} %collective-permute-done.6.right, f32[24,256]{1,0:T(8,128)S(1)} %collective-permute-done.7.left, ...), custom_call_target="tpu_custom_call" | custom-call | tf_op jit(solution)/shard_map/finish/pallas_call | solution.py:978
  (16 shorter events, 0.0 us)
Async XLA Ops:
  3.1 11.1 %copy-start.12 = (f32[40,256]{1,0:T(8,128)S(1)}, f32[40,256]{1,0:T(8,128)}, u32[]{:S(2)}) copy-start(f32[40,256]{1,0:T(8,128)} %constant.51.clone.c_above) | copy-start | bytes 122884
  3.1 11.1 %copy-start.13 = (f32[40,256]{1,0:T(8,128)S(1)}, f32[40,256]{1,0:T(8,128)}, u32[]{:S(2)}) copy-start(f32[40,256]{1,0:T(8,128)} %constant.50.clone.c_below) | copy-start | bytes 122884
  3.1 11.1 %collective-permute-start = (f32[8,6784]{1,0:T(8,128)S(1)}, f32[8,6784]{1,0:T(8,128)S(1)}, u32[]{:S(2)}, u32[]{:S(2)}) collective-permute-start(f32[8,6784]{1,0:T(8,128)S(1)} %get-tuple-element.23), channel_id=1, source_target_pairs={{0,8},{8,16},{16,24},{1,9},{9,17},{17,25},{2,10},{10,18},{18,26},{... | collective-permute-start | bytes 651272 | tf_op jit(solution)/shard_map/ppermute | solution.py:33
  6.6 13.8 %copy-start.1 = (bf16[256,256]{1,0:T(8,128)(2,1)S(1)}, bf16[256,256]{1,0:T(8,128)(2,1)}, u32[]{:S(2)}) copy-start(bf16[256,256]{1,0:T(8,128)(2,1)} %constant.58.clone.b_z) | copy-start | bytes 393220
  6.7 13.8 %copy-start.2 = (bf16[256,256]{1,0:T(8,128)(2,1)S(1)}, bf16[256,256]{1,0:T(8,128)(2,1)}, u32[]{:S(2)}) copy-start(bf16[256,256]{1,0:T(8,128)(2,1)} %constant.56.clone.f_z) | copy-start | bytes 393220
  6.7 13.8 %copy-start.3 = (bf16[256,128]{1,0:T(8,128)(2,1)S(1)}, bf16[256,128]{1,0:T(8,128)(2,1)}, u32[]{:S(2)}) copy-start(bf16[256,128]{1,0:T(8,128)(2,1)} %constant.59.clone.b_z_high) | copy-start | bytes 196612
  6.7 13.8 %copy-start.4 = (bf16[128,256]{1,0:T(8,128)(2,1)S(1)}, bf16[128,256]{1,0:T(8,128)(2,1)}, u32[]{:S(2)}) copy-start(bf16[128,256]{1,0:T(8,128)(2,1)} %constant.57.clone.f_z_low) | copy-start | bytes 196612
  6.7 13.8 %copy-start.6 = (f32[56,256]{1,0:T(8,128)S(1)}, f32[56,256]{1,0:T(8,128)}, u32[]{:S(2)}) copy-start(f32[56,256]{1,0:T(8,128)} %constant.53.clone.sums) | copy-start | bytes 172036
  6.7 13.8 %copy-start.8 = (bf16[40,168]{1,0:T(8,128)(2,1)S(1)}, bf16[40,168]{1,0:T(8,128)(2,1)}, u32[]{:S(2)}) copy-start(bf16[40,168]{1,0:T(8,128)(2,1)} %constant.55.clone.b_x) | copy-start | bytes 40324
  6.7 13.8 %copy-start.10 = (bf16[56,120]{1,0:T(8,128)(2,1)S(1)}, bf16[56,120]{1,0:T(8,128)(2,1)}, u32[]{:S(2)}) copy-start(bf16[56,120]{1,0:T(8,128)(2,1)} %constant.54.clone.f_x) | copy-start | bytes 40324
  6.7 13.8 %copy-start.19 = (f32[13]{0:T(128)S(1)}, f32[13]{0:T(128)}, u32[]{:S(2)}) copy-start(f32[13]{0:T(128)} %constant.52.clone.lam) | copy-start | bytes 160
  6.8 7.4 %collective-permute-start.1 = (f32[32,256]{1,0:T(8,128)S(1)}, f32[32,256]{1,0:T(8,128)S(1)}, u32[]{:S(2)}, u32[]{:S(2)}) collective-permute-start(f32[32,256]{1,0:T(8,128)S(1)} %get-tuple-element.22.u_first), channel_id=1, source_target_pairs={{8,0},{16,8},{24,16},{9,1},{17,9},{25,17},{10,2},{18,10},{26,18},{... | collective-permute-start | bytes 98312 | tf_op jit(solution)/shard_map/ppermute | solution.py:33
  14.7 10.2 %collective-permute-start.2 = (f32[40,1664]{1,0:T(8,128)S(1)}, f32[40,1664]{1,0:T(8,128)S(1)}, u32[]{:S(2)}, u32[]{:S(2)}) collective-permute-start(f32[40,1664]{1,0:T(8,128)S(1)} %get-tuple-element.26), channel_id=1, source_target_pairs={{0,1},{1,2},{2,3},{3,4},{4,5},{5,6},{6,7},{8,9},{9,10},{10,11},{11... | collective-permute-start | bytes 798728 | tf_op jit(solution)/shard_map/ppermute | solution.py:33
  16.6 8.2 %collective-permute-start.3 = (f32[40,256]{1,0:T(8,128)S(1)}, f32[40,256]{1,0:T(8,128)S(1)}, u32[]{:S(2)}, u32[]{:S(2)}) collective-permute-start(f32[40,256]{1,0:T(8,128)S(1)} %get-tuple-element.25.line), channel_id=1, source_target_pairs={{1,0},{2,1},{3,2},{4,3},{5,4},{6,5},{7,6},{9,8},{10,9},{11,10},{12... | collective-permute-start | bytes 122888 | tf_op jit(solution)/shard_map/ppermute | solution.py:33
  20.5 4.3 %copy-start.5 = (f32[256,256]{1,0:T(8,128)S(1)}, f32[256,256]{1,0:T(8,128)}, u32[]{:S(2)}) copy-start(f32[256,256]{1,0:T(8,128)} %constant.61.clone.q_z) | copy-start | bytes 786436
  20.5 4.3 %copy-start.7 = (f32[256,128]{1,0:T(8,128)S(1)}, f32[256,128]{1,0:T(8,128)}, u32[]{:S(2)}) copy-start(f32[256,128]{1,0:T(8,128)} %constant.62.clone.r_z) | copy-start | bytes 393220
  20.6 4.3 %copy-start.9 = (f32[128,128]{1,0:T(8,128)S(1)}, f32[128,128]{1,0:T(8,128)}, u32[]{:S(2)}) copy-start(f32[128,128]{1,0:T(8,128)} %constant.63.clone.o_z) | copy-start | bytes 196612
  20.6 4.3 %copy-start.11 = (f32[40,256]{1,0:T(8,128)S(1)}, f32[40,256]{1,0:T(8,128)}, u32[]{:S(2)}) copy-start(f32[40,256]{1,0:T(8,128)} %constant.60.clone.m_xz) | copy-start | bytes 122884
  20.6 4.3 %copy-start.16 = (bf16[32,120]{1,0:T(8,128)(2,1)S(1)}, bf16[32,120]{1,0:T(8,128)(2,1)}, u32[]{:S(2)}) copy-start(bf16[32,120]{1,0:T(8,128)(2,1)} %constant.65.clone.q_x) | copy-start | bytes 23044
  20.6 4.3 %copy-start.17 = (bf16[16,120]{1,0:T(8,128)(2,1)S(1)}, bf16[16,120]{1,0:T(8,128)(2,1)}, u32[]{:S(2)}) copy-start(bf16[16,120]{1,0:T(8,128)(2,1)} %constant.66.clone.r_x) | copy-start | bytes 11524
  20.6 4.3 %copy-start.18 = (f32[8,16]{1,0:T(8,128)S(1)}, f32[8,16]{1,0:T(8,128)}, u32[]{:S(2)}) copy-start(f32[8,16]{1,0:T(8,128)} %constant.64.clone.o_x) | copy-start | bytes 1540
  24.8 21.0 %copy-start.14 = (f32[28,256]{1,0:T(8,128)S(1)}, f32[28,256]{1,0:T(8,128)}, u32[]{:S(2)}) copy-start(f32[28,256]{1,0:T(8,128)} %constant.67.clone.weight) | copy-start | bytes 86020
  24.9 20.9 %copy-start = (f32[28,6272]{1,0:T(8,128)S(1)}, f32[28,6272]{1,0:T(8,128)}, u32[]{:S(2)}) copy-start(f32[28,6272]{1,0:T(8,128)} %guess.1) | copy-start | bytes 2107396
  32.5 7.2 %collective-permute-start.4 = (f32[40,1792]{1,0:T(8,128)S(1)}, f32[40,1792]{1,0:T(8,128)S(1)}, u32[]{:S(2)}, u32[]{:S(2)}) collective-permute-start(f32[40,1792]{1,0:T(8,128)S(1)} %get-tuple-element.28), channel_id=1, source_target_pairs={{1,0},{2,1},{3,2},{4,3},{5,4},{6,5},{7,6},{9,8},{10,9},{11,10},{12... | collective-permute-start | bytes 860168 | tf_op jit(solution)/shard_map/ppermute | solution.py:33
  34.4 5.2 %collective-permute-start.5 = (f32[16,512]{1,0:T(8,128)S(1)}, f32[16,512]{1,0:T(8,128)S(1)}, u32[]{:S(2)}, u32[]{:S(2)}) collective-permute-start(f32[16,512]{1,0:T(8,128)S(1)} %get-tuple-element.32), channel_id=1, source_target_pairs={{0,1},{1,2},{2,3},{3,4},{4,5},{5,6},{6,7},{8,9},{9,10},{10,11},{11... | collective-permute-start | bytes 98312 | tf_op jit(solution)/shard_map/ppermute | solution.py:33
  40.0 9.7 %collective-permute-start.6 = (f32[24,1920]{1,0:T(8,128)S(1)}, f32[24,1920]{1,0:T(8,128)S(1)}, u32[]{:S(2)}, u32[]{:S(2)}) collective-permute-start(f32[24,1920]{1,0:T(8,128)S(1)} %get-tuple-element.33), channel_id=1, source_target_pairs={{8,0},{16,8},{24,16},{9,1},{17,9},{25,17},{10,2},{18,10},{26,18},{... | collective-permute-start | bytes 552968 | tf_op jit(solution)/shard_map/ppermute | solution.py:33
  43.0 6.6 %collective-permute-start.7 = (f32[24,256]{1,0:T(8,128)S(1)}, f32[24,256]{1,0:T(8,128)S(1)}, u32[]{:S(2)}, u32[]{:S(2)}) collective-permute-start(f32[24,256]{1,0:T(8,128)S(1)} %get-tuple-element.34), channel_id=1, source_target_pairs={{0,8},{8,16},{16,24},{1,9},{9,17},{17,25},{2,10},{10,18},{18,26},{... | collective-permute-start | bytes 73736 | tf_op jit(solution)/shard_map/ppermute | solution.py:33
  45.8 3.8 %copy-start.15 = (f32[6,224]{1,0:T(8,128)S(1)}, f32[6,224]{1,0:T(8,128)}, u32[]{:S(2)}) copy-start(f32[6,224]{1,0:T(8,128)} %constant.68.clone.weight) | copy-start | bytes 16132

commit v10 on v9

--- a/solution.py
+++ b/solution.py
@@ -307,7 +307,7 @@
         one_z,
         one_x,
     ]
-    own_x = placed(line_x["own"], (s.coarse_rows, s.rows), col=8).astype(np.float64)
+    own_x = placed(line_x["own"], (s.coarse_rows, s.rows - 8)).astype(np.float64)
     high_q, low_q = two_parts(coarse_of_x)
     high_r, low_r = two_parts(own_x)
     solve = [
@@ -479,7 +479,7 @@
                 r[plane, at, :] = r[plane, at, :] - out[i] * scale
         return carry
 
-    lax.fori_loop(0, rows // 8, along_y, 0)
+    lax.fori_loop(0, rows // 8, along_y, 0, unroll=True)
 
 
 def started(sources, targets, sems):
@@ -605,7 +605,7 @@
                     xf[b, i, at, :] = sum(odd[a] * float(eigbasis[7 + a, b]) for a in range(6))
         return carry
 
-    lax.fori_loop(0, rows // 8, along_y, 0)
+    lax.fori_loop(0, rows // 8, along_y, 0, unroll=True)
 
     def spectral(modes_of):
         pieces = []
@@ -717,7 +717,7 @@
                     c[7 * v + a, at, :] = out[a]
             return carry
 
-        lax.fori_loop(0, rows // 8, back_y, 0)
+        lax.fori_loop(0, rows // 8, back_y, 0, unroll=True)
 
         for j in range(6):
             down_out[:, lanes * j : lanes * (j + 1)] = c[j]
@@ -729,7 +729,8 @@
         cz[...] = mm(c[...].reshape((ny + 6) * rows, lanes), q_z[...]).reshape(
             ny + 6, rows, 2 * half
         )
-        rz[...] = mm(r[6 : ny + 6].reshape(ny * rows, lanes), r_z[...]).reshape(ny, rows, half)
+        own_rows = r[6 : ny + 6, 8:, :].reshape(ny * (rows - 8), lanes)
+        rz[...] = mm(own_rows, r_z[...]).reshape(ny, rows - 8, half)
         for y in range(ny + 6):
             plane = dot(q_x[...], stacked_rows(cz[y]))
             hx[y] = plane[:rows_c, :half]
@@ -1066,7 +1067,7 @@
             (13, 2, rows, lanes),
             (ny + 6, rows, lanes),
             (ny + 6, rows, 2 * half),
-            (ny, rows, half),
+            (ny, rows - 8, half),
             (ny + 6, s.coarse_rows, half),
             (ny + 6, s.coarse_rows, half),
             (ny, s.coarse_rows, half),

time: 51.7 us -> 51.1 us (0.988)
  Pallas kernels: 22.7 us -> 22.1 us
    pallas_call x8, Pallas kernels: 22.7 us -> 22.1 us  [call(): pl.pallas_call(kernel, out_shape=tuple((shape(*dims) for dims in outputs)...]
where the time goes in v10:
time: 51.1 us; the launch traced here: 50.4 us
  starting transfers between devices  22.9 us (45%)
  Pallas kernels  22.1 us (43%)
  waiting for transfers between devices  4.15 us (8%)
  between operations  1.07 us (2%)
    ppermute x8, starting transfers between devices, shifted(): return lax.ppermute(array, axis, pairs)  22.9 us
    pallas_call x8, Pallas kernels, call(): pl.pallas_call(kernel, out_shape=tuple((shape(*dims) for dims in outputs)...  22.1 us
    ppermute x8, waiting for transfers between devices, shifted(): return lax.ppermute(array, axis, pairs)  4.15 us
  transfers between devices with their start and end apart: 8, of which 2 were waited for; matrix products, arithmetic and copies ran while one was open for 0% of the time, Pallas kernels for 21%

profile of v10, /device:TPU:20, one launch (start us, length us, event | category | flops | bytes accessed | tf_op | source)
XLA Modules:
  0.0 50.4 jit_solution(11217942257021157652)
XLA Ops:
  0.6 2.4 %send.1 = (f32[8,6784]{1,0:T(8,128)S(1)}, f32[32,256]{1,0:T(8,128)S(1)}) custom-call(f32[28,6272]{1,0:T(8,128)} %guess.1, f32[28,6272]{1,0:T(8,128)} %load_hbm.3, f32[280,256]{1,0:T(8,128)} %constant.46.clone.table_hbm, bf16[8,48]{1,0:T(8,128)(2,1)} %constant.47.clone.k_x_hbm), custom_call_target="tpu_custom_call" | custom-call | tf_op jit(solution)/shard_map/send/pallas_call | solution.py:979
  3.1 0.0 copy-start.12
  3.1 0.0 copy-start.13
  3.1 3.5 %collective-permute-start = (f32[8,6784]{1,0:T(8,128)S(1)}, f32[8,6784]{1,0:T(8,128)S(1)}, u32[]{:S(2)}, u32[]{:S(2)}) collective-permute-start(f32[8,6784]{1,0:T(8,128)S(1)} %get-tuple-element.23), channel_id=1, source_target_pairs={{0,8},{8,16},{16,24},{1,9},{9,17},{17,25},{2,10},{10,18},{18,26},{... | collective-permute-start | bytes 651272 | tf_op jit(solution)/shard_map/ppermute | solution.py:33
  6.6 0.0 copy-start.1
  6.7 0.0 copy-start.2
  6.7 0.0 copy-start.3
  6.7 0.0 copy-start.4
  6.7 0.0 copy-start.6
  6.7 0.0 copy-start.8
  6.7 0.0 copy-start.10
  6.7 0.0 copy-start.19
  6.8 3.5 %collective-permute-start.1 = (f32[32,256]{1,0:T(8,128)S(1)}, f32[32,256]{1,0:T(8,128)S(1)}, u32[]{:S(2)}, u32[]{:S(2)}) collective-permute-start(f32[32,256]{1,0:T(8,128)S(1)} %get-tuple-element.22.u_first), channel_id=1, source_target_pairs={{8,0},{16,8},{24,16},{9,1},{17,9},{25,17},{10,2},{18,10},{26,18},{... | collective-permute-start | bytes 98312 | tf_op jit(solution)/shard_map/ppermute | solution.py:33
  10.2 3.9 %residual.1 = (f32[29,32,256]{2,1,0:T(8,128)S(1)}, f32[32,256]{1,0:T(8,128)S(1)}) custom-call(f32[28,6272]{1,0:T(8,128)} %guess.1, f32[28,6272]{1,0:T(8,128)} %load_hbm.3, f32[352,256]{1,0:T(8,128)} %constant.48.clone.table_hbm, bf16[32,192]{1,0:T(8,128)(2,1)} %constant.49.clone.k_x_hbm), custom_call_target="tpu_custom_call" | custom-call | tf_op jit(solution)/shard_map/residual/pallas_call | solution.py:979
  14.1 0.0 collective-permute-done.1.above
  14.1 0.0 collective-permute-done.below
  14.1 0.0 copy-done.12
  14.1 0.0 copy-done.13
  14.1 0.5 joined_x.1
  14.6 1.9 %collective-permute-start.2 = (f32[40,1664]{1,0:T(8,128)S(1)}, f32[40,1664]{1,0:T(8,128)S(1)}, u32[]{:S(2)}, u32[]{:S(2)}) collective-permute-start(f32[40,1664]{1,0:T(8,128)S(1)} %get-tuple-element.26), channel_id=1, source_target_pairs={{0,1},{1,2},{2,3},{3,4},{4,5},{5,6},{6,7},{8,9},{9,10},{10,11},{11... | collective-permute-start | bytes 798728 | tf_op jit(solution)/shard_map/ppermute | solution.py:33
  16.5 3.8 %collective-permute-start.3 = (f32[40,256]{1,0:T(8,128)S(1)}, f32[40,256]{1,0:T(8,128)S(1)}, u32[]{:S(2)}, u32[]{:S(2)}) collective-permute-start(f32[40,256]{1,0:T(8,128)S(1)} %get-tuple-element.25.line), channel_id=1, source_target_pairs={{1,0},{2,1},{3,2},{4,3},{5,4},{6,5},{7,6},{9,8},{10,9},{11,10},{12... | collective-permute-start | bytes 122888 | tf_op jit(solution)/shard_map/ppermute | solution.py:33
  20.4 0.0 copy-done.1
  20.4 0.0 copy-done.2
  20.5 0.0 copy-start.5
  20.5 0.0 copy-start.7
  20.5 0.0 copy-start.9
  20.5 0.0 copy-start.11
  20.5 0.0 copy-start.16
  20.5 0.0 copy-start.17
  20.5 0.0 copy-start.18
  20.5 4.2 %inner.1 = f32[13,2,40,256]{3,2,1,0:T(8,128)S(1)} custom-call(f32[29,40,256]{2,1,0:T(8,128)S(1)} %get-tuple-element.24.r_own, f32[13]{0:T(128)S(1)} %copy-done.19, f32[56,256]{1,0:T(8,128)S(1)} %copy-done.6, bf16[56,120]{1,0:T(8,128)(2,1)S(1)} %copy-done.10, bf16[40,168]{1,0:T(8,128)(2,1)S(1)} %copy-done.8, bf16[256,256]{1,0:T(8,128)(2,1)S(1)} %copy-done.2, ...), custom_call_target="tpu_custom_call" | custom-call | tf_op jit(solution)/shard_map/inner/pallas_call | solution.py:979
  24.7 0.0 copy-start.14
  24.7 0.0 collective-permute-done.3.above
  24.7 0.0 collective-permute-done.2.below
  24.8 0.0 copy-start
  24.8 7.0 %patches.1 = (f32[28,8,256]{2,1,0:T(8,128)S(1)}, f32[28,32,256]{2,1,0:T(8,128)S(1)}, f32[16,16,128]{2,1,0:T(8,128)S(1)}, f32[6,8,128]{2,1,0:T(8,128)S(1)}, f32[4...) custom-call(f32[29,40,256]{2,1,0:T(8,128)S(1)} %get-tuple-element.24.r_own, f32[40,256]{1,0:T(8,128)S(1)} %get-tuple-element.25.line, ...), custom_call_target="tpu_custom_call" | custom-call | tf_op jit(solution)/shard_map/patches/pallas_call | solution.py:979
  31.8 1.9 %collective-permute-start.4 = (f32[40,1792]{1,0:T(8,128)S(1)}, f32[40,1792]{1,0:T(8,128)S(1)}, u32[]{:S(2)}, u32[]{:S(2)}) collective-permute-start(f32[40,1792]{1,0:T(8,128)S(1)} %get-tuple-element.28), channel_id=1, source_target_pairs={{1,0},{2,1},{3,2},{4,3},{5,4},{6,5},{7,6},{9,8},{10,9},{11,10},{12... | collective-permute-start | bytes 860168 | tf_op jit(solution)/shard_map/ppermute | solution.py:33
  33.8 2.4 %collective-permute-start.5 = (f32[16,512]{1,0:T(8,128)S(1)}, f32[16,512]{1,0:T(8,128)S(1)}, u32[]{:S(2)}, u32[]{:S(2)}) collective-permute-start(f32[16,512]{1,0:T(8,128)S(1)} %get-tuple-element.32), channel_id=1, source_target_pairs={{0,1},{1,2},{2,3},{3,4},{4,5},{5,6},{6,7},{8,9},{9,10},{10,11},{11... | collective-permute-start | bytes 98312 | tf_op jit(solution)/shard_map/ppermute | solution.py:33
  36.2 2.8 %collective-permute-done.5.up = f32[16,512]{1,0:T(8,128)S(1)} collective-permute-done((f32[16,512]{1,0:T(8,128)S(1)}, f32[16,512]{1,0:T(8,128)S(1)}, u32[]{:S(2)}, u32[]{:S(2)}) %collective-permute-start.5) | collective-permute-done | bytes 32800 | tf_op jit(solution)/shard_map/ppermute | solution.py:33
  39.0 0.0 collective-permute-done.4.down
  39.0 0.3 join.1
  39.3 3.1 %collective-permute-start.6 = (f32[24,1920]{1,0:T(8,128)S(1)}, f32[24,1920]{1,0:T(8,128)S(1)}, u32[]{:S(2)}, u32[]{:S(2)}) collective-permute-start(f32[24,1920]{1,0:T(8,128)S(1)} %get-tuple-element.33), channel_id=1, source_target_pairs={{8,0},{16,8},{24,16},{9,1},{17,9},{25,17},{10,2},{18,10},{26,18},{... | collective-permute-start | bytes 552968 | tf_op jit(solution)/shard_map/ppermute | solution.py:33
  42.4 2.8 %collective-permute-start.7 = (f32[24,256]{1,0:T(8,128)S(1)}, f32[24,256]{1,0:T(8,128)S(1)}, u32[]{:S(2)}, u32[]{:S(2)}) collective-permute-start(f32[24,256]{1,0:T(8,128)S(1)} %get-tuple-element.34), channel_id=1, source_target_pairs={{0,8},{8,16},{16,24},{1,9},{9,17},{17,25},{2,10},{10,18},{18,26},{... | collective-permute-start | bytes 73736 | tf_op jit(solution)/shard_map/ppermute | solution.py:33
  45.2 0.0 copy-start.15
  45.2 2.5 %base.1 = f32[28,6272]{1,0:T(8,128)S(1)} custom-call(f32[28,6272]{1,0:T(8,128)S(1)} %copy-done, f32[28,256]{1,0:T(8,128)S(1)} %copy-done.14, f32[28,32,256]{2,1,0:T(8,128)S(1)} %get-tuple-element.27.own, f32[40,1792]{1,0:T(8,128)S(1)} %collective-permute-done.4.down), custom_call_target="tpu_custom_call" | custom-call | tf_op jit(solution)/shard_map/base/pallas_call | solution.py:979
  47.7 1.3 %collective-permute-done.7.left = f32[24,256]{1,0:T(8,128)S(1)} collective-permute-done((f32[24,256]{1,0:T(8,128)S(1)}, f32[24,256]{1,0:T(8,128)S(1)}, u32[]{:S(2)}, u32[]{:S(2)}) %collective-permute-start.7) | collective-permute-done | bytes 24608 | tf_op jit(solution)/shard_map/ppermute | solution.py:33
  49.0 0.0 collective-permute-done.6.right
  49.0 1.4 %finish.1 = (f32[28,6272]{1,0:T(8,128)}, f32[12,1152]{1,0:T(8,128)}, f32[4,128]{1,0:T(4,128)}) custom-call(f32[28,6272]{1,0:T(8,128)S(1)} %base.1, f32[6,224]{1,0:T(8,128)S(1)} %copy-done.15, f32[24,1920]{1,0:T(8,128)S(1)} %collective-permute-done.6.right, f32[24,256]{1,0:T(8,128)S(1)} %collective-permute-done.7.left, ...), custom_call_target="tpu_custom_call" | custom-call | tf_op jit(solution)/shard_map/finish/pallas_call | solution.py:979
  (16 shorter events, 0.0 us)
Async XLA Ops:
  3.1 11.0 %copy-start.12 = (f32[40,256]{1,0:T(8,128)S(1)}, f32[40,256]{1,0:T(8,128)}, u32[]{:S(2)}) copy-start(f32[40,256]{1,0:T(8,128)} %constant.51.clone.c_above) | copy-start | bytes 122884
  3.1 11.0 %copy-start.13 = (f32[40,256]{1,0:T(8,128)S(1)}, f32[40,256]{1,0:T(8,128)}, u32[]{:S(2)}) copy-start(f32[40,256]{1,0:T(8,128)} %constant.50.clone.c_below) | copy-start | bytes 122884
  3.1 11.0 %collective-permute-start = (f32[8,6784]{1,0:T(8,128)S(1)}, f32[8,6784]{1,0:T(8,128)S(1)}, u32[]{:S(2)}, u32[]{:S(2)}) collective-permute-start(f32[8,6784]{1,0:T(8,128)S(1)} %get-tuple-element.23), channel_id=1, source_target_pairs={{0,8},{8,16},{16,24},{1,9},{9,17},{17,25},{2,10},{10,18},{18,26},{... | collective-permute-start | bytes 651272 | tf_op jit(solution)/shard_map/ppermute | solution.py:33
  6.6 13.7 %copy-start.1 = (bf16[256,256]{1,0:T(8,128)(2,1)S(1)}, bf16[256,256]{1,0:T(8,128)(2,1)}, u32[]{:S(2)}) copy-start(bf16[256,256]{1,0:T(8,128)(2,1)} %constant.58.clone.b_z) | copy-start | bytes 393220
  6.7 13.7 %copy-start.2 = (bf16[256,256]{1,0:T(8,128)(2,1)S(1)}, bf16[256,256]{1,0:T(8,128)(2,1)}, u32[]{:S(2)}) copy-start(bf16[256,256]{1,0:T(8,128)(2,1)} %constant.56.clone.f_z) | copy-start | bytes 393220
  6.7 13.7 %copy-start.3 = (bf16[256,128]{1,0:T(8,128)(2,1)S(1)}, bf16[256,128]{1,0:T(8,128)(2,1)}, u32[]{:S(2)}) copy-start(bf16[256,128]{1,0:T(8,128)(2,1)} %constant.59.clone.b_z_high) | copy-start | bytes 196612
  6.7 13.7 %copy-start.4 = (bf16[128,256]{1,0:T(8,128)(2,1)S(1)}, bf16[128,256]{1,0:T(8,128)(2,1)}, u32[]{:S(2)}) copy-start(bf16[128,256]{1,0:T(8,128)(2,1)} %constant.57.clone.f_z_low) | copy-start | bytes 196612
  6.7 13.7 %copy-start.6 = (f32[56,256]{1,0:T(8,128)S(1)}, f32[56,256]{1,0:T(8,128)}, u32[]{:S(2)}) copy-start(f32[56,256]{1,0:T(8,128)} %constant.53.clone.sums) | copy-start | bytes 172036
  6.7 13.7 %copy-start.8 = (bf16[40,168]{1,0:T(8,128)(2,1)S(1)}, bf16[40,168]{1,0:T(8,128)(2,1)}, u32[]{:S(2)}) copy-start(bf16[40,168]{1,0:T(8,128)(2,1)} %constant.55.clone.b_x) | copy-start | bytes 40324
  6.7 13.7 %copy-start.10 = (bf16[56,120]{1,0:T(8,128)(2,1)S(1)}, bf16[56,120]{1,0:T(8,128)(2,1)}, u32[]{:S(2)}) copy-start(bf16[56,120]{1,0:T(8,128)(2,1)} %constant.54.clone.f_x) | copy-start | bytes 40324
  6.7 13.7 %copy-start.19 = (f32[13]{0:T(128)S(1)}, f32[13]{0:T(128)}, u32[]{:S(2)}) copy-start(f32[13]{0:T(128)} %constant.52.clone.lam) | copy-start | bytes 160
  6.8 7.3 %collective-permute-start.1 = (f32[32,256]{1,0:T(8,128)S(1)}, f32[32,256]{1,0:T(8,128)S(1)}, u32[]{:S(2)}, u32[]{:S(2)}) collective-permute-start(f32[32,256]{1,0:T(8,128)S(1)} %get-tuple-element.22.u_first), channel_id=1, source_target_pairs={{8,0},{16,8},{24,16},{9,1},{17,9},{25,17},{10,2},{18,10},{26,18},{... | collective-permute-start | bytes 98312 | tf_op jit(solution)/shard_map/ppermute | solution.py:33
  14.6 10.1 %collective-permute-start.2 = (f32[40,1664]{1,0:T(8,128)S(1)}, f32[40,1664]{1,0:T(8,128)S(1)}, u32[]{:S(2)}, u32[]{:S(2)}) collective-permute-start(f32[40,1664]{1,0:T(8,128)S(1)} %get-tuple-element.26), channel_id=1, source_target_pairs={{0,1},{1,2},{2,3},{3,4},{4,5},{5,6},{6,7},{8,9},{9,10},{10,11},{11... | collective-permute-start | bytes 798728 | tf_op jit(solution)/shard_map/ppermute | solution.py:33
  16.5 8.2 %collective-permute-start.3 = (f32[40,256]{1,0:T(8,128)S(1)}, f32[40,256]{1,0:T(8,128)S(1)}, u32[]{:S(2)}, u32[]{:S(2)}) collective-permute-start(f32[40,256]{1,0:T(8,128)S(1)} %get-tuple-element.25.line), channel_id=1, source_target_pairs={{1,0},{2,1},{3,2},{4,3},{5,4},{6,5},{7,6},{9,8},{10,9},{11,10},{12... | collective-permute-start | bytes 122888 | tf_op jit(solution)/shard_map/ppermute | solution.py:33
  20.5 4.3 %copy-start.5 = (f32[256,256]{1,0:T(8,128)S(1)}, f32[256,256]{1,0:T(8,128)}, u32[]{:S(2)}) copy-start(f32[256,256]{1,0:T(8,128)} %constant.61.clone.q_z) | copy-start | bytes 786436
  20.5 4.3 %copy-start.7 = (f32[256,128]{1,0:T(8,128)S(1)}, f32[256,128]{1,0:T(8,128)}, u32[]{:S(2)}) copy-start(f32[256,128]{1,0:T(8,128)} %constant.62.clone.r_z) | copy-start | bytes 393220
  20.5 4.3 %copy-start.9 = (f32[128,128]{1,0:T(8,128)S(1)}, f32[128,128]{1,0:T(8,128)}, u32[]{:S(2)}) copy-start(f32[128,128]{1,0:T(8,128)} %constant.63.clone.o_z) | copy-start | bytes 196612
  20.5 4.3 %copy-start.11 = (f32[40,256]{1,0:T(8,128)S(1)}, f32[40,256]{1,0:T(8,128)}, u32[]{:S(2)}) copy-start(f32[40,256]{1,0:T(8,128)} %constant.60.clone.m_xz) | copy-start | bytes 122884
  20.5 4.3 %copy-start.16 = (bf16[32,120]{1,0:T(8,128)(2,1)S(1)}, bf16[32,120]{1,0:T(8,128)(2,1)}, u32[]{:S(2)}) copy-start(bf16[32,120]{1,0:T(8,128)(2,1)} %constant.65.clone.q_x) | copy-start | bytes 23044
  20.5 4.3 %copy-start.17 = (bf16[16,96]{1,0:T(8,128)(2,1)S(1)}, bf16[16,96]{1,0:T(8,128)(2,1)}, u32[]{:S(2)}) copy-start(bf16[16,96]{1,0:T(8,128)(2,1)} %constant.66.clone.r_x) | copy-start | bytes 9220
  20.5 4.3 %copy-start.18 = (f32[8,16]{1,0:T(8,128)S(1)}, f32[8,16]{1,0:T(8,128)}, u32[]{:S(2)}) copy-start(f32[8,16]{1,0:T(8,128)} %constant.64.clone.o_x) | copy-start | bytes 1540
  24.7 20.5 %copy-start.14 = (f32[28,256]{1,0:T(8,128)S(1)}, f32[28,256]{1,0:T(8,128)}, u32[]{:S(2)}) copy-start(f32[28,256]{1,0:T(8,128)} %constant.67.clone.weight) | copy-start | bytes 86020
  24.8 20.4 %copy-start = (f32[28,6272]{1,0:T(8,128)S(1)}, f32[28,6272]{1,0:T(8,128)}, u32[]{:S(2)}) copy-start(f32[28,6272]{1,0:T(8,128)} %guess.1) | copy-start | bytes 2107396
  31.8 7.2 %collective-permute-start.4 = (f32[40,1792]{1,0:T(8,128)S(1)}, f32[40,1792]{1,0:T(8,128)S(1)}, u32[]{:S(2)}, u32[]{:S(2)}) collective-permute-start(f32[40,1792]{1,0:T(8,128)S(1)} %get-tuple-element.28), channel_id=1, source_target_pairs={{1,0},{2,1},{3,2},{4,3},{5,4},{6,5},{7,6},{9,8},{10,9},{11,10},{12... | collective-permute-start | bytes 860168 | tf_op jit(solution)/shard_map/ppermute | solution.py:33
  33.8 5.2 %collective-permute-start.5 = (f32[16,512]{1,0:T(8,128)S(1)}, f32[16,512]{1,0:T(8,128)S(1)}, u32[]{:S(2)}, u32[]{:S(2)}) collective-permute-start(f32[16,512]{1,0:T(8,128)S(1)} %get-tuple-element.32), channel_id=1, source_target_pairs={{0,1},{1,2},{2,3},{3,4},{4,5},{5,6},{6,7},{8,9},{9,10},{10,11},{11... | collective-permute-start | bytes 98312 | tf_op jit(solution)/shard_map/ppermute | solution.py:33
  39.3 9.7 %collective-permute-start.6 = (f32[24,1920]{1,0:T(8,128)S(1)}, f32[24,1920]{1,0:T(8,128)S(1)}, u32[]{:S(2)}, u32[]{:S(2)}) collective-permute-start(f32[24,1920]{1,0:T(8,128)S(1)} %get-tuple-element.33), channel_id=1, source_target_pairs={{8,0},{16,8},{24,16},{9,1},{17,9},{25,17},{10,2},{18,10},{26,18},{... | collective-permute-start | bytes 552968 | tf_op jit(solution)/shard_map/ppermute | solution.py:33
  42.4 6.6 %collective-permute-start.7 = (f32[24,256]{1,0:T(8,128)S(1)}, f32[24,256]{1,0:T(8,128)S(1)}, u32[]{:S(2)}, u32[]{:S(2)}) collective-permute-start(f32[24,256]{1,0:T(8,128)S(1)} %get-tuple-element.34), channel_id=1, source_target_pairs={{0,8},{8,16},{16,24},{1,9},{9,17},{17,25},{2,10},{10,18},{18,26},{... | collective-permute-start | bytes 73736 | tf_op jit(solution)/shard_map/ppermute | solution.py:33
  45.2 3.8 %copy-start.15 = (f32[6,224]{1,0:T(8,128)S(1)}, f32[6,224]{1,0:T(8,128)}, u32[]{:S(2)}) copy-start(f32[6,224]{1,0:T(8,128)} %constant.68.clone.weight) | copy-start | bytes 16132
